TPU v7x, 32 devices: a whole 2x2x4 slice. The times are simulated.
32 devices in a mesh: dp: 4 (over y, x), seq: 8 (over z, core).
Axes of the slice: x: 2, y: 2, z: 4, core: 2. Of those that a mesh axis runs over, the one named last changes fastest.
Arguments:
- tokens: bfloat16 [4, 1024, 2048], P('dp', 'seq'), may hold values from -6 to 6
- attn_gain: bfloat16 [2048], P(('dp', 'seq')), may hold values from 0.5 to 1.5
- w_query: bfloat16 [2048, 2048], P(('dp', 'seq')), may hold values from -0.125 to 0.125
- w_key: bfloat16 [2048, 2048], P(('dp', 'seq')), may hold values from -0.125 to 0.125
- w_value: bfloat16 [2048, 4096], P(('dp', 'seq')), may hold values from -0.125 to 0.125
- w_decay: bfloat16 [2048, 16], P(('dp', 'seq')), may hold values from -0.125 to 0.125
- w_beta: bfloat16 [2048, 16], P(('dp', 'seq')), may hold values from -0.125 to 0.125
- w_gate: bfloat16 [2048, 4096], P(('dp', 'seq')), may hold values from -0.125 to 0.125
- w_out: bfloat16 [2048, 4096], P(('dp', 'seq')), may hold values from -0.1875 to 0.1875
- conv_query: float32 [4, 2048], replicated, may hold values from -2.5 to 2.5
- conv_key: float32 [4, 2048], replicated, may hold values from -2.5 to 2.5
- conv_value: float32 [4, 4096], replicated, may hold values from -2.5 to 2.5
- decay_log: float32 [16], replicated, may hold values from -9 to -3
- decay_bias: float32 [16], replicated, may hold values from -1 to 1
- out_gain: float32 [256], replicated, may hold values from 0.5 to 1.5
- mlp_gain: bfloat16 [2048], P(('dp', 'seq')), may hold values from 0.5 to 1.5
- w_hidden: bfloat16 [2048, 5632], P(('dp', 'seq')), may hold values from -0.125 to 0.125
- w_up: bfloat16 [2048, 5632], P(('dp', 'seq')), may hold values from -0.125 to 0.125
- w_down: bfloat16 [2048, 5632], P(('dp', 'seq')), may hold values from -0.15625 to 0.15625
- offsets: int32 [4, 1024], P('dp', 'seq'), may hold values from 0 to 1023, as said below
- cotangent: bfloat16 [4, 1024, 2048], P('dp', 'seq'), may hold values from -6 to 6
Outputs:
- output: bfloat16 [4, 1024, 2048], P('dp', 'seq')
- grad_tokens: bfloat16 [4, 1024, 2048], P('dp', 'seq')
- grad_attn_gain: float32 [2048], P(('dp', 'seq'))
- grad_w_query: float32 [2048, 2048], P(('dp', 'seq'))
- grad_w_key: float32 [2048, 2048], P(('dp', 'seq'))
- grad_w_value: float32 [2048, 4096], P(('dp', 'seq'))
- grad_w_decay: float32 [2048, 16], P(('dp', 'seq'))
- grad_w_beta: float32 [2048, 16], P(('dp', 'seq'))
- grad_w_gate: float32 [2048, 4096], P(('dp', 'seq'))
- grad_w_out: float32 [2048, 4096], P(('dp', 'seq'))
- grad_conv_query: float32 [4, 2048], replicated
- grad_conv_key: float32 [4, 2048], replicated
- grad_conv_value: float32 [4, 4096], replicated
- grad_decay_log: float32 [16], replicated
- grad_decay_bias: float32 [16], replicated
- grad_out_gain: float32 [256], replicated
- grad_mlp_gain: float32 [2048], P(('dp', 'seq'))
- grad_w_hidden: float32 [2048, 5632], P(('dp', 'seq'))
- grad_w_up: float32 [2048, 5632], P(('dp', 'seq'))
- grad_w_down: float32 [2048, 5632], P(('dp', 'seq'))
Inputs may be any that keep to these rules, and one draw needn't show every extreme that they name: `offsets`: every packed row begins a document: its first position has offset 0. Along a row, a position's offset is 0 where a new document starts and otherwise one more than the previous position's offset. The first packed row holds a single document.
All inputs are finite; a program needn't handle non-finite values.
Results may differ from a plain program's by a relative error of at most 0.017.
Values may be sent and summed in bfloat16 or wider, within the bound.
No kernel may reach another device: no remote copies, remote signals or barrier semaphores. Data moves between devices by JAX's collectives and lax.ppermute only.
A program may use at most 512 MiB of HBM per device.

v0:
```python
import jax
import jax.numpy as jnp
from jax import lax
from jax.sharding import PartitionSpec as P

KERNEL = 4


HIGHEST = lax.Precision.HIGHEST


def passed_along(array, axis, by):
    count = lax.axis_size(axis)
    pairs = [(i, i + by) for i in range(count) if 0 <= i + by < count]
    return lax.ppermute(array, axis, pairs)


def rms_scale(value):
    return lax.rsqrt(jnp.mean(value * value, axis=-1, keepdims=True) + 1e-05)


def unit_rows(value):
    return value * lax.rsqrt(jnp.sum(value * value, axis=-1, keepdims=True) + 1e-06)


def norm_apply(value, gain_full):
    return value * rms_scale(value) * gain_full


def low_dot(left, weight):
    return jnp.einsum("rtd,de->rte", left, weight, preferred_element_type=jnp.float32)


def back_dot(left, weight):
    return jnp.einsum("rte,de->rtd", left, weight, preferred_element_type=jnp.float32)


def weight_grad(left, right):
    return jnp.einsum("rtd,rte->de", left, right, preferred_element_type=jnp.float32)


def causal_taps(extended, kernel_taps, offsets):
    tok_count = offsets.shape[1]
    rim_len = extended.shape[1] - tok_count
    summed = kernel_taps[0] * extended[:, rim_len:]
    for shift_by in range(1, rim_len + 1):
        delayed = extended[:, rim_len - shift_by : rim_len - shift_by + tok_count]
        summed = summed + kernel_taps[shift_by] * jnp.where(
            (offsets >= shift_by)[..., None], delayed, 0.0
        )
    return summed


def block_rule(carried, pieces):
    queries, key_vecs, values, beta_rows, logdecay, block_offsets = pieces
    block_len = queries.shape[2]
    where_t = jnp.arange(block_len, dtype=jnp.int32)
    distance = where_t[:, None] - where_t[None, :]
    same_doc = (distance >= 0) & (block_offsets[:, None, :, None] >= distance)
    total_log = jnp.cumsum(logdecay, axis=-1)
    exponent = total_log[..., :, None] - total_log[..., None, :]
    decay_pair = jnp.where(same_doc, jnp.exp(jnp.where(same_doc, exponent, 0.0)), 0.0)
    from_start = jnp.where(block_offsets[:, None, :] > where_t, jnp.exp(total_log), 0.0)
    key_key = jnp.einsum("rhtk,rhsk->rhts", key_vecs, key_vecs, precision=HIGHEST)
    strict_lower = jnp.where(distance > 0, decay_pair * key_key, 0.0) * beta_rows[..., :, None]
    recalled = jnp.einsum("rhvk,rhtk->rhtv", carried, key_vecs, precision=HIGHEST)
    target = beta_rows[..., None] * (values - from_start[..., None] * recalled)
    identity_block = jnp.eye(block_len, dtype=jnp.float32)
    updates = jax.scipy.linalg.solve_triangular(
        strict_lower + identity_block, target, lower=True, unit_diagonal=True
    )
    query_key = jnp.einsum("rhtk,rhsk->rhts", queries, key_vecs, precision=HIGHEST)
    outputs = from_start[..., None] * jnp.einsum(
        "rhvk,rhtk->rhtv", carried, queries, precision=HIGHEST
    )
    outputs = outputs + jnp.einsum(
        "rhts,rhsv->rhtv", decay_pair * query_key, updates, precision=HIGHEST
    )
    to_end = decay_pair[..., block_len - 1, :]
    advanced = from_start[..., block_len - 1][..., None, None] * carried
    advanced = advanced + jnp.einsum(
        "rhsv,rhsk->rhvk", updates * to_end[..., None], key_vecs, precision=HIGHEST
    )
    return (advanced, outputs)


def group_rule(carried, queries, key_vecs, values, beta_rows, logdecay, offsets):
    row_count, tok_count = (queries.shape[0], queries.shape[1])
    block_len = min(64, tok_count)
    blocks = tok_count // block_len

    def to_blocks(array_in):
        shaped = array_in.reshape((row_count, blocks, block_len) + array_in.shape[2:])
        shaped = jnp.moveaxis(shaped, 1, 0)
        if shaped.ndim > 3:
            shaped = jnp.moveaxis(shaped, 3, 2)
        return shaped

    pieces = tuple(
        (
            to_blocks(array_in)
            for array_in in (queries, key_vecs, values, beta_rows, logdecay, offsets)
        )
    )
    final_state, outputs = lax.scan(block_rule, carried, pieces)
    outputs = jnp.moveaxis(jnp.moveaxis(outputs, 2, 3), 0, 1)
    return (outputs.reshape((row_count, tok_count) + outputs.shape[3:]), final_state)


def fetch_mixer(
    gain_part, query_part, key_part, value_part, decay_part, beta_part, gate_part, out_part
):
    return (
        lax.all_gather(gain_part, ("dp", "seq"), axis=0, tiled=True),
        lax.all_gather(query_part, ("dp", "seq"), axis=0, tiled=True),
        lax.all_gather(key_part, ("dp", "seq"), axis=0, tiled=True),
        lax.all_gather(value_part, ("dp", "seq"), axis=0, tiled=True),
        lax.all_gather(decay_part, ("dp", "seq"), axis=0, tiled=True),
        lax.all_gather(beta_part, ("dp", "seq"), axis=0, tiled=True),
        lax.all_gather(gate_part, ("dp", "seq"), axis=0, tiled=True),
        lax.all_gather(out_part, ("dp", "seq"), axis=0, tiled=True),
    )


def local(
    tokens,
    attn_gain,
    w_query,
    w_key,
    w_value,
    w_decay,
    w_beta,
    w_gate,
    w_out,
    conv_query,
    conv_key,
    conv_value,
    decay_log,
    decay_bias,
    out_gain,
    mlp_gain,
    w_hidden,
    w_up,
    w_down,
    offsets,
    cotangent,
):
    row_count, tok_count = (tokens.shape[0], tokens.shape[1])
    head_count = decay_log.shape[0]
    rim_len = KERNEL - 1
    gain_attn, query_full, key_full, value_full, decay_full, beta_full, gate_full, out_full = (
        fetch_mixer(attn_gain, w_query, w_key, w_value, w_decay, w_beta, w_gate, w_out)
    )
    inputs = tokens.astype(jnp.float32)
    attn_normed_f, attn_norm_back = jax.vjp(norm_apply, inputs, gain_attn.astype(jnp.float32))
    attn_normed = attn_normed_f.astype(jnp.bfloat16)
    pre_query = low_dot(attn_normed, query_full).astype(jnp.bfloat16)
    pre_key = low_dot(attn_normed, key_full).astype(jnp.bfloat16)
    pre_value = low_dot(attn_normed, value_full).astype(jnp.bfloat16)
    pre_gate = low_dot(attn_normed, gate_full)
    normed_wide = attn_normed.astype(jnp.float32)
    small_weights = jnp.concatenate([decay_full, beta_full], axis=1).astype(jnp.float32)
    small_pre = jnp.einsum("rtd,de->rte", normed_wide, small_weights, precision=HIGHEST)
    pre_decay = small_pre[..., :head_count]
    pre_beta = small_pre[..., head_count:]
    left_rims = passed_along(
        (
            pre_query[:, tok_count - rim_len :],
            pre_key[:, tok_count - rim_len :],
            pre_value[:, tok_count - rim_len :],
        ),
        "seq",
        1,
    )
    ext_query = jnp.concatenate([left_rims[0], pre_query], axis=1).astype(jnp.float32)
    ext_key = jnp.concatenate([left_rims[1], pre_key], axis=1).astype(jnp.float32)
    ext_value = jnp.concatenate([left_rims[2], pre_value], axis=1).astype(jnp.float32)

    def front_piece(
        query_in,
        key_in,
        value_in,
        taps_query,
        taps_key,
        taps_value,
        decay_in,
        beta_in,
        log_rates,
        rate_bias,
    ):
        shape_rows = (row_count, tok_count, head_count, -1)
        queries_out = unit_rows(
            jax.nn.silu(causal_taps(query_in, taps_query, offsets)).reshape(shape_rows)
        )
        queries_out = queries_out * queries_out.shape[-1] ** (-0.5)
        keys_out = unit_rows(
            jax.nn.silu(causal_taps(key_in, taps_key, offsets)).reshape(shape_rows)
        )
        values_out = jax.nn.silu(causal_taps(value_in, taps_value, offsets)).reshape(shape_rows)
        betas_out = jax.nn.sigmoid(beta_in)
        decay_out = -jnp.exp(log_rates) * jax.nn.softplus(decay_in + rate_bias)
        return (queries_out, keys_out, values_out, betas_out, decay_out)

    fronted, front_back = jax.vjp(
        front_piece,
        ext_query,
        ext_key,
        ext_value,
        conv_query,
        conv_key,
        conv_value,
        pre_decay,
        pre_beta,
        decay_log,
        decay_bias,
    )
    queries, key_vecs, values, beta_rows, logdecay = fronted
    key_dim = key_vecs.shape[-1]
    value_dim = values.shape[-1]

    def local_rule(initial, queries_in, keys_in, values_in, betas_in, decay_in):
        return group_rule(initial, queries_in, keys_in, values_in, betas_in, decay_in, offsets)

    identity_keys = jnp.broadcast_to(
        jnp.eye(key_dim, dtype=jnp.float32), (row_count, head_count, key_dim, key_dim)
    )
    zero_state = jnp.zeros((row_count, head_count, value_dim, key_dim), jnp.float32)
    stacked_values = jnp.concatenate(
        [values, jnp.zeros((row_count, tok_count, head_count, key_dim), jnp.float32)], axis=3
    )
    stacked_out, stacked_end = local_rule(
        jnp.concatenate([zero_state, identity_keys], axis=2),
        queries,
        key_vecs,
        stacked_values,
        beta_rows,
        logdecay,
    )
    local_out = stacked_out[..., :value_dim]
    start_map = stacked_out[..., value_dim:]
    local_end = stacked_end[:, :, :value_dim]
    passage = stacked_end[:, :, value_dim:]

    def relay_step(step_index, relay_carry):
        incoming_now = passed_along(relay_carry[0], "seq", 1)
        advanced = local_end + jnp.einsum(
            "rhvk,rhkj->rhvj", incoming_now, passage, precision=HIGHEST
        )
        return (advanced, incoming_now)

    relay_end, incoming = lax.fori_loop(
        0, lax.axis_size("seq") - 1, relay_step, (local_end, zero_state)
    )
    mixed = local_out + jnp.einsum("rhvk,rthk->rthv", incoming, start_map, precision=HIGHEST)

    def gate_out(mixed_in, gate_in, gain_in):
        gate_rows = jax.nn.silu(gate_in).reshape(mixed_in.shape)
        return (mixed_in * rms_scale(mixed_in) * gain_in * gate_rows).reshape(
            row_count, tok_count, -1
        )

    gated, gate_back = jax.vjp(gate_out, mixed, pre_gate, out_gain)
    gated_low = gated.astype(jnp.bfloat16)
    middle = inputs + back_dot(gated_low, out_full)
    gain_mlp, hidden_full, up_full, down_full = (
        lax.all_gather(mlp_gain, ("dp", "seq"), axis=0, tiled=True),
        lax.all_gather(w_hidden, ("dp", "seq"), axis=0, tiled=True),
        lax.all_gather(w_up, ("dp", "seq"), axis=0, tiled=True),
        lax.all_gather(w_down, ("dp", "seq"), axis=0, tiled=True),
    )
    mlp_normed_f, mlp_norm_back = jax.vjp(norm_apply, middle, gain_mlp.astype(jnp.float32))
    mlp_normed = mlp_normed_f.astype(jnp.bfloat16)
    hidden_pre = low_dot(mlp_normed, hidden_full)
    up_pre = low_dot(mlp_normed, up_full)

    def swiglu(hidden_in, up_in):
        return jax.nn.silu(hidden_in) * up_in

    product_f, swiglu_back = jax.vjp(swiglu, hidden_pre, up_pre)
    product = product_f.astype(jnp.bfloat16)
    output = middle + back_dot(product, down_full)
    d_output = cotangent.astype(jnp.float32)
    d_mlp = d_output.astype(jnp.bfloat16)
    d_product = low_dot(d_mlp, down_full)
    grad_down = weight_grad(d_mlp, product)
    d_hidden_f, d_up_f = swiglu_back(d_product)
    d_hidden = d_hidden_f.astype(jnp.bfloat16)
    d_up = d_up_f.astype(jnp.bfloat16)
    grad_hidden = weight_grad(mlp_normed, d_hidden)
    grad_up = weight_grad(mlp_normed, d_up)
    d_mlp_normed = back_dot(d_hidden, hidden_full) + back_dot(d_up, up_full)
    d_middle_norm, grad_mlp_gain = mlp_norm_back(d_mlp_normed)
    d_middle = d_output + d_middle_norm
    mlp_grads = (
        lax.psum_scatter(grad_mlp_gain, ("dp", "seq"), scatter_dimension=0, tiled=True),
        lax.psum_scatter(grad_hidden, ("dp", "seq"), scatter_dimension=0, tiled=True),
        lax.psum_scatter(grad_up, ("dp", "seq"), scatter_dimension=0, tiled=True),
        lax.psum_scatter(grad_down, ("dp", "seq"), scatter_dimension=0, tiled=True),
    )
    d_branch = d_middle.astype(jnp.bfloat16)
    held_mixer = lax.optimization_barrier(
        (attn_gain, w_query, w_key, w_value, w_decay, w_beta, w_gate, w_out, d_branch)
    )
    gain_attn, query_full, key_full, value_full, decay_full, beta_full, gate_full, out_full = (
        fetch_mixer(*held_mixer[:8])
    )
    d_gated = low_dot(d_branch, out_full)
    grad_out = weight_grad(d_branch, gated_low)
    d_mixed, d_gate_f, grad_out_gain = gate_back(d_gated)
    d_gate = d_gate_f.astype(jnp.bfloat16)
    local_term = jnp.einsum("rthv,rthk->rhvk", d_mixed, start_map, precision=HIGHEST)

    def grad_step(step_index, relay_carry):
        incoming_now = passed_along(relay_carry[0], "seq", -1)
        advanced = local_term + jnp.einsum(
            "rhvk,rhjk->rhvj", incoming_now, passage, precision=HIGHEST
        )
        return (advanced, incoming_now)

    relay_unused, d_end = lax.fori_loop(
        0, lax.axis_size("seq") - 1, grad_step, (local_term, zero_state)
    )
    primal, rule_back = jax.vjp(
        local_rule, incoming, queries, key_vecs, values, beta_rows, logdecay
    )
    d_start, d_queries, d_keys, d_values, d_betas, d_logdecay = rule_back((d_mixed, d_end))
    back_front = front_back((d_queries, d_keys, d_values, d_betas, d_logdecay))
    d_ext_query, d_ext_key, d_ext_value = (back_front[0], back_front[1], back_front[2])
    grad_conv_query, grad_conv_key, grad_conv_value = (back_front[3], back_front[4], back_front[5])
    d_pre_decay, d_pre_beta, grad_decay_log, grad_decay_bias = (
        back_front[6],
        back_front[7],
        back_front[8],
        back_front[9],
    )
    right_rims = (
        passed_along(d_ext_query[:, :rim_len].astype(jnp.bfloat16), "seq", -1).astype(jnp.float32),
        passed_along(d_ext_key[:, :rim_len].astype(jnp.bfloat16), "seq", -1).astype(jnp.float32),
        passed_along(d_ext_value[:, :rim_len].astype(jnp.bfloat16), "seq", -1).astype(jnp.float32),
    )

    def own_rows(extended, returned):
        return extended[:, rim_len:].at[:, tok_count - rim_len :].add(returned).astype(jnp.bfloat16)

    d_pre_query = own_rows(d_ext_query, right_rims[0])
    d_pre_key = own_rows(d_ext_key, right_rims[1])
    d_pre_value = own_rows(d_ext_value, right_rims[2])
    small_weights = jnp.concatenate([decay_full, beta_full], axis=1).astype(jnp.float32)
    d_small = jnp.concatenate([d_pre_decay, d_pre_beta], axis=2)
    d_attn_normed = back_dot(d_pre_query, query_full) + back_dot(d_pre_key, key_full)
    d_attn_normed = d_attn_normed + back_dot(d_pre_value, value_full) + back_dot(d_gate, gate_full)
    d_attn_normed = d_attn_normed + jnp.einsum(
        "rte,de->rtd", d_small, small_weights, precision=HIGHEST
    )
    grad_query = weight_grad(attn_normed, d_pre_query)
    grad_key = weight_grad(attn_normed, d_pre_key)
    grad_value = weight_grad(attn_normed, d_pre_value)
    grad_gate = weight_grad(attn_normed, d_gate)
    grad_small = jnp.einsum("rtd,rte->de", normed_wide, d_small, precision=HIGHEST)
    d_tokens_norm, grad_attn_gain = attn_norm_back(d_attn_normed)
    grad_tokens = (d_middle + d_tokens_norm).astype(jnp.bfloat16)
    mixer_grads = (
        lax.psum_scatter(grad_attn_gain, ("dp", "seq"), scatter_dimension=0, tiled=True),
        lax.psum_scatter(grad_query, ("dp", "seq"), scatter_dimension=0, tiled=True),
        lax.psum_scatter(grad_key, ("dp", "seq"), scatter_dimension=0, tiled=True),
        lax.psum_scatter(grad_value, ("dp", "seq"), scatter_dimension=0, tiled=True),
        lax.psum_scatter(
            grad_small[:, :head_count], ("dp", "seq"), scatter_dimension=0, tiled=True
        ),
        lax.psum_scatter(
            grad_small[:, head_count:], ("dp", "seq"), scatter_dimension=0, tiled=True
        ),
        lax.psum_scatter(grad_gate, ("dp", "seq"), scatter_dimension=0, tiled=True),
        lax.psum_scatter(grad_out, ("dp", "seq"), scatter_dimension=0, tiled=True),
    )
    small_sums = lax.psum(
        (
            grad_conv_query,
            grad_conv_key,
            grad_conv_value,
            grad_decay_log,
            grad_decay_bias,
            grad_out_gain,
        ),
        ("dp", "seq"),
    )
    return (
        output.astype(jnp.bfloat16),
        grad_tokens,
        mixer_grads[0],
        mixer_grads[1],
        mixer_grads[2],
        mixer_grads[3],
        mixer_grads[4],
        mixer_grads[5],
        mixer_grads[6],
        mixer_grads[7],
        small_sums[0],
        small_sums[1],
        small_sums[2],
        small_sums[3],
        small_sums[4],
        small_sums[5],
        mlp_grads[0],
        mlp_grads[1],
        mlp_grads[2],
        mlp_grads[3],
    )


def solution(mesh):
    in_specs = (
        P("dp", "seq", None),
        P(("dp", "seq")),
        P(("dp", "seq"), None),
        P(("dp", "seq"), None),
        P(("dp", "seq"), None),
        P(("dp", "seq"), None),
        P(("dp", "seq"), None),
        P(("dp", "seq"), None),
        P(("dp", "seq"), None),
        P(),
        P(),
        P(),
        P(),
        P(),
        P(),
        P(("dp", "seq")),
        P(("dp", "seq"), None),
        P(("dp", "seq"), None),
        P(("dp", "seq"), None),
        P("dp", "seq"),
        P("dp", "seq", None),
    )
    out_specs = (
        P("dp", "seq", None),
        P("dp", "seq", None),
        P(("dp", "seq")),
        P(("dp", "seq"), None),
        P(("dp", "seq"), None),
        P(("dp", "seq"), None),
        P(("dp", "seq"), None),
        P(("dp", "seq"), None),
        P(("dp", "seq"), None),
        P(("dp", "seq"), None),
        P(),
        P(),
        P(),
        P(),
        P(),
        P(),
        P(("dp", "seq")),
        P(("dp", "seq"), None),
        P(("dp", "seq"), None),
        P(("dp", "seq"), None),
    )
    return jax.shard_map(local, mesh=mesh, in_specs=in_specs, out_specs=out_specs, check_vma=False)
```

profile of v0, /device:TPU:0, one launch (start us, length us, event | category | flops | bytes accessed | tf_op | source)
XLA Modules:
  0.0 5672.9 jit_solution(13379226251824947460)
XLA Ops:
  13.3 42.5 all-reduce.33
  57.7 42.0 all-gather.1
  99.9 37.3 all-gather
  149.1 22.4 all-gather.18.cloned.1.call-done
  191.5 96.6 %all-gather.20.cloned.1.call-done = bf16[2048,4096]{1,0:T(8,128)(2,1)} async-done(((bf16[64,4096]{1,0:T(8,128)(2,1)}), bf16[2048,4096]{1,0:T(8,128)(2,1)}) %all-gather.20.cloned.1.call-update) | async-done | bytes 16777232 | tf_op jit(solution)/shard_map/all_gather | solution.py:117
  288.0 8.4 fusion.221
  299.6 104.4 %all-gather.24.cloned.1.call-done = bf16[2048,4096]{1,0:T(8,128)(2,1)} async-done(((bf16[64,4096]{1,0:T(8,128)(2,1)}), bf16[2048,4096]{1,0:T(8,128)(2,1)}) %all-gather.24.cloned.1.call-update) | async-done | bytes 16777232 | tf_op jit(solution)/shard_map/all_gather | solution.py:120
  404.0 10.7 fusion.242
  428.0 234.0 %while.126 = (s32[]{:T(128)}, f32[1,16,384,128]{3,2,1,0:T(8,128)S(1)}, f32[2,1,16,64,384]{4,3,2,1,0:T(8,128)}, s32[2,1,64]{2,1,0:T(1,128)}, f32[2,1,16,64]{3,2,1...) while((s32[]{:T(128)}, ...), condition=%wide.region_5.6_spmd, body=%wide.region_3.5_spmd.sunk | while | flops 2622143488 | bytes 75223688 | solution.py:105
  443.1 80.0 %custom-call.49 = f32[16,1,64,64]{2,3,1,0:T(8,128)} custom-call(f32[16,1,64,64]{3,2,1,0:T(8,128)} %fusion.475), custom_call_target="InvertDiagBlocksLowerTriangular" | custom-call | tf_op jit(solution)/shard_map/while/body/eval_jaxpr/jit(_solve_triangular)/vmap()/triangular_solve | solution.py:69
  559.7 80.0 %custom-call.49 = f32[16,1,64,64]{2,3,1,0:T(8,128)} custom-call(f32[16,1,64,64]{3,2,1,0:T(8,128)} %fusion.475), custom_call_target="InvertDiagBlocksLowerTriangular" | custom-call | tf_op jit(solution)/shard_map/while/body/eval_jaxpr/jit(_solve_triangular)/vmap()/triangular_solve | solution.py:69
  669.6 381.5 %while.127 = (s32[]{:T(128)}, f32[1,16,256,128]{3,2,1,0:T(8,128)}, f32[1,16,256,128]{3,2,1,0:T(8,128)}, f32[1,16,256,128]{3,2,1,0:T(8,128)}, f32[1,16,128,128]{3,2,1,0:T(8,128)S(1)}, /*index=5*/s32[]{:T(128)}) while((s32[]{:T(128)}, f32[1,16,256,128]{3,2,1,0:T(8,128)}, f32[1,16,256,128]{3,2,1,0:T(8,128)}, f32[1,16,256,128]{3,2,1,0:T(8,128)}, ...), condition=%wide.region_7.8_spmd, body=%wide.region_6.7_spmd.sunk | while | flops 805830656 | bytes 24117384 | solution.py:251
  681.0 42.9 collective-permute-start
  732.9 56.1 collective-permute-start
  798.0 58.0 %collective-permute-start = (f32[1,16,256,128]{3,2,1,0:T(8,128)}, f32[1,16,256,128]{3,2,1,0:T(8,128)S(1)}, u32[]{:S(2)}, u32[]{:S(2)}) collective-permute-start(f32[1,16,256,128]{3,2,1,0:T(8,128)} %get-tuple-element.3067), channel_id=1, source_target_pairs={{0,1},{1,2},{2,3},{3,4},{4,5},{5,6},{6,7},{8,9},{9,10},{10,11},{11... | collective-permute-start | bytes 6291464 | tf_op jit(solution)/shard_map/while/body/eval_jaxpr/ppermute | solution.py:15
  865.0 55.4 collective-permute-start
  929.3 56.1 collective-permute-start
  994.5 47.6 collective-permute-start
  1058.7 11.5 multiply_reduce_fusion.16
  1070.4 12.6 fusion.345
  1083.0 12.4 fusion.346
  1095.5 14.9 multiply_convert_fusion
  1110.3 13.9 fusion.347
  1124.2 13.1 fusion.266
  1152.8 228.5 %while.129 = (s32[]{:T(128)}, f32[1,16,256,128]{3,2,1,0:T(8,128)S(1)}, pred[2,1,16,64,64]{4,3,2,1,0:T(32,128)(4,1)S(1)}, f32[2,1,16,64,64]{4,3,2,1,0:T(8,128)}, ...) while((s32[]{:T(128)}, ...), condition=%wide.region_16.17_spmd.clone, body=%wide.region_14.16_spmd.clone.sunk | while | flops 1615244416 | bytes 87821280 | solution.py:105
  1171.1 80.0 %custom-call.50 = f32[16,1,64,64]{2,3,1,0:T(8,128)} custom-call(f32[16,1,64,64]{3,2,1,0:T(8,128)} %add_bitcast_fusion.4), custom_call_target="InvertDiagBlocksLowerTriangular" | custom-call | tf_op jit(solution)/shard_map/jvp()/while/body/eval_jaxpr/jit(_solve_triangular)/vmap()/triangular_solve | solution.py:69
  1285.2 80.0 %custom-call.50 = f32[16,1,64,64]{2,3,1,0:T(8,128)} custom-call(f32[16,1,64,64]{3,2,1,0:T(8,128)} %add_bitcast_fusion.4), custom_call_target="InvertDiagBlocksLowerTriangular" | custom-call | tf_op jit(solution)/shard_map/jvp()/while/body/eval_jaxpr/jit(_solve_triangular)/vmap()/triangular_solve | solution.py:69
  1381.3 75.7 %all-gather.3 = bf16[32,64,16]{1,2,0:T(8,128)(2,1)S(1)} all-gather(bf16[1,64,16]{1,2,0:T(8,128)(2,1)S(1)} %bitcast.1020), channel_id=1, replica_groups=mesh['dp'=4,'seq'=8] {'dp','seq'}, dimensions={0}, use_global_device_ids=true | all-gather | bytes 67584 | tf_op jit(solution)/shard_map/all_gather | solution.py:119
  1457.8 40.1 all-gather.2
  1498.9 14.5 fusion.288
  1532.7 290.0 %while.128 = (s32[]{:T(128)}, f32[1,16,256,128]{3,2,1,0:T(8,128)}, f32[1,16,256,128]{3,2,1,0:T(8,128)}, f32[1,16,256,128]{3,2,1,0:T(8,128)}, f32[1,16,128,128]{3,2,1,0:T(8,128)}, /*index=5*/s32[]{:T(128)}) while((s32[]{:T(128)}, f32[1,16,256,128]{3,2,1,0:T(8,128)}, f32[1,16,256,128]{3,2,1,0:T(8,128)}, f32[1,16,256,128]{3,2,1,0:T(8,128)}, ...), condition=%wide.region_13.14_spmd, body=%wide.region_12.13_spmd.sunk | while | flops 805830656 | bytes 24117384 | solution.py:320
  1548.2 64.5 %collective-permute-done.1 = f32[1,16,256,128]{3,2,1,0:T(8,128)S(1)} collective-permute-done((f32[1,16,256,128]{3,2,1,0:T(8,128)}, f32[1,16,256,128]{3,2,1,0:T(8,128)S(1)}, u32[]{:S(2)}, u32[]{:S(2)}) %collective-permute-start.1) | collective-permute-done | bytes 2097184 | tf_op jit(solution)/shard_map/while/body/eval_jaxpr/ppermute | solution.py:15
  1621.9 29.3 collective-permute-done.1
  1660.3 45.8 collective-permute-done.1
  1706.1 8.0 fusion.484
  1715.4 28.5 collective-permute-done.1
  1753.1 26.3 collective-permute-done.1
  1788.6 26.3 collective-permute-done.1
  1827.6 250.5 %while.130 = (s32[]{:T(128)}, f32[1,16,256,128]{3,2,1,0:T(8,128)S(1)}, f32[2,1,16,64,128]{4,2,3,0,1:T(8,128)}, f32[2,1,16,64,128]{4,2,3,0,1:T(8,128)}, f32[2,1,1...) while((s32[]{:T(128)}, ...), condition=%wide.region_27.28_spmd.clone, body=%wide.region_17.27_spmd.clone.sunk | while | flops 3684708352 | bytes 211715088 | solution.py:105
  1844.9 80.0 %custom-call.51 = f32[16,1,64,64]{2,3,1,0:T(8,128)} custom-call(f32[16,1,64,64]{3,2,1,0:T(8,128)} %add_bitcast_fusion.5), custom_call_target="InvertDiagBlocksLowerTriangular" | custom-call | tf_op jit(solution)/shard_map/transpose(jvp())/while/body/eval_jaxpr/jit(_solve_triangular)/vmap()/triangular_solve | solution.py:69
  1966.2 80.0 %custom-call.51 = f32[16,1,64,64]{2,3,1,0:T(8,128)} custom-call(f32[16,1,64,64]{3,2,1,0:T(8,128)} %add_bitcast_fusion.5), custom_call_target="InvertDiagBlocksLowerTriangular" | custom-call | tf_op jit(solution)/shard_map/transpose(jvp())/while/body/eval_jaxpr/jit(_solve_triangular)/vmap()/triangular_solve | solution.py:69
  2124.8 12.7 fusion.348
  2151.3 12.7 fusion.269
  2177.4 8.3 fusion.282
  2185.9 8.2 fusion.279
  2195.5 13.4 fusion.286
  2210.4 18.0 fusion.349
  2229.7 17.9 fusion.350
  2249.1 17.9 convolution_bitcast_fusion.4
  2267.0 42.4 copy.291
  2310.6 13.3 fusion.322
  2325.1 13.2 fusion.267
  2339.6 12.9 fusion.230
  2356.5 112.6 %reduce-scatter.31.cloned.1.call-done = f32[64,16]{1,0:T(8,128)} async-done(((f32[2048,16]{1,0:T(8,128)}), f32[64,16]{1,0:T(8,128)}) %reduce-scatter.31.cloned.1.call-update) | async-done | bytes 4112
  2470.6 132.2 %reduce-scatter.33.cloned.1.call-done = f32[64,16]{1,0:T(8,128)} async-done(((f32[2048,16]{1,0:T(8,128)}), f32[64,16]{1,0:T(8,128)}) %reduce-scatter.33.cloned.1.call-update) | async-done | bytes 4112
  2604.2 119.3 %all-reduce.37.cloned.1.call-done = f32[4,4096]{1,0:T(4,128)} async-done(((f32[4,4096]{1,0:T(4,128)}), f32[4,4096]{1,0:T(4,128)}) %all-reduce.37.cloned.1.call-update) | async-done | bytes 65552 | tf_op jit(solution)/shard_map/psum | solution.py:376
  2723.6 190.3 %reduce-scatter.17.cloned.1.call-done = f32[64,2048]{1,0:T(8,128)} async-done(((f32[2048,2048]{1,0:T(8,128)}), f32[64,2048]{1,0:T(8,128)}) %reduce-scatter.17.cloned.1.call-update) | async-done | bytes 524304 | tf_op jit(solution)/shard_map/reduce_scatter | solution.py:364
  2913.9 187.4 %reduce-scatter.19.cloned.1.call-done = f32[64,2048]{1,0:T(8,128)} async-done(((f32[2048,2048]{1,0:T(8,128)}), f32[64,2048]{1,0:T(8,128)}) %reduce-scatter.19.cloned.1.call-update) | async-done | bytes 524304 | tf_op jit(solution)/shard_map/reduce_scatter | solution.py:365
  3101.2 361.6 %reduce-scatter.25.cloned.1.call-done = f32[64,4096]{1,0:T(8,128)} async-done(((f32[2048,4096]{1,0:T(8,128)}), f32[64,4096]{1,0:T(8,128)}) %reduce-scatter.25.cloned.1.call-update) | async-done | bytes 1048592 | tf_op jit(solution)/shard_map/reduce_scatter | solution.py:374
  3462.9 491.4 %reduce-scatter.27.cloned.1.call-done = f32[64,5632]{1,0:T(8,128)} async-done(((f32[2048,5632]{1,0:T(8,128)}), f32[64,5632]{1,0:T(8,128)}) %reduce-scatter.27.cloned.1.call-update) | async-done | bytes 1441808 | tf_op jit(solution)/shard_map/reduce_scatter | solution.py:296
  3954.3 491.5 %reduce-scatter.29.cloned.1.call-done = f32[64,5632]{1,0:T(8,128)} async-done(((f32[2048,5632]{1,0:T(8,128)}), f32[64,5632]{1,0:T(8,128)}) %reduce-scatter.29.cloned.1.call-update) | async-done | bytes 1441808 | tf_op jit(solution)/shard_map/reduce_scatter | solution.py:297
  4445.8 491.5 %reduce-scatter.35.cloned.1.call-done = f32[64,5632]{1,0:T(8,128)} async-done(((f32[2048,5632]{1,0:T(8,128)}), f32[64,5632]{1,0:T(8,128)}) %reduce-scatter.35.cloned.1.call-update) | async-done | bytes 1441808
  4937.2 360.5 %reduce-scatter.23.cloned.1.call-done = f32[64,4096]{1,0:T(8,128)} async-done(((f32[2048,4096]{1,0:T(8,128)}), f32[64,4096]{1,0:T(8,128)}) %reduce-scatter.23.cloned.1.call-update) | async-done | bytes 1048592 | tf_op jit(solution)/shard_map/reduce_scatter | solution.py:373
  5297.7 360.6 %reduce-scatter.21.cloned.1.call-done = f32[64,4096]{1,0:T(8,128)} async-done(((f32[2048,4096]{1,0:T(8,128)}), f32[64,4096]{1,0:T(8,128)}) %reduce-scatter.21.cloned.1.call-update) | async-done | bytes 1048592 | tf_op jit(solution)/shard_map/reduce_scatter | solution.py:366
  (952 shorter events, 558.3 us)
Async XLA Ops:
  7.2 49.1 copy-start.180
  7.2 50.4 copy-start.164
  7.2 132.7 %all-gather.22.cloned.1.call-start = ((), (), s32[]{:S(2)}) async-start(), calls=%async_computation.12 | async-start | bytes 8650752 | tf_op jit(solution)/shard_map/all_gather | solution.py:115
  8.0 163.5 %all-gather.18.cloned.1.call-start = ((), (), s32[]{:S(2)}) async-start(), calls=%async_computation.10 | async-start | bytes 8650752 | tf_op jit(solution)/shard_map/all_gather | solution.py:116
  8.7 91.2 %copy-start.166 = (bf16[64,16]{0,1:T(8,128)(2,1)S(1)}, bf16[64,16]{0,1:T(8,128)(2,1)}, u32[]{:S(2)}) copy-start(bf16[64,16]{0,1:T(8,128)(2,1)} %param.42) | copy-start | bytes 6148
  8.7 279.3 %all-gather.20.cloned.1.call-start = ((), (), s32[]{:S(2)}) async-start(), calls=%async_computation.11 | async-start | bytes 17301504 | tf_op jit(solution)/shard_map/all_gather | solution.py:117
  9.5 394.6 %all-gather.24.cloned.1.call-start = ((), (), s32[]{:S(2)}) async-start(), calls=%async_computation.13 | async-start | bytes 17301504 | tf_op jit(solution)/shard_map/all_gather | solution.py:120
  10.0 127.4 %copy-start.25 = (bf16[1,128,2048]{2,1,0:T(8,128)(2,1)S(1)}, bf16[1,128,2048]{2,1,0:T(8,128)(2,1)}, u32[]{:S(2)}) copy-start(bf16[1,128,2048]{2,1,0:T(8,128)(2,1)} %param.37) | copy-start | bytes 1572868
  10.1 1048.3 %all-gather.26.cloned.1.call-start = ((), (), s32[]{:S(2)}) async-start(), calls=%async_computation.14 | async-start | bytes 17301504 | tf_op jit(solution)/shard_map/all_gather | solution.py:121
  10.6 1059.7 %all-gather.28.cloned.1.call-start = ((), (), s32[]{:S(2)}) async-start(), calls=%async_computation.15 | async-start | bytes 23789568 | tf_op jit(solution)/shard_map/all_gather | solution.py:267
  11.2 127.0 %copy-start.183 = (f32[16]{0:T(128)S(1)}, f32[16]{0:T(128)}, u32[]{:S(2)}) copy-start(f32[16]{0:T(128)} %param.49) | copy-start | bytes 196
  11.2 127.0 %copy-start.171 = (f32[16]{0:T(128)S(1)}, f32[16]{0:T(128)}, u32[]{:S(2)}) copy-start(f32[16]{0:T(128)} %param.50) | copy-start | bytes 196
  11.2 1071.8 %all-gather.30.cloned.1.call-start = ((), (), s32[]{:S(2)}) async-start(), calls=%async_computation.16 | async-start | bytes 23789568 | tf_op jit(solution)/shard_map/all_gather | solution.py:268
  12.0 1083.5 %all-gather.32.cloned.1.call-start = ((), (), s32[]{:S(2)}) async-start(), calls=%async_computation.17 | async-start | bytes 23789568 | tf_op jit(solution)/shard_map/all_gather | solution.py:269
  12.7 1486.2 %all-gather.34.cloned.1.call-start = ((), (), s32[]{:S(2)}) async-start(), calls=%async_computation.18 | async-start | bytes 17301504 | tf_op jit(solution)/shard_map/all_gather | solution.py:121
  55.8 348.2 %copy-start.98 = (f32[2048]{0:T(1024)}, f32[2048]{0:T(1024)S(1)}, u32[]{:S(2)}) copy-start(f32[2048]{0:T(1024)S(1)} %convert_element_type.152) | copy-start | bytes 24580
  137.6 266.4 %copy-start.112 = (f32[128]{0:T(128)}, f32[128]{0:T(128)S(1)}, u32[]{:S(2)}) copy-start(f32[128]{0:T(128)S(1)} %fusion.315) | copy-start | bytes 1540
  138.5 998.9 %copy-start.110 = (f32[2048]{0:T(1024)}, f32[2048]{0:T(1024)S(1)}, u32[]{:S(2)}) copy-start(f32[2048]{0:T(1024)S(1)} %convert_element_type.165) | copy-start | bytes 24580
  139.3 282.8 %copy-start.158 = (pred[128]{0:T(512)(128)(4,1)}, pred[128]{0:T(512)(128)(4,1)S(1)}, u32[]{:S(2)}) copy-start(pred[128]{0:T(512)(128)(4,1)S(1)} %get-tuple-element.2443) | copy-start | bytes 388
  139.3 282.8 %copy-start.160 = (pred[128]{0:T(512)(128)(4,1)}, pred[128]{0:T(512)(128)(4,1)S(1)}, u32[]{:S(2)}) copy-start(pred[128]{0:T(512)(128)(4,1)S(1)} %get-tuple-element.2444) | copy-start | bytes 388
  139.3 282.8 %copy-start.162 = (pred[128]{0:T(512)(128)(4,1)}, pred[128]{0:T(512)(128)(4,1)S(1)}, u32[]{:S(2)}) copy-start(pred[128]{0:T(512)(128)(4,1)S(1)} %get-tuple-element.2445) | copy-start | bytes 388
  139.9 282.3 %copy-start.114 = (f32[1,4096]{1,0:T(1,128)}, f32[1,4096]{1,0:T(1,128)S(1)}, u32[]{:S(2)}) copy-start(f32[1,4096]{1,0:T(1,128)S(1)} %get-tuple-element.2419) | copy-start | bytes 49156
  139.9 282.3 %copy-start.116 = (f32[1,4096]{1,0:T(1,128)}, f32[1,4096]{1,0:T(1,128)S(1)}, u32[]{:S(2)}) copy-start(f32[1,4096]{1,0:T(1,128)S(1)} %get-tuple-element.2420) | copy-start | bytes 49156
  139.9 282.3 %copy-start.118 = (f32[1,4096]{1,0:T(1,128)}, f32[1,4096]{1,0:T(1,128)S(1)}, u32[]{:S(2)}) copy-start(f32[1,4096]{1,0:T(1,128)S(1)} %get-tuple-element.2421) | copy-start | bytes 49156
  139.9 282.3 %copy-start.120 = (f32[1,4096]{1,0:T(1,128)}, f32[1,4096]{1,0:T(1,128)S(1)}, u32[]{:S(2)}) copy-start(f32[1,4096]{1,0:T(1,128)S(1)} %get-tuple-element.2422) | copy-start | bytes 49156
  146.8 32.0 collective-permute-start.4
  176.4 3.0 collective-permute-start.2
  297.5 123.1 %collective-permute-start.3 = (bf16[1,3,4096]{2,1,0:T(4,128)(2,1)S(1)}, bf16[1,3,4096]{2,1,0:T(4,128)(2,1)S(1)}, u32[]{:S(2)}, u32[]{:S(2)}) collective-permute-start(bf16[1,3,4096]{2,1,0:T(4,128)(2,1)S(1)} %slice.312), channel_id=1, source_target_pairs={{0,1},{1,2},{2,3},{3,4},{4,5},{5,6},{6,7},{8,9},{9,10},{10,11},{11... | collective-permute-start | bytes 73736 | tf_op jit(solution)/shard_map/ppermute | solution.py:15
  669.6 6.3 collective-permute-start
  681.0 46.8 collective-permute-start
  732.9 60.0 %collective-permute-start = (f32[1,16,256,128]{3,2,1,0:T(8,128)}, f32[1,16,256,128]{3,2,1,0:T(8,128)S(1)}, u32[]{:S(2)}, u32[]{:S(2)}) collective-permute-start(f32[1,16,256,128]{3,2,1,0:T(8,128)} %get-tuple-element.3067), channel_id=1, source_target_pairs={{0,1},{1,2},{2,3},{3,4},{4,5},{5,6},{6,7},{8,9},{9,10},{10,11},{11... | collective-permute-start | bytes 6291464 | tf_op jit(solution)/shard_map/while/body/eval_jaxpr/ppermute | solution.py:15
  798.0 61.8 %collective-permute-start = (f32[1,16,256,128]{3,2,1,0:T(8,128)}, f32[1,16,256,128]{3,2,1,0:T(8,128)S(1)}, u32[]{:S(2)}, u32[]{:S(2)}) collective-permute-start(f32[1,16,256,128]{3,2,1,0:T(8,128)} %get-tuple-element.3067), channel_id=1, source_target_pairs={{0,1},{1,2},{2,3},{3,4},{4,5},{5,6},{6,7},{8,9},{9,10},{10,11},{11... | collective-permute-start | bytes 6291464 | tf_op jit(solution)/shard_map/while/body/eval_jaxpr/ppermute | solution.py:15
  865.0 59.3 %collective-permute-start = (f32[1,16,256,128]{3,2,1,0:T(8,128)}, f32[1,16,256,128]{3,2,1,0:T(8,128)S(1)}, u32[]{:S(2)}, u32[]{:S(2)}) collective-permute-start(f32[1,16,256,128]{3,2,1,0:T(8,128)} %get-tuple-element.3067), channel_id=1, source_target_pairs={{0,1},{1,2},{2,3},{3,4},{4,5},{5,6},{6,7},{8,9},{9,10},{10,11},{11... | collective-permute-start | bytes 6291464 | tf_op jit(solution)/shard_map/while/body/eval_jaxpr/ppermute | solution.py:15
  929.3 60.0 %collective-permute-start = (f32[1,16,256,128]{3,2,1,0:T(8,128)}, f32[1,16,256,128]{3,2,1,0:T(8,128)S(1)}, u32[]{:S(2)}, u32[]{:S(2)}) collective-permute-start(f32[1,16,256,128]{3,2,1,0:T(8,128)} %get-tuple-element.3067), channel_id=1, source_target_pairs={{0,1},{1,2},{2,3},{3,4},{4,5},{5,6},{6,7},{8,9},{9,10},{10,11},{11... | collective-permute-start | bytes 6291464 | tf_op jit(solution)/shard_map/while/body/eval_jaxpr/ppermute | solution.py:15
  994.5 51.4 collective-permute-start
  1070.2 67.2 %copy-start.41 = (f32[1,128,2048]{2,1,0:T(8,128)}, f32[1,128,2048]{2,1,0:T(8,128)S(1)}, u32[]{:S(2)}) copy-start(f32[1,128,2048]{2,1,0:T(8,128)S(1)} %get-tuple-element.2451) | copy-start | bytes 3145732
  1070.2 67.2 %copy-start.169 = (f32[128]{0:T(128)}, f32[128]{0:T(128)S(1)}, u32[]{:S(2)}) copy-start(f32[128]{0:T(128)S(1)} %fusion.316) | copy-start | bytes 1540
  1138.6 986.2 %all-gather.42.cloned.1.call-start = ((), (), s32[]{:S(2)}) async-start(), calls=%async_computation.22 | async-start | bytes 17301504 | tf_op jit(solution)/shard_map/all_gather | solution.py:120
  1139.2 1002.4 %all-gather.36.cloned.1.call-start = ((), (), s32[]{:S(2)}) async-start(), calls=%async_computation.19 | async-start | bytes 8650752 | tf_op jit(solution)/shard_map/all_gather | solution.py:115
  1140.0 1011.3 %all-gather.40.cloned.1.call-start = ((), (), s32[]{:S(2)}) async-start(), calls=%async_computation.21 | async-start | bytes 17301504 | tf_op jit(solution)/shard_map/all_gather | solution.py:117
  1140.5 1023.5 %all-gather.38.cloned.1.call-start = ((), (), s32[]{:S(2)}) async-start(), calls=%async_computation.20 | async-start | bytes 8650752 | tf_op jit(solution)/shard_map/all_gather | solution.py:116
  1152.8 228.5 %copy-start.165 = (bf16[64,16]{0,1:T(8,128)(2,1)S(1)}, bf16[64,16]{0,1:T(8,128)(2,1)}, u32[]{:S(2)}) copy-start(bf16[64,16]{0,1:T(8,128)(2,1)} %param.43) | copy-start | bytes 6148
  1498.8 855.2 %all-reduce.39.cloned.1.call-start = ((), (), s32[]{:S(2)}) async-start(), calls=%async_computation.34 | async-start | bytes 167936
  1532.7 6.3 collective-permute-start.1
  1546.9 65.8 %collective-permute-start.1 = (f32[1,16,256,128]{3,2,1,0:T(8,128)}, f32[1,16,256,128]{3,2,1,0:T(8,128)S(1)}, u32[]{:S(2)}, u32[]{:S(2)}) collective-permute-start(f32[1,16,256,128]{3,2,1,0:T(8,128)} %get-tuple-element.3085), channel_id=1, source_target_pairs={{1,0},{2,1},{3,2},{4,3},{5,4},{6,5},{7,6},{9,8},{10,9},{11,10},{12... | collective-permute-start | bytes 6291464 | tf_op jit(solution)/shard_map/while/body/eval_jaxpr/ppermute | solution.py:15
  1620.6 30.6 collective-permute-start.1
  1659.0 47.1 collective-permute-start.1
  1714.1 29.8 collective-permute-start.1
  1751.8 27.6 collective-permute-start.1
  1787.3 27.6 collective-permute-start.1
  2097.1 52.9 collective-permute-start.7
  2115.5 25.9 collective-permute-start.5
  2117.3 31.5 collective-permute-start.6
  2173.7 295.5 %reduce-scatter.31.cloned.1.call-start = ((), (), s32[]{:S(2)}) async-start(), calls=%async_computation.31 | async-start | bytes 1081344
  2175.1 427.7 %reduce-scatter.33.cloned.1.call-start = ((), (), s32[]{:S(2)}) async-start(), calls=%async_computation.32 | async-start | bytes 1081344
  2176.6 547.0 %all-reduce.37.cloned.1.call-start = ((), (), s32[]{:S(2)}) async-start(), calls=%async_computation.28 | async-start | bytes 131072 | tf_op jit(solution)/shard_map/psum | solution.py:376
  2177.3 736.5 %reduce-scatter.17.cloned.1.call-start = ((), (), s32[]{:S(2)}) async-start(), calls=%async_computation.23 | async-start | bytes 17301504 | tf_op jit(solution)/shard_map/reduce_scatter | solution.py:364
  2185.7 915.6 %reduce-scatter.19.cloned.1.call-start = ((), (), s32[]{:S(2)}) async-start(), calls=%async_computation.24 | async-start | bytes 17301504 | tf_op jit(solution)/shard_map/reduce_scatter | solution.py:365
  2194.1 1268.7 %reduce-scatter.25.cloned.1.call-start = ((), (), s32[]{:S(2)}) async-start(), calls=%async_computation.27 | async-start | bytes 34603008 | tf_op jit(solution)/shard_map/reduce_scatter | solution.py:374
  2208.9 1745.4 %reduce-scatter.27.cloned.1.call-start = ((), (), s32[]{:S(2)}) async-start(), calls=%async_computation.29 | async-start | bytes 47579136 | tf_op jit(solution)/shard_map/reduce_scatter | solution.py:296
  2228.4 2217.4 %reduce-scatter.29.cloned.1.call-start = ((), (), s32[]{:S(2)}) async-start(), calls=%async_computation.30 | async-start | bytes 47579136 | tf_op jit(solution)/shard_map/reduce_scatter | solution.py:297
  2247.7 2689.6 %reduce-scatter.35.cloned.1.call-start = ((), (), s32[]{:S(2)}) async-start(), calls=%async_computation.33 | async-start | bytes 47579136
  2309.4 2988.3 %reduce-scatter.23.cloned.1.call-start = ((), (), s32[]{:S(2)}) async-start(), calls=%async_computation.26 | async-start | bytes 34603008 | tf_op jit(solution)/shard_map/reduce_scatter | solution.py:373
  2323.9 3334.4 %reduce-scatter.21.cloned.1.call-start = ((), (), s32[]{:S(2)}) async-start(), calls=%async_computation.25 | async-start | bytes 34603008 | tf_op jit(solution)/shard_map/reduce_scatter | solution.py:366
  (227 other events, 1209.7 us)
Sparse Core Ops, SparseCore 0:
  11.1 80.5 all-gather.21
  94.7 76.7 all-gather.17
  174.5 113.4 all-gather.19
  290.9 113.0 all-gather.23
  406.9 113.6 all-gather.25
  523.3 144.1 all-gather.27
  670.3 173.1 all-gather.29
  846.3 177.9 all-gather.31
  1138.7 156.2 all-gather.33
  1297.9 114.2 all-gather.41
  1415.2 76.2 all-gather.35
  1494.3 124.9 all-gather.39
  1622.3 89.5 all-gather.37
  2173.8 157.1 all-reduce.38
  2333.1 135.9 reduce-scatter.30
  2471.3 131.4 reduce-scatter.32
  2609.7 113.7 all-reduce.36
  2726.4 187.4 reduce-scatter.16
  2916.8 184.3 reduce-scatter.18
  3104.1 358.7 reduce-scatter.24
  3465.9 488.4 reduce-scatter.26
  3957.3 488.4 reduce-scatter.28
  4448.8 488.4 reduce-scatter.34
  4940.1 357.6 reduce-scatter.22
  5300.7 357.6 reduce-scatter.20
where the time goes:
time: 5680 us; the launch traced here: 5670 us
  waiting for transfers between devices  3780 us (67%)
  matrix products  555 us (10%)
  other arithmetic  547 us (10%)
  starting transfers between devices  340 us (6%)
  blocking collectives  238 us (4%)
  local copies, waits for them, and re-layouts  184 us (3%)
    unnamed x29, waiting for transfers between devices  743 us
    reduce_scatter x1, waiting for transfers between devices, local(): lax.psum_scatter(grad_up, ('dp', 'seq'), scatter_dimension=0, tiled=True)  491 us
    reduce_scatter x1, waiting for transfers between devices, local(): lax.psum_scatter(grad_hidden, ('dp', 'seq'), scatter_dimension=0, tiled=T...  491 us
    another operation x24, other arithmetic, block_rule(): jax.scipy.linalg.solve_triangular(strict_lower + identity_block, target,...  487 us
    reduce_scatter x1, waiting for transfers between devices, local(): lax.psum_scatter(grad_out, ('dp', 'seq'), scatter_dimension=0, tiled=True)  362 us
    reduce_scatter x1, waiting for transfers between devices, local(): lax.psum_scatter(grad_value, ('dp', 'seq'), scatter_dimension=0, tiled=True)  361 us
    reduce_scatter x1, waiting for transfers between devices, local(): lax.psum_scatter(grad_gate, ('dp', 'seq'), scatter_dimension=0, tiled=True)  360 us
    ppermute x20, starting transfers between devices, passed_along(): return lax.ppermute(array, axis, pairs)  339 us
  transfers between devices with their start and end apart: 45, of which 29 were waited for; matrix products, arithmetic and copies ran while one was open for 21% of the time, Pallas kernels for 0%

commit v1 on v0

v1 whole, which is shorter than its diff:
```python
import jax
import jax.numpy as jnp
from jax import lax
from jax.sharding import PartitionSpec as P

KERNEL = 4
LANES = 128
HIGHEST = lax.Precision.HIGHEST
BF = jnp.bfloat16
F32 = jnp.float32
CHUNK = 128


def rms_scale(value):
    return lax.rsqrt(jnp.mean(value * value, axis=-1, keepdims=True) + 1e-05)


def dot_f32(left, right, dims):
    return lax.dot_general(left, right, (dims, ((), ())), preferred_element_type=F32)


def nn(left, right):
    return dot_f32(left, right, ((1,), (0,)))


def nt(left, right):
    return dot_f32(left, right, ((1,), (1,)))


def tn(left, right):
    return dot_f32(left, right, ((0,), (0,)))


def exact(spec, left, right):
    return jnp.einsum(spec, left, right, precision=HIGHEST)


def silu(value):
    return value * jax.nn.sigmoid(value)


def silu_slope(value):
    s = jax.nn.sigmoid(value)
    return s * (1.0 + value * (1.0 - s))


class Plan:
    def __init__(self, ranks, heads, key_dim, value_dim, hidden):
        self.ranks = ranks
        self.heads = heads
        self.key_dim = key_dim
        self.hp = max(1, heads // ranks)
        self.vs = max(1, ranks // heads)
        self.dv = value_dim // self.vs
        self.value_dim = value_dim
        self.ff = hidden // ranks

    def split_keys(self, array):
        rows = array.shape[0]
        grouped = array.reshape(rows, self.heads // self.hp, -1)
        return jnp.repeat(grouped, self.vs, axis=1) if self.vs > 1 else grouped

    def split_even(self, array):
        return array.reshape(array.shape[0], self.ranks, -1)

    def join_keys(self, array):
        ranks, rows, width = array.shape
        array = array.astype(F32)
        if self.vs > 1:
            array = array.reshape(ranks // self.vs, self.vs, rows, width).sum(axis=1)
        return jnp.transpose(array, (1, 0, 2)).reshape(rows, -1)

    def join_even(self, array):
        return jnp.transpose(array, (1, 0, 2)).reshape(array.shape[1], -1).astype(F32)

    def value_sum(self, array):
        step = 1
        while step < self.vs:
            pairs = [(i, i ^ step) for i in range(self.ranks)]
            array = array + lax.ppermute(array, "seq", pairs)
            step *= 2
        return array


def to_columns(packed):
    ranks = packed.shape[1]
    turned = jnp.transpose(packed, (1, 0, 2)).reshape(-1, packed.shape[2])
    own = lax.all_to_all(turned, "seq", 0, 0, tiled=True)
    return lax.all_gather(own, "dp", axis=0, tiled=True)


def to_rows(grads, ranks):
    mine = lax.psum_scatter(grads.astype(BF), "dp", scatter_dimension=0, tiled=True)
    turned = lax.all_to_all(mine, "seq", 0, 0, tiled=True)
    return turned.reshape(ranks, -1, grads.shape[1])


def causal_taps(pre, taps, offsets):
    summed = taps[0] * pre
    for by in range(1, KERNEL):
        delayed = jnp.pad(pre, ((by, 0), (0, 0)))[:-by]
        summed = summed + taps[by] * jnp.where((offsets >= by)[:, None], delayed, 0.0)
    return summed


def unit_lower_inverse(strict):
    n = strict.shape[-1]
    where = jnp.arange(n, dtype=jnp.int32)
    base = 8
    same = (where[:, None] // base) == (where[None, :] // base)
    eye = jnp.eye(n, dtype=F32)
    small = jnp.where(same, strict, 0.0)
    square = exact("...ij,...jk->...ik", small, small)
    fourth = exact("...ij,...jk->...ik", square, square)
    inverse = exact("...ij,...jk->...ik", eye - small, eye + square)
    inverse = exact("...ij,...jk->...ik", inverse, eye + fourth)
    size = base
    while size < n:
        pair = (where[:, None] // (2 * size)) == (where[None, :] // (2 * size))
        other = (where[:, None] // size) != (where[None, :] // size)
        part = jnp.where(pair & other, strict, 0.0)
        merged = exact("...ij,...jk->...ik", inverse, part)
        inverse = inverse - exact("...ij,...jk->...ik", merged, inverse)
        size *= 2
    return inverse


def delta_rule(queries, key_vecs, values, beta_rows, logdecay, offsets):
    h, t, k = queries.shape
    n = CHUNK
    b = t // n
    q = queries.reshape(h, b, n, k)
    ks = key_vecs.reshape(h, b, n, k)
    v = values.reshape(h, b, n, -1)
    beta = beta_rows.reshape(h, b, n)
    logs = logdecay.reshape(h, b, n)
    offs = offsets.reshape(b, n)
    where = jnp.arange(n, dtype=jnp.int32)
    distance = where[:, None] - where[None, :]
    same_doc = (distance >= 0) & (offs[:, :, None] >= distance)
    total = exact("hbs,ts->hbt", logs, (distance >= 0).astype(F32))
    exponent = total[..., :, None] - total[..., None, :]
    decay = jnp.where(same_doc, jnp.exp(jnp.where(same_doc, exponent, 0.0)), 0.0)
    start = jnp.where(offs > where, jnp.exp(total), 0.0)
    key_key = exact("hbtk,hbsk->hbts", ks, ks)
    strict = jnp.where(distance > 0, decay * key_key, 0.0) * beta[..., None]
    inverse = unit_lower_inverse(strict)
    fresh = exact("hbts,hbsv->hbtv", inverse, beta[..., None] * v)
    seen = exact("hbts,hbsk->hbtk", inverse, (beta * start)[..., None] * ks)
    query_key = decay * exact("hbtk,hbsk->hbts", q, ks)
    q_start = q * start[..., None]
    k_end = ks * decay[..., n - 1, :][..., None]
    last = start[..., n - 1]
    state = jnp.zeros((h, k, v.shape[-1]), F32)
    outs = []
    for c in range(b):
        update = fresh[:, c] - exact("htk,hkv->htv", seen[:, c], state)
        outs.append(
            exact("htk,hkv->htv", q_start[:, c], state)
            + exact("hts,hsv->htv", query_key[:, c], update)
        )
        state = last[:, c][:, None, None] * state + exact("htk,htv->hkv", k_end[:, c], update)
    return jnp.concatenate(outs, axis=1)


def local(
    tokens,
    attn_gain,
    w_query,
    w_key,
    w_value,
    w_decay,
    w_beta,
    w_gate,
    w_out,
    conv_query,
    conv_key,
    conv_value,
    decay_log,
    decay_bias,
    out_gain,
    mlp_gain,
    w_hidden,
    w_up,
    w_down,
    offsets,
    cotangent,
):
    ranks = lax.axis_size("seq")
    rank = lax.axis_index("seq")
    heads = decay_log.shape[0]
    width = tokens.shape[-1]
    tok = tokens.shape[1]
    length = tok * ranks
    plan = Plan(ranks, heads, w_query.shape[1] // heads, out_gain.shape[0], w_hidden.shape[1])
    hp, vs, dk, dv, ff = plan.hp, plan.vs, plan.key_dim, plan.dv, plan.ff
    rows = w_query.shape[0]

    own_tokens = tokens[0]
    own_cot = cotangent[0]
    rider = jnp.concatenate(
        [
            (offsets[0] // 64).astype(BF)[:, None],
            (offsets[0] % 64).astype(BF)[:, None],
            jnp.zeros((tok, LANES - 2), BF),
        ],
        axis=1,
    )
    gathered = lax.all_gather(
        jnp.concatenate([own_tokens, rider], axis=1), "seq", axis=0, tiled=True
    )
    small = jnp.concatenate(
        [
            plan.split_keys(w_decay),
            plan.split_keys(w_beta),
            jnp.broadcast_to(attn_gain[:, None, None], (rows, ranks, 1)),
            jnp.broadcast_to(mlp_gain[:, None, None], (rows, ranks, 1)),
            jnp.zeros((rows, ranks, LANES - 2 - 2 * hp), BF),
        ],
        axis=2,
    )
    w_in = to_columns(
        jnp.concatenate(
            [
                plan.split_keys(w_query),
                plan.split_keys(w_key),
                plan.split_even(w_value),
                plan.split_even(w_gate),
                small,
            ],
            axis=2,
        )
    )
    out_cols = to_columns(plan.split_even(w_out))
    mlp_cols = to_columns(
        jnp.concatenate(
            [plan.split_even(w_hidden), plan.split_even(w_up), plan.split_even(w_down)], axis=2
        )
    )
    cot_all = lax.all_gather(own_cot, "seq", axis=0, tiled=True)

    at_k = hp * dk
    at_v = 2 * hp * dk
    at_g = at_v + hp * dv
    at_s = at_g + hp * dv
    attn_gain_full = w_in[:, at_s + 2 * hp].astype(F32)
    mlp_gain_full = w_in[:, at_s + 2 * hp + 1].astype(F32)

    tokens_all = gathered[:, :width].astype(F32)
    offs = (
        gathered[:, width].astype(F32) * 64.0 + gathered[:, width + 1].astype(F32)
    ).astype(jnp.int32)
    normed_all = tokens_all * rms_scale(tokens_all)
    attn = (normed_all * attn_gain_full).astype(BF)
    pre = nn(attn, w_in)
    pre_query = pre[:, :at_k].astype(BF).astype(F32)
    pre_key = pre[:, at_k:at_v].astype(BF).astype(F32)
    pre_value = pre[:, at_v:at_g].astype(BF).astype(F32)
    pre_gate = pre[:, at_g:at_s]
    pre_decay = pre[:, at_s : at_s + hp]
    pre_beta = pre[:, at_s + hp : at_s + 2 * hp]

    group = rank // vs
    taps_query = lax.dynamic_slice_in_dim(conv_query, group * hp * dk, hp * dk, 1)
    taps_key = lax.dynamic_slice_in_dim(conv_key, group * hp * dk, hp * dk, 1)
    taps_value = lax.dynamic_slice_in_dim(conv_value, rank * hp * dv, hp * dv, 1)
    own_log = lax.dynamic_slice_in_dim(decay_log, group * hp, hp, 0)
    own_bias = lax.dynamic_slice_in_dim(decay_bias, group * hp, hp, 0)
    own_gain = lax.dynamic_slice_in_dim(out_gain, (rank % vs) * dv, dv, 0)

    def head_major(array):
        return jnp.transpose(array.reshape(length, hp, -1), (1, 0, 2))

    def front(query_in, key_in, value_in, tq, tk, tv, decay_in, beta_in, log_rates, rate_bias):
        q = head_major(silu(causal_taps(query_in, tq, offs)))
        q = q * lax.rsqrt(jnp.sum(q * q, axis=-1, keepdims=True) + 1e-06) * dk ** (-0.5)
        k = head_major(silu(causal_taps(key_in, tk, offs)))
        k = k * lax.rsqrt(jnp.sum(k * k, axis=-1, keepdims=True) + 1e-06)
        v = head_major(silu(causal_taps(value_in, tv, offs)))
        beta = jax.nn.sigmoid(beta_in).T
        logs = (-jnp.exp(log_rates) * jax.nn.softplus(decay_in + rate_bias)).T
        return q, k, v, beta, logs

    fronted, front_back = jax.vjp(
        front,
        pre_query,
        pre_key,
        pre_value,
        taps_query,
        taps_key,
        taps_value,
        pre_decay,
        pre_beta,
        own_log,
        own_bias,
    )
    mixed, rule_back = jax.vjp(lambda *a: delta_rule(*a, offs), *fronted)
    gate = head_major(pre_gate)
    mix_scale = lax.rsqrt(
        plan.value_sum(jnp.sum(mixed * mixed, axis=-1, keepdims=True)) / plan.value_dim + 1e-05
    )
    m = mixed * mix_scale
    sg = silu(gate)

    def token_major(array):
        return jnp.transpose(array, (1, 0, 2)).reshape(length, -1)

    gated = token_major(m * own_gain * sg).astype(BF)
    branch = lax.psum_scatter(
        nt(gated, out_cols).astype(BF), "seq", scatter_dimension=0, tiled=True
    )
    inputs = own_tokens.astype(F32)
    middle = inputs + branch.astype(F32)
    r2 = rms_scale(middle)
    n2 = middle * r2
    mlp_own = (n2 * mlp_gain_full).astype(BF)
    mlp_all = lax.all_gather(mlp_own, "seq", axis=0, tiled=True)
    hidden_w = mlp_cols[:, :ff]
    up_w = mlp_cols[:, ff : 2 * ff]
    down_w = mlp_cols[:, 2 * ff :]
    hidden_pre = nn(mlp_all, hidden_w)
    up_pre = nn(mlp_all, up_w)
    sh = silu(hidden_pre)
    product = (sh * up_pre).astype(BF)
    d_product = nn(cot_all, down_w)
    d_hidden = (d_product * up_pre * silu_slope(hidden_pre)).astype(BF)
    d_up = (d_product * sh).astype(BF)
    d_mlp = lax.psum_scatter(
        (nt(d_hidden, hidden_w) + nt(d_up, up_w)).astype(BF), "seq", scatter_dimension=0, tiled=True
    ).astype(F32)
    d_output = own_cot.astype(F32)
    grad_mlp_gain = jnp.sum(d_mlp * n2, axis=0)
    e2 = d_mlp * mlp_gain_full
    d_middle = d_output + r2 * (e2 - n2 * jnp.mean(e2 * n2, axis=-1, keepdims=True))
    d_branch_all = lax.all_gather(d_middle.astype(BF), "seq", axis=0, tiled=True)
    mlp_out = lax.psum_scatter(
        nt(product, down_w).astype(BF), "seq", scatter_dimension=0, tiled=True
    )
    output = (middle + mlp_out.astype(F32)).astype(BF)
    grad_mlp = jnp.concatenate(
        [tn(mlp_all, d_hidden), tn(mlp_all, d_up), tn(cot_all, product)], axis=1
    )
    mlp_rows = to_rows(grad_mlp, ranks)

    d_gated = head_major(nn(d_branch_all, out_cols))
    out_rows = to_rows(tn(d_branch_all, gated), ranks)
    grad_out_gain = jnp.sum(d_gated * m * sg, axis=(0, 1))
    em = d_gated * own_gain * sg
    em_mean = plan.value_sum(jnp.sum(em * m, axis=-1, keepdims=True)) / plan.value_dim
    d_mixed = mix_scale * (em - m * em_mean)
    d_gate = token_major(d_gated * m * own_gain * silu_slope(gate)).astype(BF)
    back = front_back(rule_back(d_mixed))
    d_pre = jnp.concatenate(
        [
            back[0].astype(BF),
            back[1].astype(BF),
            back[2].astype(BF),
            d_gate,
            back[6].astype(BF),
            back[7].astype(BF),
            jnp.zeros((length, LANES - 2 * hp), BF),
        ],
        axis=1,
    )
    d_attn_part = nt(d_pre, w_in)
    grad_attn_gain = jnp.sum(d_attn_part * normed_all, axis=0)
    d_attn = lax.psum_scatter(
        d_attn_part.astype(BF), "seq", scatter_dimension=0, tiled=True
    ).astype(F32)
    grad_in = tn(attn, d_pre)
    grad_in = jnp.concatenate(
        [
            grad_in[:, : at_s + 2 * hp],
            grad_attn_gain[:, None],
            grad_mlp_gain[:, None],
            grad_in[:, at_s + 2 * hp + 2 :],
        ],
        axis=1,
    )
    in_rows = to_rows(grad_in, ranks)

    n = inputs * rms_scale(inputs)
    e = d_attn * attn_gain_full
    grad_tokens = (
        d_middle + rms_scale(inputs) * (e - n * jnp.mean(e * n, axis=-1, keepdims=True))
    ).astype(BF)

    sums = jnp.concatenate(
        [
            back[3].reshape(-1),
            back[4].reshape(-1),
            back[5].reshape(-1),
            back[8],
            back[9],
            grad_out_gain,
        ]
    )
    every = lax.all_gather(sums, ("dp", "seq"), axis=0, tiled=False)
    every = every.reshape(-1, ranks, sums.shape[0]).sum(axis=0)

    def per_head(part, lead):
        part = part.reshape(ranks // vs, vs, lead, -1).sum(axis=1)
        return jnp.transpose(part, (1, 0, 2)).reshape(lead, -1)

    a0 = KERNEL * hp * dk
    a1 = 2 * a0
    a2 = a1 + KERNEL * hp * dv
    grad_conv_value = jnp.transpose(
        every[:, a1:a2].reshape(ranks, KERNEL, -1), (1, 0, 2)
    ).reshape(KERNEL, -1)
    gain_sum = every[:, a2 + 2 * hp :].reshape(ranks // vs, vs, dv).sum(axis=0).reshape(-1)
    grad_small = in_rows[:, :, at_s : at_s + LANES].astype(F32)
    gain_rows = jnp.sum(grad_small[:, :, 2 * hp : 2 * hp + 2], axis=0)
    return (
        output[None],
        grad_tokens[None],
        gain_rows[:, 0],
        plan.join_keys(in_rows[:, :, :at_k]),
        plan.join_keys(in_rows[:, :, at_k:at_v]),
        plan.join_even(in_rows[:, :, at_v:at_g]),
        plan.join_keys(grad_small[:, :, :hp]),
        plan.join_keys(grad_small[:, :, hp : 2 * hp]),
        plan.join_even(in_rows[:, :, at_g:at_s]),
        plan.join_even(out_rows),
        per_head(every[:, :a0], KERNEL),
        per_head(every[:, a0:a1], KERNEL),
        grad_conv_value,
        per_head(every[:, a2 : a2 + hp], 1)[0],
        per_head(every[:, a2 + hp : a2 + 2 * hp], 1)[0],
        gain_sum,
        gain_rows[:, 1],
        plan.join_even(mlp_rows[:, :, :ff]),
        plan.join_even(mlp_rows[:, :, ff : 2 * ff]),
        plan.join_even(mlp_rows[:, :, 2 * ff :]),
    )


def solution(mesh):
    flat = ("dp", "seq")
    tok_spec = P("dp", "seq", None)
    row_spec = P(flat, None)
    gain_spec = P(flat)
    in_specs = (
        (tok_spec, gain_spec)
        + (row_spec,) * 7
        + (P(),) * 6
        + (gain_spec,)
        + (row_spec,) * 3
        + (P("dp", "seq"), tok_spec)
    )
    out_specs = (
        (tok_spec, tok_spec, gain_spec)
        + (row_spec,) * 7
        + (P(),) * 6
        + (gain_spec,)
        + (row_spec,) * 3
    )
    return jax.shard_map(local, mesh=mesh, in_specs=in_specs, out_specs=out_specs, check_vma=False)
```

time: 5680 us -> 1290 us (0.23)
  waiting for transfers between devices: 3780 us -> 592 us
  other arithmetic: 547 us -> 77.4 us
  starting transfers between devices: 340 us -> 16.2 us
  matrix products: 555 us -> 274 us
  blocking collectives: 238 us -> 159 us
    reduce_scatter x7, waiting for transfers between devices: 2440 us -> 174 us  [the longest x1 48.9 us: local(): lax.psum_scatter(nt(product, down_w).astype(BF), 'seq', scatter_dimension...]
    unnamed x29 -> x16, waiting for transfers between devices: 743 us -> 126 us
    another operation x45 -> x0, other arithmetic: 492 us -> none  [the longest x24 487 us: block_rule(): jax.scipy.linalg.solve_triangular(strict_lower + identity_block, target,...]
    ppermute x20 -> x0, starting transfers between devices: 339 us -> none  [passed_along(): return lax.ppermute(array, axis, pairs)]
    dot_general x91 -> x156, matrix products: 528 us -> 274 us  [the longest x141 157 us: exact(): return jnp.einsum(spec, left, right, precision=HIGHEST)]
    ppermute x20 -> x0, waiting for transfers between devices: 253 us -> none  [passed_along(): return lax.ppermute(array, axis, pairs)]
    all_gather x4 -> x0, blocking collectives: 195 us -> none  [the longest x2 118 us: fetch_mixer(): lax.all_gather(beta_part, ('dp', 'seq'), axis=0, tiled=True)]
    all_to_all x0 -> x2, blocking collectives: none -> 159 us  [to_columns(): own = lax.all_to_all(turned, 'seq', 0, 0, tiled=True)]
  transfers between devices with their start and end apart: 45 -> 19, of which waited for: 29 -> 13; matrix products, arithmetic and copies ran while one was open for 21% -> 33% of each run, Pallas kernels for 0% -> 0%
where the time goes in v1:
time: 1290 us; the launch traced here: 1280 us
  waiting for transfers between devices  592 us (46%)
  matrix products  274 us (21%)
  blocking collectives  159 us (12%)
  local copies, waits for them, and re-layouts  142 us (11%)
  other arithmetic  77.4 us (6%)
  between operations  19.6 us (2%)
  starting transfers between devices  16.2 us (1%)
    all_to_all x2, blocking collectives, to_columns(): own = lax.all_to_all(turned, 'seq', 0, 0, tiled=True)  159 us
    dot_general x141, matrix products, exact(): return jnp.einsum(spec, left, right, precision=HIGHEST)  157 us
    all_gather x3, waiting for transfers between devices, to_columns(): return lax.all_gather(own, 'dp', axis=0, tiled=True)  134 us
    unnamed x16, waiting for transfers between devices  126 us
    dot_general x15, matrix products, dot_f32(): lax.dot_general(left, right, (dims, ((), ())), preferred_element_type=F32)  117 us
    all_gather x1, waiting for transfers between devices, local(): mlp_all = lax.all_gather(mlp_own, 'seq', axis=0, tiled=True)  49.2 us
    reduce_scatter x1, waiting for transfers between devices, local(): lax.psum_scatter(nt(product, down_w).astype(BF), 'seq', scatter_dimension...  48.9 us
    reduce_scatter x1, waiting for transfers between devices, local(): lax.psum_scatter((nt(d_hidden, hidden_w) + nt(d_up, up_w)).astype(BF), 's...  48.8 us
  transfers between devices with their start and end apart: 19, of which 13 were waited for; matrix products, arithmetic and copies ran while one was open for 33% of the time, Pallas kernels for 0%

profile of v1, /device:TPU:0, one launch (start us, length us, event | category | flops | bytes accessed | tf_op | source)
XLA Modules:
  0.0 1280.5 jit_solution(1458201438944757570)
XLA Ops:
  15.7 81.4 %all_to_all.54 = bf16[8,64,1664]{2,1,0:T(8,128)(2,1)} all-to-all(bf16[8,64,1664]{2,1,0:T(8,128)(2,1)S(1)} %copy.779), channel_id=1, replica_groups=mesh['dp'=4,'seq'=8] {'seq'}, dimensions={0} | all-to-all | bytes 3407872 | tf_op jit(solution)/shard_map/all_to_all | solution.py:88
  98.3 3.5 all-to-all-start.1
  104.9 12.2 all-to-all-done.1
  118.0 3.1 fusion.4
  124.9 48.3 %all-gather.12.cloned.1.call-done = bf16[2048,1664]{1,0:T(8,128)(2,1)} async-done(((bf16[512,1664]{1,0:T(8,128)(2,1)}), bf16[2048,1664]{1,0:T(8,128)(2,1)}) %all-gather.12.cloned.1.call-update) | async-done | bytes 6815760 | tf_op jit(solution)/shard_map/all_gather | solution.py:89
  175.8 13.6 %fusion.360 = (bf16[1024,1664]{1,0:T(8,128)(2,1)S(1)}, f32[1024,1664]{1,0:T(8,128)}) fusion(bf16[2048,1664]{1,0:T(8,128)(2,1)} %all-gather.12.cloned.1.call-done, f32[2048]{0:T(1024)S(1)} %get-tuple-element.21, f32[1024]{0:T(1024)S(1)} %add_rsqrt_fusion.3, bf16[1024,2176]{1,0:T(8,128)(2,1)} %all-gather.10.cloned.1.call-done), kind=kOutput, calls=%fused_computation.685 | convolution fusion | flops 6989414400 | bytes 21245952 | tf_op jit(solution)/shard_map/dot_general | solution.py:19
  189.6 3.9 multiply_bitcast_fusion
  212.4 3.7 fusion.125
  229.5 3.7 fusion.48
  233.1 3.7 reshape.956
  263.2 6.2 convolution_convert_fusion.2
  283.5 5.0 concatenate.29
  288.5 77.6 %all_to_all.55 = bf16[8,64,2112]{2,1,0:T(8,128)(2,1)} all-to-all(bf16[8,64,2112]{2,1,0:T(8,128)(2,1)} %bitcast.825), channel_id=1, replica_groups=mesh['dp'=4,'seq'=8] {'seq'}, dimensions={0} | all-to-all | bytes 4325376 | tf_op jit(solution)/shard_map/all_to_all | solution.py:88
  371.6 85.2 %all-gather.18.cloned.1.call-done = bf16[2048,2112]{1,0:T(8,128)(2,1)} async-done(((bf16[512,2112]{1,0:T(8,128)(2,1)}), bf16[2048,2112]{1,0:T(8,128)(2,1)}) %all-gather.18.cloned.1.call-update) | async-done | bytes 8650768 | tf_op jit(solution)/shard_map/all_gather | solution.py:89
  456.9 49.2 %all-gather.16.cloned.1.call-done = bf16[1024,2048]{1,0:T(8,128)(2,1)} async-done(((bf16[128,2048]{1,0:T(8,128)(2,1)}), bf16[1024,2048]{1,0:T(8,128)(2,1)}) %all-gather.16.cloned.1.call-update) | async-done | bytes 4194320 | tf_op jit(solution)/shard_map/all_gather | solution.py:317
  506.1 9.0 fusion.22
  515.1 6.7 fusion.26
  521.8 31.8 %all-gather.22.cloned.1.call-done = bf16[1,1024,2048]{2,1,0:T(8,128)(2,1)} async-done(((bf16[1,128,2048]{2,1,0:T(8,128)(2,1)}), bf16[1,1024,2048]{2,1,0:T(8,128)(2,1)}) %all-gather.22.cloned.1.call-update) | async-done | bytes 4194320 | tf_op jit(solution)/shard_map/all_gather | solution.py:240
  553.6 10.4 fusion.17
  563.9 6.6 fusion.24
  570.6 9.2 add_convert_fusion
  579.9 48.8 %reduce-scatter.12.cloned.1.call-done = bf16[128,2048]{1,0:T(8,128)(2,1)} async-done(((bf16[1024,2048]{1,0:T(8,128)(2,1)}), bf16[128,2048]{1,0:T(8,128)(2,1)}) %reduce-scatter.12.cloned.1.call-update) | async-done | bytes 524304 | tf_op jit(solution)/shard_map/reduce_scatter | solution.py:328
  631.8 2.8 fusion.338
  634.7 45.4 %all-gather.20.cloned.1.call-done = bf16[1024,2048]{1,0:T(8,128)(2,1)} async-done(((bf16[128,2048]{1,0:T(8,128)(2,1)}), bf16[1024,2048]{1,0:T(8,128)(2,1)}) %all-gather.20.cloned.1.call-update) | async-done | bytes 4194320 | tf_op jit(solution)/shard_map/all_gather | solution.py:335
  680.1 6.2 convolution_convert_fusion.5
  686.6 5.9 convolution_convert_fusion.3
  692.6 3.4 convolution_convert_fusion.4
  696.0 3.4 fusion.12
  699.4 4.2 pad_maximum_fusion
  704.9 6.6 fusion.363
  711.5 2.9 copy.799
  714.5 5.1 multiply_reduce_fusion
  719.7 2.8 subtract_multiply_fusion.1
  743.3 3.3 multiply_reduce_fusion.5
  754.7 2.7 convolution_add_fusion.12
  761.7 2.7 convolution_add_fusion.10
  778.4 3.6 multiply_reduce_fusion.18
  782.0 2.7 convolution_add_fusion.8
  784.7 3.1 convolution_add_fusion.7
  796.8 4.0 fusion.142
  800.9 2.7 convolution_add_fusion.6
  830.4 6.0 multiply_reduce_fusion.16
  837.5 3.3 convolution_add_fusion
  840.8 2.6 copy.870
  861.6 2.8 fusion.353
  864.5 5.9 multiply_reduce_fusion.8
  880.1 5.5 concatenate.30
  885.5 10.6 convolution_convert_fusion
  896.2 3.2 slice.485
  899.6 11.4 fusion.3
  911.0 31.8 %concatenate.31 = bf16[2048,1664]{0,1:T(8,128)(2,1)} concatenate(bf16[2048,1540]{0,1:T(8,128)(2,1)} %slice.485, bf16[2048,1]{0,1:T(2,128)(2,1)S(1)} %broadcast_in_dim.487, bf16[2048,1]{0,1:T(2,128)(2,1)S(1)} %copy-done.214, bf16[2048,122]{0,1:T(8,128)(2,1)S(1)} %slice.486), dimensions={1} | concatenate | bytes 13631488 | tf_op jit(solution)/shard_map/concatenate | solution.py:371
  946.3 7.5 convolution_convert_fusion.1
  953.9 3.5 all-to-all-start.4
  957.4 4.1 copy.893
  961.5 11.2 all-to-all-done.4
  972.7 3.6 all-to-all-start.5
  976.3 40.0 %reduce-scatter.16.cloned.1.call-done = bf16[512,1664]{0,1:T(8,128)(2,1)} async-done(((bf16[2048,1664]{0,1:T(8,128)(2,1)}), bf16[512,1664]{0,1:T(8,128)(2,1)}) %reduce-scatter.16.cloned.1.call-update) | async-done | bytes 1703952 | tf_op jit(solution)/shard_map/reduce_scatter | solution.py:93
  1016.3 3.6 copy.885
  1019.9 8.2 all-to-all-done.5
  1028.1 4.3 all-to-all-start.3
  1032.4 124.7 %all-reduce.81.cloned.1.call-done = f32[139392]{0:T(1024)} async-done(((f32[139392]{0:T(1024)}), f32[139392]{0:T(1024)}) %all-reduce.81.cloned.1.call-update) | async-done | bytes 557584
  1173.7 36.5 %reduce-scatter.14.cloned.1.call-done = bf16[128,2048]{1,0:T(8,128)(2,1)} async-done(((bf16[1024,2048]{1,0:T(8,128)(2,1)}), bf16[128,2048]{1,0:T(8,128)(2,1)}) %reduce-scatter.14.cloned.1.call-update) | async-done | bytes 524304 | tf_op jit(solution)/shard_map/reduce_scatter | solution.py:367
  1211.6 48.9 %reduce-scatter.10.cloned.1.call-done = bf16[128,2048]{1,0:T(8,128)(2,1)} async-done(((bf16[1024,2048]{1,0:T(8,128)(2,1)}), bf16[128,2048]{1,0:T(8,128)(2,1)}) %reduce-scatter.10.cloned.1.call-update) | async-done | bytes 524304 | tf_op jit(solution)/shard_map/reduce_scatter | solution.py:336
  1260.6 3.2 fusion.184
  (896 shorter events, 242.0 us)
Async XLA Ops:
  7.2 110.7 %all-gather.10.cloned.1.call-start = ((), (), s32[]{:S(2)}) async-start(), calls=%async_computation.13 | async-start | bytes 5013504 | tf_op jit(solution)/shard_map/all_gather | solution.py:209
  10.1 163.0 %all-gather.12.cloned.1.call-start = ((), (), s32[]{:S(2)}) async-start(), calls=%async_computation.14 | async-start | bytes 8519680 | tf_op jit(solution)/shard_map/all_gather | solution.py:89
  15.7 81.5 %copy-start.140 = (bf16[64,4096]{1,0:T(8,128)(2,1)S(1)}, bf16[64,4096]{1,0:T(8,128)(2,1)}, u32[]{:S(2)}) copy-start(bf16[64,4096]{1,0:T(8,128)(2,1)} %param.29) | copy-start | bytes 1572868
  98.3 18.8 %all-to-all-start.1 = ((bf16[8,64,512]{2,1,0:T(8,128)(2,1)}), bf16[8,64,512]{2,1,0:T(8,128)(2,1)S(1)}, u32[]{:S(2)}, u32[]{:S(2)}) async-start(bf16[8,64,512]{2,1,0:T(8,128)(2,1)} %copy.795), calls=%async_computation.1 | async-start | bytes 1048576 | tf_op jit(solution)/shard_map/all_to_all | solution.py:88
  101.8 161.4 %all-gather.14.cloned.1.call-start = ((), (), s32[]{:S(2)}) async-start(), calls=%async_computation.15 | async-start | bytes 2621440 | tf_op jit(solution)/shard_map/all_gather | solution.py:89
  102.0 96.6 %copy-start.269 = (f32[2]{0:T(128)}, f32[2]{0:T(128)S(1)}, u32[]{:S(2)}) copy-start(f32[2]{0:T(128)S(1)} %fusion.336) | copy-start | bytes 28
  102.0 96.6 %copy-start.271 = (f32[2]{0:T(128)}, f32[2]{0:T(128)S(1)}, u32[]{:S(2)}) copy-start(f32[2]{0:T(128)S(1)} %dynamic_slice.18) | copy-start | bytes 28
  104.5 85.0 %copy-start.223 = (f32[1,256]{1,0:T(1,128)}, f32[1,256]{1,0:T(1,128)S(1)}, u32[]{:S(2)}) copy-start(f32[1,256]{1,0:T(1,128)S(1)} %get-tuple-element.127) | copy-start | bytes 3076
  104.5 85.0 %copy-start.225 = (f32[1,256]{1,0:T(1,128)}, f32[1,256]{1,0:T(1,128)S(1)}, u32[]{:S(2)}) copy-start(f32[1,256]{1,0:T(1,128)S(1)} %get-tuple-element.171) | copy-start | bytes 3076
  104.5 85.0 %copy-start.227 = (f32[1,256]{1,0:T(1,128)}, f32[1,256]{1,0:T(1,128)S(1)}, u32[]{:S(2)}) copy-start(f32[1,256]{1,0:T(1,128)S(1)} %get-tuple-element.128) | copy-start | bytes 3076
  104.5 85.0 %copy-start.229 = (f32[1,256]{1,0:T(1,128)}, f32[1,256]{1,0:T(1,128)S(1)}, u32[]{:S(2)}) copy-start(f32[1,256]{1,0:T(1,128)S(1)} %get-tuple-element.129) | copy-start | bytes 3076
  104.5 85.0 %copy-start.231 = (f32[1,256]{1,0:T(1,128)}, f32[1,256]{1,0:T(1,128)S(1)}, u32[]{:S(2)}) copy-start(f32[1,256]{1,0:T(1,128)S(1)} %get-tuple-element.130) | copy-start | bytes 3076
  104.5 85.0 %copy-start.233 = (f32[1,256]{1,0:T(1,128)}, f32[1,256]{1,0:T(1,128)S(1)}, u32[]{:S(2)}) copy-start(f32[1,256]{1,0:T(1,128)S(1)} %get-tuple-element.168) | copy-start | bytes 3076
  104.6 85.0 %copy-start.235 = (f32[1,256]{1,0:T(1,128)}, f32[1,256]{1,0:T(1,128)S(1)}, u32[]{:S(2)}) copy-start(f32[1,256]{1,0:T(1,128)S(1)} %get-tuple-element.169) | copy-start | bytes 3076
  104.6 85.0 %copy-start.237 = (f32[1,256]{1,0:T(1,128)}, f32[1,256]{1,0:T(1,128)S(1)}, u32[]{:S(2)}) copy-start(f32[1,256]{1,0:T(1,128)S(1)} %get-tuple-element.170) | copy-start | bytes 3076
  104.6 102.4 %copy-start.125 = (f32[128,128]{1,0:T(8,128)}, f32[128,128]{1,0:T(8,128)S(1)}, u32[]{:S(2)}) copy-start(f32[128,128]{1,0:T(8,128)S(1)} %get-tuple-element.172) | copy-start | bytes 196612
  104.7 121.8 %copy-start.122 = (pred[128,128]{1,0:T(8,128)(4,1)}, pred[128,128]{1,0:T(8,128)(4,1)S(1)}, u32[]{:S(2)}) copy-start(pred[128,128]{1,0:T(8,128)(4,1)S(1)} %get-tuple-element.173) | copy-start | bytes 49156
  104.8 102.3 %copy-start.199 = (pred[128,128]{1,0:T(8,128)(4,1)}, pred[128,128]{1,0:T(8,128)(4,1)S(1)}, u32[]{:S(2)}) copy-start(pred[128,128]{1,0:T(8,128)(4,1)S(1)} %get-tuple-element.142) | copy-start | bytes 49156
  104.8 112.6 %copy-start.158 = (pred[128,128]{1,0:T(8,128)(4,1)}, pred[128,128]{1,0:T(8,128)(4,1)S(1)}, u32[]{:S(2)}) copy-start(pred[128,128]{1,0:T(8,128)(4,1)S(1)} %get-tuple-element.141) | copy-start | bytes 49156
  104.9 115.9 %copy-start.160 = (pred[128,128]{1,0:T(8,128)(4,1)}, pred[128,128]{1,0:T(8,128)(4,1)S(1)}, u32[]{:S(2)}) copy-start(pred[128,128]{1,0:T(8,128)(4,1)S(1)} %get-tuple-element.140) | copy-start | bytes 49156
  104.9 118.8 %copy-start.163 = (pred[128,128]{1,0:T(8,128)(4,1)}, pred[128,128]{1,0:T(8,128)(4,1)S(1)}, u32[]{:S(2)}) copy-start(pred[128,128]{1,0:T(8,128)(4,1)S(1)} %get-tuple-element.139) | copy-start | bytes 49156
  104.9 121.6 %copy-start.166 = (pred[128,128]{1,0:T(8,128)(4,1)}, pred[128,128]{1,0:T(8,128)(4,1)S(1)}, u32[]{:S(2)}) copy-start(pred[128,128]{1,0:T(8,128)(4,1)S(1)} %get-tuple-element.138) | copy-start | bytes 49156
  117.9 248.3 %reduce-scatter.8.cloned.1.call-start = ((), (), s32[]{:S(2)}) async-start(), calls=%async_computation.16 | async-start | bytes 4718592 | tf_op jit(solution)/shard_map/reduce_scatter | solution.py:309
  121.1 68.3 %copy-start.260 = (f32[1024]{0:T(1024)}, f32[1024]{0:T(1024)S(1)}, u32[]{:S(2)}) copy-start(f32[1024]{0:T(1024)S(1)} %add_rsqrt_fusion.3) | copy-start | bytes 12292
  124.9 104.5 %copy-start.201 = (pred[1024]{0:T(1024)(128)(4,1)}, pred[1024]{0:T(1024)(128)(4,1)S(1)}, u32[]{:S(2)}) copy-start(pred[1024]{0:T(1024)(128)(4,1)S(1)} %get-tuple-element.24) | copy-start | bytes 3076
  124.9 104.5 %copy-start.203 = (pred[1024]{0:T(1024)(128)(4,1)}, pred[1024]{0:T(1024)(128)(4,1)S(1)}, u32[]{:S(2)}) copy-start(pred[1024]{0:T(1024)(128)(4,1)S(1)} %get-tuple-element.25) | copy-start | bytes 3076
  124.9 104.5 %copy-start.205 = (pred[1024]{0:T(1024)(128)(4,1)}, pred[1024]{0:T(1024)(128)(4,1)S(1)}, u32[]{:S(2)}) copy-start(pred[1024]{0:T(1024)(128)(4,1)S(1)} %get-tuple-element.26) | copy-start | bytes 3076
  175.8 13.6 %copy-start.187 = (f32[2048]{0:T(1024)}, f32[2048]{0:T(1024)S(1)}, u32[]{:S(2)}) copy-start(f32[2048]{0:T(1024)S(1)} %get-tuple-element.21) | copy-start | bytes 24580
  193.6 18.5 %copy-start.5 = (f32[128,2,8,128]{3,2,1,0:T(8,128)}, f32[128,2,8,128]{3,2,1,0:T(8,128)S(1)}, u32[]{:S(2)}) copy-start(f32[128,2,8,128]{3,2,1,0:T(8,128)S(1)} %get-tuple-element.136) | copy-start | bytes 3145732
  195.0 17.5 %copy-start.7 = (f32[2,1024,128]{2,1,0:T(8,128)}, f32[2,1024,128]{2,1,0:T(8,128)S(1)}, u32[]{:S(2)}) copy-start(f32[2,1024,128]{2,1,0:T(8,128)S(1)} %fusion.112) | copy-start | bytes 3145732
  210.7 18.7 %copy-start.16 = (f32[1024,512]{1,0:T(8,128)}, f32[1024,512]{1,0:T(8,128)S(1)}, u32[]{:S(2)}) copy-start(f32[1024,512]{1,0:T(8,128)S(1)} %slice_convert_fusion) | copy-start | bytes 6291460
  216.2 22.5 %copy-start.209 = (f32[2,8,128]{2,0,1:T(2,128)}, f32[2,8,128]{2,0,1:T(2,128)S(1)}, u32[]{:S(2)}) copy-start(f32[2,8,128]{2,0,1:T(2,128)S(1)} %copy.791) | copy-start | bytes 24580
  216.2 22.4 %copy-start.211 = (f32[2,8,128]{2,0,1:T(2,128)}, f32[2,8,128]{2,0,1:T(2,128)S(1)}, u32[]{:S(2)}) copy-start(f32[2,8,128]{2,0,1:T(2,128)S(1)} %copy.788) | copy-start | bytes 24580
  258.0 456.4 %copy-start = (f32[2,1024,256]{2,1,0:T(8,128)}, f32[2,1024,256]{2,1,0:T(8,128)S(1)}, u32[]{:S(2)}) copy-start(f32[2,1024,256]{2,1,0:T(8,128)S(1)} %fusion.71) | copy-start | bytes 6291460
  269.5 187.4 %all-gather.18.cloned.1.call-start = ((), (), s32[]{:S(2)}) async-start(), calls=%async_computation.18 | async-start | bytes 11141120 | tf_op jit(solution)/shard_map/all_gather | solution.py:89
  366.1 139.9 %all-gather.16.cloned.1.call-start = ((), (), s32[]{:S(2)}) async-start(), calls=%async_computation.17 | async-start | bytes 4718592 | tf_op jit(solution)/shard_map/all_gather | solution.py:317
  370.4 183.2 %all-gather.22.cloned.1.call-start = ((), (), s32[]{:S(2)}) async-start(), calls=%async_computation.26 | async-start | bytes 4718592 | tf_op jit(solution)/shard_map/all_gather | solution.py:240
  371.2 257.6 %reduce-scatter.12.cloned.1.call-start = ((), (), s32[]{:S(2)}) async-start(), calls=%async_computation.20 | async-start | bytes 4718592 | tf_op jit(solution)/shard_map/reduce_scatter | solution.py:328
  579.9 100.2 %all-gather.20.cloned.1.call-start = ((), (), s32[]{:S(2)}) async-start(), calls=%async_computation.21 | async-start | bytes 4718592 | tf_op jit(solution)/shard_map/all_gather | solution.py:335
  634.6 319.3 %reduce-scatter.18.cloned.1.call-start = ((), (), s32[]{:S(2)}) async-start(), calls=%async_computation.24 | async-start | bytes 2621440 | tf_op jit(solution)/shard_map/reduce_scatter | solution.py:93
  686.3 271.1 %reduce-scatter.20.cloned.1.call-start = ((), (), s32[]{:S(2)}) async-start(), calls=%async_computation.25 | async-start | bytes 10813440 | tf_op jit(solution)/shard_map/reduce_scatter | solution.py:93
  703.6 312.7 %reduce-scatter.16.cloned.1.call-start = ((), (), s32[]{:S(2)}) async-start(), calls=%async_computation.23 | async-start | bytes 8519680 | tf_op jit(solution)/shard_map/reduce_scatter | solution.py:93
  769.5 18.3 %copy-start.141 = (f32[2,1,128,128]{2,3,0,1:T(8,128)}, f32[2,1,128,128]{2,3,0,1:T(8,128)S(1)}, u32[]{:S(2)}) copy-start(f32[2,1,128,128]{2,3,0,1:T(8,128)S(1)} %convolution_bitcast_fusion.14) | copy-start | bytes 393220
  770.0 17.8 %copy-start.143 = (f32[2,1,128,128]{2,3,0,1:T(8,128)}, f32[2,1,128,128]{2,3,0,1:T(8,128)S(1)}, u32[]{:S(2)}) copy-start(f32[2,1,128,128]{2,3,0,1:T(8,128)S(1)} %convolution_bitcast_fusion.13) | copy-start | bytes 393220
  770.4 17.4 %copy-start.145 = (f32[2,1,128,128]{2,3,0,1:T(8,128)}, f32[2,1,128,128]{2,3,0,1:T(8,128)S(1)}, u32[]{:S(2)}) copy-start(f32[2,1,128,128]{2,3,0,1:T(8,128)S(1)} %convolution_bitcast_fusion.12) | copy-start | bytes 393220
  770.8 17.0 %copy-start.147 = (f32[2,1,128,128]{2,3,0,1:T(8,128)}, f32[2,1,128,128]{2,3,0,1:T(8,128)S(1)}, u32[]{:S(2)}) copy-start(f32[2,1,128,128]{2,3,0,1:T(8,128)S(1)} %convolution_bitcast_fusion.11) | copy-start | bytes 393220
  771.2 16.6 %copy-start.149 = (f32[2,1,128,128]{2,3,0,1:T(8,128)}, f32[2,1,128,128]{2,3,0,1:T(8,128)S(1)}, u32[]{:S(2)}) copy-start(f32[2,1,128,128]{2,3,0,1:T(8,128)S(1)} %convolution_bitcast_fusion.10) | copy-start | bytes 393220
  771.7 16.2 %copy-start.151 = (f32[2,1,128,128]{2,3,0,1:T(8,128)}, f32[2,1,128,128]{2,3,0,1:T(8,128)S(1)}, u32[]{:S(2)}) copy-start(f32[2,1,128,128]{2,3,0,1:T(8,128)S(1)} %convolution_bitcast_fusion.9) | copy-start | bytes 393220
  772.1 15.8 %copy-start.153 = (f32[2,1,128,128]{2,3,0,1:T(8,128)}, f32[2,1,128,128]{2,3,0,1:T(8,128)S(1)}, u32[]{:S(2)}) copy-start(f32[2,1,128,128]{2,3,0,1:T(8,128)S(1)} %convolution_bitcast_fusion.8) | copy-start | bytes 393220
  796.8 33.6 %copy-start.183 = (f32[2,1,128,128]{3,2,1,0:T(8,128)}, f32[2,1,128,128]{3,2,1,0:T(8,128)S(1)}, u32[]{:S(2)}) copy-start(f32[2,1,128,128]{3,2,1,0:T(8,128)S(1)} %convolution_bitcast_fusion.15) | copy-start | bytes 393220
  880.0 19.5 %slice-start = ((s8[4456448]{0:T(1024)(128)(4,1)}), s8[262144]{0:T(1024)(128)(4,1)S(1)}, s32[]{:S(2)}) async-start(s8[4456448]{0:T(1024)(128)(4,1)} %bitcast.835), calls=%async_computation.28 | async-start | bytes 524288
  885.5 14.0 %slice-start.1 = ((s8[4456448]{0:T(1024)(128)(4,1)}), s8[4194304]{0:T(1024)(128)(4,1)S(1)}, s32[]{:S(2)}) async-start(s8[4456448]{0:T(1024)(128)(4,1)} %bitcast.835), calls=%async_computation.29 | async-start | bytes 8388608
  942.7 214.3 %all-reduce.81.cloned.1.call-start = ((), (), s32[]{:S(2)}) async-start(), calls=%async_computation.27 | async-start | bytes 1122304
  944.9 265.4 %reduce-scatter.14.cloned.1.call-start = ((), (), s32[]{:S(2)}) async-start(), calls=%async_computation.22 | async-start | bytes 4718592 | tf_op jit(solution)/shard_map/reduce_scatter | solution.py:367
  945.4 315.1 %reduce-scatter.10.cloned.1.call-start = ((), (), s32[]{:S(2)}) async-start(), calls=%async_computation.19 | async-start | bytes 4718592 | tf_op jit(solution)/shard_map/reduce_scatter | solution.py:336
  953.9 18.8 %all-to-all-start.4 = ((bf16[8,64,512]{2,1,0:T(8,128)(2,1)}), bf16[8,64,512]{2,1,0:T(8,128)(2,1)S(1)}, u32[]{:S(2)}, u32[]{:S(2)}) async-start(bf16[8,64,512]{2,1,0:T(8,128)(2,1)} %bitcast.871), calls=%async_computation.10 | async-start | bytes 1048576 | tf_op jit(solution)/shard_map/all_to_all | solution.py:94
  972.7 55.4 %all-to-all-start.5 = ((bf16[8,64,2112]{2,1,0:T(8,128)(2,1)}), bf16[8,64,2112]{2,1,0:T(8,128)(2,1)S(1)}, u32[]{:S(2)}, u32[]{:S(2)}) async-start(bf16[8,64,2112]{2,1,0:T(8,128)(2,1)} %bitcast.824), calls=%async_computation.12 | async-start | bytes 4456448 | tf_op jit(solution)/shard_map/all_to_all | solution.py:94
  1028.1 235.7 %all-to-all-start.3 = ((bf16[8,64,1664]{2,1,0:T(8,128)(2,1)}), bf16[8,64,1664]{2,1,0:T(8,128)(2,1)}, u32[]{:S(2)}, u32[]{:S(2)}) async-start(bf16[8,64,1664]{2,1,0:T(8,128)(2,1)} %bitcast.833), calls=%async_computation.8 | async-start | bytes 3407872 | tf_op jit(solution)/shard_map/all_to_all | solution.py:94
  1172.0 38.3 %copy-start.15 = (bf16[1,128,2048]{2,1,0:T(8,128)(2,1)S(1)}, bf16[1,128,2048]{2,1,0:T(8,128)(2,1)}, u32[]{:S(2)}) copy-start(bf16[1,128,2048]{2,1,0:T(8,128)(2,1)} %param.21) | copy-start | bytes 1572868
  1172.0 88.6 %copy-start.34 = (bf16[128,2048]{1,0:T(8,128)(2,1)S(1)}, bf16[128,2048]{1,0:T(8,128)(2,1)}, u32[]{:S(2)}) copy-start(bf16[128,2048]{1,0:T(8,128)(2,1)} %reduce-scatter.8.cloned.1.call-done) | copy-start | bytes 1572868
  1172.0 88.6 %copy-start.99 = (bf16[128,2048]{1,0:T(8,128)(2,1)S(1)}, bf16[128,2048]{1,0:T(8,128)(2,1)}, u32[]{:S(2)}) copy-start(bf16[128,2048]{1,0:T(8,128)(2,1)} %reduce-scatter.12.cloned.1.call-done) | copy-start | bytes 1572868
  1172.0 88.6 %copy-start.157 = (f32[2048]{0:T(1024)S(1)}, f32[2048]{0:T(1024)}, u32[]{:S(2)}) copy-start(f32[2048]{0:T(1024)} %get-tuple-element.20) | copy-start | bytes 24580
  1172.0 88.6 %copy-start.243 = (f32[128]{0:T(128)S(1)}, f32[128]{0:T(128)}, u32[]{:S(2)}) copy-start(f32[128]{0:T(128)} %copy-done.242) | copy-start | bytes 1540
  1172.0 88.6 %copy-start.274 = (f32[128]{0:T(128)S(1)}, f32[128]{0:T(128)}, u32[]{:S(2)}) copy-start(f32[128]{0:T(128)} %copy-done.273) | copy-start | bytes 1540
  (246 other events, 874.5 us)
Sparse Core Ops, SparseCore 0:
  10.3 87.6 all-gather.9
  99.8 73.3 all-gather.11
  175.6 35.4 all-gather.13
  269.6 71.3 reduce-scatter.7
  366.2 90.5 all-gather.17
  458.9 47.1 all-gather.15
  507.7 45.8 all-gather.21
  580.0 48.7 reduce-scatter.11
  634.7 45.2 all-gather.19
  686.4 33.9 reduce-scatter.17
  723.8 88.5 reduce-scatter.19
  942.9 73.3 reduce-scatter.15
  1022.9 134.0 all-reduce.80
  1159.2 50.9 reduce-scatter.13
  1212.4 48.1 reduce-scatter.9

commit v2 on v1

--- a/solution.py
+++ b/solution.py
@@ -82,17 +82,102 @@
         return array
 
 
-def to_columns(packed):
-    ranks = packed.shape[1]
+def after(value, *earlier):
+    return lax.optimization_barrier((value,) + earlier)[0]
+
+
+def ring_order(count):
+    return [0, 1, 3, 2] if count == 4 else list(range(count))
+
+
+def ring_pairs(count):
+    order = ring_order(count)
+    right = [(order[i], order[(i + 1) % count]) for i in range(count)]
+    return right, [(there, here) for here, there in right]
+
+
+def ring_places():
+    me = lax.axis_index("dp")
+    order = ring_order(4)
+    place = jnp.array([order.index(i) for i in range(4)], jnp.int32)[me]
+    ring = jnp.array(order, jnp.int32)
+    return me, ring[(place + 3) % 4], ring[(place + 1) % 4], ring[(place + 2) % 4]
+
+
+def gather_dp(own):
+    if lax.axis_size("dp") != 4:
+        return lax.all_gather(own, "dp", axis=0, tiled=True)
+    right, left = ring_pairs(4)
+    rows = own.shape[0]
+    half = rows // 2
+    from_left = lax.ppermute(own, "dp", right)
+    from_right = lax.ppermute(own, "dp", left)
+    far_a = lax.ppermute(from_left[:half], "dp", right)
+    far_b = lax.ppermute(from_right[half:], "dp", left)
+    me, at_left, at_right, at_far = ring_places()
+    full = jnp.zeros((4 * rows, own.shape[1]), own.dtype)
+    full = lax.dynamic_update_slice(full, own, (me * rows, 0))
+    full = lax.dynamic_update_slice(full, from_left, (at_left * rows, 0))
+    full = lax.dynamic_update_slice(full, from_right, (at_right * rows, 0))
+    full = lax.dynamic_update_slice(full, far_a, (at_far * rows, 0))
+    return lax.dynamic_update_slice(full, far_b, (at_far * rows + half, 0))
+
+
+def scatter_dp(partial):
+    if lax.axis_size("dp") != 4:
+        return lax.psum_scatter(partial, "dp", scatter_dimension=0, tiled=True)
+    right, left = ring_pairs(4)
+    rows = partial.shape[0] // 4
+    half = rows // 2
+    me, at_left, at_right, at_far = ring_places()
+
+    def part(block, offset, size):
+        return lax.dynamic_slice_in_dim(partial, block * rows + offset, size, 0)
+
+    def plus(own, received):
+        return (own.astype(F32) + received.astype(F32)).astype(BF)
+
+    far_a = lax.ppermute(part(at_far, 0, half), "dp", right)
+    far_b = lax.ppermute(part(at_far, half, half), "dp", left)
+    right_b = lax.ppermute(part(at_right, half, half), "dp", right)
+    left_a = lax.ppermute(part(at_left, 0, half), "dp", left)
+    right_a = lax.ppermute(plus(part(at_right, 0, half), far_a), "dp", right)
+    left_b = lax.ppermute(plus(part(at_left, half, half), far_b), "dp", left)
+    own = part(me, 0, rows).astype(F32)
+    from_left = jnp.concatenate([right_a, right_b]).astype(F32)
+    from_right = jnp.concatenate([left_a, left_b]).astype(F32)
+    return (own + from_left + from_right).astype(BF)
+
+
+def exchange(packed):
     turned = jnp.transpose(packed, (1, 0, 2)).reshape(-1, packed.shape[2])
-    own = lax.all_to_all(turned, "seq", 0, 0, tiled=True)
-    return lax.all_gather(own, "dp", axis=0, tiled=True)
+    return lax.all_to_all(turned, "seq", 0, 0, tiled=True)
 
 
 def to_rows(grads, ranks):
-    mine = lax.psum_scatter(grads.astype(BF), "dp", scatter_dimension=0, tiled=True)
+    mine = scatter_dp(grads.astype(BF))
     turned = lax.all_to_all(mine, "seq", 0, 0, tiled=True)
     return turned.reshape(ranks, -1, grads.shape[1])
+
+
+def sum_everywhere(values):
+    count = lax.axis_size("dp")
+    ranks = lax.axis_size("seq")
+    if count & (count - 1) or ranks & (ranks - 1):
+        return lax.all_gather(lax.psum(values, "dp"), "seq", axis=0, tiled=False)
+    step = 1
+    while step < count:
+        values = values + lax.ppermute(values, "dp", [(i, i ^ step) for i in range(count)])
+        step *= 2
+    rank = lax.axis_index("seq")
+    held = values.reshape(1, -1)
+    step = 1
+    while step < ranks:
+        other = lax.ppermute(held, "seq", [(i, i ^ step) for i in range(ranks)])
+        upper = (rank & step) != 0
+        held = jnp.concatenate([jnp.where(upper, other, held), jnp.where(upper, held, other)])
+        step *= 2
+    return held
 
 
 def causal_taps(pre, taps, offsets):
@@ -206,9 +291,6 @@
         ],
         axis=1,
     )
-    gathered = lax.all_gather(
-        jnp.concatenate([own_tokens, rider], axis=1), "seq", axis=0, tiled=True
-    )
     small = jnp.concatenate(
         [
             plan.split_keys(w_decay),
@@ -219,32 +301,46 @@
         ],
         axis=2,
     )
-    w_in = to_columns(
+    mix_own = exchange(
         jnp.concatenate(
             [
                 plan.split_keys(w_query),
                 plan.split_keys(w_key),
                 plan.split_even(w_value),
-                plan.split_even(w_gate),
                 small,
             ],
             axis=2,
         )
     )
-    out_cols = to_columns(plan.split_even(w_out))
-    mlp_cols = to_columns(
-        jnp.concatenate(
-            [plan.split_even(w_hidden), plan.split_even(w_up), plan.split_even(w_down)], axis=2
+    gathered = lax.all_gather(
+        after(jnp.concatenate([own_tokens, rider], axis=1), mix_own), "seq", axis=0, tiled=True
+    )
+    w_mix = gather_dp(mix_own)
+    side_own = exchange(
+        after(
+            jnp.concatenate([plan.split_even(w_gate), plan.split_even(w_out)], axis=2), gathered
         )
     )
-    cot_all = lax.all_gather(own_cot, "seq", axis=0, tiled=True)
+    w_side = gather_dp(after(side_own, w_mix))
+    mlp_own_cols = exchange(
+        after(
+            jnp.concatenate(
+                [plan.split_even(w_hidden), plan.split_even(w_up), plan.split_even(w_down)],
+                axis=2,
+            ),
+            side_own,
+        )
+    )
+    mlp_cols = gather_dp(after(mlp_own_cols, w_side))
+    cot_all = lax.all_gather(after(own_cot, gathered), "seq", axis=0, tiled=True)
 
     at_k = hp * dk
     at_v = 2 * hp * dk
-    at_g = at_v + hp * dv
-    at_s = at_g + hp * dv
-    attn_gain_full = w_in[:, at_s + 2 * hp].astype(F32)
-    mlp_gain_full = w_in[:, at_s + 2 * hp + 1].astype(F32)
+    at_s = at_v + hp * dv
+    attn_gain_full = w_mix[:, at_s + 2 * hp].astype(F32)
+    mlp_gain_full = w_mix[:, at_s + 2 * hp + 1].astype(F32)
+    gate_cols = w_side[:, : hp * dv]
+    out_cols = w_side[:, hp * dv :]
 
     tokens_all = gathered[:, :width].astype(F32)
     offs = (
@@ -252,11 +348,11 @@
     ).astype(jnp.int32)
     normed_all = tokens_all * rms_scale(tokens_all)
     attn = (normed_all * attn_gain_full).astype(BF)
-    pre = nn(attn, w_in)
+    pre = nn(attn, w_mix)
     pre_query = pre[:, :at_k].astype(BF).astype(F32)
     pre_key = pre[:, at_k:at_v].astype(BF).astype(F32)
-    pre_value = pre[:, at_v:at_g].astype(BF).astype(F32)
-    pre_gate = pre[:, at_g:at_s]
+    pre_value = pre[:, at_v:at_s].astype(BF).astype(F32)
+    pre_gate = nn(attn, gate_cols)
     pre_decay = pre[:, at_s : at_s + hp]
     pre_beta = pre[:, at_s + hp : at_s + 2 * hp]
 
@@ -281,7 +377,7 @@
         logs = (-jnp.exp(log_rates) * jax.nn.softplus(decay_in + rate_bias)).T
         return q, k, v, beta, logs
 
-    fronted, front_back = jax.vjp(
+    fronted_free, front_back = jax.vjp(
         front,
         pre_query,
         pre_key,
@@ -294,6 +390,7 @@
         own_log,
         own_bias,
     )
+    fronted = lax.optimization_barrier(tuple(fronted_free) + (side_own,))[:5]
     mixed, rule_back = jax.vjp(lambda *a: delta_rule(*a, offs), *fronted)
     gate = head_major(pre_gate)
     mix_scale = lax.rsqrt(
@@ -305,7 +402,7 @@
     def token_major(array):
         return jnp.transpose(array, (1, 0, 2)).reshape(length, -1)
 
-    gated = token_major(m * own_gain * sg).astype(BF)
+    gated = after(token_major(m * own_gain * sg).astype(BF), mlp_own_cols, cot_all)
     branch = lax.psum_scatter(
         nt(gated, out_cols).astype(BF), "seq", scatter_dimension=0, tiled=True
     )
@@ -315,32 +412,34 @@
     n2 = middle * r2
     mlp_own = (n2 * mlp_gain_full).astype(BF)
     mlp_all = lax.all_gather(mlp_own, "seq", axis=0, tiled=True)
-    hidden_w = mlp_cols[:, :ff]
-    up_w = mlp_cols[:, ff : 2 * ff]
+    both_w = mlp_cols[:, : 2 * ff]
     down_w = mlp_cols[:, 2 * ff :]
-    hidden_pre = nn(mlp_all, hidden_w)
-    up_pre = nn(mlp_all, up_w)
+    d_product = nn(cot_all, down_w)
+    both_pre = nn(mlp_all, both_w)
+    hidden_pre = both_pre[:, :ff]
+    up_pre = both_pre[:, ff:]
     sh = silu(hidden_pre)
     product = (sh * up_pre).astype(BF)
-    d_product = nn(cot_all, down_w)
-    d_hidden = (d_product * up_pre * silu_slope(hidden_pre)).astype(BF)
-    d_up = (d_product * sh).astype(BF)
+    d_both = jnp.concatenate(
+        [
+            (d_product * up_pre * silu_slope(hidden_pre)).astype(BF),
+            (d_product * sh).astype(BF),
+        ],
+        axis=1,
+    )
     d_mlp = lax.psum_scatter(
-        (nt(d_hidden, hidden_w) + nt(d_up, up_w)).astype(BF), "seq", scatter_dimension=0, tiled=True
+        nt(d_both, both_w).astype(BF), "seq", scatter_dimension=0, tiled=True
     ).astype(F32)
     d_output = own_cot.astype(F32)
-    grad_mlp_gain = jnp.sum(d_mlp * n2, axis=0)
     e2 = d_mlp * mlp_gain_full
     d_middle = d_output + r2 * (e2 - n2 * jnp.mean(e2 * n2, axis=-1, keepdims=True))
     d_branch_all = lax.all_gather(d_middle.astype(BF), "seq", axis=0, tiled=True)
     mlp_out = lax.psum_scatter(
-        nt(product, down_w).astype(BF), "seq", scatter_dimension=0, tiled=True
+        after(nt(product, down_w).astype(BF), d_branch_all), "seq", scatter_dimension=0, tiled=True
     )
     output = (middle + mlp_out.astype(F32)).astype(BF)
-    grad_mlp = jnp.concatenate(
-        [tn(mlp_all, d_hidden), tn(mlp_all, d_up), tn(cot_all, product)], axis=1
-    )
-    mlp_rows = to_rows(grad_mlp, ranks)
+    both_rows = to_rows(tn(mlp_all, d_both), ranks)
+    down_rows = to_rows(tn(cot_all, product), ranks)
 
     d_gated = head_major(nn(d_branch_all, out_cols))
     out_rows = to_rows(tn(d_branch_all, gated), ranks)
@@ -349,35 +448,27 @@
     em_mean = plan.value_sum(jnp.sum(em * m, axis=-1, keepdims=True)) / plan.value_dim
     d_mixed = mix_scale * (em - m * em_mean)
     d_gate = token_major(d_gated * m * own_gain * silu_slope(gate)).astype(BF)
-    back = front_back(rule_back(d_mixed))
+    gate_rows = to_rows(tn(attn, d_gate), ranks)
+    d_attn_gate = nt(d_gate, gate_cols)
+    ruled = lax.optimization_barrier(
+        tuple(rule_back(d_mixed)) + (mlp_out, both_rows, down_rows, out_rows, gate_rows)
+    )[:5]
+    back = front_back(ruled)
     d_pre = jnp.concatenate(
         [
-            back[0].astype(BF),
-            back[1].astype(BF),
-            back[2].astype(BF),
-            d_gate,
-            back[6].astype(BF),
-            back[7].astype(BF),
-            jnp.zeros((length, LANES - 2 * hp), BF),
+            back[0],
+            back[1],
+            back[2],
+            back[6],
+            back[7],
+            jnp.zeros((length, LANES - 2 * hp), F32),
         ],
         axis=1,
-    )
-    d_attn_part = nt(d_pre, w_in)
-    grad_attn_gain = jnp.sum(d_attn_part * normed_all, axis=0)
+    ).astype(BF)
+    mix_rows = to_rows(tn(attn, d_pre), ranks)
     d_attn = lax.psum_scatter(
-        d_attn_part.astype(BF), "seq", scatter_dimension=0, tiled=True
+        (d_attn_gate + nt(d_pre, w_mix)).astype(BF), "seq", scatter_dimension=0, tiled=True
     ).astype(F32)
-    grad_in = tn(attn, d_pre)
-    grad_in = jnp.concatenate(
-        [
-            grad_in[:, : at_s + 2 * hp],
-            grad_attn_gain[:, None],
-            grad_mlp_gain[:, None],
-            grad_in[:, at_s + 2 * hp + 2 :],
-        ],
-        axis=1,
-    )
-    in_rows = to_rows(grad_in, ranks)
 
     n = inputs * rms_scale(inputs)
     e = d_attn * attn_gain_full
@@ -395,8 +486,7 @@
             grad_out_gain,
         ]
     )
-    every = lax.all_gather(sums, ("dp", "seq"), axis=0, tiled=False)
-    every = every.reshape(-1, ranks, sums.shape[0]).sum(axis=0)
+    every = sum_everywhere(jnp.pad(sums, (0, -sums.shape[0] % 1024)))
 
     def per_head(part, lead):
         part = part.reshape(ranks // vs, vs, lead, -1).sum(axis=1)
@@ -408,19 +498,40 @@
     grad_conv_value = jnp.transpose(
         every[:, a1:a2].reshape(ranks, KERNEL, -1), (1, 0, 2)
     ).reshape(KERNEL, -1)
-    gain_sum = every[:, a2 + 2 * hp :].reshape(ranks // vs, vs, dv).sum(axis=0).reshape(-1)
-    grad_small = in_rows[:, :, at_s : at_s + LANES].astype(F32)
-    gain_rows = jnp.sum(grad_small[:, :, 2 * hp : 2 * hp + 2], axis=0)
+    gain_sum = every[:, a2 + 2 * hp : a2 + 2 * hp + dv].reshape(ranks // vs, vs, dv).sum(axis=0).reshape(-1)
+    grad_query = plan.join_keys(mix_rows[:, :, :at_k])
+    grad_key = plan.join_keys(mix_rows[:, :, at_k:at_v])
+    grad_value = plan.join_even(mix_rows[:, :, at_v:at_s])
+    grad_decay = plan.join_keys(mix_rows[:, :, at_s : at_s + hp])
+    grad_beta = plan.join_keys(mix_rows[:, :, at_s + hp : at_s + 2 * hp])
+    grad_gate = plan.join_even(gate_rows)
+    grad_hidden = plan.join_even(both_rows[:, :, :ff])
+    grad_up = plan.join_even(both_rows[:, :, ff:])
+
+    def gain_grad(gain, pairs):
+        total = sum(jnp.sum(w.astype(F32) * g, axis=1) for w, g in pairs)
+        return total / gain.astype(F32)
+
     return (
         output[None],
         grad_tokens[None],
-        gain_rows[:, 0],
-        plan.join_keys(in_rows[:, :, :at_k]),
-        plan.join_keys(in_rows[:, :, at_k:at_v]),
-        plan.join_even(in_rows[:, :, at_v:at_g]),
-        plan.join_keys(grad_small[:, :, :hp]),
-        plan.join_keys(grad_small[:, :, hp : 2 * hp]),
-        plan.join_even(in_rows[:, :, at_g:at_s]),
+        gain_grad(
+            attn_gain,
+            (
+                (w_query, grad_query),
+                (w_key, grad_key),
+                (w_value, grad_value),
+                (w_decay, grad_decay),
+                (w_beta, grad_beta),
+                (w_gate, grad_gate),
+            ),
+        ),
+        grad_query,
+        grad_key,
+        grad_value,
+        grad_decay,
+        grad_beta,
+        grad_gate,
         plan.join_even(out_rows),
         per_head(every[:, :a0], KERNEL),
         per_head(every[:, a0:a1], KERNEL),
@@ -428,10 +539,10 @@
         per_head(every[:, a2 : a2 + hp], 1)[0],
         per_head(every[:, a2 + hp : a2 + 2 * hp], 1)[0],
         gain_sum,
-        gain_rows[:, 1],
-        plan.join_even(mlp_rows[:, :, :ff]),
-        plan.join_even(mlp_rows[:, :, ff : 2 * ff]),
-        plan.join_even(mlp_rows[:, :, 2 * ff :]),
+        gain_grad(mlp_gain, ((w_hidden, grad_hidden), (w_up, grad_up))),
+        grad_hidden,
+        grad_up,
+        plan.join_even(down_rows),
     )
 
 

time: 1290 us -> 1050 us (0.81)
  waiting for transfers between devices: 592 us -> 363 us
  blocking collectives: 159 us -> 0 us
  starting transfers between devices: 16.2 us -> 86.2 us
  local copies, waits for them, and re-layouts: 142 us -> 171 us
  matrix products: 274 us -> 299 us
  other arithmetic: 77.4 us -> 97.6 us
    ppermute x0 -> x47, waiting for transfers between devices: none -> 177 us  [the longest x3 44.8 us: gather_dp(): from_left = lax.ppermute(own, 'dp', right)]
    all_gather x5 -> x2, waiting for transfers between devices: 165 us -> 0.01 us  [the longest x1 0.01 us: local(): lax.all_gather(after(jnp.concatenate([own_tokens, rider], axis=1), mix_ow...]
    all_to_all x2 -> x0, blocking collectives: 159 us -> none  [to_columns(): own = lax.all_to_all(turned, 'seq', 0, 0, tiled=True)]
    reduce_scatter x6 -> x3, waiting for transfers between devices: 174 us -> 39.7 us  [the longest x1 39.7 us: local(): lax.psum_scatter(nt(d_both, both_w).astype(BF), 'seq', scatter_dimension=...]
    unnamed x16 -> x8, waiting for transfers between devices: 126 us -> 0.59 us
    all_to_all x1 -> x3, waiting for transfers between devices: 12.2 us -> 69.5 us  [exchange(): return lax.all_to_all(turned, 'seq', 0, 0, tiled=True)]
    ppermute x0 -> x47, starting transfers between devices: none -> 49.4 us  [the longest x5 6.61 us: scatter_dp(): right_b = lax.ppermute(part(at_right, half, half), 'dp', right)]
    all_gather x1, waiting for transfers between devices: 49.2 us -> 0.01 us  [local(): mlp_all = lax.all_gather(mlp_own, 'seq', axis=0, tiled=True)]
  transfers between devices with their start and end apart: 19 -> 63, of which waited for: 13 -> 27; matrix products, arithmetic and copies ran while one was open for 33% -> 31% of each run, Pallas kernels for 0% -> 0%
where the time goes in v2:
time: 1050 us; the launch traced here: 1040 us
  waiting for transfers between devices  363 us (35%)
  matrix products  299 us (28%)
  local copies, waits for them, and re-layouts  171 us (16%)
  other arithmetic  97.6 us (9%)
  starting transfers between devices  86.2 us (8%)
  between operations  23.6 us (2%)
    dot_general x141, matrix products, exact(): return jnp.einsum(spec, left, right, precision=HIGHEST)  183 us
    dot_general x15, matrix products, dot_f32(): lax.dot_general(left, right, (dims, ((), ())), preferred_element_type=F32)  116 us
    all_to_all x3, waiting for transfers between devices, exchange(): return lax.all_to_all(turned, 'seq', 0, 0, tiled=True)  69.5 us
    reduce_scatter x1, waiting for transfers between devices, local(): lax.psum_scatter(nt(gated, out_cols).astype(BF), 'seq', scatter_dimension...  48.1 us
    ppermute x3, waiting for transfers between devices, gather_dp(): from_left = lax.ppermute(own, 'dp', right)  44.8 us
    reduce_scatter x1, waiting for transfers between devices, local(): lax.psum_scatter(nt(d_both, both_w).astype(BF), 'seq', scatter_dimension=...  39.7 us
    ppermute x5, waiting for transfers between devices, scatter_dp(): right_a = lax.ppermute(plus(part(at_right, 0, half), far_a), 'dp', right)  30.5 us
    unnamed x653, local copies, waits for them, and re-layouts  30.4 us
  transfers between devices with their start and end apart: 63, of which 27 were waited for; matrix products, arithmetic and copies ran while one was open for 31% of the time, Pallas kernels for 0%

profile of v2, /device:TPU:0, one launch (start us, length us, event | category | flops | bytes accessed | tf_op | source)
XLA Modules:
  0.0 1040.6 jit_solution(1642816896303071910)
XLA Ops:
  14.6 6.5 all-to-all-start
  22.3 28.2 %all-to-all-done = bf16[8,64,1152]{2,1,0:T(8,128)(2,1)S(1)} async-done(((bf16[8,64,1152]{2,1,0:T(8,128)(2,1)}), bf16[8,64,1152]{2,1,0:T(8,128)(2,1)S(1)}, u32[]{:S(2)}, u32[]{:S(2)}) %all-to-all-start) | async-done | bytes 1179680 | tf_op jit(solution)/shard_map/all_to_all | solution.py:154
  70.3 4.4 concatenate.68
  109.0 10.5 %fusion.352 = (bf16[1024,1152]{1,0:T(8,128)(2,1)S(1)}, f32[1024,1152]{1,0:T(8,128)}) fusion(bf16[2048,1152]{0,1:T(8,128)(2,1)} %constant_dynamic-update-slice_fusion.10, f32[2048]{0:T(1024)S(1)} %bitcast.835, f32[1024]{0:T(1024)S(1)} %add_rsqrt_fusion.3, bf16[1024,2176]{1,0:T(8,128)(2,1)} %all-gather.5.cloned.1.call-done), kind=kOutput, calls=%fused_computation.754 | convolution fusion | flops 4841406464 | bytes 16003072 | tf_op jit(solution)/shard_map/dot_general | solution.py:19
  123.0 3.1 multiply_bitcast_fusion
  126.6 3.7 fusion.31
  130.3 3.5 reshape.1062
  139.1 4.4 all-to-all-start.1
  148.0 39.2 %all-to-all-done.1 = bf16[8,64,1024]{2,1,0:T(8,128)(2,1)} async-done(((bf16[8,64,1024]{2,1,0:T(8,128)(2,1)}), bf16[8,64,1024]{2,1,0:T(8,128)(2,1)}, u32[]{:S(2)}, u32[]{:S(2)}) %all-to-all-start.1) | async-done | bytes 1048608 | tf_op jit(solution)/shard_map/all_to_all | solution.py:154
  213.7 3.4 fusion.108
  231.1 4.4 all-to-all-start.2
  266.0 6.1 collective-permute-done.6
  274.8 3.9 fusion.43
  287.3 6.3 convolution_convert_fusion.2
  293.7 48.1 %reduce-scatter.5.cloned.1.call-done = bf16[128,2048]{1,0:T(8,128)(2,1)} async-done(((bf16[1024,2048]{1,0:T(8,128)(2,1)}), bf16[128,2048]{1,0:T(8,128)(2,1)}) %reduce-scatter.5.cloned.1.call-update) | async-done | bytes 524304 | tf_op jit(solution)/shard_map/reduce_scatter | solution.py:406
  345.3 4.1 copy.598
  351.4 44.8 %collective-permute-done.8 = bf16[512,2112]{0,1:T(8,128)(2,1)S(1)} collective-permute-done((bf16[512,2112]{0,1:T(8,128)(2,1)}, bf16[512,2112]{0,1:T(8,128)(2,1)S(1)}, u32[]{:S(2)}, u32[]{:S(2)}) %collective-permute-start.8) | collective-permute-done | bytes 2162720 | tf_op jit(solution)/shard_map/ppermute | solution.py:113
  402.2 4.1 broadcast_in_dim.437
  406.2 3.2 constant_dynamic-update-slice_fusion.4
  409.4 4.1 copy.599
  413.5 4.1 copy.601
  417.6 3.4 constant_dynamic-update-slice_fusion.3
  430.8 10.6 %fusion.5 = f32[1024,1408]{1,0:T(8,128)S(1)} fusion(bf16[1024,2048]{1,0:T(8,128)(2,1)} %all-gather.9.cloned.1.call-done, bf16[2048,2112]{1,0:T(8,128)(2,1)} %constant_dynamic-update-slice_fusion), kind=kOutput, calls=%fused_computation.10 | convolution fusion | flops 5905580032 | bytes 15728640 | tf_op jit(solution)/shard_map/dot_general | solution.py:19
  441.4 7.2 multiply_convert_fusion.1
  450.2 10.9 %fusion.7 = bf16[1024,2048]{1,0:T(8,128)(2,1)} fusion(bf16[2048,2112]{1,0:T(8,128)(2,1)} %constant_dynamic-update-slice_fusion, bf16[1024,704]{1,0:T(8,128)(2,1)S(1)} %get-tuple-element.104, bf16[1024,704]{1,0:T(8,128)(2,1)S(1)} %get-tuple-element.103), kind=kOutput, calls=%fused_computation.12 | convolution fusion | flops 5913444352 | bytes 12845056 | tf_op jit(solution)/shard_map/dot_general | solution.py:19
  461.4 5.9 convolution_convert_fusion.4
  473.6 39.7 %reduce-scatter.7.cloned.1.call-done = bf16[128,2048]{1,0:T(8,128)(2,1)} async-done(((bf16[1024,2048]{1,0:T(8,128)(2,1)}), bf16[128,2048]{1,0:T(8,128)(2,1)}) %reduce-scatter.7.cloned.1.call-update) | async-done | bytes 524304 | tf_op jit(solution)/shard_map/reduce_scatter | solution.py:430
  517.7 9.7 convolution_convert_fusion.1
  538.4 20.0 %collective-permute-done.21 = bf16[256,704]{0,1:T(8,128)(2,1)S(1)} collective-permute-done((bf16[256,704]{0,1:T(8,128)(2,1)S(1)}, bf16[256,704]{0,1:T(8,128)(2,1)S(1)}, u32[]{:S(2)}, u32[]{:S(2)}) %collective-permute-start.21) | collective-permute-done | bytes 360480 | tf_op jit(solution)/shard_map/ppermute | solution.py:143
  560.4 5.7 collective-permute-done.23
  568.6 3.5 all-to-all-start.4
  578.3 14.4 %collective-permute-done.13 = bf16[256,1408]{1,0:T(8,128)(2,1)S(1)} collective-permute-done((bf16[256,1408]{1,0:T(8,128)(2,1)S(1)}, bf16[256,1408]{1,0:T(8,128)(2,1)S(1)}, u32[]{:S(2)}, u32[]{:S(2)}) %collective-permute-start.13) | collective-permute-done | bytes 720928 | tf_op jit(solution)/shard_map/ppermute | solution.py:144
  593.9 3.4 add_convert_fusion.1
  597.4 4.8 all-to-all-start.3
  603.1 7.8 convolution_convert_fusion.3
  615.9 21.4 %all-to-all-done.3 = bf16[8,64,1408]{2,1,0:T(8,128)(2,1)} async-done(((bf16[8,64,1408]{2,1,0:T(8,128)(2,1)}), bf16[8,64,1408]{2,1,0:T(8,128)(2,1)}, u32[]{:S(2)}, u32[]{:S(2)}) %all-to-all-start.3) | async-done | bytes 1441824 | tf_op jit(solution)/shard_map/all_to_all | solution.py:159
  645.1 3.5 copy.701
  654.2 6.6 fusion.39
  663.7 4.8 multiply_reduce_fusion
  714.9 3.7 multiply_reduce_fusion.23
  744.2 3.3 fusion.125
  754.9 4.9 convolution_convert_fusion.6
  766.4 5.5 convolution_convert_fusion.5
  802.5 4.6 multiply_reduce_fusion.5
  809.6 5.8 multiply_select_fusion.9
  815.5 5.2 convolution_add_fusion.15
  825.6 4.4 collective-permute-done.33
  832.0 3.6 collective-permute-done.35
  836.6 4.1 all-to-all-start.6
  844.3 3.3 convolution_add_fusion
  856.1 4.1 all-to-all-start.5
  871.8 3.8 all-to-all-done.5
  883.6 3.9 multiply_reduce_fusion.4
  887.6 3.2 multiply_select_fusion
  894.2 5.6 multiply_reduce_fusion.10
  906.7 3.8 concatenate.78
  910.5 10.2 fusion.357
  921.6 8.3 add_convert_fusion
  930.6 7.9 convolution_convert_fusion
  943.1 13.4 %collective-permute-done.40 = bf16[256,1152]{1,0:T(8,128)(2,1)S(1)} collective-permute-done((bf16[256,1152]{1,0:T(8,128)(2,1)S(1)}, bf16[256,1152]{1,0:T(8,128)(2,1)S(1)}, u32[]{:S(2)}, u32[]{:S(2)}) %collective-permute-start.40) | collective-permute-done | bytes 589856 | tf_op jit(solution)/shard_map/ppermute | solution.py:141
  956.5 10.8 %collective-permute-done.36 = bf16[256,1152]{1,0:T(8,128)(2,1)S(1)} collective-permute-done((bf16[256,1152]{1,0:T(8,128)(2,1)S(1)}, bf16[256,1152]{1,0:T(8,128)(2,1)S(1)}, u32[]{:S(2)}, u32[]{:S(2)}) %collective-permute-start.36) | collective-permute-done | bytes 589856 | tf_op jit(solution)/shard_map/ppermute | solution.py:140
  969.7 12.9 %collective-permute-done.37 = bf16[256,1152]{1,0:T(8,128)(2,1)S(1)} collective-permute-done((bf16[256,1152]{1,0:T(8,128)(2,1)S(1)}, bf16[256,1152]{1,0:T(8,128)(2,1)S(1)}, u32[]{:S(2)}, u32[]{:S(2)}) %collective-permute-start.37) | collective-permute-done | bytes 589856 | tf_op jit(solution)/shard_map/ppermute | solution.py:144
  985.2 3.7 all-to-all-start.7
  994.4 27.4 %collective-permute-done.46 = f32[4,5120]{1,0:T(4,128)S(1)} collective-permute-done((f32[4,5120]{1,0:T(4,128)S(1)}, f32[4,5120]{1,0:T(4,128)S(1)}, u32[]{:S(2)}, u32[]{:S(2)}) %collective-permute-start.46) | collective-permute-done | bytes 81952 | tf_op jit(solution)/shard_map/ppermute | solution.py:176
  (1091 shorter events, 426.8 us)
Async XLA Ops:
  14.6 35.9 %all-to-all-start = ((bf16[8,64,1152]{2,1,0:T(8,128)(2,1)}), bf16[8,64,1152]{2,1,0:T(8,128)(2,1)S(1)}, u32[]{:S(2)}, u32[]{:S(2)}) async-start(bf16[8,64,1152]{2,1,0:T(8,128)(2,1)} %copy.573), calls=%async_computation | async-start | bytes 2359296 | tf_op jit(solution)/shard_map/all_to_all | solution.py:154
  21.0 84.8 %all-gather.5.cloned.1.call-start = ((), (), s32[]{:S(2)}) async-start(), calls=%async_computation.12 | async-start | bytes 5013504 | tf_op jit(solution)/shard_map/all_gather | solution.py:315
  50.5 30.9 %collective-permute-start = (bf16[512,1152]{1,0:T(8,128)(2,1)S(1)}, bf16[512,1152]{1,0:T(8,128)(2,1)}, u32[]{:S(2)}, u32[]{:S(2)}) collective-permute-start(bf16[512,1152]{1,0:T(8,128)(2,1)S(1)} %bitcast.759), channel_id=1, source_target_pairs={{0,8},{8,24},{24,16},{16,0},{1,9},{9,25},{25,17},{17,1},{2,10},{10... | collective-permute-start | bytes 3538952 | tf_op jit(solution)/shard_map/ppermute | solution.py:113
  52.0 32.8 %collective-permute-start.1 = (bf16[512,1152]{1,0:T(8,128)(2,1)S(1)}, bf16[512,1152]{1,0:T(8,128)(2,1)}, u32[]{:S(2)}, u32[]{:S(2)}) collective-permute-start(bf16[512,1152]{1,0:T(8,128)(2,1)S(1)} %bitcast.760), channel_id=1, source_target_pairs={{8,0},{24,8},{16,24},{0,16},{9,1},{25,9},{17,25},{1,17},{10,2},{26... | collective-permute-start | bytes 3538952 | tf_op jit(solution)/shard_map/ppermute | solution.py:114
  83.3 14.7 %collective-permute-start.2 = (bf16[256,1152]{1,0:T(8,128)(2,1)}, bf16[256,1152]{1,0:T(8,128)(2,1)}, u32[]{:S(2)}, u32[]{:S(2)}) collective-permute-start(bf16[256,1152]{1,0:T(8,128)(2,1)} %slice.429), channel_id=1, source_target_pairs={{0,8},{8,24},{24,16},{16,0},{1,9},{9,25},{25,17},{17,1},{2,10},{10... | collective-permute-start | bytes 1769480 | tf_op jit(solution)/shard_map/ppermute | solution.py:115
  86.7 14.6 %collective-permute-start.3 = (bf16[256,1152]{1,0:T(8,128)(2,1)}, bf16[256,1152]{1,0:T(8,128)(2,1)}, u32[]{:S(2)}, u32[]{:S(2)}) collective-permute-start(bf16[256,1152]{1,0:T(8,128)(2,1)} %slice.430), channel_id=1, source_target_pairs={{8,0},{24,8},{16,24},{0,16},{9,1},{25,9},{17,25},{1,17},{10,2},{26... | collective-permute-start | bytes 1769480 | tf_op jit(solution)/shard_map/ppermute | solution.py:116
  139.1 48.1 %all-to-all-start.1 = ((bf16[8,64,1024]{2,1,0:T(8,128)(2,1)}), bf16[8,64,1024]{2,1,0:T(8,128)(2,1)}, u32[]{:S(2)}, u32[]{:S(2)}) async-start(bf16[8,64,1024]{2,1,0:T(8,128)(2,1)} %copy.582), calls=%async_computation.1 | async-start | bytes 2097152 | tf_op jit(solution)/shard_map/all_to_all | solution.py:154
  143.4 143.9 %all-gather.7.cloned.1.call-start = ((), (), s32[]{:S(2)}) async-start(), calls=%async_computation.13 | async-start | bytes 4718592 | tf_op jit(solution)/shard_map/all_gather | solution.py:335
  229.0 27.6 %collective-permute-start.4 = (bf16[512,1024]{1,0:T(8,128)(2,1)}, bf16[512,1024]{1,0:T(8,128)(2,1)}, u32[]{:S(2)}, u32[]{:S(2)}) collective-permute-start(bf16[512,1024]{1,0:T(8,128)(2,1)} %bitcast.31), channel_id=1, source_target_pairs={{0,8},{8,24},{24,16},{16,0},{1,9},{9,25},{25,17},{17,1},{2,10},{10... | collective-permute-start | bytes 3145736 | tf_op jit(solution)/shard_map/ppermute | solution.py:113
  230.6 28.9 %collective-permute-start.5 = (bf16[512,1024]{1,0:T(8,128)(2,1)}, bf16[512,1024]{1,0:T(8,128)(2,1)}, u32[]{:S(2)}, u32[]{:S(2)}) collective-permute-start(bf16[512,1024]{1,0:T(8,128)(2,1)} %bitcast.31), channel_id=1, source_target_pairs={{8,0},{24,8},{16,24},{0,16},{9,1},{25,9},{17,25},{1,17},{10,2},{26... | collective-permute-start | bytes 3145736 | tf_op jit(solution)/shard_map/ppermute | solution.py:114
  231.1 56.2 %all-to-all-start.2 = ((bf16[8,64,2112]{2,1,0:T(8,128)(2,1)}), bf16[8,64,2112]{2,1,0:T(8,128)(2,1)}, u32[]{:S(2)}, u32[]{:S(2)}) async-start(bf16[8,64,2112]{2,1,0:T(8,128)(2,1)} %bitcast.749), calls=%async_computation.2 | async-start | bytes 4456448 | tf_op jit(solution)/shard_map/all_to_all | solution.py:154
  235.5 106.3 %reduce-scatter.5.cloned.1.call-start = ((), (), s32[]{:S(2)}) async-start(), calls=%async_computation.14 | async-start | bytes 4718592 | tf_op jit(solution)/shard_map/reduce_scatter | solution.py:406
  257.9 14.2 %collective-permute-start.6 = (bf16[256,1024]{1,0:T(8,128)(2,1)S(1)}, bf16[256,1024]{1,0:T(8,128)(2,1)S(1)}, u32[]{:S(2)}, u32[]{:S(2)}) collective-permute-start(bf16[256,1024]{1,0:T(8,128)(2,1)S(1)} %slice.480), channel_id=1, source_target_pairs={{0,8},{8,24},{24,16},{16,0},{1,9},{9,25},{25,17},{17,1},{2,10},{10... | collective-permute-start | bytes 1572872 | tf_op jit(solution)/shard_map/ppermute | solution.py:115
  260.6 14.1 %collective-permute-start.7 = (bf16[256,1024]{1,0:T(8,128)(2,1)S(1)}, bf16[256,1024]{1,0:T(8,128)(2,1)S(1)}, u32[]{:S(2)}, u32[]{:S(2)}) collective-permute-start(bf16[256,1024]{1,0:T(8,128)(2,1)S(1)} %slice.481), channel_id=1, source_target_pairs={{8,0},{24,8},{16,24},{0,16},{9,1},{25,9},{17,25},{1,17},{10,2},{26... | collective-permute-start | bytes 1572872 | tf_op jit(solution)/shard_map/ppermute | solution.py:116
  293.6 137.1 %all-gather.9.cloned.1.call-start = ((), (), s32[]{:S(2)}) async-start(), calls=%async_computation.15 | async-start | bytes 4718592 | tf_op jit(solution)/shard_map/all_gather | solution.py:414
  343.1 171.5 %copy-start.283 = (f32[128]{0:T(128)}, f32[128]{0:T(128)S(1)}, u32[]{:S(2)}) copy-start(f32[128]{0:T(128)S(1)} %add_rsqrt_fusion.5) | copy-start | bytes 1540
  345.2 168.0 %reduce-scatter.7.cloned.1.call-start = ((), (), s32[]{:S(2)}) async-start(), calls=%async_computation.16 | async-start | bytes 4718592 | tf_op jit(solution)/shard_map/reduce_scatter | solution.py:430
  349.4 46.9 %collective-permute-start.8 = (bf16[512,2112]{0,1:T(8,128)(2,1)}, bf16[512,2112]{0,1:T(8,128)(2,1)S(1)}, u32[]{:S(2)}, u32[]{:S(2)}) collective-permute-start(bf16[512,2112]{0,1:T(8,128)(2,1)} %copy.598), channel_id=1, source_target_pairs={{0,8},{8,24},{24,16},{16,0},{1,9},{9,25},{25,17},{17,1},{2,10},{10... | collective-permute-start | bytes 6488072 | tf_op jit(solution)/shard_map/ppermute | solution.py:113
  350.8 48.0 %collective-permute-start.9 = (bf16[512,2112]{0,1:T(8,128)(2,1)}, bf16[512,2112]{0,1:T(8,128)(2,1)S(1)}, u32[]{:S(2)}, u32[]{:S(2)}) collective-permute-start(bf16[512,2112]{0,1:T(8,128)(2,1)} %copy.598), channel_id=1, source_target_pairs={{8,0},{24,8},{16,24},{0,16},{9,1},{25,9},{17,25},{1,17},{10,2},{26... | collective-permute-start | bytes 6488072 | tf_op jit(solution)/shard_map/ppermute | solution.py:114
  397.4 25.1 %collective-permute-start.10 = (bf16[256,2112]{0,1:T(8,128)(2,1)}, bf16[256,2112]{0,1:T(8,128)(2,1)}, u32[]{:S(2)}, u32[]{:S(2)}) collective-permute-start(bf16[256,2112]{0,1:T(8,128)(2,1)} %slice.485), channel_id=1, source_target_pairs={{0,8},{8,24},{24,16},{16,0},{1,9},{9,25},{25,17},{17,1},{2,10},{10... | collective-permute-start | bytes 3244040 | tf_op jit(solution)/shard_map/ppermute | solution.py:115
  401.3 23.6 %collective-permute-start.11 = (bf16[256,2112]{0,1:T(8,128)(2,1)}, bf16[256,2112]{0,1:T(8,128)(2,1)}, u32[]{:S(2)}, u32[]{:S(2)}) collective-permute-start(bf16[256,2112]{0,1:T(8,128)(2,1)} %slice.486), channel_id=1, source_target_pairs={{8,0},{24,8},{16,24},{0,16},{9,1},{25,9},{17,25},{1,17},{10,2},{26... | collective-permute-start | bytes 3244040 | tf_op jit(solution)/shard_map/ppermute | solution.py:116
  461.1 193.1 %all-gather.11.cloned.1.call-start = ((), (), s32[]{:S(2)}) async-start(), calls=%async_computation.17 | async-start | bytes 4718592 | tf_op jit(solution)/shard_map/all_gather | solution.py:436
  470.0 66.9 %collective-permute-start.20 = (bf16[256,704]{0,1:T(8,128)(2,1)}, bf16[256,704]{0,1:T(8,128)(2,1)}, u32[]{:S(2)}, u32[]{:S(2)}) collective-permute-start(bf16[256,704]{0,1:T(8,128)(2,1)} %get-tuple-element.126), channel_id=1, source_target_pairs={{0,8},{8,24},{24,16},{16,0},{1,9},{9,25},{25,17},{17,1},{2,10},{10... | collective-permute-start | bytes 1081352 | tf_op jit(solution)/shard_map/ppermute | solution.py:142
  471.6 61.8 %collective-permute-start.22 = (bf16[256,704]{0,1:T(8,128)(2,1)}, bf16[256,704]{0,1:T(8,128)(2,1)}, u32[]{:S(2)}, u32[]{:S(2)}) collective-permute-start(bf16[256,704]{0,1:T(8,128)(2,1)} %get-tuple-element.125), channel_id=1, source_target_pairs={{8,0},{24,8},{16,24},{0,16},{9,1},{25,9},{17,25},{1,17},{10,2},{26... | collective-permute-start | bytes 1081352 | tf_op jit(solution)/shard_map/ppermute | solution.py:141
  472.1 62.8 %collective-permute-start.18 = (bf16[256,704]{0,1:T(8,128)(2,1)}, bf16[256,704]{0,1:T(8,128)(2,1)}, u32[]{:S(2)}, u32[]{:S(2)}) collective-permute-start(bf16[256,704]{0,1:T(8,128)(2,1)} %get-tuple-element.127), channel_id=1, source_target_pairs={{0,8},{8,24},{24,16},{16,0},{1,9},{9,25},{25,17},{17,1},{2,10},{10... | collective-permute-start | bytes 1081352 | tf_op jit(solution)/shard_map/ppermute | solution.py:140
  531.4 40.8 %collective-permute-start.16 = (bf16[256,1408]{1,0:T(8,128)(2,1)}, bf16[256,1408]{1,0:T(8,128)(2,1)}, u32[]{:S(2)}, u32[]{:S(2)}) collective-permute-start(bf16[256,1408]{1,0:T(8,128)(2,1)} %get-tuple-element.107), channel_id=1, source_target_pairs={{8,0},{24,8},{16,24},{0,16},{9,1},{25,9},{17,25},{1,17},{10,2},{26... | collective-permute-start | bytes 2162696 | tf_op jit(solution)/shard_map/ppermute | solution.py:141
  532.9 39.3 %collective-permute-start.12 = (bf16[256,1408]{1,0:T(8,128)(2,1)}, bf16[256,1408]{1,0:T(8,128)(2,1)}, u32[]{:S(2)}, u32[]{:S(2)}) collective-permute-start(bf16[256,1408]{1,0:T(8,128)(2,1)} %get-tuple-element.109), channel_id=1, source_target_pairs={{0,8},{8,24},{24,16},{16,0},{1,9},{9,25},{25,17},{17,1},{2,10},{10... | collective-permute-start | bytes 2162696 | tf_op jit(solution)/shard_map/ppermute | solution.py:140
  533.4 25.0 %collective-permute-start.21 = (bf16[256,704]{0,1:T(8,128)(2,1)S(1)}, bf16[256,704]{0,1:T(8,128)(2,1)S(1)}, u32[]{:S(2)}, u32[]{:S(2)}) collective-permute-start(bf16[256,704]{0,1:T(8,128)(2,1)S(1)} %copy-done.193), channel_id=1, source_target_pairs={{8,0},{24,8},{16,24},{0,16},{9,1},{25,9},{17,25},{1,17},{10,2},{26... | collective-permute-start | bytes 1081352 | tf_op jit(solution)/shard_map/ppermute | solution.py:143
  536.3 23.6 %collective-permute-start.19 = (bf16[256,704]{0,1:T(8,128)(2,1)S(1)}, bf16[256,704]{0,1:T(8,128)(2,1)S(1)}, u32[]{:S(2)}, u32[]{:S(2)}) collective-permute-start(bf16[256,704]{0,1:T(8,128)(2,1)S(1)} %get-tuple-element.129), channel_id=1, source_target_pairs={{0,8},{8,24},{24,16},{16,0},{1,9},{9,25},{25,17},{17,1},{2,10},{10... | collective-permute-start | bytes 1081352 | tf_op jit(solution)/shard_map/ppermute | solution.py:144
  536.9 29.2 %collective-permute-start.23 = (bf16[256,704]{0,1:T(8,128)(2,1)S(1)}, bf16[256,704]{0,1:T(8,128)(2,1)S(1)}, u32[]{:S(2)}, u32[]{:S(2)}) collective-permute-start(bf16[256,704]{0,1:T(8,128)(2,1)S(1)} %get-tuple-element.128), channel_id=1, source_target_pairs={{8,0},{24,8},{16,24},{0,16},{9,1},{25,9},{17,25},{1,17},{10,2},{26... | collective-permute-start | bytes 1081352 | tf_op jit(solution)/shard_map/ppermute | solution.py:145
  558.4 18.0 %collective-permute-start.14 = (bf16[256,1408]{1,0:T(8,128)(2,1)}, bf16[256,1408]{1,0:T(8,128)(2,1)}, u32[]{:S(2)}, u32[]{:S(2)}) collective-permute-start(bf16[256,1408]{1,0:T(8,128)(2,1)} %get-tuple-element.108), channel_id=1, source_target_pairs={{0,8},{8,24},{24,16},{16,0},{1,9},{9,25},{25,17},{17,1},{2,10},{10... | collective-permute-start | bytes 2162696 | tf_op jit(solution)/shard_map/ppermute | solution.py:142
  559.9 18.5 %collective-permute-start.15 = (bf16[256,1408]{1,0:T(8,128)(2,1)}, bf16[256,1408]{1,0:T(8,128)(2,1)}, u32[]{:S(2)}, u32[]{:S(2)}) collective-permute-start(bf16[256,1408]{1,0:T(8,128)(2,1)} %get-tuple-element.106), channel_id=1, source_target_pairs={{8,0},{24,8},{16,24},{0,16},{9,1},{25,9},{17,25},{1,17},{10,2},{26... | collective-permute-start | bytes 2162696 | tf_op jit(solution)/shard_map/ppermute | solution.py:143
  568.6 28.8 %all-to-all-start.4 = ((bf16[8,64,704]{2,1,0:T(8,128)(2,1)}), bf16[8,64,704]{2,1,0:T(8,128)(2,1)S(1)}, u32[]{:S(2)}, u32[]{:S(2)}) async-start(bf16[8,64,704]{2,1,0:T(8,128)(2,1)} %bitcast.143), calls=%async_computation.7 | async-start | bytes 1572864 | tf_op jit(solution)/shard_map/all_to_all | solution.py:159
  574.3 18.5 %collective-permute-start.13 = (bf16[256,1408]{1,0:T(8,128)(2,1)S(1)}, bf16[256,1408]{1,0:T(8,128)(2,1)S(1)}, u32[]{:S(2)}, u32[]{:S(2)}) collective-permute-start(bf16[256,1408]{1,0:T(8,128)(2,1)S(1)} %get-tuple-element.111), channel_id=1, source_target_pairs={{0,8},{8,24},{24,16},{16,0},{1,9},{9,25},{25,17},{17,1},{2,10},{10... | collective-permute-start | bytes 2162696 | tf_op jit(solution)/shard_map/ppermute | solution.py:144
  575.8 18.1 %collective-permute-start.17 = (bf16[256,1408]{1,0:T(8,128)(2,1)S(1)}, bf16[256,1408]{1,0:T(8,128)(2,1)S(1)}, u32[]{:S(2)}, u32[]{:S(2)}) collective-permute-start(bf16[256,1408]{1,0:T(8,128)(2,1)S(1)} %get-tuple-element.110), channel_id=1, source_target_pairs={{8,0},{24,8},{16,24},{0,16},{9,1},{25,9},{17,25},{1,17},{10,2},{26... | collective-permute-start | bytes 2162696 | tf_op jit(solution)/shard_map/ppermute | solution.py:145
  597.4 39.9 %all-to-all-start.3 = ((bf16[8,64,1408]{2,1,0:T(8,128)(2,1)}), bf16[8,64,1408]{2,1,0:T(8,128)(2,1)}, u32[]{:S(2)}, u32[]{:S(2)}) async-start(bf16[8,64,1408]{2,1,0:T(8,128)(2,1)} %bitcast.758), calls=%async_computation.6 | async-start | bytes 2883584 | tf_op jit(solution)/shard_map/all_to_all | solution.py:159
  602.1 275.6 %reduce-scatter.9.cloned.1.call-start = ((), (), s32[]{:S(2)}) async-start(), calls=%async_computation.18 | async-start | bytes 4718592 | tf_op jit(solution)/shard_map/reduce_scatter | solution.py:437
  762.1 78.7 %collective-permute-start.28 = (bf16[256,512]{1,0:T(8,128)(2,1)}, bf16[256,512]{1,0:T(8,128)(2,1)}, u32[]{:S(2)}, u32[]{:S(2)}) collective-permute-start(bf16[256,512]{1,0:T(8,128)(2,1)} %get-tuple-element.144), channel_id=1, source_target_pairs={{8,0},{24,8},{16,24},{0,16},{9,1},{25,9},{17,25},{1,17},{10,2},{26... | collective-permute-start | bytes 786440 | tf_op jit(solution)/shard_map/ppermute | solution.py:141
  762.7 78.0 %collective-permute-start.24 = (bf16[256,512]{1,0:T(8,128)(2,1)}, bf16[256,512]{1,0:T(8,128)(2,1)}, u32[]{:S(2)}, u32[]{:S(2)}) collective-permute-start(bf16[256,512]{1,0:T(8,128)(2,1)} %get-tuple-element.146), channel_id=1, source_target_pairs={{0,8},{8,24},{24,16},{16,0},{1,9},{9,25},{25,17},{17,1},{2,10},{10... | collective-permute-start | bytes 786440 | tf_op jit(solution)/shard_map/ppermute | solution.py:140
  772.0 50.9 %collective-permute-start.32 = (bf16[256,512]{1,0:T(8,128)(2,1)S(1)}, bf16[256,512]{1,0:T(8,128)(2,1)S(1)}, u32[]{:S(2)}, u32[]{:S(2)}) collective-permute-start(bf16[256,512]{1,0:T(8,128)(2,1)S(1)} %get-tuple-element.139), channel_id=1, source_target_pairs={{0,8},{8,24},{24,16},{16,0},{1,9},{9,25},{25,17},{17,1},{2,10},{10... | collective-permute-start | bytes 786440 | tf_op jit(solution)/shard_map/ppermute | solution.py:142
  773.5 47.2 %collective-permute-start.34 = (bf16[256,512]{1,0:T(8,128)(2,1)S(1)}, bf16[256,512]{1,0:T(8,128)(2,1)S(1)}, u32[]{:S(2)}, u32[]{:S(2)}) collective-permute-start(bf16[256,512]{1,0:T(8,128)(2,1)S(1)} %get-tuple-element.138), channel_id=1, source_target_pairs={{8,0},{24,8},{16,24},{0,16},{9,1},{25,9},{17,25},{1,17},{10,2},{26... | collective-permute-start | bytes 786440 | tf_op jit(solution)/shard_map/ppermute | solution.py:141
  774.1 47.2 %collective-permute-start.30 = (bf16[256,512]{1,0:T(8,128)(2,1)S(1)}, bf16[256,512]{1,0:T(8,128)(2,1)S(1)}, u32[]{:S(2)}, u32[]{:S(2)}) collective-permute-start(bf16[256,512]{1,0:T(8,128)(2,1)S(1)} %get-tuple-element.140), channel_id=1, source_target_pairs={{0,8},{8,24},{24,16},{16,0},{1,9},{9,25},{25,17},{17,1},{2,10},{10... | collective-permute-start | bytes 786440 | tf_op jit(solution)/shard_map/ppermute | solution.py:140
  820.7 9.2 collective-permute-start.33
  821.4 9.2 collective-permute-start.31
  823.0 12.6 %collective-permute-start.35 = (bf16[256,512]{1,0:T(8,128)(2,1)S(1)}, bf16[256,512]{1,0:T(8,128)(2,1)S(1)}, u32[]{:S(2)}, u32[]{:S(2)}) collective-permute-start(bf16[256,512]{1,0:T(8,128)(2,1)S(1)} %get-tuple-element.141), channel_id=1, source_target_pairs={{8,0},{24,8},{16,24},{0,16},{9,1},{25,9},{17,25},{1,17},{10,2},{26... | collective-permute-start | bytes 786440 | tf_op jit(solution)/shard_map/ppermute | solution.py:145
  830.0 17.7 %collective-permute-start.26 = (bf16[256,512]{1,0:T(8,128)(2,1)}, bf16[256,512]{1,0:T(8,128)(2,1)}, u32[]{:S(2)}, u32[]{:S(2)}) collective-permute-start(bf16[256,512]{1,0:T(8,128)(2,1)} %get-tuple-element.145), channel_id=1, source_target_pairs={{0,8},{8,24},{24,16},{16,0},{1,9},{9,25},{25,17},{17,1},{2,10},{10... | collective-permute-start | bytes 786440 | tf_op jit(solution)/shard_map/ppermute | solution.py:142
  830.6 17.1 %collective-permute-start.27 = (bf16[256,512]{1,0:T(8,128)(2,1)}, bf16[256,512]{1,0:T(8,128)(2,1)}, u32[]{:S(2)}, u32[]{:S(2)}) collective-permute-start(bf16[256,512]{1,0:T(8,128)(2,1)} %get-tuple-element.143), channel_id=1, source_target_pairs={{8,0},{24,8},{16,24},{0,16},{9,1},{25,9},{17,25},{1,17},{10,2},{26... | collective-permute-start | bytes 786440 | tf_op jit(solution)/shard_map/ppermute | solution.py:143
  836.6 19.5 %all-to-all-start.6 = ((bf16[8,64,512]{2,1,0:T(8,128)(2,1)}), bf16[8,64,512]{2,1,0:T(8,128)(2,1)}, u32[]{:S(2)}, u32[]{:S(2)}) async-start(bf16[8,64,512]{2,1,0:T(8,128)(2,1)} %bitcast.783), calls=%async_computation.9 | async-start | bytes 1048576 | tf_op jit(solution)/shard_map/all_to_all | solution.py:159
  842.2 8.6 collective-permute-start.25
  842.9 8.3 collective-permute-start.29
  856.1 19.5 %all-to-all-start.5 = ((bf16[8,64,512]{2,1,0:T(8,128)(2,1)}), bf16[8,64,512]{2,1,0:T(8,128)(2,1)}, u32[]{:S(2)}, u32[]{:S(2)}) async-start(bf16[8,64,512]{2,1,0:T(8,128)(2,1)} %bitcast.144), calls=%async_computation.8 | async-start | bytes 1048576 | tf_op jit(solution)/shard_map/all_to_all | solution.py:159
  860.2 168.8 %reduce-scatter.11.cloned.1.call-start = ((), (), s32[]{:S(2)}) async-start(), calls=%async_computation.19 | async-start | bytes 4718592 | tf_op jit(solution)/shard_map/reduce_scatter | solution.py:469
  920.9 9.0 collective-permute-start.42
  930.0 8.6 collective-permute-start.43
  938.5 4.4 collective-permute-start.44
  938.8 30.9 %collective-permute-start.38 = (bf16[256,1152]{1,0:T(8,128)(2,1)S(1)}, bf16[256,1152]{1,0:T(8,128)(2,1)S(1)}, u32[]{:S(2)}, u32[]{:S(2)}) collective-permute-start(bf16[256,1152]{1,0:T(8,128)(2,1)S(1)} %get-tuple-element.116), channel_id=1, source_target_pairs={{0,8},{8,24},{24,16},{16,0},{1,9},{9,25},{25,17},{17,1},{2,10},{10... | collective-permute-start | bytes 1769480 | tf_op jit(solution)/shard_map/ppermute | solution.py:142
  940.3 16.2 %collective-permute-start.40 = (bf16[256,1152]{1,0:T(8,128)(2,1)S(1)}, bf16[256,1152]{1,0:T(8,128)(2,1)S(1)}, u32[]{:S(2)}, u32[]{:S(2)}) collective-permute-start(bf16[256,1152]{1,0:T(8,128)(2,1)S(1)} %get-tuple-element.115), channel_id=1, source_target_pairs={{8,0},{24,8},{16,24},{0,16},{9,1},{25,9},{17,25},{1,17},{10,2},{26... | collective-permute-start | bytes 1769480 | tf_op jit(solution)/shard_map/ppermute | solution.py:141
  940.9 26.3 %collective-permute-start.36 = (bf16[256,1152]{1,0:T(8,128)(2,1)S(1)}, bf16[256,1152]{1,0:T(8,128)(2,1)S(1)}, u32[]{:S(2)}, u32[]{:S(2)}) collective-permute-start(bf16[256,1152]{1,0:T(8,128)(2,1)S(1)} %get-tuple-element.117), channel_id=1, source_target_pairs={{0,8},{8,24},{24,16},{16,0},{1,9},{9,25},{25,17},{17,1},{2,10},{10... | collective-permute-start | bytes 1769480 | tf_op jit(solution)/shard_map/ppermute | solution.py:140
  942.3 27.4 %collective-permute-start.39 = (bf16[256,1152]{1,0:T(8,128)(2,1)S(1)}, bf16[256,1152]{1,0:T(8,128)(2,1)S(1)}, u32[]{:S(2)}, u32[]{:S(2)}) collective-permute-start(bf16[256,1152]{1,0:T(8,128)(2,1)S(1)} %get-tuple-element.114), channel_id=1, source_target_pairs={{8,0},{24,8},{16,24},{0,16},{9,1},{25,9},{17,25},{1,17},{10,2},{26... | collective-permute-start | bytes 1769480 | tf_op jit(solution)/shard_map/ppermute | solution.py:143
  943.0 26.6 %collective-permute-start.45 = (f32[2,5120]{1,0:T(2,128)S(1)}, f32[2,5120]{1,0:T(2,128)S(1)}, u32[]{:S(2)}, u32[]{:S(2)}) collective-permute-start(f32[2,5120]{1,0:T(2,128)S(1)} %pad_maximum_fusion.5), channel_id=1, source_target_pairs={{0,2},{1,3},{2,0},{3,1},{4,6},{5,7},{6,4},{7,5},{8,10},{9,11},{10,... | collective-permute-start | bytes 122888 | tf_op jit(solution)/shard_map/ppermute | solution.py:176
  967.5 15.1 %collective-permute-start.37 = (bf16[256,1152]{1,0:T(8,128)(2,1)S(1)}, bf16[256,1152]{1,0:T(8,128)(2,1)S(1)}, u32[]{:S(2)}, u32[]{:S(2)}) collective-permute-start(bf16[256,1152]{1,0:T(8,128)(2,1)S(1)} %get-tuple-element.119), channel_id=1, source_target_pairs={{0,8},{8,24},{24,16},{16,0},{1,9},{9,25},{25,17},{17,1},{2,10},{10... | collective-permute-start | bytes 1769480 | tf_op jit(solution)/shard_map/ppermute | solution.py:144
  969.0 14.8 %collective-permute-start.41 = (bf16[256,1152]{1,0:T(8,128)(2,1)S(1)}, bf16[256,1152]{1,0:T(8,128)(2,1)S(1)}, u32[]{:S(2)}, u32[]{:S(2)}) collective-permute-start(bf16[256,1152]{1,0:T(8,128)(2,1)S(1)} %get-tuple-element.118), channel_id=1, source_target_pairs={{8,0},{24,8},{16,24},{0,16},{9,1},{25,9},{17,25},{1,17},{10,2},{26... | collective-permute-start | bytes 1769480 | tf_op jit(solution)/shard_map/ppermute | solution.py:145
  985.2 40.5 %all-to-all-start.7 = ((bf16[8,64,1152]{2,1,0:T(8,128)(2,1)}), bf16[8,64,1152]{2,1,0:T(8,128)(2,1)S(1)}, u32[]{:S(2)}, u32[]{:S(2)}) async-start(bf16[8,64,1152]{2,1,0:T(8,128)(2,1)} %bitcast.152), calls=%async_computation.11 | async-start | bytes 2359296 | tf_op jit(solution)/shard_map/all_to_all | solution.py:159
  989.0 32.8 %collective-permute-start.46 = (f32[4,5120]{1,0:T(4,128)S(1)}, f32[4,5120]{1,0:T(4,128)S(1)}, u32[]{:S(2)}, u32[]{:S(2)}) collective-permute-start(f32[4,5120]{1,0:T(4,128)S(1)} %pad_maximum_fusion.4), channel_id=1, source_target_pairs={{0,4},{1,5},{2,6},{3,7},{4,0},{5,1},{6,2},{7,3},{8,12},{9,13},{10,... | collective-permute-start | bytes 245768 | tf_op jit(solution)/shard_map/ppermute | solution.py:176
  (318 other events, 3083.7 us)
Sparse Core Ops, SparseCore 0:
  50.6 48.4 all-gather.4
  145.9 59.5 all-gather.6
  293.8 47.9 reduce-scatter.4
  345.3 45.2 all-gather.8
  461.3 51.9 reduce-scatter.6
  517.8 45.3 all-gather.10
  755.0 47.9 reduce-scatter.8
  930.1 48.7 reduce-scatter.10

commit v3 on v2

--- a/solution.py
+++ b/solution.py
@@ -1,6 +1,10 @@
+import functools
+
 import jax
 import jax.numpy as jnp
 from jax import lax
+from jax.experimental import pallas as pl
+from jax.experimental.pallas import tpu as pltpu
 from jax.sharding import PartitionSpec as P
 
 KERNEL = 4
@@ -104,49 +108,84 @@
     return me, ring[(place + 3) % 4], ring[(place + 1) % 4], ring[(place + 2) % 4]
 
 
-def gather_dp(own):
+def to_ring(array):
+    if lax.axis_size("dp") != 4:
+        return array
+    size = array.shape[1] // 4
+    return jnp.concatenate(
+        [lax.dynamic_slice_in_dim(array, at * size, size, 1) for at in ring_places()], axis=1
+    )
+
+
+def from_ring(array):
+    if lax.axis_size("dp") != 4:
+        return array
+    size = array.shape[1] // 4
+    me, left, right, _ = ring_places()
+    parts = []
+    for block in range(4):
+        at = jnp.where(block == me, 0, jnp.where(block == left, 1, jnp.where(block == right, 2, 3)))
+        parts.append(lax.dynamic_slice_in_dim(array, at * size, size, 1))
+    return jnp.concatenate(parts, axis=1)
+
+
+def gather_start(own):
+    if lax.axis_size("dp") != 4:
+        return ()
+    right, left = ring_pairs(4)
+    return lax.ppermute(own, "dp", right), lax.ppermute(own, "dp", left)
+
+
+def gather_end(own, near):
     if lax.axis_size("dp") != 4:
         return lax.all_gather(own, "dp", axis=0, tiled=True)
     right, left = ring_pairs(4)
-    rows = own.shape[0]
-    half = rows // 2
-    from_left = lax.ppermute(own, "dp", right)
-    from_right = lax.ppermute(own, "dp", left)
+    half = own.shape[0] // 2
+    from_left, from_right = near
     far_a = lax.ppermute(from_left[:half], "dp", right)
     far_b = lax.ppermute(from_right[half:], "dp", left)
-    me, at_left, at_right, at_far = ring_places()
-    full = jnp.zeros((4 * rows, own.shape[1]), own.dtype)
-    full = lax.dynamic_update_slice(full, own, (me * rows, 0))
-    full = lax.dynamic_update_slice(full, from_left, (at_left * rows, 0))
-    full = lax.dynamic_update_slice(full, from_right, (at_right * rows, 0))
-    full = lax.dynamic_update_slice(full, far_a, (at_far * rows, 0))
-    return lax.dynamic_update_slice(full, far_b, (at_far * rows + half, 0))
-
-
-def scatter_dp(partial):
-    if lax.axis_size("dp") != 4:
-        return lax.psum_scatter(partial, "dp", scatter_dimension=0, tiled=True)
-    right, left = ring_pairs(4)
-    rows = partial.shape[0] // 4
-    half = rows // 2
-    me, at_left, at_right, at_far = ring_places()
-
-    def part(block, offset, size):
-        return lax.dynamic_slice_in_dim(partial, block * rows + offset, size, 0)
-
-    def plus(own, received):
-        return (own.astype(F32) + received.astype(F32)).astype(BF)
-
-    far_a = lax.ppermute(part(at_far, 0, half), "dp", right)
-    far_b = lax.ppermute(part(at_far, half, half), "dp", left)
-    right_b = lax.ppermute(part(at_right, half, half), "dp", right)
-    left_a = lax.ppermute(part(at_left, 0, half), "dp", left)
-    right_a = lax.ppermute(plus(part(at_right, 0, half), far_a), "dp", right)
-    left_b = lax.ppermute(plus(part(at_left, half, half), far_b), "dp", left)
-    own = part(me, 0, rows).astype(F32)
-    from_left = jnp.concatenate([right_a, right_b]).astype(F32)
-    from_right = jnp.concatenate([left_a, left_b]).astype(F32)
-    return (own + from_left + from_right).astype(BF)
+    return jnp.concatenate([own, from_left, from_right, far_a, far_b])
+
+
+def add_low(own, received):
+    return (own.astype(F32) + received.astype(F32)).astype(BF)
+
+
+class RingSum:
+    def __init__(self, partial):
+        self.ring = lax.axis_size("dp") == 4
+        self.partial = partial
+        rows = self.rows = partial.shape[0] // lax.axis_size("dp")
+        half = self.half = rows // 2
+        if self.ring:
+            right, left = ring_pairs(4)
+            far = 3 * rows
+            self.far_a = lax.ppermute(partial[far : far + half], "dp", right)
+            self.far_b = lax.ppermute(partial[far + half :], "dp", left)
+            self.right_b = lax.ppermute(partial[2 * rows + half : far], "dp", right)
+            self.left_a = lax.ppermute(partial[rows : rows + half], "dp", left)
+
+    def second(self, *earlier):
+        if self.ring:
+            right, left = ring_pairs(4)
+            rows, half = self.rows, self.half
+            held = lax.optimization_barrier((self.partial, self.far_a, self.far_b) + earlier)
+            part, far_a, far_b = held[:3]
+            self.right_a = lax.ppermute(
+                add_low(part[2 * rows : 2 * rows + half], far_a), "dp", right
+            )
+            self.left_b = lax.ppermute(add_low(part[rows + half : 2 * rows], far_b), "dp", left)
+
+    def total(self, *earlier):
+        if not self.ring:
+            return lax.psum_scatter(self.partial, "dp", scatter_dimension=0, tiled=True)
+        held = lax.optimization_barrier(
+            (self.partial, self.right_a, self.right_b, self.left_a, self.left_b) + earlier
+        )
+        part, right_a, right_b, left_a, left_b = held[:5]
+        from_left = jnp.concatenate([right_a, right_b]).astype(F32)
+        from_right = jnp.concatenate([left_a, left_b]).astype(F32)
+        return (part[: self.rows].astype(F32) + from_left + from_right).astype(BF)
 
 
 def exchange(packed):
@@ -154,10 +193,9 @@
     return lax.all_to_all(turned, "seq", 0, 0, tiled=True)
 
 
-def to_rows(grads, ranks):
-    mine = scatter_dp(grads.astype(BF))
+def to_rows(mine, ranks):
     turned = lax.all_to_all(mine, "seq", 0, 0, tiled=True)
-    return turned.reshape(ranks, -1, grads.shape[1])
+    return turned.reshape(ranks, -1, mine.shape[1])
 
 
 def sum_everywhere(values):
@@ -188,64 +226,221 @@
     return summed
 
 
-def unit_lower_inverse(strict):
-    n = strict.shape[-1]
-    where = jnp.arange(n, dtype=jnp.int32)
-    base = 8
-    same = (where[:, None] // base) == (where[None, :] // base)
-    eye = jnp.eye(n, dtype=F32)
-    small = jnp.where(same, strict, 0.0)
-    square = exact("...ij,...jk->...ik", small, small)
-    fourth = exact("...ij,...jk->...ik", square, square)
-    inverse = exact("...ij,...jk->...ik", eye - small, eye + square)
-    inverse = exact("...ij,...jk->...ik", inverse, eye + fourth)
-    size = base
+class Pair:
+    def __init__(self, value):
+        self.value = value
+        self.high = value.astype(BF)
+        self.low = (value - self.high.astype(F32)).astype(BF)
+
+def pair(x):
+    return x if isinstance(x, Pair) else Pair(x)
+
+def dot3(a, b, dims):
+    a, b = pair(a), pair(b)
+    d = lambda x, y: lax.dot_general(x, y, (dims, ((), ())), preferred_element_type=F32)
+    return d(a.high, b.high) + (d(a.high, b.low) + d(a.low, b.high))
+
+NN=((1,),(0,)); NT=((1,),(1,)); TN=((0,),(0,))
+
+def stack(a, b):
+    return jnp.concatenate([a, b], axis=0)
+
+def masks(n):
+    t = lax.broadcasted_iota(jnp.int32, (n, n), 0)
+    s = lax.broadcasted_iota(jnp.int32, (n, n), 1)
+    return t, s
+
+def inverses(stricts, t, s, dot):
+    n = t.shape[0]
+    eye = jnp.where(t == s, 1.0, 0.0).astype(F32)
+    same = (t // 8) == (s // 8)
+    small = [Pair(jnp.where(same, a, 0.0)) for a in stricts]
+    square = [Pair(dot(a, a, NN)) for a in small]
+    fourth = [dot(a, a, NN) for a in square]
+    first = [eye - a.value for a in small]
+    inv = [f + dot(f, a, NN) for f, a in zip(first, square)]
+    inv = [f + dot(f, a, NN) for f, a in zip(inv, fourth)]
+    size = 8
     while size < n:
-        pair = (where[:, None] // (2 * size)) == (where[None, :] // (2 * size))
-        other = (where[:, None] // size) != (where[None, :] // size)
-        part = jnp.where(pair & other, strict, 0.0)
-        merged = exact("...ij,...jk->...ik", inverse, part)
-        inverse = inverse - exact("...ij,...jk->...ik", merged, inverse)
+        take = ((t // (2 * size)) == (s // (2 * size))) & ((t // size) != (s // size))
+        held = [Pair(f) for f in inv]
+        part = [dot(f, jnp.where(take, a, 0.0), NN) for f, a in zip(held, stricts)]
+        inv = [f.value - dot(p, f, NN) for f, p in zip(held, part)]
         size *= 2
-    return inverse
-
-
-def delta_rule(queries, key_vecs, values, beta_rows, logdecay, offsets):
-    h, t, k = queries.shape
+    return inv
+
+def decays(cols_block, hp, t, s, dot):
+    n = t.shape[0]
+    tri = jnp.where(t >= s, 1.0, 0.0).astype(F32)
+    run = dot(tri, cols_block, NN)
+    turned = jnp.transpose(run)
+    offs = cols_block[:, 2 * hp : 2 * hp + 1]
+    row = t[:, :1].astype(F32)
+    gap = (t - s).astype(F32)
+    same = (gap >= 0.0) & (offs >= gap)
+    out = []
+    for h in range(hp):
+        g = run[:, hp + h : hp + h + 1]
+        g_row = turned[hp + h : hp + h + 1, :]
+        pairwise = jnp.where(same, jnp.exp(jnp.where(same, g - g_row, 0.0)), 0.0)
+        start = jnp.where(offs > row, jnp.exp(g), 0.0)
+        keep = offs[n - 1 : n, :] >= (n - 1.0) - row
+        end = jnp.where(keep, jnp.exp(jnp.where(keep, g[n - 1 : n, :] - g, 0.0)), 0.0)
+        out.append((pairwise, start, end, start[n - 1 : n, :], cols_block[:, h : h + 1]))
+    return out
+
+def fwd_kernel(hp, dk, dv, group, q_ref, k_ref, v_ref, cols_ref, mixed_ref, state_ref, upd_ref, inv_ref, seen_ref, p_ref, cur_ref):
     n = CHUNK
-    b = t // n
-    q = queries.reshape(h, b, n, k)
-    ks = key_vecs.reshape(h, b, n, k)
-    v = values.reshape(h, b, n, -1)
-    beta = beta_rows.reshape(h, b, n)
-    logs = logdecay.reshape(h, b, n)
-    offs = offsets.reshape(b, n)
-    where = jnp.arange(n, dtype=jnp.int32)
-    distance = where[:, None] - where[None, :]
-    same_doc = (distance >= 0) & (offs[:, :, None] >= distance)
-    total = exact("hbs,ts->hbt", logs, (distance >= 0).astype(F32))
-    exponent = total[..., :, None] - total[..., None, :]
-    decay = jnp.where(same_doc, jnp.exp(jnp.where(same_doc, exponent, 0.0)), 0.0)
-    start = jnp.where(offs > where, jnp.exp(total), 0.0)
-    key_key = exact("hbtk,hbsk->hbts", ks, ks)
-    strict = jnp.where(distance > 0, decay * key_key, 0.0) * beta[..., None]
-    inverse = unit_lower_inverse(strict)
-    fresh = exact("hbts,hbsv->hbtv", inverse, beta[..., None] * v)
-    seen = exact("hbts,hbsk->hbtk", inverse, (beta * start)[..., None] * ks)
-    query_key = decay * exact("hbtk,hbsk->hbts", q, ks)
-    q_start = q * start[..., None]
-    k_end = ks * decay[..., n - 1, :][..., None]
-    last = start[..., n - 1]
-    state = jnp.zeros((h, k, v.shape[-1]), F32)
-    outs = []
-    for c in range(b):
-        update = fresh[:, c] - exact("htk,hkv->htv", seen[:, c], state)
-        outs.append(
-            exact("htk,hkv->htv", q_start[:, c], state)
-            + exact("hts,hsv->htv", query_key[:, c], update)
-        )
-        state = last[:, c][:, None, None] * state + exact("htk,htv->hkv", k_end[:, c], update)
-    return jnp.concatenate(outs, axis=1)
+    total = q_ref.shape[0]
+    chunks = total // n
+    t, s = masks(n)
+    dot = dot3
+
+    def prepare(step, carry):
+        jobs = []
+        for j in range(group):
+            rows = pl.ds(pl.multiple_of((step * group + j) * n, n), n)
+            for h, d in enumerate(decays(cols_ref[rows, :], hp, t, s, dot)):
+                jobs.append((step * group + j, rows, h) + d)
+        ks = [k_ref[r, h * dk : (h + 1) * dk] for _, r, h, *_ in jobs]
+        qs = [q_ref[r, h * dk : (h + 1) * dk] for _, r, h, *_ in jobs]
+        both = [dot(stack(k, q), k, NT) for k, q in zip(ks, qs)]
+        strict = [jnp.where(t > s, job[3] * b[:n], 0.0) * job[7] for job, b in zip(jobs, both)]
+        inv = [Pair(i) for i in inverses(strict, t, s, dot)]
+        for job, b, i, k in zip(jobs, both, inv, ks):
+            c, r, h, pairwise, start, end, last, beta = job
+            p_ref[c * hp + h] = pairwise * b[n:]
+            inv_ref[c * hp + h] = i.value
+            upd_ref[r, h * dv : (h + 1) * dv] = dot(i, beta * v_ref[r, h * dv : (h + 1) * dv], NN)
+            seen_ref[r, h * dk : (h + 1) * dk] = dot(i, (beta * start) * k, NN)
+        return carry
+
+    lax.fori_loop(0, chunks // group, prepare, 0)
+    cur_ref[...] = jnp.zeros_like(cur_ref)
+
+    def advance(c, carry):
+        rows = pl.ds(pl.multiple_of(c * n, n), n)
+        for h, (pairwise, start, end, last, beta) in enumerate(decays(cols_ref[rows, :], hp, t, s, dot)):
+            kk = slice(h * dk, (h + 1) * dk)
+            vv = slice(h * dv, (h + 1) * dv)
+            state = cur_ref[h]
+            state_ref[c * hp + h] = state
+            both = dot(stack(seen_ref[rows, kk], q_ref[rows, kk] * start), state, NN)
+            update = Pair(upd_ref[rows, vv] - both[:n])
+            upd_ref[rows, vv] = update.value
+            mixed_ref[rows, vv] = both[n:] + dot(p_ref[c * hp + h], update, NN)
+            cur_ref[h] = last * state + dot(k_ref[rows, kk] * end, update, TN)
+        return carry
+
+    lax.fori_loop(0, chunks, advance, 0)
+
+def bwd_kernel(hp, dk, dv, group, q_ref, k_ref, v_ref, cols_ref, state_ref, upd_ref, inv_ref, seen_ref, dm_ref,
+               dq_ref, dk_ref, dv_ref, dcols_ref, du_ref, ds_ref, cur_ref):
+    n = CHUNK
+    total = q_ref.shape[0]
+    chunks = total // n
+    t, s = masks(n)
+    dot = dot3
+    cur_ref[...] = jnp.zeros_like(cur_ref)
+
+    def retreat(step, carry):
+        c = chunks - 1 - step
+        rows = pl.ds(pl.multiple_of(c * n, n), n)
+        for h, (pairwise, start, end, last, beta) in enumerate(decays(cols_ref[rows, :], hp, t, s, dot)):
+            kk = slice(h * dk, (h + 1) * dk)
+            vv = slice(h * dv, (h + 1) * dv)
+            d_state = cur_ref[h]
+            ds_ref[c * hp + h] = d_state
+            dm = Pair(dm_ref[rows, vv])
+            k = k_ref[rows, kk]
+            p = pairwise * dot(q_ref[rows, kk], k, NT)
+            du = dot(p, dm, TN) + dot(k * end, d_state, NN)
+            du_ref[rows, vv] = du
+            cur_ref[h] = last * d_state + dot(q_ref[rows, kk] * start, dm, TN) - dot(seen_ref[rows, kk], du, TN)
+        return carry
+
+    lax.fori_loop(0, chunks, retreat, 0)
+    lane = lax.broadcasted_iota(jnp.int32, (n, LANES), 1)
+
+    def finish(step, carry):
+        for j in range(group):
+            c = step * group + j
+            rows = pl.ds(pl.multiple_of(c * n, n), n)
+            d_cols = jnp.zeros((n, LANES), F32)
+            for h, (pairwise, start, end, last, beta) in enumerate(decays(cols_ref[rows, :], hp, t, s, dot)):
+                kk = slice(h * dk, (h + 1) * dk)
+                vv = slice(h * dv, (h + 1) * dv)
+                q, k, v, dm = q_ref[rows, kk], k_ref[rows, kk], v_ref[rows, vv], dm_ref[rows, vv]
+                q_p, k_p, u_p = Pair(q), Pair(k), Pair(upd_ref[rows, vv])
+                state = Pair(state_ref[c * hp + h])
+                d_state = Pair(ds_ref[c * hp + h])
+                w = dot(inv_ref[c * hp + h], du_ref[rows, vv], TN)
+                scores = dot(stack(w, dm), u_p, NT)
+                d_a = jnp.where(t > s, -scores[:n], 0.0)
+                d_p = scores[n:]
+                keys = dot(stack(k, q), k_p, NT)
+                seen = dot(stack(k, q), state, NN)
+                r, qs = seen[:n], seen[n:]
+                d_r = -(beta * start) * w
+                back = dot(stack(start * dm, d_r), state, NT)
+                x = dot(u_p, d_state, NT)
+                d_qk = pairwise * d_p
+                d_kk = beta * (pairwise * d_a)
+                dq_ref[rows, kk] = back[:n] + dot(d_qk, k_p, NN)
+                dk_ref[rows, kk] = back[n:] + dot(d_qk, q_p, TN) + dot(d_kk + jnp.transpose(d_kk), k_p, NN) + end * x
+                dv_ref[rows, vv] = beta * w
+                inner = pairwise * d_a * keys[:n]
+                d_beta = jnp.sum(w * (v - start * r), axis=1, keepdims=True) + jnp.sum(inner, axis=1, keepdims=True)
+                d_start = jnp.sum(dm * qs, axis=1, keepdims=True) - beta * jnp.sum(w * r, axis=1, keepdims=True)
+                e = pairwise * d_p * keys[n:] + beta * inner
+                d_end = end * jnp.sum(k * x, axis=1, keepdims=True)
+                d_g = (jnp.sum(e, axis=1, keepdims=True) - jnp.sum(jnp.transpose(e), axis=1, keepdims=True)
+                       + d_start * start - d_end)
+                tail = jnp.sum(d_end, axis=0, keepdims=True) + last * jnp.sum(
+                    jnp.sum(state.value * d_state.value, axis=1, keepdims=True), axis=0, keepdims=True)
+                d_g = d_g + jnp.where(t[:, :1] == n - 1, tail, 0.0)
+                d_cols = jnp.where(lane == h, d_beta, d_cols)
+                d_cols = jnp.where(lane == hp + h, d_g, d_cols)
+            tri = jnp.where(t >= s, 1.0, 0.0).astype(F32)
+            dcols_ref[rows, :] = jnp.where(lane < hp, d_cols, dot(tri, d_cols, TN))
+        return carry
+
+    lax.fori_loop(0, chunks // group, finish, 0)
+
+LIMIT = 60 * 2**20
+
+def delta_forward(q, k, v, cols, hp):
+    total = q.shape[0]
+    dk, dv = q.shape[1] // hp, v.shape[1] // hp
+    jobs = total // CHUNK * hp
+    sd = jax.ShapeDtypeStruct
+    return pl.pallas_call(
+        functools.partial(fwd_kernel, hp, dk, dv, 2),
+        out_shape=(sd((total, hp * dv), F32), sd((jobs, dk, dv), F32), sd((total, hp * dv), F32),
+                   sd((jobs, CHUNK, CHUNK), F32), sd((total, hp * dk), F32)),
+        scratch_shapes=[pltpu.VMEM((jobs, CHUNK, CHUNK), F32), pltpu.VMEM((hp, dk, dv), F32)],
+        compiler_params=pltpu.CompilerParams(vmem_limit_bytes=LIMIT),
+        cost_estimate=pl.CostEstimate(
+            flops=total * hp * 9_000_000, transcendentals=total * hp * CHUNK, bytes_accessed=total * hp * 10_000
+        ),
+        name="delta_forward",
+    )(q, k, v, cols)
+
+def delta_backward(q, k, v, cols, saved, dm, hp):
+    total = q.shape[0]
+    dk, dv = q.shape[1] // hp, v.shape[1] // hp
+    jobs = total // CHUNK * hp
+    sd = jax.ShapeDtypeStruct
+    return pl.pallas_call(
+        functools.partial(bwd_kernel, hp, dk, dv, 1),
+        out_shape=(sd((total, hp * dk), F32), sd((total, hp * dk), F32), sd((total, hp * dv), F32), sd((total, LANES), F32)),
+        scratch_shapes=[pltpu.VMEM((total, hp * dv), F32), pltpu.VMEM((jobs, dk, dv), F32), pltpu.VMEM((hp, dk, dv), F32)],
+        compiler_params=pltpu.CompilerParams(vmem_limit_bytes=LIMIT),
+        cost_estimate=pl.CostEstimate(
+            flops=total * hp * 14_000_000, transcendentals=total * hp * CHUNK, bytes_accessed=total * hp * 15_000
+        ),
+        name="delta_backward",
+    )(q, k, v, cols, *saved, dm)
 
 
 def local(
@@ -281,8 +476,8 @@
     hp, vs, dk, dv, ff = plan.hp, plan.vs, plan.key_dim, plan.dv, plan.ff
     rows = w_query.shape[0]
 
-    own_tokens = tokens[0]
-    own_cot = cotangent[0]
+    own_tokens = to_ring(tokens[0])
+    own_cot = to_ring(cotangent[0])
     rider = jnp.concatenate(
         [
             (offsets[0] // 64).astype(BF)[:, None],
@@ -315,13 +510,14 @@
     gathered = lax.all_gather(
         after(jnp.concatenate([own_tokens, rider], axis=1), mix_own), "seq", axis=0, tiled=True
     )
-    w_mix = gather_dp(mix_own)
+    w_mix = gather_end(mix_own, gather_start(mix_own))
     side_own = exchange(
         after(
             jnp.concatenate([plan.split_even(w_gate), plan.split_even(w_out)], axis=2), gathered
         )
     )
-    w_side = gather_dp(after(side_own, w_mix))
+    side_own = after(side_own, w_mix)
+    w_side = gather_end(side_own, gather_start(side_own))
     mlp_own_cols = exchange(
         after(
             jnp.concatenate(
@@ -331,8 +527,8 @@
             side_own,
         )
     )
-    mlp_cols = gather_dp(after(mlp_own_cols, w_side))
-    cot_all = lax.all_gather(after(own_cot, gathered), "seq", axis=0, tiled=True)
+    mlp_near = gather_start(after(mlp_own_cols, w_side))
+    cot_all = lax.all_gather(after(own_cot, side_own), "seq", axis=0, tiled=True)
 
     at_k = hp * dk
     at_v = 2 * hp * dk
@@ -364,17 +560,22 @@
     own_bias = lax.dynamic_slice_in_dim(decay_bias, group * hp, hp, 0)
     own_gain = lax.dynamic_slice_in_dim(out_gain, (rank % vs) * dv, dv, 0)
 
-    def head_major(array):
-        return jnp.transpose(array.reshape(length, hp, -1), (1, 0, 2))
+    def by_head(array):
+        return array.reshape(length, hp, -1)
+
+    def flat(array):
+        return array.reshape(length, -1)
+
+    def unit(array):
+        array = by_head(array)
+        return flat(array * lax.rsqrt(jnp.sum(array * array, axis=-1, keepdims=True) + 1e-06))
 
     def front(query_in, key_in, value_in, tq, tk, tv, decay_in, beta_in, log_rates, rate_bias):
-        q = head_major(silu(causal_taps(query_in, tq, offs)))
-        q = q * lax.rsqrt(jnp.sum(q * q, axis=-1, keepdims=True) + 1e-06) * dk ** (-0.5)
-        k = head_major(silu(causal_taps(key_in, tk, offs)))
-        k = k * lax.rsqrt(jnp.sum(k * k, axis=-1, keepdims=True) + 1e-06)
-        v = head_major(silu(causal_taps(value_in, tv, offs)))
-        beta = jax.nn.sigmoid(beta_in).T
-        logs = (-jnp.exp(log_rates) * jax.nn.softplus(decay_in + rate_bias)).T
+        q = unit(silu(causal_taps(query_in, tq, offs))) * dk ** (-0.5)
+        k = unit(silu(causal_taps(key_in, tk, offs)))
+        v = silu(causal_taps(value_in, tv, offs))
+        beta = jax.nn.sigmoid(beta_in)
+        logs = -jnp.exp(log_rates) * jax.nn.softplus(decay_in + rate_bias)
         return q, k, v, beta, logs
 
     fronted_free, front_back = jax.vjp(
@@ -390,19 +591,28 @@
         own_log,
         own_bias,
     )
-    fronted = lax.optimization_barrier(tuple(fronted_free) + (side_own,))[:5]
-    mixed, rule_back = jax.vjp(lambda *a: delta_rule(*a, offs), *fronted)
-    gate = head_major(pre_gate)
+    query_rows, key_rows, value_rows, beta_rows, logdecay = lax.optimization_barrier(
+        tuple(fronted_free) + (side_own,)
+    )[:5]
+    cols = jnp.concatenate(
+        [
+            beta_rows,
+            logdecay,
+            offs.astype(F32)[:, None],
+            jnp.zeros((length, LANES - 2 * hp - 1), F32),
+        ],
+        axis=1,
+    )
+    mixed_flat, *saved = delta_forward(query_rows, key_rows, value_rows, cols, hp)
+    mixed_flat = after(mixed_flat, mlp_own_cols, cot_all)
+    mixed = by_head(mixed_flat)
+    gate = by_head(pre_gate)
     mix_scale = lax.rsqrt(
         plan.value_sum(jnp.sum(mixed * mixed, axis=-1, keepdims=True)) / plan.value_dim + 1e-05
     )
     m = mixed * mix_scale
     sg = silu(gate)
-
-    def token_major(array):
-        return jnp.transpose(array, (1, 0, 2)).reshape(length, -1)
-
-    gated = after(token_major(m * own_gain * sg).astype(BF), mlp_own_cols, cot_all)
+    gated = flat(m * own_gain * sg).astype(BF)
     branch = lax.psum_scatter(
         nt(gated, out_cols).astype(BF), "seq", scatter_dimension=0, tiled=True
     )
@@ -410,7 +620,11 @@
     middle = inputs + branch.astype(F32)
     r2 = rms_scale(middle)
     n2 = middle * r2
-    mlp_own = (n2 * mlp_gain_full).astype(BF)
+    near_and_cot = lax.optimization_barrier(
+        ((n2 * mlp_gain_full).astype(BF), cot_all) + tuple(mlp_near)
+    )
+    mlp_own, cot_all, mlp_near = near_and_cot[0], near_and_cot[1], near_and_cot[2:]
+    mlp_cols = gather_end(mlp_own_cols, mlp_near)
     mlp_all = lax.all_gather(mlp_own, "seq", axis=0, tiled=True)
     both_w = mlp_cols[:, : 2 * ff]
     down_w = mlp_cols[:, 2 * ff :]
@@ -434,26 +648,35 @@
     e2 = d_mlp * mlp_gain_full
     d_middle = d_output + r2 * (e2 - n2 * jnp.mean(e2 * n2, axis=-1, keepdims=True))
     d_branch_all = lax.all_gather(d_middle.astype(BF), "seq", axis=0, tiled=True)
+    both_sum = RingSum(tn(mlp_all, d_both).astype(BF))
+    down_sum = RingSum(tn(cot_all, product).astype(BF))
     mlp_out = lax.psum_scatter(
         after(nt(product, down_w).astype(BF), d_branch_all), "seq", scatter_dimension=0, tiled=True
     )
-    output = (middle + mlp_out.astype(F32)).astype(BF)
-    both_rows = to_rows(tn(mlp_all, d_both), ranks)
-    down_rows = to_rows(tn(cot_all, product), ranks)
-
-    d_gated = head_major(nn(d_branch_all, out_cols))
-    out_rows = to_rows(tn(d_branch_all, gated), ranks)
+    output = from_ring((middle + mlp_out.astype(F32)).astype(BF))
+
+    d_gated = by_head(nn(d_branch_all, out_cols))
     grad_out_gain = jnp.sum(d_gated * m * sg, axis=(0, 1))
     em = d_gated * own_gain * sg
     em_mean = plan.value_sum(jnp.sum(em * m, axis=-1, keepdims=True)) / plan.value_dim
-    d_mixed = mix_scale * (em - m * em_mean)
-    d_gate = token_major(d_gated * m * own_gain * silu_slope(gate)).astype(BF)
-    gate_rows = to_rows(tn(attn, d_gate), ranks)
+    d_mixed = flat(mix_scale * (em - m * em_mean))
+    d_gate = flat(d_gated * m * own_gain * silu_slope(gate)).astype(BF)
+    side_sum = RingSum(
+        jnp.concatenate([tn(attn, d_gate).astype(BF), tn(d_branch_all, gated).astype(BF)], axis=1)
+    )
     d_attn_gate = nt(d_gate, gate_cols)
-    ruled = lax.optimization_barrier(
-        tuple(rule_back(d_mixed)) + (mlp_out, both_rows, down_rows, out_rows, gate_rows)
-    )[:5]
-    back = front_back(ruled)
+    both_sum.second(d_mixed)
+    down_sum.second(d_mixed)
+    d_query, d_key, d_value, d_cols = delta_backward(
+        query_rows, key_rows, value_rows, cols, saved, d_mixed, hp
+    )
+    side_sum.second(d_cols)
+    both_rows = to_rows(both_sum.total(d_cols), ranks)
+    down_rows = to_rows(down_sum.total(d_cols), ranks)
+    ruled = lax.optimization_barrier((d_query, d_key, d_value, d_cols, mlp_out))
+    back = front_back(
+        (ruled[0], ruled[1], ruled[2], ruled[3][:, :hp], ruled[3][:, hp : 2 * hp])
+    )
     d_pre = jnp.concatenate(
         [
             back[0],
@@ -465,16 +688,19 @@
         ],
         axis=1,
     ).astype(BF)
-    mix_rows = to_rows(tn(attn, d_pre), ranks)
+    side_rows = to_rows(side_sum.total(d_pre), ranks)
+    mix_sum = RingSum(tn(attn, d_pre).astype(BF))
+    mix_sum.second()
+    mix_rows = to_rows(mix_sum.total(), ranks)
     d_attn = lax.psum_scatter(
         (d_attn_gate + nt(d_pre, w_mix)).astype(BF), "seq", scatter_dimension=0, tiled=True
     ).astype(F32)
 
     n = inputs * rms_scale(inputs)
     e = d_attn * attn_gain_full
-    grad_tokens = (
-        d_middle + rms_scale(inputs) * (e - n * jnp.mean(e * n, axis=-1, keepdims=True))
-    ).astype(BF)
+    grad_tokens = from_ring(
+        (d_middle + rms_scale(inputs) * (e - n * jnp.mean(e * n, axis=-1, keepdims=True))).astype(BF)
+    )
 
     sums = jnp.concatenate(
         [
@@ -504,7 +730,7 @@
     grad_value = plan.join_even(mix_rows[:, :, at_v:at_s])
     grad_decay = plan.join_keys(mix_rows[:, :, at_s : at_s + hp])
     grad_beta = plan.join_keys(mix_rows[:, :, at_s + hp : at_s + 2 * hp])
-    grad_gate = plan.join_even(gate_rows)
+    grad_gate = plan.join_even(side_rows[:, :, : hp * dv])
     grad_hidden = plan.join_even(both_rows[:, :, :ff])
     grad_up = plan.join_even(both_rows[:, :, ff:])
 
@@ -532,7 +758,7 @@
         grad_decay,
         grad_beta,
         grad_gate,
-        plan.join_even(out_rows),
+        plan.join_even(side_rows[:, :, hp * dv :]),
         per_head(every[:, :a0], KERNEL),
         per_head(every[:, a0:a1], KERNEL),
         grad_conv_value,

time: 1050 us -> 853 us (0.81)
  matrix products: 299 us -> 106 us
  waiting for transfers between devices: 363 us -> 292 us
  Pallas kernels: 0 us -> 60.7 us
  other arithmetic: 97.6 us -> 121 us
  starting transfers between devices: 86.2 us -> 73.8 us
    dot_general x141 -> x0, matrix products: 183 us -> none  [exact(): return jnp.einsum(spec, left, right, precision=HIGHEST)]
    ppermute x42 -> x36, waiting for transfers between devices: 150 us -> 67.6 us  [the longest x4 14.8 us: second(): lax.ppermute(add_low(part[rows + half:2 * rows], far_b), 'dp', left)]
    pallas_call x0 -> x2, Pallas kernels: none -> 60.7 us  [the longest x1 35.2 us: delta_backward(): pl.pallas_call(functools.partial(bwd_kernel, hp, dk, dv, 1), out_shape=(s...]
    all_to_all x3, waiting for transfers between devices: 69.5 us -> 38.4 us  [exchange(): return lax.all_to_all(turned, 'seq', 0, 0, tiled=True)]
    ppermute x3, waiting for transfers between devices: 27.4 us -> 0.69 us  [sum_everywhere(): other = lax.ppermute(held, 'seq', [(i, i ^ step) for i in range(ranks)])]
    dynamic_update_slice x15 -> x0, local copies, waits for them, and re-layouts: 21.1 us -> none  [the longest x3 5.85 us: gather_dp(): full = lax.dynamic_update_slice(full, from_left, (at_left * rows, 0))]
    mul x2 -> x10, local copies, waits for them, and re-layouts: 0.01 us -> 19.8 us  [the longest x4 10.3 us: unit(): array * lax.rsqrt(jnp.sum(array * array, axis=-1, keepdims=True) + 1e-06)]
    ppermute x8 -> x2, local copies, waits for them, and re-layouts: 18.6 us -> 3.3 us  [the longest x1 1.65 us: gather_end(): far_a = lax.ppermute(from_left[:half], 'dp', right)]
  transfers between devices with their start and end apart: 63 -> 56, of which waited for: 27 -> 20; matrix products, arithmetic and copies ran while one was open for 31% -> 38% of each run, Pallas kernels for 0% -> 7%
where the time goes in v3:
time: 853 us; the launch traced here: 843 us
  waiting for transfers between devices  292 us (34%)
  local copies, waits for them, and re-layouts  163 us (19%)
  other arithmetic  121 us (14%)
  matrix products  106 us (12%)
  starting transfers between devices  73.8 us (9%)
  Pallas kernels  60.7 us (7%)
  between operations  25.9 us (3%)
    dot_general x15, matrix products, dot_f32(): lax.dot_general(left, right, (dims, ((), ())), preferred_element_type=F32)  106 us
    reduce_scatter x1, waiting for transfers between devices, local(): lax.psum_scatter(nt(d_both, both_w).astype(BF), 'seq', scatter_dimension=...  48.8 us
    reduce_scatter x1, waiting for transfers between devices, local(): lax.psum_scatter(nt(gated, out_cols).astype(BF), 'seq', scatter_dimension...  44.4 us
    unnamed x355, local copies, waits for them, and re-layouts  43.5 us
    all_to_all x4, waiting for transfers between devices, to_rows(): turned = lax.all_to_all(mine, 'seq', 0, 0, tiled=True)  38.9 us
    all_to_all x3, waiting for transfers between devices, exchange(): return lax.all_to_all(turned, 'seq', 0, 0, tiled=True)  38.4 us
    pallas_call x1, Pallas kernels, delta_backward(): pl.pallas_call(functools.partial(bwd_kernel, hp, dk, dv, 1), out_shape=(s...  35.2 us
    pallas_call x1, Pallas kernels, delta_forward(): pl.pallas_call(functools.partial(fwd_kernel, hp, dk, dv, 2), out_shape=(s...  25.6 us
  transfers between devices with their start and end apart: 56, of which 20 were waited for; matrix products, arithmetic and copies ran while one was open for 38% of the time, Pallas kernels for 7%

profile of v3, /device:TPU:0, one launch (start us, length us, event | category | flops | bytes accessed | tf_op | source)
XLA Modules:
  0.0 842.9 jit_solution(8572226982393582393)
XLA Ops:
  14.6 6.3 all-to-all-start
  27.4 22.9 %all-to-all-done = bf16[8,64,1152]{2,1,0:T(8,128)(2,1)S(1)} async-done(((bf16[8,64,1152]{2,1,0:T(8,128)(2,1)}), bf16[8,64,1152]{2,1,0:T(8,128)(2,1)S(1)}, u32[]{:S(2)}, u32[]{:S(2)}) %all-to-all-start) | async-done | bytes 1179680 | tf_op jit(solution)/shard_map/all_to_all | solution.py:193
  66.6 4.4 concatenate.89
  84.6 14.4 %all-gather.5.cloned.1.call-done = bf16[1024,2176]{1,0:T(8,128)(2,1)} async-done(((bf16[128,2176]{1,0:T(8,128)(2,1)}), bf16[1024,2176]{1,0:T(8,128)(2,1)}) %all-gather.5.cloned.1.call-update) | async-done | bytes 4456464 | tf_op jit(solution)/shard_map/all_gather | solution.py:510
  100.5 4.3 all-to-all-start.1
  115.8 15.5 %all-to-all-done.1 = bf16[8,64,1024]{2,1,0:T(8,128)(2,1)} async-done(((bf16[8,64,1024]{2,1,0:T(8,128)(2,1)}), bf16[8,64,1024]{2,1,0:T(8,128)(2,1)}, u32[]{:S(2)}, u32[]{:S(2)}) %all-to-all-start.1) | async-done | bytes 1048608 | tf_op jit(solution)/shard_map/all_to_all | solution.py:193
  131.4 10.5 %fusion.109 = (bf16[1024,1152]{1,0:T(8,128)(2,1)S(1)}, f32[1024,1152]{1,0:T(8,128)}) fusion(bf16[2048,1152]{1,0:T(8,128)(2,1)} %constant_dynamic-update-slice_fusion, f32[2048]{0:T(1024)S(1)} %get-tuple-element.145, f32[1024]{0:T(1024)S(1)} %add_rsqrt_fusion.3, bf16[1024,2176]{1,0:T(8,128)(2,1)} %all-gather.5.cloned.1.call-done), kind=kOutput, calls=%fused_computation.330 | convolution fusion | flops 4841406464 | bytes 16003072 | tf_op jit(solution)/shard_map/dot_general | solution.py:23
  144.3 3.2 fusion.94
  147.6 3.5 mul.794
  151.1 3.2 reduce_sum.329
  167.1 3.6 fusion.26
  174.8 3.6 all-to-all-start.2
  185.4 10.4 %collective-permute-done.4 = bf16[512,1024]{1,0:T(8,128)(2,1)} collective-permute-done((bf16[512,1024]{1,0:T(8,128)(2,1)}, bf16[512,1024]{1,0:T(8,128)(2,1)}, u32[]{:S(2)}, u32[]{:S(2)}) %collective-permute-start.4) | collective-permute-done | bytes 1048608 | tf_op jit(solution)/shard_map/ppermute | solution.py:136
  199.2 25.6 %delta_forward.1 = (f32[1024,512]{1,0:T(8,128)}, f32[16,128,256]{2,1,0:T(8,128)}, f32[1024,512]{1,0:T(8,128)}, f32[16,128,128]{2,1,0:T(8,128)}, f32[1024,256]{1,0:T(8,128)}) custom-call(f32[1024,256]{1,0:T(8,128)} %fusion.59.q_ref, f32[1024,256]{1,0:T(8,128)} %bitcast_multiply_fusion.4.k_ref, f32[1024,512]{1,0:T(8,128)} %get-tuple-element.87.v_ref, ...), custom_call_target="tpu_custom_call" | custom-call | flops 18432000000 | bytes 20480000 | tf_op jit(solution)/shard_map/delta_forward/pallas_call | solution.py:417
  228.1 9.0 %collective-permute-done.7 = bf16[256,1024]{1,0:T(8,128)(2,1)S(1)} collective-permute-done((bf16[256,1024]{1,0:T(8,128)(2,1)S(1)}, bf16[256,1024]{1,0:T(8,128)(2,1)S(1)}, u32[]{:S(2)}, u32[]{:S(2)}) %collective-permute-start.7) | collective-permute-done | bytes 524320 | tf_op jit(solution)/shard_map/ppermute | solution.py:146
  239.1 6.1 fusion.31
  245.2 2.9 copy.369
  248.2 3.5 reshape.611
  251.7 2.8 multiply_reduce_fusion.5
  261.8 4.4 convolution_convert_fusion.2
  270.7 44.4 %reduce-scatter.5.cloned.1.call-done = bf16[128,2048]{1,0:T(8,128)(2,1)} async-done(((bf16[1024,2048]{1,0:T(8,128)(2,1)}), bf16[128,2048]{1,0:T(8,128)(2,1)}) %reduce-scatter.5.cloned.1.call-update) | async-done | bytes 524304 | tf_op jit(solution)/shard_map/reduce_scatter | solution.py:616
  326.8 2.9 copy.372
  329.7 4.1 copy.373
  337.8 6.7 collective-permute-done.10
  352.0 11.9 %all-gather.9.cloned.1.call-done = bf16[1024,2048]{1,0:T(8,128)(2,1)} async-done(((bf16[128,2048]{1,0:T(8,128)(2,1)}), bf16[1024,2048]{1,0:T(8,128)(2,1)}) %all-gather.9.cloned.1.call-update) | async-done | bytes 4194320 | tf_op jit(solution)/shard_map/all_gather | solution.py:628
  363.9 10.6 %fusion.5 = f32[1024,1408]{1,0:T(8,128)S(1)} fusion(bf16[1024,2048]{1,0:T(8,128)(2,1)} %all-gather.9.cloned.1.call-done, bf16[2048,2112]{1,0:T(8,128)(2,1)} %constant_dynamic-update-slice_fusion.10), kind=kOutput, calls=%fused_computation.19 | convolution fusion | flops 5905580032 | bytes 15728640 | tf_op jit(solution)/shard_map/dot_general | solution.py:23
  374.6 5.2 multiply_convert_fusion.1
  381.4 8.3 fusion.7
  389.8 48.8 %reduce-scatter.7.cloned.1.call-done = bf16[128,2048]{1,0:T(8,128)(2,1)} async-done(((bf16[1024,2048]{1,0:T(8,128)(2,1)}), bf16[128,2048]{1,0:T(8,128)(2,1)}) %reduce-scatter.7.cloned.1.call-update) | async-done | bytes 524304 | tf_op jit(solution)/shard_map/reduce_scatter | solution.py:644
  445.9 6.1 convolution_convert_fusion.4
  456.6 7.3 convolution_convert_fusion.1
  469.4 6.9 convolution_convert_fusion.3
  476.2 12.8 %all-gather.11.cloned.1.call-done = bf16[1024,2048]{1,0:T(8,128)(2,1)} async-done(((bf16[128,2048]{1,0:T(8,128)(2,1)}), bf16[1024,2048]{1,0:T(8,128)(2,1)}) %all-gather.11.cloned.1.call-update) | async-done | bytes 4194320 | tf_op jit(solution)/shard_map/all_gather | solution.py:650
  489.0 5.2 fusion.27
  496.3 3.0 copy.381
  499.3 3.1 fusion.24
  506.9 6.7 multiply_convert_fusion.3
  520.0 35.2 %delta_backward.1 = (f32[1024,256]{1,0:T(8,128)}, f32[1024,256]{1,0:T(8,128)}, f32[1024,512]{1,0:T(8,128)}, f32[1024,128]{1,0:T(8,128)}) custom-call(f32[1024,256]{1,0:T(8,128)} %fusion.59.q_ref, f32[1024,256]{1,0:T(8,128)} %bitcast_multiply_fusion.4.k_ref, f32[1024,512]{1,0:T(8,128)} %get-tuple-element.87.v_ref, f32[1024,128]{1,0:T(8,128)} %maximum_maximum_fusion.cols_ref, ...), custom_call_target="tpu_custom_call" | custom-call | flops 28672000000 | bytes 30720000 | tf_op jit(solution)/shard_map/delta_backward/pallas_call | solution.py:434
  555.2 3.2 add_convert_fusion.5
  564.7 3.5 all-to-all-start.6
  573.5 4.0 collective-permute-done.33
  577.6 13.4 %collective-permute-done.34 = bf16[256,1408]{1,0:T(8,128)(2,1)} collective-permute-done((bf16[256,1408]{1,0:T(8,128)(2,1)}, bf16[256,1408]{1,0:T(8,128)(2,1)}, u32[]{:S(2)}, u32[]{:S(2)}) %collective-permute-start.34) | collective-permute-done | bytes 720928 | tf_op jit(solution)/shard_map/ppermute | solution.py:177
  591.0 3.6 add_convert_fusion.1
  595.5 3.6 all-to-all-start.5
  599.1 5.0 convolution_convert_fusion.5
  604.1 4.9 convolution_convert_fusion.6
  617.8 8.3 collective-permute-done.18
  643.6 6.3 multiply_reduce_fusion.4
  651.2 2.8 mul.874
  654.1 3.2 reduce_sum.338
  662.0 2.8 mul.888
  664.8 3.2 reduce_sum.342
  674.9 6.0 multiply_reduce_fusion.8
  681.1 2.6 fusion.100
  690.6 3.8 concatenate.95
  694.5 10.9 %fusion.110 = f32[1024,2048]{1,0:T(8,128)} fusion(bf16[1024,1152]{1,0:T(8,128)(2,1)} %concatenate.95, bf16[2048,1152]{1,0:T(8,128)(2,1)} %constant_dynamic-update-slice_fusion), kind=kOutput, calls=%fused_computation.331 | convolution fusion | flops 4831838208 | bytes 15466496 | tf_op jit(solution)/shard_map/dot_general | solution.py:23
  705.4 6.2 convolution_convert_fusion
  722.6 4.9 all-to-all-start.4
  727.5 13.8 %collective-permute-done.25 = f32[5120]{0:T(1024)S(1)} collective-permute-done((f32[5120]{0:T(1024)S(1)}, f32[5120]{0:T(1024)S(1)}, u32[]{:S(2)}, u32[]{:S(2)}) %collective-permute-start.25) | collective-permute-done | bytes 20512 | tf_op jit(solution)/shard_map/ppermute | solution.py:208
  741.3 8.4 add_convert_fusion
  756.8 10.9 %collective-permute-done.14 = bf16[256,1152]{1,0:T(8,128)(2,1)S(1)} collective-permute-done((bf16[256,1152]{1,0:T(8,128)(2,1)S(1)}, bf16[256,1152]{1,0:T(8,128)(2,1)S(1)}, u32[]{:S(2)}, u32[]{:S(2)}) %collective-permute-start.14) | collective-permute-done | bytes 589856 | tf_op jit(solution)/shard_map/ppermute | solution.py:174
  769.1 3.2 add_convert_fusion.2
  772.3 3.9 all-to-all-start.3
  782.8 38.9 %all-to-all-done.3 = bf16[8,64,1152]{2,1,0:T(8,128)(2,1)S(1)} async-done(((bf16[8,64,1152]{2,1,0:T(8,128)(2,1)}), bf16[8,64,1152]{2,1,0:T(8,128)(2,1)S(1)}, u32[]{:S(2)}, u32[]{:S(2)}) %all-to-all-start.3) | async-done | bytes 1179680 | tf_op jit(solution)/shard_map/all_to_all | solution.py:197
  (617 shorter events, 246.2 us)
Async XLA Ops:
  14.6 35.7 %all-to-all-start = ((bf16[8,64,1152]{2,1,0:T(8,128)(2,1)}), bf16[8,64,1152]{2,1,0:T(8,128)(2,1)S(1)}, u32[]{:S(2)}, u32[]{:S(2)}) async-start(bf16[8,64,1152]{2,1,0:T(8,128)(2,1)} %copy.357), calls=%async_computation | async-start | bytes 2359296 | tf_op jit(solution)/shard_map/all_to_all | solution.py:193
  20.9 78.0 %all-gather.5.cloned.1.call-start = ((), (), s32[]{:S(2)}) async-start(), calls=%async_computation.11 | async-start | bytes 5013504 | tf_op jit(solution)/shard_map/all_gather | solution.py:510
  26.3 414.3 %copy-start.26 = (bf16[128,512]{1,0:T(8,128)(2,1)}, bf16[128,512]{1,0:T(8,128)(2,1)S(1)}, u32[]{:S(2)}) copy-start(bf16[128,512]{1,0:T(8,128)(2,1)S(1)} %get-tuple-element.249) | copy-start | bytes 393220
  26.4 414.3 %copy-start.28 = (bf16[128,512]{1,0:T(8,128)(2,1)}, bf16[128,512]{1,0:T(8,128)(2,1)S(1)}, u32[]{:S(2)}) copy-start(bf16[128,512]{1,0:T(8,128)(2,1)S(1)} %get-tuple-element.250) | copy-start | bytes 393220
  50.3 27.9 %collective-permute-start = (bf16[512,1152]{1,0:T(8,128)(2,1)S(1)}, bf16[512,1152]{1,0:T(8,128)(2,1)}, u32[]{:S(2)}, u32[]{:S(2)}) collective-permute-start(bf16[512,1152]{1,0:T(8,128)(2,1)S(1)} %bitcast.219), channel_id=1, source_target_pairs={{0,8},{8,24},{24,16},{16,0},{1,9},{9,25},{25,17},{17,1},{2,10},{10... | collective-permute-start | bytes 3538952 | tf_op jit(solution)/shard_map/ppermute | solution.py:136
  51.9 30.9 %collective-permute-start.1 = (bf16[512,1152]{1,0:T(8,128)(2,1)S(1)}, bf16[512,1152]{1,0:T(8,128)(2,1)}, u32[]{:S(2)}, u32[]{:S(2)}) collective-permute-start(bf16[512,1152]{1,0:T(8,128)(2,1)S(1)} %bitcast.220), channel_id=1, source_target_pairs={{8,0},{24,8},{16,24},{0,16},{9,1},{25,9},{17,25},{1,17},{10,2},{26... | collective-permute-start | bytes 3538952 | tf_op jit(solution)/shard_map/ppermute | solution.py:136
  80.2 29.8 %collective-permute-start.2 = (bf16[256,1152]{1,0:T(8,128)(2,1)}, bf16[256,1152]{1,0:T(8,128)(2,1)}, u32[]{:S(2)}, u32[]{:S(2)}) collective-permute-start(bf16[256,1152]{1,0:T(8,128)(2,1)} %slice.365), channel_id=1, source_target_pairs={{0,8},{8,24},{24,16},{16,0},{1,9},{9,25},{25,17},{17,1},{2,10},{10... | collective-permute-start | bytes 1769480 | tf_op jit(solution)/shard_map/ppermute | solution.py:145
  83.9 28.0 %collective-permute-start.3 = (bf16[256,1152]{1,0:T(8,128)(2,1)S(1)}, bf16[256,1152]{1,0:T(8,128)(2,1)S(1)}, u32[]{:S(2)}, u32[]{:S(2)}) collective-permute-start(bf16[256,1152]{1,0:T(8,128)(2,1)S(1)} %slice.366), channel_id=1, source_target_pairs={{8,0},{24,8},{16,24},{0,16},{9,1},{25,9},{17,25},{1,17},{10,2},{26... | collective-permute-start | bytes 1769480 | tf_op jit(solution)/shard_map/ppermute | solution.py:146
  100.5 30.9 %all-to-all-start.1 = ((bf16[8,64,1024]{2,1,0:T(8,128)(2,1)}), bf16[8,64,1024]{2,1,0:T(8,128)(2,1)}, u32[]{:S(2)}, u32[]{:S(2)}) async-start(bf16[8,64,1024]{2,1,0:T(8,128)(2,1)} %copy.362), calls=%async_computation.1 | async-start | bytes 2097152 | tf_op jit(solution)/shard_map/all_to_all | solution.py:193
  104.7 143.4 %all-gather.7.cloned.1.call-start = ((), (), s32[]{:S(2)}) async-start(), calls=%async_computation.12 | async-start | bytes 4718592 | tf_op jit(solution)/shard_map/all_gather | solution.py:531
  114.9 122.3 %copy-start.85 = (f32[2048]{0:T(1024)}, f32[2048]{0:T(1024)S(1)}, u32[]{:S(2)}) copy-start(f32[2048]{0:T(1024)S(1)} %get-tuple-element.145) | copy-start | bytes 24580
  114.9 325.8 %copy-start.83 = (f32[2048]{0:T(1024)}, f32[2048]{0:T(1024)S(1)}, u32[]{:S(2)}) copy-start(f32[2048]{0:T(1024)S(1)} %get-tuple-element.144) | copy-start | bytes 24580
  170.8 25.1 %collective-permute-start.4 = (bf16[512,1024]{1,0:T(8,128)(2,1)}, bf16[512,1024]{1,0:T(8,128)(2,1)}, u32[]{:S(2)}, u32[]{:S(2)}) collective-permute-start(bf16[512,1024]{1,0:T(8,128)(2,1)} %bitcast.28), channel_id=1, source_target_pairs={{0,8},{8,24},{24,16},{16,0},{1,9},{9,25},{25,17},{17,1},{2,10},{10... | collective-permute-start | bytes 3145736 | tf_op jit(solution)/shard_map/ppermute | solution.py:136
  174.8 73.4 %all-to-all-start.2 = ((bf16[8,64,2112]{2,1,0:T(8,128)(2,1)}), bf16[8,64,2112]{2,1,0:T(8,128)(2,1)S(1)}, u32[]{:S(2)}, u32[]{:S(2)}) async-start(bf16[8,64,2112]{2,1,0:T(8,128)(2,1)} %bitcast.211), calls=%async_computation.2 | async-start | bytes 4456448 | tf_op jit(solution)/shard_map/all_to_all | solution.py:193
  178.4 136.7 %reduce-scatter.5.cloned.1.call-start = ((), (), s32[]{:S(2)}) async-start(), calls=%async_computation.13 | async-start | bytes 4718592 | tf_op jit(solution)/shard_map/reduce_scatter | solution.py:616
  183.7 41.1 %collective-permute-start.5 = (bf16[512,1024]{1,0:T(8,128)(2,1)}, bf16[512,1024]{1,0:T(8,128)(2,1)S(1)}, u32[]{:S(2)}, u32[]{:S(2)}) collective-permute-start(bf16[512,1024]{1,0:T(8,128)(2,1)} %bitcast.28), channel_id=1, source_target_pairs={{8,0},{24,8},{16,24},{0,16},{9,1},{25,9},{17,25},{1,17},{10,2},{26... | collective-permute-start | bytes 3145736 | tf_op jit(solution)/shard_map/ppermute | solution.py:136
  197.7 30.4 %collective-permute-start.6 = (bf16[256,1024]{1,0:T(8,128)(2,1)}, bf16[256,1024]{1,0:T(8,128)(2,1)S(1)}, u32[]{:S(2)}, u32[]{:S(2)}) collective-permute-start(bf16[256,1024]{1,0:T(8,128)(2,1)} %slice.375), channel_id=1, source_target_pairs={{0,8},{8,24},{24,16},{16,0},{1,9},{9,25},{25,17},{17,1},{2,10},{10... | collective-permute-start | bytes 1572872 | tf_op jit(solution)/shard_map/ppermute | solution.py:145
  224.8 12.3 %collective-permute-start.7 = (bf16[256,1024]{1,0:T(8,128)(2,1)S(1)}, bf16[256,1024]{1,0:T(8,128)(2,1)S(1)}, u32[]{:S(2)}, u32[]{:S(2)}) collective-permute-start(bf16[256,1024]{1,0:T(8,128)(2,1)S(1)} %slice.376), channel_id=1, source_target_pairs={{8,0},{24,8},{16,24},{0,16},{9,1},{25,9},{17,25},{1,17},{10,2},{26... | collective-permute-start | bytes 1572872 | tf_op jit(solution)/shard_map/ppermute | solution.py:146
  266.2 97.7 %all-gather.9.cloned.1.call-start = ((), (), s32[]{:S(2)}) async-start(), calls=%async_computation.14 | async-start | bytes 4718592 | tf_op jit(solution)/shard_map/all_gather | solution.py:628
  268.7 49.7 %collective-permute-start.8 = (bf16[512,2112]{0,1:T(8,128)(2,1)}, bf16[512,2112]{0,1:T(8,128)(2,1)}, u32[]{:S(2)}, u32[]{:S(2)}) collective-permute-start(bf16[512,2112]{0,1:T(8,128)(2,1)} %copy.370), channel_id=1, source_target_pairs={{0,8},{8,24},{24,16},{16,0},{1,9},{9,25},{25,17},{17,1},{2,10},{10... | collective-permute-start | bytes 6488072 | tf_op jit(solution)/shard_map/ppermute | solution.py:136
  270.2 48.2 %collective-permute-start.9 = (bf16[512,2112]{0,1:T(8,128)(2,1)}, bf16[512,2112]{0,1:T(8,128)(2,1)}, u32[]{:S(2)}, u32[]{:S(2)}) collective-permute-start(bf16[512,2112]{0,1:T(8,128)(2,1)} %copy.370), channel_id=1, source_target_pairs={{8,0},{24,8},{16,24},{0,16},{9,1},{25,9},{17,25},{1,17},{10,2},{26... | collective-permute-start | bytes 6488072 | tf_op jit(solution)/shard_map/ppermute | solution.py:136
  316.4 124.3 %copy-start.128 = (f32[128]{0:T(128)}, f32[128]{0:T(128)S(1)}, u32[]{:S(2)}) copy-start(f32[128]{0:T(128)S(1)} %add_rsqrt_fusion.5) | copy-start | bytes 1540
  318.5 120.2 %reduce-scatter.7.cloned.1.call-start = ((), (), s32[]{:S(2)}) async-start(), calls=%async_computation.15 | async-start | bytes 4718592 | tf_op jit(solution)/shard_map/reduce_scatter | solution.py:644
  320.8 23.8 %collective-permute-start.10 = (bf16[256,2112]{0,1:T(8,128)(2,1)}, bf16[256,2112]{0,1:T(8,128)(2,1)}, u32[]{:S(2)}, u32[]{:S(2)}) collective-permute-start(bf16[256,2112]{0,1:T(8,128)(2,1)} %slice.313), channel_id=1, source_target_pairs={{0,8},{8,24},{24,16},{16,0},{1,9},{9,25},{25,17},{17,1},{2,10},{10... | collective-permute-start | bytes 3244040 | tf_op jit(solution)/shard_map/ppermute | solution.py:145
  324.6 23.6 %collective-permute-start.11 = (bf16[256,2112]{0,1:T(8,128)(2,1)}, bf16[256,2112]{0,1:T(8,128)(2,1)}, u32[]{:S(2)}, u32[]{:S(2)}) collective-permute-start(bf16[256,2112]{0,1:T(8,128)(2,1)} %slice.314), channel_id=1, source_target_pairs={{8,0},{24,8},{16,24},{0,16},{9,1},{25,9},{17,25},{1,17},{10,2},{26... | collective-permute-start | bytes 3244040 | tf_op jit(solution)/shard_map/ppermute | solution.py:146
  389.7 51.5 %copy-start.66 = (bf16[128,512]{1,0:T(8,128)(2,1)S(1)}, bf16[128,512]{1,0:T(8,128)(2,1)}, u32[]{:S(2)}) copy-start(bf16[128,512]{1,0:T(8,128)(2,1)} %copy-done.65) | copy-start | bytes 393220
  389.7 51.5 %copy-start.69 = (bf16[128,512]{1,0:T(8,128)(2,1)S(1)}, bf16[128,512]{1,0:T(8,128)(2,1)}, u32[]{:S(2)}) copy-start(bf16[128,512]{1,0:T(8,128)(2,1)} %copy-done.68) | copy-start | bytes 393220
  389.8 54.0 %copy-start.23 = (f32[1024,512]{0,1:T(8,128)S(1)}, f32[1024,512]{0,1:T(8,128)}, u32[]{:S(2)}) copy-start(f32[1024,512]{0,1:T(8,128)} %fusion.31) | copy-start | bytes 6291460
  389.8 99.2 %all-gather.11.cloned.1.call-start = ((), (), s32[]{:S(2)}) async-start(), calls=%async_computation.16 | async-start | bytes 4718592 | tf_op jit(solution)/shard_map/all_gather | solution.py:650
  443.5 200.1 %reduce-scatter.9.cloned.1.call-start = ((), (), s32[]{:S(2)}) async-start(), calls=%async_computation.17 | async-start | bytes 4718592 | tf_op jit(solution)/shard_map/reduce_scatter | solution.py:653
  453.2 60.5 %collective-permute-start.35 = (bf16[256,704]{0,1:T(8,128)(2,1)}, bf16[256,704]{0,1:T(8,128)(2,1)}, u32[]{:S(2)}, u32[]{:S(2)}) collective-permute-start(bf16[256,704]{0,1:T(8,128)(2,1)} %get-tuple-element.215), channel_id=1, source_target_pairs={{0,8},{8,24},{24,16},{16,0},{1,9},{9,25},{25,17},{17,1},{2,10},{10... | collective-permute-start | bytes 1081352 | tf_op jit(solution)/shard_map/ppermute | solution.py:163
  454.6 60.4 %collective-permute-start.36 = (bf16[256,704]{0,1:T(8,128)(2,1)}, bf16[256,704]{0,1:T(8,128)(2,1)}, u32[]{:S(2)}, u32[]{:S(2)}) collective-permute-start(bf16[256,704]{0,1:T(8,128)(2,1)} %get-tuple-element.214), channel_id=1, source_target_pairs={{8,0},{24,8},{16,24},{0,16},{9,1},{25,9},{17,25},{1,17},{10,2},{26... | collective-permute-start | bytes 1081352 | tf_op jit(solution)/shard_map/ppermute | solution.py:164
  455.2 103.2 %collective-permute-start.38 = (bf16[256,704]{0,1:T(8,128)(2,1)}, bf16[256,704]{0,1:T(8,128)(2,1)}, u32[]{:S(2)}, u32[]{:S(2)}) collective-permute-start(bf16[256,704]{0,1:T(8,128)(2,1)} %get-tuple-element.213), channel_id=1, source_target_pairs={{0,8},{8,24},{24,16},{16,0},{1,9},{9,25},{25,17},{17,1},{2,10},{10... | collective-permute-start | bytes 1081352 | tf_op jit(solution)/shard_map/ppermute | solution.py:165
  466.9 51.1 %collective-permute-start.29 = (bf16[256,1408]{1,0:T(8,128)(2,1)}, bf16[256,1408]{1,0:T(8,128)(2,1)}, u32[]{:S(2)}, u32[]{:S(2)}) collective-permute-start(bf16[256,1408]{1,0:T(8,128)(2,1)} %get-tuple-element.192), channel_id=1, source_target_pairs={{0,8},{8,24},{24,16},{16,0},{1,9},{9,25},{25,17},{17,1},{2,10},{10... | collective-permute-start | bytes 2162696 | tf_op jit(solution)/shard_map/ppermute | solution.py:163
  468.4 50.8 %collective-permute-start.30 = (bf16[256,1408]{1,0:T(8,128)(2,1)}, bf16[256,1408]{1,0:T(8,128)(2,1)}, u32[]{:S(2)}, u32[]{:S(2)}) collective-permute-start(bf16[256,1408]{1,0:T(8,128)(2,1)} %get-tuple-element.191), channel_id=1, source_target_pairs={{8,0},{24,8},{16,24},{0,16},{9,1},{25,9},{17,25},{1,17},{10,2},{26... | collective-permute-start | bytes 2162696 | tf_op jit(solution)/shard_map/ppermute | solution.py:164
  513.6 46.0 %collective-permute-start.39 = (bf16[256,704]{0,1:T(8,128)(2,1)S(1)}, bf16[256,704]{0,1:T(8,128)(2,1)S(1)}, u32[]{:S(2)}, u32[]{:S(2)}) collective-permute-start(bf16[256,704]{0,1:T(8,128)(2,1)S(1)} %copy-done.79), channel_id=1, source_target_pairs={{8,0},{24,8},{16,24},{0,16},{9,1},{25,9},{17,25},{1,17},{10,2},{26... | collective-permute-start | bytes 1081352 | tf_op jit(solution)/shard_map/ppermute | solution.py:166
  515.0 58.5 %collective-permute-start.32 = (bf16[256,1408]{1,0:T(8,128)(2,1)S(1)}, bf16[256,1408]{1,0:T(8,128)(2,1)S(1)}, u32[]{:S(2)}, u32[]{:S(2)}) collective-permute-start(bf16[256,1408]{1,0:T(8,128)(2,1)S(1)} %get-tuple-element.190), channel_id=1, source_target_pairs={{0,8},{8,24},{24,16},{16,0},{1,9},{9,25},{25,17},{17,1},{2,10},{10... | collective-permute-start | bytes 2162696 | tf_op jit(solution)/shard_map/ppermute | solution.py:165
  518.0 42.4 %collective-permute-start.37 = (bf16[256,704]{0,1:T(8,128)(2,1)}, bf16[256,704]{0,1:T(8,128)(2,1)S(1)}, u32[]{:S(2)}, u32[]{:S(2)}) collective-permute-start(bf16[256,704]{0,1:T(8,128)(2,1)} %get-tuple-element.211), channel_id=1, source_target_pairs={{0,8},{8,24},{24,16},{16,0},{1,9},{9,25},{25,17},{17,1},{2,10},{10... | collective-permute-start | bytes 1081352 | tf_op jit(solution)/shard_map/ppermute | solution.py:174
  519.3 42.6 %collective-permute-start.40 = (bf16[256,704]{0,1:T(8,128)(2,1)S(1)}, bf16[256,704]{0,1:T(8,128)(2,1)}, u32[]{:S(2)}, u32[]{:S(2)}) collective-permute-start(bf16[256,704]{0,1:T(8,128)(2,1)S(1)} %get-tuple-element.210), channel_id=1, source_target_pairs={{8,0},{24,8},{16,24},{0,16},{9,1},{25,9},{17,25},{1,17},{10,2},{26... | collective-permute-start | bytes 1081352 | tf_op jit(solution)/shard_map/ppermute | solution.py:177
  558.4 19.2 %collective-permute-start.33 = (bf16[256,1408]{1,0:T(8,128)(2,1)S(1)}, bf16[256,1408]{1,0:T(8,128)(2,1)}, u32[]{:S(2)}, u32[]{:S(2)}) collective-permute-start(bf16[256,1408]{1,0:T(8,128)(2,1)S(1)} %get-tuple-element.189), channel_id=1, source_target_pairs={{8,0},{24,8},{16,24},{0,16},{9,1},{25,9},{17,25},{1,17},{10,2},{26... | collective-permute-start | bytes 2162696 | tf_op jit(solution)/shard_map/ppermute | solution.py:166
  559.7 17.9 %collective-permute-start.31 = (bf16[256,1408]{1,0:T(8,128)(2,1)}, bf16[256,1408]{1,0:T(8,128)(2,1)}, u32[]{:S(2)}, u32[]{:S(2)}) collective-permute-start(bf16[256,1408]{1,0:T(8,128)(2,1)} %get-tuple-element.188), channel_id=1, source_target_pairs={{0,8},{8,24},{24,16},{16,0},{1,9},{9,25},{25,17},{17,1},{2,10},{10... | collective-permute-start | bytes 2162696 | tf_op jit(solution)/shard_map/ppermute | solution.py:174
  560.4 30.6 %collective-permute-start.34 = (bf16[256,1408]{1,0:T(8,128)(2,1)}, bf16[256,1408]{1,0:T(8,128)(2,1)}, u32[]{:S(2)}, u32[]{:S(2)}) collective-permute-start(bf16[256,1408]{1,0:T(8,128)(2,1)} %get-tuple-element.187), channel_id=1, source_target_pairs={{8,0},{24,8},{16,24},{0,16},{9,1},{25,9},{17,25},{1,17},{10,2},{26... | collective-permute-start | bytes 2162696 | tf_op jit(solution)/shard_map/ppermute | solution.py:177
  564.7 29.9 %all-to-all-start.6 = ((bf16[8,64,704]{2,1,0:T(8,128)(2,1)}), bf16[8,64,704]{2,1,0:T(8,128)(2,1)S(1)}, u32[]{:S(2)}, u32[]{:S(2)}) async-start(bf16[8,64,704]{2,1,0:T(8,128)(2,1)} %bitcast.76), calls=%async_computation.10 | async-start | bytes 1572864 | tf_op jit(solution)/shard_map/all_to_all | solution.py:197
  595.5 39.2 %all-to-all-start.5 = ((bf16[8,64,1408]{2,1,0:T(8,128)(2,1)}), bf16[8,64,1408]{2,1,0:T(8,128)(2,1)S(1)}, u32[]{:S(2)}, u32[]{:S(2)}) async-start(bf16[8,64,1408]{2,1,0:T(8,128)(2,1)} %bitcast.73), calls=%async_computation.9 | async-start | bytes 2883584 | tf_op jit(solution)/shard_map/all_to_all | solution.py:197
  611.0 15.1 %collective-permute-start.18 = (bf16[256,1024]{0,1:T(8,128)(2,1)}, bf16[256,1024]{0,1:T(8,128)(2,1)}, u32[]{:S(2)}, u32[]{:S(2)}) collective-permute-start(bf16[256,1024]{0,1:T(8,128)(2,1)} %get-tuple-element.207), channel_id=1, source_target_pairs={{0,8},{8,24},{24,16},{16,0},{1,9},{9,25},{25,17},{17,1},{2,10},{10... | collective-permute-start | bytes 1572872 | tf_op jit(solution)/shard_map/ppermute | solution.py:163
  612.4 15.1 %collective-permute-start.19 = (bf16[256,1024]{0,1:T(8,128)(2,1)}, bf16[256,1024]{0,1:T(8,128)(2,1)}, u32[]{:S(2)}, u32[]{:S(2)}) collective-permute-start(bf16[256,1024]{0,1:T(8,128)(2,1)} %get-tuple-element.208), channel_id=1, source_target_pairs={{8,0},{24,8},{16,24},{0,16},{9,1},{25,9},{17,25},{1,17},{10,2},{26... | collective-permute-start | bytes 1572872 | tf_op jit(solution)/shard_map/ppermute | solution.py:164
  613.6 100.6 %collective-permute-start.21 = (bf16[256,1024]{0,1:T(8,128)(2,1)}, bf16[256,1024]{0,1:T(8,128)(2,1)}, u32[]{:S(2)}, u32[]{:S(2)}) collective-permute-start(bf16[256,1024]{0,1:T(8,128)(2,1)} %get-tuple-element.209), channel_id=1, source_target_pairs={{0,8},{8,24},{24,16},{16,0},{1,9},{9,25},{25,17},{17,1},{2,10},{10... | collective-permute-start | bytes 1572872 | tf_op jit(solution)/shard_map/ppermute | solution.py:165
  615.0 99.7 %collective-permute-start.22 = (bf16[256,1024]{0,1:T(8,128)(2,1)}, bf16[256,1024]{0,1:T(8,128)(2,1)}, u32[]{:S(2)}, u32[]{:S(2)}) collective-permute-start(bf16[256,1024]{0,1:T(8,128)(2,1)} %get-tuple-element.206), channel_id=1, source_target_pairs={{8,0},{24,8},{16,24},{0,16},{9,1},{25,9},{17,25},{1,17},{10,2},{26... | collective-permute-start | bytes 1572872 | tf_op jit(solution)/shard_map/ppermute | solution.py:166
  629.9 86.3 %collective-permute-start.20 = (bf16[256,1024]{0,1:T(8,128)(2,1)}, bf16[256,1024]{0,1:T(8,128)(2,1)}, u32[]{:S(2)}, u32[]{:S(2)}) collective-permute-start(bf16[256,1024]{0,1:T(8,128)(2,1)} %get-tuple-element.205), channel_id=1, source_target_pairs={{0,8},{8,24},{24,16},{16,0},{1,9},{9,25},{25,17},{17,1},{2,10},{10... | collective-permute-start | bytes 1572872 | tf_op jit(solution)/shard_map/ppermute | solution.py:174
  631.4 85.4 %collective-permute-start.23 = (bf16[256,1024]{0,1:T(8,128)(2,1)}, bf16[256,1024]{0,1:T(8,128)(2,1)}, u32[]{:S(2)}, u32[]{:S(2)}) collective-permute-start(bf16[256,1024]{0,1:T(8,128)(2,1)} %get-tuple-element.204), channel_id=1, source_target_pairs={{8,0},{24,8},{16,24},{0,16},{9,1},{25,9},{17,25},{1,17},{10,2},{26... | collective-permute-start | bytes 1572872 | tf_op jit(solution)/shard_map/ppermute | solution.py:177
  683.9 34.3 %collective-permute-start.24 = (f32[5120]{0:T(1024)S(1)}, f32[5120]{0:T(1024)S(1)}, u32[]{:S(2)}, u32[]{:S(2)}) collective-permute-start(f32[5120]{0:T(1024)S(1)} %pad.181), channel_id=1, source_target_pairs={{0,8},{8,0},{16,24},{24,16},{1,9},{9,1},{17,25},{25,17},{2,10},{10... | collective-permute-start | bytes 61448 | tf_op jit(solution)/shard_map/ppermute | solution.py:208
  714.2 36.1 %collective-permute-start.12 = (bf16[256,1152]{1,0:T(8,128)(2,1)}, bf16[256,1152]{1,0:T(8,128)(2,1)}, u32[]{:S(2)}, u32[]{:S(2)}) collective-permute-start(bf16[256,1152]{1,0:T(8,128)(2,1)} %get-tuple-element.201), channel_id=1, source_target_pairs={{0,8},{8,24},{24,16},{16,0},{1,9},{9,25},{25,17},{17,1},{2,10},{10... | collective-permute-start | bytes 1769480 | tf_op jit(solution)/shard_map/ppermute | solution.py:163
  714.7 35.6 %collective-permute-start.13 = (bf16[256,1152]{1,0:T(8,128)(2,1)}, bf16[256,1152]{1,0:T(8,128)(2,1)}, u32[]{:S(2)}, u32[]{:S(2)}) collective-permute-start(bf16[256,1152]{1,0:T(8,128)(2,1)} %get-tuple-element.200), channel_id=1, source_target_pairs={{8,0},{24,8},{16,24},{0,16},{9,1},{25,9},{17,25},{1,17},{10,2},{26... | collective-permute-start | bytes 1769480 | tf_op jit(solution)/shard_map/ppermute | solution.py:164
  716.2 40.6 %collective-permute-start.15 = (bf16[256,1152]{1,0:T(8,128)(2,1)S(1)}, bf16[256,1152]{1,0:T(8,128)(2,1)}, u32[]{:S(2)}, u32[]{:S(2)}) collective-permute-start(bf16[256,1152]{1,0:T(8,128)(2,1)S(1)} %get-tuple-element.199), channel_id=1, source_target_pairs={{0,8},{8,24},{24,16},{16,0},{1,9},{9,25},{25,17},{17,1},{2,10},{10... | collective-permute-start | bytes 1769480 | tf_op jit(solution)/shard_map/ppermute | solution.py:165
  716.8 40.1 %collective-permute-start.16 = (bf16[256,1152]{1,0:T(8,128)(2,1)S(1)}, bf16[256,1152]{1,0:T(8,128)(2,1)}, u32[]{:S(2)}, u32[]{:S(2)}) collective-permute-start(bf16[256,1152]{1,0:T(8,128)(2,1)S(1)} %get-tuple-element.198), channel_id=1, source_target_pairs={{8,0},{24,8},{16,24},{0,16},{9,1},{25,9},{17,25},{1,17},{10,2},{26... | collective-permute-start | bytes 1769480 | tf_op jit(solution)/shard_map/ppermute | solution.py:166
  718.2 23.0 %collective-permute-start.25 = (f32[5120]{0:T(1024)S(1)}, f32[5120]{0:T(1024)S(1)}, u32[]{:S(2)}, u32[]{:S(2)}) collective-permute-start(f32[5120]{0:T(1024)S(1)} %pad_add_fusion), channel_id=1, source_target_pairs={{0,16},{8,24},{16,0},{24,8},{1,17},{9,25},{17,1},{25,9},{2,18},{10... | collective-permute-start | bytes 61448 | tf_op jit(solution)/shard_map/ppermute | solution.py:208
  722.6 49.7 %all-to-all-start.4 = ((bf16[8,64,1024]{2,1,0:T(8,128)(2,1)}), bf16[8,64,1024]{2,1,0:T(8,128)(2,1)S(1)}, u32[]{:S(2)}, u32[]{:S(2)}) async-start(bf16[8,64,1024]{2,1,0:T(8,128)(2,1)} %bitcast.51), calls=%async_computation.8 | async-start | bytes 2097152 | tf_op jit(solution)/shard_map/all_to_all | solution.py:197
  727.5 104.0 %reduce-scatter.11.cloned.1.call-start = ((), (), s32[]{:S(2)}) async-start(), calls=%async_computation.18 | async-start | bytes 4718592 | tf_op jit(solution)/shard_map/reduce_scatter | solution.py:695
  741.3 8.5 %collective-permute-start.26 = (f32[1,5120]{1,0:T(1,128)S(1)}, f32[1,5120]{1,0:T(1,128)S(1)}, u32[]{:S(2)}, u32[]{:S(2)}) collective-permute-start(f32[1,5120]{1,0:T(1,128)S(1)} %bitcast.248), channel_id=1, source_target_pairs={{0,1},{1,0},{2,3},{3,2},{4,5},{5,4},{6,7},{7,6},{8,9},{9,8},{10,11... | collective-permute-start | bytes 61448 | tf_op jit(solution)/shard_map/ppermute | solution.py:214
  749.9 5.1 collective-permute-start.27
  752.2 15.5 %collective-permute-start.14 = (bf16[256,1152]{1,0:T(8,128)(2,1)S(1)}, bf16[256,1152]{1,0:T(8,128)(2,1)S(1)}, u32[]{:S(2)}, u32[]{:S(2)}) collective-permute-start(bf16[256,1152]{1,0:T(8,128)(2,1)S(1)} %get-tuple-element.197), channel_id=1, source_target_pairs={{0,8},{8,24},{24,16},{16,0},{1,9},{9,25},{25,17},{17,1},{2,10},{10... | collective-permute-start | bytes 1769480 | tf_op jit(solution)/shard_map/ppermute | solution.py:174
  753.6 15.5 %collective-permute-start.17 = (bf16[256,1152]{1,0:T(8,128)(2,1)S(1)}, bf16[256,1152]{1,0:T(8,128)(2,1)S(1)}, u32[]{:S(2)}, u32[]{:S(2)}) collective-permute-start(bf16[256,1152]{1,0:T(8,128)(2,1)S(1)} %get-tuple-element.196), channel_id=1, source_target_pairs={{8,0},{24,8},{16,24},{0,16},{9,1},{25,9},{17,25},{1,17},{10,2},{26... | collective-permute-start | bytes 1769480 | tf_op jit(solution)/shard_map/ppermute | solution.py:177
  755.0 21.6 %collective-permute-start.28 = (f32[4,5120]{1,0:T(4,128)S(1)}, f32[4,5120]{1,0:T(4,128)S(1)}, u32[]{:S(2)}, u32[]{:S(2)}) collective-permute-start(f32[4,5120]{1,0:T(4,128)S(1)} %pad_maximum_fusion.7), channel_id=1, source_target_pairs={{0,4},{1,5},{2,6},{3,7},{4,0},{5,1},{6,2},{7,3},{8,12},{9,13},{10,... | collective-permute-start | bytes 245768 | tf_op jit(solution)/shard_map/ppermute | solution.py:214
  772.3 49.5 %all-to-all-start.3 = ((bf16[8,64,1152]{2,1,0:T(8,128)(2,1)}), bf16[8,64,1152]{2,1,0:T(8,128)(2,1)S(1)}, u32[]{:S(2)}, u32[]{:S(2)}) async-start(bf16[8,64,1152]{2,1,0:T(8,128)(2,1)} %bitcast.43), calls=%async_computation.7 | async-start | bytes 2359296 | tf_op jit(solution)/shard_map/all_to_all | solution.py:197
  (156 other events, 1187.3 us)
Sparse Core Ops, SparseCore 0:
  50.5 48.4 all-gather.4
  131.5 45.9 all-gather.6
  266.3 48.7 reduce-scatter.4
  318.6 45.2 all-gather.8
  389.9 48.7 reduce-scatter.6
  443.7 45.2 all-gather.10
  505.5 48.7 reduce-scatter.8
  749.9 68.4 reduce-scatter.10

commit v4 on v3

v4 whole, which is shorter than its diff:
```python
import functools

import jax
import jax.numpy as jnp
from jax import lax
from jax.experimental import pallas as pl
from jax.experimental.pallas import tpu as pltpu
from jax.sharding import PartitionSpec as P

KERNEL = 4
LANES = 128
BF = jnp.bfloat16
F32 = jnp.float32
CHUNK = 128


def rms_scale(value):
    return lax.rsqrt(jnp.mean(value * value, axis=-1, keepdims=True) + 1e-05)


def dot_f32(left, right, dims):
    return lax.dot_general(left, right, (dims, ((), ())), preferred_element_type=F32)


def nn(left, right):
    return dot_f32(left, right, ((1,), (0,)))


def nt(left, right):
    return dot_f32(left, right, ((1,), (1,)))


def tn(left, right):
    return dot_f32(left, right, ((0,), (0,)))


def silu(value):
    return value * jax.nn.sigmoid(value)


def silu_slope(value):
    s = jax.nn.sigmoid(value)
    return s * (1.0 + value * (1.0 - s))


class Plan:
    def __init__(self, ranks, heads, key_dim, value_dim, hidden):
        self.ranks = ranks
        self.heads = heads
        self.key_dim = key_dim
        self.hp = max(1, heads // ranks)
        self.vs = max(1, ranks // heads)
        self.dv = value_dim // self.vs
        self.value_dim = value_dim
        self.ff = hidden // ranks

    def split_keys(self, array):
        rows = array.shape[0]
        grouped = array.reshape(rows, self.heads // self.hp, -1)
        return jnp.repeat(grouped, self.vs, axis=1) if self.vs > 1 else grouped

    def split_even(self, array):
        return array.reshape(array.shape[0], self.ranks, -1)

    def join_keys(self, array):
        ranks, rows, width = array.shape
        array = array.astype(F32)
        if self.vs > 1:
            array = array.reshape(ranks // self.vs, self.vs, rows, width).sum(axis=1)
        return jnp.transpose(array, (1, 0, 2)).reshape(rows, -1)

    def join_even(self, array):
        return jnp.transpose(array, (1, 0, 2)).reshape(array.shape[1], -1).astype(F32)

    def value_sum(self, array):
        step = 1
        while step < self.vs:
            pairs = [(i, i ^ step) for i in range(self.ranks)]
            array = array + lax.ppermute(array, "seq", pairs)
            step *= 2
        return array


def after(value, *earlier):
    return lax.optimization_barrier((value,) + earlier)[0]


def ring_order(count):
    return [0, 1, 3, 2] if count == 4 else list(range(count))


def ring_pairs(count):
    order = ring_order(count)
    right = [(order[i], order[(i + 1) % count]) for i in range(count)]
    return right, [(there, here) for here, there in right]


def ring_place():
    me = lax.axis_index("dp")
    return me ^ (me >> 1)


def swap_blocks(array):
    size = array.shape[1] // 4
    return jnp.concatenate(
        [array[:, : 2 * size], array[:, 3 * size :], array[:, 2 * size : 3 * size]], axis=1
    )


def to_ring(array):
    if lax.axis_size("dp") != 4:
        return array
    width = array.shape[1]
    turned = swap_blocks(array)
    twice = jnp.concatenate([turned, turned], axis=1)
    return lax.dynamic_slice_in_dim(twice, ring_place() * (width // 4), width, 1)


def from_ring(array):
    if lax.axis_size("dp") != 4:
        return array
    width = array.shape[1]
    twice = jnp.concatenate([array, array], axis=1)
    at = (4 - ring_place()) * (width // 4)
    return swap_blocks(lax.dynamic_slice_in_dim(twice, at, width, 1))


def gather_start(own):
    if lax.axis_size("dp") != 4:
        return ()
    right, left = ring_pairs(4)
    return lax.ppermute(own, "dp", right), lax.ppermute(own, "dp", left)


def gather_end(own, near):
    if lax.axis_size("dp") != 4:
        return lax.all_gather(own, "dp", axis=0, tiled=True)
    right, left = ring_pairs(4)
    half = own.shape[0] // 2
    from_left, from_right = near
    far_a = lax.ppermute(from_left[:half], "dp", right)
    far_b = lax.ppermute(from_right[half:], "dp", left)
    return jnp.concatenate([own, from_right, far_a, far_b, from_left])


class RingGrad:
    def __init__(self, left, right):
        self.ring = lax.axis_size("dp") == 4
        self.left, self.right = left, right
        rows = self.rows = left.shape[1] // lax.axis_size("dp")
        self.half = rows // 2
        self.sent, self.near, self.late = (), (), ()
        if self.ring:
            to_right, to_left = ring_pairs(4)
            self.sent = tuple(self.part(i).astype(BF) for i in (4, 5, 3, 6))
            self.near = (
                lax.ppermute(self.sent[0], "dp", to_right),
                lax.ppermute(self.sent[1], "dp", to_left),
                lax.ppermute(self.sent[2], "dp", to_right),
                lax.ppermute(self.sent[3], "dp", to_left),
            )

    def part(self, index):
        at = index * self.half
        return tn(self.left[:, at : at + self.half], self.right)

    def second(self, *earlier):
        if self.ring:
            to_right, to_left = ring_pairs(4)
            far_a, far_b = lax.optimization_barrier(self.near[:2] + earlier)[:2]
            self.late = (
                lax.ppermute((self.part(2) + far_a.astype(F32)).astype(BF), "dp", to_right),
                lax.ppermute((self.part(7) + far_b.astype(F32)).astype(BF), "dp", to_left),
            )

    def total(self, *earlier):
        if not self.ring:
            whole = tn(self.left, self.right).astype(BF)
            return lax.psum_scatter(whole, "dp", scatter_dimension=0, tiled=True)
        held = lax.optimization_barrier(self.near[2:] + self.late + earlier)
        right_b, left_a, right_a, left_b = held[:4]
        own = tn(self.left[:, : self.rows], self.right)
        from_left = jnp.concatenate([right_a, right_b]).astype(F32)
        from_right = jnp.concatenate([left_a, left_b]).astype(F32)
        return (own + from_left + from_right).astype(BF)


def exchange(packed):
    turned = jnp.transpose(packed, (1, 0, 2)).reshape(-1, packed.shape[2])
    return lax.all_to_all(turned, "seq", 0, 0, tiled=True)


def to_rows(mine, ranks):
    turned = lax.all_to_all(mine, "seq", 0, 0, tiled=True)
    return turned.reshape(ranks, -1, mine.shape[1])


def sum_everywhere(values):
    count = lax.axis_size("dp")
    ranks = lax.axis_size("seq")
    if count & (count - 1) or ranks & (ranks - 1):
        return lax.all_gather(lax.psum(values, "dp"), "seq", axis=0, tiled=False)
    step = 1
    while step < count:
        values = values + lax.ppermute(values, "dp", [(i, i ^ step) for i in range(count)])
        step *= 2
    rank = lax.axis_index("seq")
    held = values.reshape(1, -1)
    step = 1
    while step < ranks:
        other = lax.ppermute(held, "seq", [(i, i ^ step) for i in range(ranks)])
        upper = (rank & step) != 0
        held = jnp.concatenate([jnp.where(upper, other, held), jnp.where(upper, held, other)])
        step *= 2
    return held


class Pair:
    def __init__(self, value):
        self.value = value
        self.high = value.astype(BF)
        self.low = (value - self.high.astype(F32)).astype(BF)


def pair(value):
    return value if isinstance(value, Pair) else Pair(value)


NN = ((1,), (0,))
NT = ((1,), (1,))
TN = ((0,), (0,))


def dot(left, right, dims):
    a, b = pair(left), pair(right)
    return dot_f32(a.high, b.high, dims) + (
        dot_f32(a.high, b.low, dims) + dot_f32(a.low, b.high, dims)
    )


def stack(top, bottom):
    return jnp.concatenate([top, bottom], axis=0)


def grids(n):
    t = lax.broadcasted_iota(jnp.int32, (n, n), 0)
    s = lax.broadcasted_iota(jnp.int32, (n, n), 1)
    return t, s


def inverses(stricts, t, s):
    n = t.shape[0]
    eye = jnp.where(t == s, 1.0, 0.0).astype(F32)
    same = (t // 8) == (s // 8)
    small = [Pair(jnp.where(same, a, 0.0)) for a in stricts]
    square = [Pair(dot(a, a, NN)) for a in small]
    fourth = [dot(a, a, NN) for a in square]
    first = [eye - a.value for a in small]
    inv = [f + dot(f, a, NN) for f, a in zip(first, square)]
    inv = [f + dot(f, a, NN) for f, a in zip(inv, fourth)]
    size = 8
    while size < n:
        take = ((t // (2 * size)) == (s // (2 * size))) & ((t // size) != (s // size))
        held = [Pair(f) for f in inv]
        part = [dot(f, jnp.where(take, a, 0.0), NN) for f, a in zip(held, stricts)]
        inv = [f.value - dot(p, f, NN) for f, p in zip(held, part)]
        size *= 2
    return inv


def decays(cols, hp, t, s):
    n = t.shape[0]
    tri = jnp.where(t >= s, 1.0, 0.0).astype(F32)
    run = dot(tri, cols, NN)
    turned = jnp.transpose(run)
    offs = cols[:, 2 * hp : 2 * hp + 1]
    row = t[:, :1].astype(F32)
    gap = (t - s).astype(F32)
    same = (gap >= 0.0) & (offs >= gap)
    keep = offs[n - 1 : n, :] >= (n - 1.0) - row
    out = []
    for h in range(hp):
        g = run[:, h : h + 1]
        g_row = turned[h : h + 1, :]
        pairwise = jnp.where(same, jnp.exp(jnp.where(same, g - g_row, 0.0)), 0.0)
        start = jnp.where(offs > row, jnp.exp(g), 0.0)
        end = jnp.where(keep, jnp.exp(jnp.where(keep, g[n - 1 : n, :] - g, 0.0)), 0.0)
        out.append((pairwise, start, end, start[n - 1 : n, :], cols[:, hp + h : hp + h + 1]))
    return out


def lanes_of(hp, dk, dv):
    q = [slice(h * dk, (h + 1) * dk) for h in range(hp)]
    k = [slice((hp + h) * dk, (hp + h + 1) * dk) for h in range(hp)]
    v = [slice(2 * hp * dk + h * dv, 2 * hp * dk + (h + 1) * dv) for h in range(hp)]
    return q, k, v


def chunk_rows(c):
    return pl.ds(pl.multiple_of(c * CHUNK, CHUNK), CHUNK)


def chunk_cols(hp, rows, small_ref, rider_ref, const_ref):
    lane = lax.broadcasted_iota(jnp.int32, (CHUNK, LANES), 1)
    x = small_ref[rows, :]
    y = x + const_ref[1:2, :]
    logs = const_ref[0:1, :] * (jnp.maximum(y, 0.0) + jnp.log1p(jnp.exp(-jnp.abs(y))))
    beta = jax.nn.sigmoid(x)
    rider = rider_ref[rows, :].astype(F32)
    offs = rider[:, 0:1] * 64.0 + rider[:, 1:2]
    cols = jnp.where(lane < hp, logs, jnp.where(lane < 2 * hp, beta, 0.0))
    return jnp.where(lane == 2 * hp, offs, cols), offs


def conved_lanes(c, lanes, offs, pre_ref, taps_ref):
    rows = chunk_rows(c)
    above = pl.ds(pl.multiple_of(jnp.maximum(c * CHUNK - 16, 0), 16), 16)
    block = pre_ref[rows, lanes].astype(F32)
    ext = stack(pre_ref[above, lanes].astype(F32), block)
    total = taps_ref[0:1, lanes] * block
    for by in range(1, KERNEL):
        moved = pltpu.roll(ext, by, 0)[16:]
        total = total + taps_ref[by : by + 1, lanes] * jnp.where(offs >= by, moved, 0.0)
    return total


def unit_scale(u):
    return lax.rsqrt(jnp.sum(u * u, axis=1, keepdims=True) + 1e-06)


def fill_front(hp, dk, dv, c, pre_ref, small_ref, rider_ref, taps_ref, const_ref, qkv_ref, cols_ref, conv_ref):
    rows = chunk_rows(c)
    cols, offs = chunk_cols(hp, rows, small_ref, rider_ref, const_ref)
    cols_ref[rows, :] = cols
    for kind, slices in enumerate(lanes_of(hp, dk, dv)):
        for lanes in slices:
            conved = conved_lanes(c, lanes, offs, pre_ref, taps_ref)
            if conv_ref is not None:
                conv_ref[rows, lanes] = conved
            u = conved * jax.nn.sigmoid(conved)
            if kind == 0:
                u = u * (unit_scale(u) * dk ** (-0.5))
            elif kind == 1:
                u = u * unit_scale(u)
            qkv_ref[rows, lanes] = u


def fwd_kernel(
    hp, dk, dv, pre_ref, small_ref, rider_ref, taps_ref, const_ref,
    mixed_ref, state_ref, upd_ref, inv_ref, seen_ref,
    qkv_ref, cols_ref, p_ref, cur_ref,
):
    n = CHUNK
    chunks = pre_ref.shape[0] // n
    group = 2 if chunks % 2 == 0 else 1
    t, s = grids(n)
    q_at, k_at, v_at = lanes_of(hp, dk, dv)

    def prepare(step, carry):
        jobs = []
        for j in range(group):
            c = step * group + j
            fill_front(
                hp, dk, dv, c, pre_ref, small_ref, rider_ref, taps_ref, const_ref, qkv_ref, cols_ref, None
            )
            rows = chunk_rows(c)
            for h, d in enumerate(decays(cols_ref[rows, :], hp, t, s)):
                jobs.append((c, rows, h) + d)
        keys = [qkv_ref[r, k_at[h]] for _, r, h, *_ in jobs]
        both = [dot(stack(k, qkv_ref[job[1], q_at[job[2]]]), k, NT) for k, job in zip(keys, jobs)]
        strict = [jnp.where(t > s, job[3] * b[:n], 0.0) * job[7] for job, b in zip(jobs, both)]
        inv = [Pair(i) for i in inverses(strict, t, s)]
        for job, b, i, k in zip(jobs, both, inv, keys):
            c, r, h, pairwise, start, end, last, beta = job
            p_ref[c * hp + h] = pairwise * b[n:]
            inv_ref[c * hp + h] = i.value
            upd_ref[r, h * dv : (h + 1) * dv] = dot(i, beta * qkv_ref[r, v_at[h]], NN)
            seen_ref[r, h * dk : (h + 1) * dk] = dot(i, (beta * start) * k, NN)
        return carry

    lax.fori_loop(0, chunks // group, prepare, 0)
    cur_ref[...] = jnp.zeros_like(cur_ref)

    def advance(c, carry):
        rows = chunk_rows(c)
        for h, (pairwise, start, end, last, beta) in enumerate(decays(cols_ref[rows, :], hp, t, s)):
            vv = slice(h * dv, (h + 1) * dv)
            state = cur_ref[h]
            state_ref[c * hp + h] = state
            seen = seen_ref[rows, h * dk : (h + 1) * dk]
            both = dot(stack(seen, qkv_ref[rows, q_at[h]] * start), state, NN)
            update = Pair(upd_ref[rows, vv] - both[:n])
            upd_ref[rows, vv] = update.value
            mixed_ref[rows, vv] = both[n:] + dot(p_ref[c * hp + h], update, NN)
            cur_ref[h] = last * state + dot(qkv_ref[rows, k_at[h]] * end, update, TN)
        return carry

    lax.fori_loop(0, chunks, advance, 0)


def bwd_kernel(
    hp, dk, dv, pre_ref, small_ref, rider_ref, taps_ref, const_ref,
    state_ref, upd_ref, inv_ref, seen_ref, dm_ref,
    dpre_ref, dtaps_ref, sums_ref,
    qkv_ref, cols_ref, conv_ref, dcon_ref, dcols_ref, du_ref, ds_ref, cur_ref,
):
    n = CHUNK
    total = pre_ref.shape[0]
    chunks = total // n
    t, s = grids(n)
    q_at, k_at, v_at = lanes_of(hp, dk, dv)
    wide = 2 * hp * dk + hp * dv
    cur_ref[...] = jnp.zeros_like(cur_ref)
    dtaps_ref[...] = jnp.zeros_like(dtaps_ref)
    sums_ref[...] = jnp.zeros_like(sums_ref)
    dcon_ref[total:, :] = jnp.zeros((dcon_ref.shape[0] - total, wide), F32)
    cols_ref[total:, :] = jnp.zeros((cols_ref.shape[0] - total, LANES), F32)

    def retreat(step, carry):
        c = chunks - 1 - step
        rows = chunk_rows(c)
        fill_front(
            hp, dk, dv, c, pre_ref, small_ref, rider_ref, taps_ref, const_ref, qkv_ref, cols_ref, conv_ref
        )
        for h, (pairwise, start, end, last, beta) in enumerate(decays(cols_ref[rows, :], hp, t, s)):
            vv = slice(h * dv, (h + 1) * dv)
            d_state = cur_ref[h]
            ds_ref[c * hp + h] = d_state
            dm = Pair(dm_ref[rows, vv])
            q, k = qkv_ref[rows, q_at[h]], qkv_ref[rows, k_at[h]]
            p = pairwise * dot(q, k, NT)
            du = dot(p, dm, TN) + dot(k * end, d_state, NN)
            du_ref[rows, vv] = du
            seen = seen_ref[rows, h * dk : (h + 1) * dk]
            cur_ref[h] = last * d_state + dot(q * start, dm, TN) - dot(seen, du, TN)
        return carry

    lax.fori_loop(0, chunks, retreat, 0)
    lane = lax.broadcasted_iota(jnp.int32, (n, LANES), 1)

    def through_silu(rows, lanes, dy, unit):
        conved = conv_ref[rows, lanes]
        sig = jax.nn.sigmoid(conved)
        if unit:
            u = conved * sig
            scale = unit_scale(u)
            dy = scale * dy - (scale * scale * scale) * u * jnp.sum(u * dy, axis=1, keepdims=True)
        dcon_ref[rows, lanes] = dy * (sig * (1.0 + conved * (1.0 - sig)))

    def finish(c, carry):
        rows = chunk_rows(c)
        d_cols = jnp.zeros((n, LANES), F32)
        for h, (pairwise, start, end, last, beta) in enumerate(decays(cols_ref[rows, :], hp, t, s)):
            vv = slice(h * dv, (h + 1) * dv)
            q, k, v = qkv_ref[rows, q_at[h]], qkv_ref[rows, k_at[h]], qkv_ref[rows, v_at[h]]
            dm = dm_ref[rows, vv]
            q_p, k_p, u_p = Pair(q), Pair(k), Pair(upd_ref[rows, vv])
            state = Pair(state_ref[c * hp + h])
            d_state = Pair(ds_ref[c * hp + h])
            w = dot(inv_ref[c * hp + h], du_ref[rows, vv], TN)
            scores = dot(stack(w, dm), u_p, NT)
            d_a = jnp.where(t > s, -scores[:n], 0.0)
            d_p = scores[n:]
            keys = dot(stack(k, q), k_p, NT)
            met = dot(stack(k, q), state, NN)
            r, qs = met[:n], met[n:]
            back = dot(stack(start * dm, -(beta * start) * w), state, NT)
            x = dot(u_p, d_state, NT)
            d_qk = pairwise * d_p
            d_kk = beta * (pairwise * d_a)
            d_query = back[:n] + dot(d_qk, k_p, NN)
            d_key = (
                back[n:]
                + dot(d_qk, q_p, TN)
                + dot(d_kk + jnp.transpose(d_kk), k_p, NN)
                + end * x
            )
            through_silu(rows, q_at[h], d_query * dk ** (-0.5), True)
            through_silu(rows, k_at[h], d_key, True)
            through_silu(rows, v_at[h], beta * w, False)
            inner = pairwise * d_a * keys[:n]
            d_beta = jnp.sum(w * (v - start * r), axis=1, keepdims=True) + jnp.sum(
                inner, axis=1, keepdims=True
            )
            d_start = jnp.sum(dm * qs, axis=1, keepdims=True) - beta * jnp.sum(
                w * r, axis=1, keepdims=True
            )
            e = pairwise * d_p * keys[n:] + beta * inner
            d_end = end * jnp.sum(k * x, axis=1, keepdims=True)
            d_g = (
                jnp.sum(e, axis=1, keepdims=True)
                - jnp.sum(jnp.transpose(e), axis=1, keepdims=True)
                + d_start * start
                - d_end
            )
            held = jnp.sum(
                jnp.sum(state.value * d_state.value, axis=1, keepdims=True), axis=0, keepdims=True
            )
            tail = jnp.sum(d_end, axis=0, keepdims=True) + last * held
            d_g = d_g + jnp.where(t[:, :1] == n - 1, tail, 0.0)
            d_cols = jnp.where(lane == h, d_g, d_cols)
            d_cols = jnp.where(lane == hp + h, d_beta, d_cols)
        tri = jnp.where(t >= s, 1.0, 0.0).astype(F32)
        dcols_ref[rows, :] = jnp.where(lane < hp, dot(tri, d_cols, TN), d_cols)
        return carry

    lax.fori_loop(0, chunks, finish, 0)

    def spread(c, carry):
        rows = chunk_rows(c)
        below = pl.ds(pl.multiple_of((c + 1) * n, n), 8)
        cols = cols_ref[rows, :]
        offs = cols[:, 2 * hp : 2 * hp + 1]
        offs_below = cols_ref[below, 2 * hp : 2 * hp + 1]
        for slices in (q_at, k_at, v_at):
            for lanes in slices:
                pre = pre_ref[rows, lanes].astype(F32)
                d_con = dcon_ref[rows, lanes]
                d_below = dcon_ref[below, lanes]
                out = taps_ref[0:1, lanes] * d_con
                dtaps_ref[0:1, lanes] += jnp.sum(pre * d_con, axis=0, keepdims=True)
                for by in range(1, KERNEL):
                    ext = stack(
                        jnp.where(offs >= by, d_con, 0.0), jnp.where(offs_below >= by, d_below, 0.0)
                    )
                    moved = pltpu.roll(ext, n + 8 - by, 0)[:n]
                    out = out + taps_ref[by : by + 1, lanes] * moved
                    dtaps_ref[by : by + 1, lanes] += jnp.sum(pre * moved, axis=0, keepdims=True)
                dpre_ref[rows, lanes] = out.astype(BF)
        d_cols = dcols_ref[rows, :]
        slope = const_ref[0:1, :] * jax.nn.sigmoid(small_ref[rows, :] + const_ref[1:2, :])
        d_small = jnp.where(lane < hp, d_cols * slope, d_cols * cols * (1.0 - cols))
        d_small = jnp.where(lane < 2 * hp, d_small, 0.0)
        dpre_ref[rows, wide:] = d_small.astype(BF)
        sums_ref[0:1, :] += jnp.sum(d_small, axis=0, keepdims=True)
        sums_ref[1:2, :] += jnp.sum(d_cols * cols, axis=0, keepdims=True)
        return carry

    lax.fori_loop(0, chunks, spread, 0)


def gate_kernel(hp, dv, mixed_ref, gate_ref, gain_ref, out_ref):
    for h in range(hp):
        at = slice(h * dv, (h + 1) * dv)
        mixed = mixed_ref[:, at]
        scale = lax.rsqrt(jnp.mean(mixed * mixed, axis=1, keepdims=True) + 1e-05)
        gate = gate_ref[:, at]
        out_ref[:, at] = (mixed * scale * gain_ref[0:1, :] * (gate * jax.nn.sigmoid(gate))).astype(BF)


def gate_back_kernel(hp, dv, d_ref, mixed_ref, gate_ref, gain_ref, dm_ref, dgate_ref, dgain_ref):
    @pl.when(pl.program_id(0) == 0)
    def _():
        dgain_ref[...] = jnp.zeros_like(dgain_ref)

    gain = gain_ref[0:1, :]
    for h in range(hp):
        at = slice(h * dv, (h + 1) * dv)
        mixed = mixed_ref[:, at]
        scale = lax.rsqrt(jnp.mean(mixed * mixed, axis=1, keepdims=True) + 1e-05)
        m = mixed * scale
        gate = gate_ref[:, at]
        sig = jax.nn.sigmoid(gate)
        through = d_ref[:, at] * (gate * sig)
        dgain_ref[0:1, :] += jnp.sum(through * m, axis=0, keepdims=True)
        em = through * gain
        dm_ref[:, at] = scale * (em - m * jnp.mean(em * m, axis=1, keepdims=True))
        slope = sig * (1.0 + gate * (1.0 - sig))
        dgate_ref[:, at] = (d_ref[:, at] * m * gain * slope).astype(BF)


VMEM_LIMIT = 60 * 2**20


def shape_of(*dims, dtype=F32):
    return jax.ShapeDtypeStruct(dims, dtype)


def delta_forward(pre, small, rider, taps, const, hp, dk, dv):
    total, wide = pre.shape
    jobs = total // CHUNK * hp
    return pl.pallas_call(
        functools.partial(fwd_kernel, hp, dk, dv),
        out_shape=(
            shape_of(total, hp * dv),
            shape_of(jobs, dk, dv),
            shape_of(total, hp * dv),
            shape_of(jobs, CHUNK, CHUNK),
            shape_of(total, hp * dk),
        ),
        scratch_shapes=[
            pltpu.VMEM((total, wide), F32),
            pltpu.VMEM((total, LANES), F32),
            pltpu.VMEM((jobs, CHUNK, CHUNK), F32),
            pltpu.VMEM((hp, dk, dv), F32),
        ],
        compiler_params=pltpu.CompilerParams(vmem_limit_bytes=VMEM_LIMIT),
        cost_estimate=pl.CostEstimate(
            flops=total * hp * 21_000_000,
            transcendentals=total * hp * CHUNK,
            bytes_accessed=total * wide * 16,
        ),
        name="delta_forward",
    )(pre, small, rider, taps, const)


def delta_backward(pre, small, rider, taps, const, saved, d_mixed, hp, dk, dv):
    total, wide = pre.shape
    jobs = total // CHUNK * hp
    return pl.pallas_call(
        functools.partial(bwd_kernel, hp, dk, dv),
        out_shape=(
            shape_of(total, wide + LANES, dtype=BF),
            shape_of(8, wide),
            shape_of(8, LANES),
        ),
        scratch_shapes=[
            pltpu.VMEM((total, wide), F32),
            pltpu.VMEM((total + 8, LANES), F32),
            pltpu.VMEM((total, wide), F32),
            pltpu.VMEM((total + 8, wide), F32),
            pltpu.VMEM((total, LANES), F32),
            pltpu.VMEM((total, hp * dv), F32),
            pltpu.VMEM((jobs, dk, dv), F32),
            pltpu.VMEM((hp, dk, dv), F32),
        ],
        compiler_params=pltpu.CompilerParams(vmem_limit_bytes=VMEM_LIMIT),
        cost_estimate=pl.CostEstimate(
            flops=total * hp * 34_000_000,
            transcendentals=total * hp * CHUNK,
            bytes_accessed=total * wide * 20,
        ),
        name="delta_backward",
    )(pre, small, rider, taps, const, *saved, d_mixed)


GATE_ROWS = 256


def gate_forward(mixed, gate, gain, hp, dv):
    total, wide = mixed.shape
    rows = min(GATE_ROWS, total)
    block = pl.BlockSpec((rows, wide), lambda i: (i, 0))
    return pl.pallas_call(
        functools.partial(gate_kernel, hp, dv),
        grid=(total // rows,),
        in_specs=[block, block, pl.BlockSpec((1, dv), lambda i: (0, 0))],
        out_specs=block,
        out_shape=shape_of(total, wide, dtype=BF),
        name="gate_forward",
    )(mixed, gate, gain)


def gate_backward(d_gated, mixed, gate, gain, hp, dv):
    total, wide = mixed.shape
    rows = min(GATE_ROWS, total)
    block = pl.BlockSpec((rows, wide), lambda i: (i, 0))
    return pl.pallas_call(
        functools.partial(gate_back_kernel, hp, dv),
        grid=(total // rows,),
        in_specs=[block, block, block, pl.BlockSpec((1, dv), lambda i: (0, 0))],
        out_specs=(block, block, pl.BlockSpec((8, dv), lambda i: (0, 0))),
        out_shape=(
            shape_of(total, wide),
            shape_of(total, wide, dtype=BF),
            shape_of(8, dv),
        ),
        name="gate_backward",
    )(d_gated, mixed, gate, gain)


def local(
    tokens,
    attn_gain,
    w_query,
    w_key,
    w_value,
    w_decay,
    w_beta,
    w_gate,
    w_out,
    conv_query,
    conv_key,
    conv_value,
    decay_log,
    decay_bias,
    out_gain,
    mlp_gain,
    w_hidden,
    w_up,
    w_down,
    offsets,
    cotangent,
):
    ranks = lax.axis_size("seq")
    rank = lax.axis_index("seq")
    heads = decay_log.shape[0]
    width = tokens.shape[-1]
    tok = tokens.shape[1]
    length = tok * ranks
    plan = Plan(ranks, heads, w_query.shape[1] // heads, out_gain.shape[0], w_hidden.shape[1])
    hp, vs, dk, dv, ff = plan.hp, plan.vs, plan.key_dim, plan.dv, plan.ff
    rows = w_query.shape[0]

    own_tokens = to_ring(tokens[0])
    own_cot = to_ring(cotangent[0])
    rider = jnp.concatenate(
        [
            (offsets[0] // 64).astype(BF)[:, None],
            (offsets[0] % 64).astype(BF)[:, None],
            jnp.zeros((tok, LANES - 2), BF),
        ],
        axis=1,
    )
    small = jnp.concatenate(
        [
            plan.split_keys(w_decay),
            plan.split_keys(w_beta),
            jnp.broadcast_to(attn_gain[:, None, None], (rows, ranks, 1)),
            jnp.broadcast_to(mlp_gain[:, None, None], (rows, ranks, 1)),
            jnp.zeros((rows, ranks, LANES - 2 - 2 * hp), BF),
        ],
        axis=2,
    )
    mix_own = exchange(
        jnp.concatenate(
            [
                plan.split_keys(w_query),
                plan.split_keys(w_key),
                plan.split_even(w_value),
                small,
            ],
            axis=2,
        )
    )
    gathered = lax.all_gather(
        after(jnp.concatenate([own_tokens, rider], axis=1), mix_own), "seq", axis=0, tiled=True
    )
    w_mix = gather_end(mix_own, gather_start(mix_own))
    side_own = exchange(
        after(
            jnp.concatenate([plan.split_even(w_gate), plan.split_even(w_out)], axis=2), mix_own
        )
    )
    side_own = after(side_own, w_mix)
    w_side = gather_end(side_own, gather_start(side_own))
    mlp_own_cols = exchange(
        after(
            jnp.concatenate(
                [plan.split_even(w_hidden), plan.split_even(w_up), plan.split_even(w_down)],
                axis=2,
            ),
            side_own,
            gathered,
        )
    )
    mlp_near = gather_start(after(mlp_own_cols, w_side))

    at_k = hp * dk
    at_v = 2 * hp * dk
    at_s = at_v + hp * dv
    attn_gain_full = w_mix[:, at_s + 2 * hp].astype(F32)
    mlp_gain_full = w_mix[:, at_s + 2 * hp + 1].astype(F32)
    gate_cols = w_side[:, : hp * dv]
    out_cols = w_side[:, hp * dv :]

    tokens_all = gathered[:, :width].astype(F32)
    normed_all = tokens_all * rms_scale(tokens_all)
    attn = (normed_all * attn_gain_full).astype(BF)
    pre = nn(attn, w_mix[:, :at_s]).astype(BF)
    pre_small = nn(attn, w_mix[:, at_s:])
    cot_all = lax.all_gather(after(own_cot, pre), "seq", axis=0, tiled=True)
    pre_gate = nn(attn, gate_cols)

    group = rank // vs
    taps_query = lax.dynamic_slice_in_dim(conv_query, group * hp * dk, hp * dk, 1)
    taps_key = lax.dynamic_slice_in_dim(conv_key, group * hp * dk, hp * dk, 1)
    taps_value = lax.dynamic_slice_in_dim(conv_value, rank * hp * dv, hp * dv, 1)
    own_log = lax.dynamic_slice_in_dim(decay_log, group * hp, hp, 0)
    own_bias = lax.dynamic_slice_in_dim(decay_bias, group * hp, hp, 0)
    own_gain = lax.dynamic_slice_in_dim(out_gain, (rank % vs) * dv, dv, 0)

    taps = jnp.concatenate([taps_query, taps_key, taps_value], axis=1)
    const = jnp.pad(jnp.stack([-jnp.exp(own_log), own_bias]), ((0, 0), (0, LANES - hp)))
    pre, pre_small = lax.optimization_barrier((pre, pre_small, side_own))[:2]
    rider_all = gathered[:, width:]
    mixed, *saved = delta_forward(pre, pre_small, rider_all, taps, const, hp, dk, dv)

    def by_head(array):
        return array.reshape(length, hp, -1)

    def gate_apply(mixed_in, gate_in, gain_in):
        m = by_head(mixed_in)
        square = plan.value_sum(jnp.sum(m * m, axis=-1, keepdims=True))
        scale = lax.rsqrt(square / plan.value_dim + 1e-05)
        return (m * scale * gain_in * silu(by_head(gate_in))).reshape(length, -1)

    def gate_apply_back(d_out, mixed_in, gate_in, gain_in):
        d, mixed_in, gate_in = by_head(d_out), by_head(mixed_in), by_head(gate_in)
        square = plan.value_sum(jnp.sum(mixed_in * mixed_in, axis=-1, keepdims=True))
        scale = lax.rsqrt(square / plan.value_dim + 1e-05)
        m = mixed_in * scale
        through = d * silu(gate_in)
        em = through * gain_in
        mean = plan.value_sum(jnp.sum(em * m, axis=-1, keepdims=True)) / plan.value_dim
        d_mix = scale * (em - m * mean)
        d_gt = d * m * gain_in * silu_slope(gate_in)
        return (
            d_mix.reshape(length, -1),
            d_gt.reshape(length, -1).astype(BF),
            jnp.sum(through * m, axis=(0, 1)),
        )

    if vs == 1:
        gated = gate_forward(mixed, pre_gate, own_gain[None], hp, dv)
    else:
        gated = gate_apply(mixed, pre_gate, own_gain).astype(BF)
    gated = after(gated, mlp_own_cols, cot_all)
    branch = lax.psum_scatter(
        nt(gated, out_cols).astype(BF), "seq", scatter_dimension=0, tiled=True
    )
    inputs = own_tokens.astype(F32)
    middle = inputs + branch.astype(F32)
    r2 = rms_scale(middle)
    n2 = middle * r2
    near_and_cot = lax.optimization_barrier(
        ((n2 * mlp_gain_full).astype(BF), cot_all) + tuple(mlp_near)
    )
    mlp_own, cot_all, mlp_near = near_and_cot[0], near_and_cot[1], near_and_cot[2:]
    mlp_cols = gather_end(mlp_own_cols, mlp_near)
    mlp_all = lax.all_gather(mlp_own, "seq", axis=0, tiled=True)
    both_w = mlp_cols[:, : 2 * ff]
    down_w = mlp_cols[:, 2 * ff :]
    d_product = nn(cot_all, down_w)
    both_pre = nn(mlp_all, both_w)
    hidden_pre = both_pre[:, :ff]
    up_pre = both_pre[:, ff:]
    sh = silu(hidden_pre)
    product = (sh * up_pre).astype(BF)
    d_both = jnp.concatenate(
        [
            (d_product * up_pre * silu_slope(hidden_pre)).astype(BF),
            (d_product * sh).astype(BF),
        ],
        axis=1,
    )
    d_mlp = lax.psum_scatter(
        nt(d_both, both_w).astype(BF), "seq", scatter_dimension=0, tiled=True
    ).astype(F32)
    d_output = own_cot.astype(F32)
    e2 = d_mlp * mlp_gain_full
    d_middle = d_output + r2 * (e2 - n2 * jnp.mean(e2 * n2, axis=-1, keepdims=True))
    both_sum = RingGrad(mlp_all, d_both)
    down_sum = RingGrad(cot_all, product)
    d_branch_own = after(d_middle.astype(BF), *both_sum.near, *down_sum.sent)
    both_sum.second(d_branch_own)
    d_branch_all = lax.all_gather(d_branch_own, "seq", axis=0, tiled=True)
    mlp_part = after(nt(product, down_w).astype(BF), d_branch_all)
    mlp_out = lax.psum_scatter(mlp_part, "seq", scatter_dimension=0, tiled=True)

    d_gated = nn(d_branch_all, out_cols)
    if vs == 1:
        d_mixed, d_gate, gain_part = gate_backward(
            d_gated, mixed, pre_gate, own_gain[None], hp, dv
        )
        grad_out_gain = gain_part[0]
    else:
        d_mixed, d_gate, grad_out_gain = gate_apply_back(d_gated, mixed, pre_gate, own_gain)
    gate_sum = RingGrad(attn, d_gate)
    out_sum = RingGrad(d_branch_all, gated)
    d_attn_gate = nt(d_gate, gate_cols)
    down_sum.second(d_branch_all)
    d_mixed = after(
        d_mixed,
        *both_sum.late,
        *down_sum.late,
        *gate_sum.sent,
        *out_sum.sent,
        mlp_part,
        d_attn_gate,
    )
    both_rows = to_rows(both_sum.total(d_mixed), ranks)
    down_rows = to_rows(down_sum.total(d_mixed), ranks)
    d_pre, d_taps, d_sums = delta_backward(
        pre, pre_small, rider_all, taps, const, saved, d_mixed, hp, dk, dv
    )
    d_pre, d_taps, d_sums, mlp_out, both_rows, down_rows = lax.optimization_barrier(
        (d_pre, d_taps, d_sums, mlp_out, both_rows, down_rows) + gate_sum.near + out_sum.near
    )[:6]
    mix_sum = RingGrad(attn, d_pre)
    gate_sum.second(d_pre)
    out_sum.second(d_pre)
    gate_rows = to_rows(gate_sum.total(), ranks)
    out_rows = to_rows(out_sum.total(), ranks)
    mix_sum.second()
    mix_rows = to_rows(mix_sum.total(), ranks)
    d_attn = lax.psum_scatter(
        (d_attn_gate + nt(d_pre, w_mix)).astype(BF), "seq", scatter_dimension=0, tiled=True
    ).astype(F32)

    output = from_ring((middle + mlp_out.astype(F32)).astype(BF))
    n = inputs * rms_scale(inputs)
    e = d_attn * attn_gain_full
    grad_tokens = from_ring(
        (d_middle + rms_scale(inputs) * (e - n * jnp.mean(e * n, axis=-1, keepdims=True))).astype(BF)
    )

    sums = jnp.concatenate(
        [
            d_taps[:KERNEL, :at_k].reshape(-1),
            d_taps[:KERNEL, at_k:at_v].reshape(-1),
            d_taps[:KERNEL, at_v:].reshape(-1),
            d_sums[1, :hp],
            d_sums[0, :hp],
            grad_out_gain,
        ]
    )
    every = sum_everywhere(jnp.pad(sums, (0, -sums.shape[0] % 1024)))

    def per_head(part, lead):
        part = part.reshape(ranks // vs, vs, lead, -1).sum(axis=1)
        return jnp.transpose(part, (1, 0, 2)).reshape(lead, -1)

    a0 = KERNEL * hp * dk
    a1 = 2 * a0
    a2 = a1 + KERNEL * hp * dv
    grad_conv_value = jnp.transpose(
        every[:, a1:a2].reshape(ranks, KERNEL, -1), (1, 0, 2)
    ).reshape(KERNEL, -1)
    gain_sum = every[:, a2 + 2 * hp : a2 + 2 * hp + dv].reshape(ranks // vs, vs, dv).sum(axis=0).reshape(-1)
    grad_query = plan.join_keys(mix_rows[:, :, :at_k])
    grad_key = plan.join_keys(mix_rows[:, :, at_k:at_v])
    grad_value = plan.join_even(mix_rows[:, :, at_v:at_s])
    grad_decay = plan.join_keys(mix_rows[:, :, at_s : at_s + hp])
    grad_beta = plan.join_keys(mix_rows[:, :, at_s + hp : at_s + 2 * hp])
    grad_gate = plan.join_even(gate_rows)
    grad_hidden = plan.join_even(both_rows[:, :, :ff])
    grad_up = plan.join_even(both_rows[:, :, ff:])

    def gain_grad(gain, pairs):
        total = sum(jnp.sum(w.astype(F32) * g, axis=1) for w, g in pairs)
        return total / gain.astype(F32)

    return (
        output[None],
        grad_tokens[None],
        gain_grad(
            attn_gain,
            (
                (w_query, grad_query),
                (w_key, grad_key),
                (w_value, grad_value),
                (w_decay, grad_decay),
                (w_beta, grad_beta),
                (w_gate, grad_gate),
            ),
        ),
        grad_query,
        grad_key,
        grad_value,
        grad_decay,
        grad_beta,
        grad_gate,
        plan.join_even(out_rows),
        per_head(every[:, :a0], KERNEL),
        per_head(every[:, a0:a1], KERNEL),
        grad_conv_value,
        per_head(every[:, a2 : a2 + hp], 1)[0],
        per_head(every[:, a2 + hp : a2 + 2 * hp], 1)[0],
        gain_sum,
        gain_grad(mlp_gain, ((w_hidden, grad_hidden), (w_up, grad_up))),
        grad_hidden,
        grad_up,
        plan.join_even(down_rows),
    )


def solution(mesh):
    flat = ("dp", "seq")
    tok_spec = P("dp", "seq", None)
    row_spec = P(flat, None)
    gain_spec = P(flat)
    in_specs = (
        (tok_spec, gain_spec)
        + (row_spec,) * 7
        + (P(),) * 6
        + (gain_spec,)
        + (row_spec,) * 3
        + (P("dp", "seq"), tok_spec)
    )
    out_specs = (
        (tok_spec, tok_spec, gain_spec)
        + (row_spec,) * 7
        + (P(),) * 6
        + (gain_spec,)
        + (row_spec,) * 3
    )
    return jax.shard_map(local, mesh=mesh, in_specs=in_specs, out_specs=out_specs, check_vma=False)
```

time: 853 us -> 812 us (0.952)
  other arithmetic: 121 us -> 39 us
  matrix products: 106 us -> 179 us
  local copies, waits for them, and re-layouts: 163 us -> 125 us
  waiting for transfers between devices: 292 us -> 264 us
  Pallas kernels: 60.7 us -> 85.6 us
  starting transfers between devices: 73.8 us -> 98.2 us
  between operations: 25.9 us -> 15.6 us
    dot_general x15 -> x46, matrix products: 106 us -> 179 us  [dot_f32(): lax.dot_general(left, right, (dims, ((), ())), preferred_element_type=F32)]
    ppermute x6, waiting for transfers between devices: 10.5 us -> 46.5 us  [gather_start(): return (lax.ppermute(own, 'dp', right), lax.ppermute(own, 'dp', left))]
    reduce_sum x10 -> x0, other arithmetic: 32.9 us -> none  [the longest x2 6.41 us: unit(): array * lax.rsqrt(jnp.sum(array * array, axis=-1, keepdims=True) + 1e-06)]
    convert_element_type x14 -> x2, other arithmetic: 34.6 us -> 5.23 us  [the longest x1 2.94 us: local(): attn = (normed_all * attn_gain_full).astype(BF)]
    reduce_scatter x1, waiting for transfers between devices: 48.8 us -> 23 us  [local(): lax.psum_scatter(nt(d_both, both_w).astype(BF), 'seq', scatter_dimension=...]
    pallas_call x2 -> x4, Pallas kernels: 60.7 us -> 85.6 us  [the longest x1 46.2 us: delta_backward(): pl.pallas_call(functools.partial(bwd_kernel, hp, dk, dv), out_shape=(shap...]
    mul x10 -> x0, local copies, waits for them, and re-layouts: 19.8 us -> none  [the longest x4 10.3 us: unit(): array * lax.rsqrt(jnp.sum(array * array, axis=-1, keepdims=True) + 1e-06)]
    ppermute x24 -> x30, waiting for transfers between devices: 39.4 us -> 23.3 us  [the longest x5 11.2 us: second(): lax.ppermute((self.part(7) + far_b.astype(F32)).astype(BF), 'dp', to_left)]
  transfers between devices with their start and end apart: 56 -> 63, of which waited for: 20 -> 24; matrix products, arithmetic and copies ran while one was open for 38% -> 31% of each run, Pallas kernels for 7% -> 11%
where the time goes in v4:
time: 812 us; the launch traced here: 806 us
  waiting for transfers between devices  264 us (33%)
  matrix products  179 us (22%)
  local copies, waits for them, and re-layouts  125 us (15%)
  starting transfers between devices  98.2 us (12%)
  Pallas kernels  85.6 us (11%)
  other arithmetic  39 us (5%)
  between operations  15.6 us (2%)
    dot_general x46, matrix products, dot_f32(): lax.dot_general(left, right, (dims, ((), ())), preferred_element_type=F32)  179 us
    all_to_all x5, waiting for transfers between devices, to_rows(): turned = lax.all_to_all(mine, 'seq', 0, 0, tiled=True)  48.7 us
    ppermute x6, waiting for transfers between devices, gather_start(): return (lax.ppermute(own, 'dp', right), lax.ppermute(own, 'dp', left))  46.5 us
    pallas_call x1, Pallas kernels, delta_backward(): pl.pallas_call(functools.partial(bwd_kernel, hp, dk, dv), out_shape=(shap...  46.2 us
    all_to_all x3, waiting for transfers between devices, exchange(): return lax.all_to_all(turned, 'seq', 0, 0, tiled=True)  40.8 us
    unnamed x177, local copies, waits for them, and re-layouts  39.6 us
    reduce_scatter x1, waiting for transfers between devices, local(): lax.psum_scatter(nt(gated, out_cols).astype(BF), 'seq', scatter_dimension...  34.7 us
    pallas_call x1, Pallas kernels, delta_forward(): pl.pallas_call(functools.partial(fwd_kernel, hp, dk, dv), out_shape=(shap...  29.5 us
  transfers between devices with their start and end apart: 63, of which 24 were waited for; matrix products, arithmetic and copies ran while one was open for 31% of the time, Pallas kernels for 11%

profile of v4, /device:TPU:0, one launch (start us, length us, event | category | flops | bytes accessed | tf_op | source)
XLA Modules:
  0.0 806.3 jit_solution(3840287943931752422)
XLA Ops:
  17.2 6.3 all-to-all-start
  25.1 27.9 %all-to-all-done = bf16[8,64,1152]{2,1,0:T(8,128)(2,1)S(1)} async-done(((bf16[8,64,1152]{2,1,0:T(8,128)(2,1)}), bf16[8,64,1152]{2,1,0:T(8,128)(2,1)S(1)}, u32[]{:S(2)}, u32[]{:S(2)}) %all-to-all-start) | async-done | bytes 1179680 | tf_op jit(solution)/shard_map/all_to_all | solution.py:190
  65.7 14.9 %collective-permute-done.1 = bf16[512,1152]{1,0:T(8,128)(2,1)S(1)} collective-permute-done((bf16[512,1152]{1,0:T(8,128)(2,1)S(1)}, bf16[512,1152]{1,0:T(8,128)(2,1)S(1)}, u32[]{:S(2)}, u32[]{:S(2)}) %collective-permute-start.1) | collective-permute-done | bytes 1179680 | tf_op jit(solution)/shard_map/ppermute | solution.py:132
  89.3 3.6 all-to-all-start.1
  105.3 3.2 fusion
  108.6 2.9 fusion.2
  113.6 5.7 fusion.22.pre_ref
  119.3 3.1 all-to-all-done.1
  126.0 21.7 %collective-permute-done.5 = bf16[512,1024]{1,0:T(8,128)(2,1)} collective-permute-done((bf16[512,1024]{1,0:T(8,128)(2,1)S(1)}, bf16[512,1024]{1,0:T(8,128)(2,1)}, u32[]{:S(2)}, u32[]{:S(2)}) %collective-permute-start.5) | collective-permute-done | bytes 1048608 | tf_op jit(solution)/shard_map/ppermute | solution.py:132
  166.6 4.8 concatenate.98
  176.1 3.5 fusion.86.small_ref
  179.6 3.6 all-to-all-start.2
  184.9 6.5 fusion.30.gate_ref
  191.4 29.5 %delta_forward.1 = (f32[1024,512]{1,0:T(8,128)}, f32[16,128,256]{2,1,0:T(8,128)}, f32[1024,512]{1,0:T(8,128)}, f32[16,128,128]{2,1,0:T(8,128)}, f32[1024,256]{1,0:T(8,128)}) custom-call(bf16[1024,1024]{1,0:T(8,128)(2,1)} %fusion.22.pre_ref, f32[1024,128]{1,0:T(8,128)} %fusion.86.small_ref, bf16[1024,128]{1,0:T(8,128)(2,1)} %slice.324.rider_ref, ...), custom_call_target="tpu_custom_call" | custom-call | flops 43008000000 | bytes 16777216 | tf_op jit(solution)/shard_map/delta_forward/pallas_call | solution.py:582
  221.0 4.3 gate_forward.1
  225.2 9.8 %all-to-all-done.2 = bf16[8,64,2112]{2,1,0:T(8,128)(2,1)S(1)} async-done(((bf16[8,64,2112]{2,1,0:T(8,128)(2,1)}), bf16[8,64,2112]{2,1,0:T(8,128)(2,1)S(1)}, u32[]{:S(2)}, u32[]{:S(2)}) %all-to-all-start.2) | async-done | bytes 2162720 | tf_op jit(solution)/shard_map/all_to_all | solution.py:190
  235.0 6.3 convolution_convert_fusion.1
  241.3 9.7 %all-gather.9.cloned.1.call-start = ((), (), s32[]{:S(2)}) async-start(), calls=%async_computation.15 | async-start | bytes 4718592 | tf_op jit(solution)/shard_map/all_gather | solution.py:831
  255.6 34.7 %reduce-scatter.5.cloned.1.call-done = bf16[128,2048]{1,0:T(8,128)(2,1)} async-done(((bf16[1024,2048]{1,0:T(8,128)(2,1)}), bf16[128,2048]{1,0:T(8,128)(2,1)}) %reduce-scatter.5.cloned.1.call-update) | async-done | bytes 524304 | tf_op jit(solution)/shard_map/reduce_scatter | solution.py:819
  293.7 8.8 %collective-permute-done.8 = bf16[512,2112]{0,1:T(8,128)(2,1)} collective-permute-done((bf16[512,2112]{0,1:T(8,128)(2,1)}, bf16[512,2112]{0,1:T(8,128)(2,1)}, u32[]{:S(2)}, u32[]{:S(2)}) %collective-permute-start.8) | collective-permute-done | bytes 2162720 | tf_op jit(solution)/shard_map/ppermute | solution.py:132
  311.8 4.1 copy.115
  315.9 3.0 copy.118
  318.9 3.2 constant_dynamic-update-slice_fusion.13
  322.0 8.5 %collective-permute-done.10 = bf16[256,2112]{0,1:T(8,128)(2,1)} collective-permute-done((bf16[256,2112]{0,1:T(8,128)(2,1)}, bf16[256,2112]{0,1:T(8,128)(2,1)}, u32[]{:S(2)}, u32[]{:S(2)}) %collective-permute-start.10) | collective-permute-done | bytes 1081376 | tf_op jit(solution)/shard_map/ppermute | solution.py:141
  341.5 7.8 all-gather.9.cloned.1.call-done
  349.3 11.4 %fusion.5 = f32[1024,1408]{0,1:T(8,128)} fusion(bf16[1024,2048]{1,0:T(8,128)(2,1)} %all-gather.9.cloned.1.call-done, bf16[2048,2112]{1,0:T(8,128)(2,1)} %constant_dynamic-update-slice_fusion.10), kind=kOutput, calls=%fused_computation.8 | convolution fusion | flops 5905580032 | bytes 15728640 | tf_op jit(solution)/shard_map/dot_general | solution.py:22
  360.7 6.2 multiply_convert_fusion.2
  368.6 8.3 %fusion.9 = bf16[1024,2048]{1,0:T(8,128)(2,1)} fusion(bf16[2048,2112]{1,0:T(8,128)(2,1)S(1)} %copy-done.25, bf16[1024,704]{0,1:T(8,128)(2,1)S(1)} %get-tuple-element.151, bf16[1024,704]{0,1:T(8,128)(2,1)S(1)} %get-tuple-element.150), kind=kOutput, calls=%fused_computation.12 | convolution fusion | flops 5913444352 | bytes 12845056 | tf_op jit(solution)/shard_map/dot_general | solution.py:22
  377.0 4.0 convolution_convert_fusion.6
  382.9 3.0 convolution_convert_fusion.7
  386.4 3.0 convolution_convert_fusion.8
  390.8 2.9 convolution_convert_fusion.9
  402.8 23.0 %reduce-scatter.7.cloned.1.call-done = bf16[128,2048]{1,0:T(8,128)(2,1)} async-done(((bf16[1024,2048]{1,0:T(8,128)(2,1)}), bf16[128,2048]{1,0:T(8,128)(2,1)}) %reduce-scatter.7.cloned.1.call-update) | async-done | bytes 524304 | tf_op jit(solution)/shard_map/reduce_scatter | solution.py:847
  433.8 8.1 %convolution_convert_fusion = bf16[1024,2048]{1,0:T(8,128)(2,1)} fusion(bf16[1024,704]{0,1:T(8,128)(2,1)} %copy-done.59, bf16[2048,2112]{1,0:T(8,128)(2,1)} %constant_dynamic-update-slice_fusion.10), kind=kOutput, calls=%fused_computation.13 | convolution fusion | flops 2954887168 | bytes 8781824 | tf_op jit(solution)/shard_map/dot_general | solution.py:22
  442.0 3.8 add_convert_fusion.2
  447.4 3.2 add_convert_fusion.3
  450.6 24.5 %all-gather.11.cloned.1.call-done = bf16[1024,2048]{1,0:T(8,128)(2,1)} async-done(((bf16[128,2048]{1,0:T(8,128)(2,1)}), bf16[1024,2048]{1,0:T(8,128)(2,1)}) %all-gather.11.cloned.1.call-update) | async-done | bytes 4194320 | tf_op jit(solution)/shard_map/all_gather | solution.py:857
  475.1 6.5 fusion.25.d_ref
  481.6 5.6 gate_backward.1
  506.6 7.4 fusion.28
  522.3 4.2 collective-permute-done.20
  530.0 3.5 all-to-all-start.4
  539.9 5.8 fusion.14
  550.1 16.1 %all-to-all-done.4 = bf16[8,64,704]{2,1,0:T(8,128)(2,1)S(1)} async-done(((bf16[8,64,704]{2,1,0:T(8,128)(2,1)}), bf16[8,64,704]{2,1,0:T(8,128)(2,1)S(1)}, u32[]{:S(2)}, u32[]{:S(2)}) %all-to-all-start.4) | async-done | bytes 720928 | tf_op jit(solution)/shard_map/all_to_all | solution.py:194
  566.2 4.5 all-to-all-start.3
  570.7 46.2 %delta_backward.1 = (bf16[1024,1152]{1,0:T(8,128)(2,1)}, f32[8,1024]{1,0:T(8,128)}, f32[8,128]{1,0:T(8,128)}) custom-call(bf16[1024,1024]{1,0:T(8,128)(2,1)} %fusion.22.pre_ref, f32[1024,128]{1,0:T(8,128)} %fusion.86.small_ref, bf16[1024,128]{1,0:T(8,128)(2,1)} %slice.324.rider_ref, f32[4,1024]{1,0:T(4,128)} %pad_maximum_fusion.4.taps_ref, ...), custom_call_target="tpu_custom_call" | custom-call | flops 69632000000 | bytes 20971520 | tf_op jit(solution)/shard_map/delta_backward/pallas_call | solution.py:610
  618.6 3.5 convolution_convert_fusion.2
  630.3 10.8 %add_convert_fusion = bf16[1024,2048]{1,0:T(8,128)(2,1)} fusion(f32[1024,2048]{1,0:T(8,128)} %fusion.28, bf16[1024,1152]{1,0:T(8,128)(2,1)S(1)} %copy-done.2, bf16[2048,1152]{1,0:T(8,128)(2,1)} %constant_dynamic-update-slice_fusion), kind=kOutput, calls=%fused_computation.5 | convolution fusion | flops 4836032512 | bytes 19660800 | tf_op jit(solution)/shard_map/dot_general | solution.py:22
  641.1 3.7 convert_bitcast_fusion.1
  646.8 2.8 reshape.386
  653.6 3.2 reshape.385
  689.5 3.1 fusion.35
  692.5 4.5 all-to-all-start.7
  697.0 11.2 %collective-permute-done.39 = bf16[256,512]{1,0:T(8,128)(2,1)} collective-permute-done((bf16[256,512]{1,0:T(8,128)(2,1)}, bf16[256,512]{1,0:T(8,128)(2,1)}, u32[]{:S(2)}, u32[]{:S(2)}) %collective-permute-start.39) | collective-permute-done | bytes 262176 | tf_op jit(solution)/shard_map/ppermute | solution.py:173
  709.4 2.9 fusion.21
  713.2 2.9 fusion.20
  717.3 3.0 fusion.34
  721.2 4.1 all-to-all-start.6
  726.0 2.8 collective-permute-start.46
  728.8 7.0 collective-permute-done.36
  735.8 4.6 fusion.15
  740.4 10.1 %all-to-all-done.6 = bf16[8,64,512]{2,1,0:T(8,128)(2,1)} async-done(((bf16[8,64,512]{2,1,0:T(8,128)(2,1)}), bf16[8,64,512]{2,1,0:T(8,128)(2,1)}, u32[]{:S(2)}, u32[]{:S(2)}) %all-to-all-start.6) | async-done | bytes 524320 | tf_op jit(solution)/shard_map/all_to_all | solution.py:194
  750.5 3.7 all-to-all-start.5
  761.8 21.7 %all-to-all-done.5 = bf16[8,64,1152]{2,1,0:T(8,128)(2,1)S(1)} async-done(((bf16[8,64,1152]{2,1,0:T(8,128)(2,1)}), bf16[8,64,1152]{2,1,0:T(8,128)(2,1)S(1)}, u32[]{:S(2)}, u32[]{:S(2)}) %all-to-all-start.5) | async-done | bytes 1179680 | tf_op jit(solution)/shard_map/all_to_all | solution.py:194
  (410 shorter events, 246.6 us)
Async XLA Ops:
  17.2 35.7 %all-to-all-start = ((bf16[8,64,1152]{2,1,0:T(8,128)(2,1)}), bf16[8,64,1152]{2,1,0:T(8,128)(2,1)S(1)}, u32[]{:S(2)}, u32[]{:S(2)}) async-start(bf16[8,64,1152]{2,1,0:T(8,128)(2,1)} %copy.108), calls=%async_computation | async-start | bytes 2359296 | tf_op jit(solution)/shard_map/all_to_all | solution.py:190
  23.5 81.8 %all-gather.5.cloned.1.call-start = ((), (), s32[]{:S(2)}) async-start(), calls=%async_computation.12 | async-start | bytes 5013504 | tf_op jit(solution)/shard_map/all_gather | solution.py:736
  23.9 403.3 %copy-start.3 = (bf16[128,4096]{1,0:T(8,128)(2,1)}, bf16[128,4096]{1,0:T(8,128)(2,1)S(1)}, u32[]{:S(2)}) copy-start(bf16[128,4096]{1,0:T(8,128)(2,1)S(1)} %slice_dynamic-update-slice_fusion.9) | copy-start | bytes 3145732
  53.0 27.6 %collective-permute-start.1 = (bf16[512,1152]{1,0:T(8,128)(2,1)S(1)}, bf16[512,1152]{1,0:T(8,128)(2,1)S(1)}, u32[]{:S(2)}, u32[]{:S(2)}) collective-permute-start(bf16[512,1152]{1,0:T(8,128)(2,1)S(1)} %bitcast.139), channel_id=1, source_target_pairs={{0,8},{8,24},{24,16},{16,0},{1,9},{9,25},{25,17},{17,1},{2,10},{10... | collective-permute-start | bytes 3538952 | tf_op jit(solution)/shard_map/ppermute | solution.py:132
  55.4 28.8 %collective-permute-start = (bf16[512,1152]{1,0:T(8,128)(2,1)S(1)}, bf16[512,1152]{1,0:T(8,128)(2,1)}, u32[]{:S(2)}, u32[]{:S(2)}) collective-permute-start(bf16[512,1152]{1,0:T(8,128)(2,1)S(1)} %bitcast.140), channel_id=1, source_target_pairs={{8,0},{24,8},{16,24},{0,16},{9,1},{25,9},{17,25},{1,17},{10,2},{26... | collective-permute-start | bytes 3538952 | tf_op jit(solution)/shard_map/ppermute | solution.py:132
  81.4 14.4 %collective-permute-start.2 = (bf16[256,1152]{1,0:T(8,128)(2,1)}, bf16[256,1152]{1,0:T(8,128)(2,1)}, u32[]{:S(2)}, u32[]{:S(2)}) collective-permute-start(bf16[256,1152]{1,0:T(8,128)(2,1)} %slice.319), channel_id=1, source_target_pairs={{0,8},{8,24},{24,16},{16,0},{1,9},{9,25},{25,17},{17,1},{2,10},{10... | collective-permute-start | bytes 1769480 | tf_op jit(solution)/shard_map/ppermute | solution.py:141
  86.2 14.1 %collective-permute-start.3 = (bf16[256,1152]{1,0:T(8,128)(2,1)}, bf16[256,1152]{1,0:T(8,128)(2,1)}, u32[]{:S(2)}, u32[]{:S(2)}) collective-permute-start(bf16[256,1152]{1,0:T(8,128)(2,1)} %slice.320), channel_id=1, source_target_pairs={{8,0},{24,8},{16,24},{0,16},{9,1},{25,9},{17,25},{1,17},{10,2},{26... | collective-permute-start | bytes 1769480 | tf_op jit(solution)/shard_map/ppermute | solution.py:142
  89.3 33.1 %all-to-all-start.1 = ((bf16[8,64,1024]{2,1,0:T(8,128)(2,1)}), bf16[8,64,1024]{2,1,0:T(8,128)(2,1)S(1)}, u32[]{:S(2)}, u32[]{:S(2)}) async-start(bf16[8,64,1024]{2,1,0:T(8,128)(2,1)} %copy.109), calls=%async_computation.1 | async-start | bytes 2097152 | tf_op jit(solution)/shard_map/all_to_all | solution.py:190
  92.9 142.1 %all-gather.7.cloned.1.call-start = ((), (), s32[]{:S(2)}) async-start(), calls=%async_computation.13 | async-start | bytes 4718592 | tf_op jit(solution)/shard_map/all_gather | solution.py:772
  122.5 25.1 %collective-permute-start.5 = (bf16[512,1024]{1,0:T(8,128)(2,1)S(1)}, bf16[512,1024]{1,0:T(8,128)(2,1)}, u32[]{:S(2)}, u32[]{:S(2)}) collective-permute-start(bf16[512,1024]{1,0:T(8,128)(2,1)S(1)} %bitcast.143), channel_id=1, source_target_pairs={{0,8},{8,24},{24,16},{16,0},{1,9},{9,25},{25,17},{17,1},{2,10},{10... | collective-permute-start | bytes 3145736 | tf_op jit(solution)/shard_map/ppermute | solution.py:132
  124.0 27.1 %collective-permute-start.4 = (bf16[512,1024]{1,0:T(8,128)(2,1)S(1)}, bf16[512,1024]{1,0:T(8,128)(2,1)}, u32[]{:S(2)}, u32[]{:S(2)}) collective-permute-start(bf16[512,1024]{1,0:T(8,128)(2,1)S(1)} %bitcast.144), channel_id=1, source_target_pairs={{8,0},{24,8},{16,24},{0,16},{9,1},{25,9},{17,25},{1,17},{10,2},{26... | collective-permute-start | bytes 3145736 | tf_op jit(solution)/shard_map/ppermute | solution.py:132
  149.5 24.1 %collective-permute-start.6 = (bf16[256,1024]{1,0:T(8,128)(2,1)}, bf16[256,1024]{1,0:T(8,128)(2,1)S(1)}, u32[]{:S(2)}, u32[]{:S(2)}) collective-permute-start(bf16[256,1024]{1,0:T(8,128)(2,1)} %slice.325), channel_id=1, source_target_pairs={{0,8},{8,24},{24,16},{16,0},{1,9},{9,25},{25,17},{17,1},{2,10},{10... | collective-permute-start | bytes 1572872 | tf_op jit(solution)/shard_map/ppermute | solution.py:141
  152.9 20.7 %collective-permute-start.7 = (bf16[256,1024]{1,0:T(8,128)(2,1)}, bf16[256,1024]{1,0:T(8,128)(2,1)}, u32[]{:S(2)}, u32[]{:S(2)}) collective-permute-start(bf16[256,1024]{1,0:T(8,128)(2,1)} %slice.326), channel_id=1, source_target_pairs={{8,0},{24,8},{16,24},{0,16},{9,1},{25,9},{17,25},{1,17},{10,2},{26... | collective-permute-start | bytes 1572872 | tf_op jit(solution)/shard_map/ppermute | solution.py:142
  179.6 55.4 %all-to-all-start.2 = ((bf16[8,64,2112]{2,1,0:T(8,128)(2,1)}), bf16[8,64,2112]{2,1,0:T(8,128)(2,1)S(1)}, u32[]{:S(2)}, u32[]{:S(2)}) async-start(bf16[8,64,2112]{2,1,0:T(8,128)(2,1)} %bitcast.138), calls=%async_computation.2 | async-start | bytes 4456448 | tf_op jit(solution)/shard_map/all_to_all | solution.py:190
  183.2 107.1 %reduce-scatter.5.cloned.1.call-start = ((), (), s32[]{:S(2)}) async-start(), calls=%async_computation.14 | async-start | bytes 4718592 | tf_op jit(solution)/shard_map/reduce_scatter | solution.py:819
  241.3 108.0 %all-gather.9.cloned.1.call-start = ((), (), s32[]{:S(2)}) async-start(), calls=%async_computation.15 | async-start | bytes 4718592 | tf_op jit(solution)/shard_map/all_gather | solution.py:831
  253.6 48.9 %collective-permute-start.8 = (bf16[512,2112]{0,1:T(8,128)(2,1)}, bf16[512,2112]{0,1:T(8,128)(2,1)}, u32[]{:S(2)}, u32[]{:S(2)}) collective-permute-start(bf16[512,2112]{0,1:T(8,128)(2,1)} %copy.113), channel_id=1, source_target_pairs={{0,8},{8,24},{24,16},{16,0},{1,9},{9,25},{25,17},{17,1},{2,10},{10... | collective-permute-start | bytes 6488072 | tf_op jit(solution)/shard_map/ppermute | solution.py:132
  255.0 48.6 %collective-permute-start.9 = (bf16[512,2112]{0,1:T(8,128)(2,1)}, bf16[512,2112]{0,1:T(8,128)(2,1)}, u32[]{:S(2)}, u32[]{:S(2)}) collective-permute-start(bf16[512,2112]{0,1:T(8,128)(2,1)} %copy.113), channel_id=1, source_target_pairs={{8,0},{24,8},{16,24},{0,16},{9,1},{25,9},{17,25},{1,17},{10,2},{26... | collective-permute-start | bytes 6488072 | tf_op jit(solution)/shard_map/ppermute | solution.py:132
  303.7 122.1 %reduce-scatter.7.cloned.1.call-start = ((), (), s32[]{:S(2)}) async-start(), calls=%async_computation.16 | async-start | bytes 4718592 | tf_op jit(solution)/shard_map/reduce_scatter | solution.py:847
  306.0 24.5 %collective-permute-start.10 = (bf16[256,2112]{0,1:T(8,128)(2,1)}, bf16[256,2112]{0,1:T(8,128)(2,1)}, u32[]{:S(2)}, u32[]{:S(2)}) collective-permute-start(bf16[256,2112]{0,1:T(8,128)(2,1)} %slice.256), channel_id=1, source_target_pairs={{0,8},{8,24},{24,16},{16,0},{1,9},{9,25},{25,17},{17,1},{2,10},{10... | collective-permute-start | bytes 3244040 | tf_op jit(solution)/shard_map/ppermute | solution.py:141
  309.8 24.2 %collective-permute-start.11 = (bf16[256,2112]{0,1:T(8,128)(2,1)}, bf16[256,2112]{0,1:T(8,128)(2,1)}, u32[]{:S(2)}, u32[]{:S(2)}) collective-permute-start(bf16[256,2112]{0,1:T(8,128)(2,1)} %slice.257), channel_id=1, source_target_pairs={{8,0},{24,8},{16,24},{0,16},{9,1},{25,9},{17,25},{1,17},{10,2},{26... | collective-permute-start | bytes 3244040 | tf_op jit(solution)/shard_map/ppermute | solution.py:142
  376.9 98.2 %all-gather.11.cloned.1.call-start = ((), (), s32[]{:S(2)}) async-start(), calls=%async_computation.17 | async-start | bytes 4718592 | tf_op jit(solution)/shard_map/all_gather | solution.py:857
  381.0 48.6 %collective-permute-start.15 = (bf16[256,1408]{1,0:T(8,128)(2,1)}, bf16[256,1408]{1,0:T(8,128)(2,1)S(1)}, u32[]{:S(2)}, u32[]{:S(2)}) collective-permute-start(bf16[256,1408]{1,0:T(8,128)(2,1)} %convolution_convert_fusion.6), channel_id=1, source_target_pairs={{8,0},{24,8},{16,24},{0,16},{9,1},{25,9},{17,25},{1,17},{10,2},{26... | collective-permute-start | bytes 2162696 | tf_op jit(solution)/shard_map/ppermute | solution.py:160
  385.8 43.8 %collective-permute-start.14 = (bf16[256,1408]{1,0:T(8,128)(2,1)}, bf16[256,1408]{1,0:T(8,128)(2,1)}, u32[]{:S(2)}, u32[]{:S(2)}) collective-permute-start(bf16[256,1408]{1,0:T(8,128)(2,1)} %convolution_convert_fusion.7), channel_id=1, source_target_pairs={{0,8},{8,24},{24,16},{16,0},{1,9},{9,25},{25,17},{17,1},{2,10},{10... | collective-permute-start | bytes 2162696 | tf_op jit(solution)/shard_map/ppermute | solution.py:159
  389.4 40.2 %collective-permute-start.13 = (bf16[256,1408]{1,0:T(8,128)(2,1)}, bf16[256,1408]{1,0:T(8,128)(2,1)}, u32[]{:S(2)}, u32[]{:S(2)}) collective-permute-start(bf16[256,1408]{1,0:T(8,128)(2,1)} %convolution_convert_fusion.8), channel_id=1, source_target_pairs={{8,0},{24,8},{16,24},{0,16},{9,1},{25,9},{17,25},{1,17},{10,2},{26... | collective-permute-start | bytes 2162696 | tf_op jit(solution)/shard_map/ppermute | solution.py:158
  393.8 35.8 %collective-permute-start.12 = (bf16[256,1408]{1,0:T(8,128)(2,1)}, bf16[256,1408]{1,0:T(8,128)(2,1)}, u32[]{:S(2)}, u32[]{:S(2)}) collective-permute-start(bf16[256,1408]{1,0:T(8,128)(2,1)} %convolution_convert_fusion.9), channel_id=1, source_target_pairs={{0,8},{8,24},{24,16},{16,0},{1,9},{9,25},{25,17},{17,1},{2,10},{10... | collective-permute-start | bytes 2162696 | tf_op jit(solution)/shard_map/ppermute | solution.py:157
  429.7 187.3 %reduce-scatter.9.cloned.1.call-start = ((), (), s32[]{:S(2)}) async-start(), calls=%async_computation.18 | async-start | bytes 4718592 | tf_op jit(solution)/shard_map/reduce_scatter | solution.py:859
  429.7 67.2 %collective-permute-start.19 = (bf16[256,704]{0,1:T(8,128)(2,1)}, bf16[256,704]{0,1:T(8,128)(2,1)S(1)}, u32[]{:S(2)}, u32[]{:S(2)}) collective-permute-start(bf16[256,704]{0,1:T(8,128)(2,1)} %convolution_convert_fusion.12), channel_id=1, source_target_pairs={{8,0},{24,8},{16,24},{0,16},{9,1},{25,9},{17,25},{1,17},{10,2},{26... | collective-permute-start | bytes 1081352 | tf_op jit(solution)/shard_map/ppermute | solution.py:158
  431.3 67.1 %collective-permute-start.18 = (bf16[256,704]{0,1:T(8,128)(2,1)}, bf16[256,704]{0,1:T(8,128)(2,1)S(1)}, u32[]{:S(2)}, u32[]{:S(2)}) collective-permute-start(bf16[256,704]{0,1:T(8,128)(2,1)} %convolution_convert_fusion.13), channel_id=1, source_target_pairs={{0,8},{8,24},{24,16},{16,0},{1,9},{9,25},{25,17},{17,1},{2,10},{10... | collective-permute-start | bytes 1081352 | tf_op jit(solution)/shard_map/ppermute | solution.py:157
  431.8 94.6 %collective-permute-start.23 = (bf16[256,704]{0,1:T(8,128)(2,1)}, bf16[256,704]{0,1:T(8,128)(2,1)}, u32[]{:S(2)}, u32[]{:S(2)}) collective-permute-start(bf16[256,704]{0,1:T(8,128)(2,1)} %convolution_convert_fusion.10), channel_id=1, source_target_pairs={{8,0},{24,8},{16,24},{0,16},{9,1},{25,9},{17,25},{1,17},{10,2},{26... | collective-permute-start | bytes 1081352 | tf_op jit(solution)/shard_map/ppermute | solution.py:160
  433.3 93.1 %collective-permute-start.22 = (bf16[256,704]{0,1:T(8,128)(2,1)}, bf16[256,704]{0,1:T(8,128)(2,1)}, u32[]{:S(2)}, u32[]{:S(2)}) collective-permute-start(bf16[256,704]{0,1:T(8,128)(2,1)} %convolution_convert_fusion.11), channel_id=1, source_target_pairs={{0,8},{8,24},{24,16},{16,0},{1,9},{9,25},{25,17},{17,1},{2,10},{10... | collective-permute-start | bytes 1081352 | tf_op jit(solution)/shard_map/ppermute | solution.py:159
  445.7 70.6 %collective-permute-start.17 = (bf16[256,1408]{1,0:T(8,128)(2,1)}, bf16[256,1408]{1,0:T(8,128)(2,1)S(1)}, u32[]{:S(2)}, u32[]{:S(2)}) collective-permute-start(bf16[256,1408]{1,0:T(8,128)(2,1)} %add_convert_fusion.2), channel_id=1, source_target_pairs={{8,0},{24,8},{16,24},{0,16},{9,1},{25,9},{17,25},{1,17},{10,2},{26... | collective-permute-start | bytes 2162696 | tf_op jit(solution)/shard_map/ppermute | solution.py:173
  496.9 25.4 %collective-permute-start.16 = (bf16[256,1408]{1,0:T(8,128)(2,1)}, bf16[256,1408]{1,0:T(8,128)(2,1)}, u32[]{:S(2)}, u32[]{:S(2)}) collective-permute-start(bf16[256,1408]{1,0:T(8,128)(2,1)} %add_convert_fusion.3), channel_id=1, source_target_pairs={{0,8},{8,24},{24,16},{16,0},{1,9},{9,25},{25,17},{17,1},{2,10},{10... | collective-permute-start | bytes 2162696 | tf_op jit(solution)/shard_map/ppermute | solution.py:172
  501.4 20.8 %collective-permute-start.21 = (bf16[256,704]{0,1:T(8,128)(2,1)}, bf16[256,704]{0,1:T(8,128)(2,1)S(1)}, u32[]{:S(2)}, u32[]{:S(2)}) collective-permute-start(bf16[256,704]{0,1:T(8,128)(2,1)} %fusion.39), channel_id=1, source_target_pairs={{8,0},{24,8},{16,24},{0,16},{9,1},{25,9},{17,25},{1,17},{10,2},{26... | collective-permute-start | bytes 1081352 | tf_op jit(solution)/shard_map/ppermute | solution.py:173
  516.3 10.1 %collective-permute-start.20 = (bf16[256,704]{0,1:T(8,128)(2,1)S(1)}, bf16[256,704]{0,1:T(8,128)(2,1)S(1)}, u32[]{:S(2)}, u32[]{:S(2)}) collective-permute-start(bf16[256,704]{0,1:T(8,128)(2,1)S(1)} %copy-done.50), channel_id=1, source_target_pairs={{0,8},{8,24},{24,16},{16,0},{1,9},{9,25},{25,17},{17,1},{2,10},{10... | collective-permute-start | bytes 1081352 | tf_op jit(solution)/shard_map/ppermute | solution.py:172
  530.0 36.1 %all-to-all-start.4 = ((bf16[8,64,704]{2,1,0:T(8,128)(2,1)}), bf16[8,64,704]{2,1,0:T(8,128)(2,1)S(1)}, u32[]{:S(2)}, u32[]{:S(2)}) async-start(bf16[8,64,704]{2,1,0:T(8,128)(2,1)} %bitcast.15), calls=%async_computation.7 | async-start | bytes 1572864 | tf_op jit(solution)/shard_map/all_to_all | solution.py:194
  533.6 12.1 %collective-permute-start.31 = (bf16[256,512]{1,0:T(8,128)(2,1)}, bf16[256,512]{1,0:T(8,128)(2,1)S(1)}, u32[]{:S(2)}, u32[]{:S(2)}) collective-permute-start(bf16[256,512]{1,0:T(8,128)(2,1)} %convolution_convert_fusion.14), channel_id=1, source_target_pairs={{8,0},{24,8},{16,24},{0,16},{9,1},{25,9},{17,25},{1,17},{10,2},{26... | collective-permute-start | bytes 786440 | tf_op jit(solution)/shard_map/ppermute | solution.py:160
  535.1 11.2 %collective-permute-start.30 = (bf16[256,512]{1,0:T(8,128)(2,1)}, bf16[256,512]{1,0:T(8,128)(2,1)S(1)}, u32[]{:S(2)}, u32[]{:S(2)}) collective-permute-start(bf16[256,512]{1,0:T(8,128)(2,1)} %convolution_convert_fusion.15), channel_id=1, source_target_pairs={{0,8},{8,24},{24,16},{16,0},{1,9},{9,25},{25,17},{17,1},{2,10},{10... | collective-permute-start | bytes 786440 | tf_op jit(solution)/shard_map/ppermute | solution.py:159
  535.7 12.9 %collective-permute-start.29 = (bf16[256,512]{1,0:T(8,128)(2,1)}, bf16[256,512]{1,0:T(8,128)(2,1)S(1)}, u32[]{:S(2)}, u32[]{:S(2)}) collective-permute-start(bf16[256,512]{1,0:T(8,128)(2,1)} %convolution_convert_fusion.16), channel_id=1, source_target_pairs={{8,0},{24,8},{16,24},{0,16},{9,1},{25,9},{17,25},{1,17},{10,2},{26... | collective-permute-start | bytes 786440 | tf_op jit(solution)/shard_map/ppermute | solution.py:158
  537.1 79.8 %collective-permute-start.28 = (bf16[256,512]{1,0:T(8,128)(2,1)}, bf16[256,512]{1,0:T(8,128)(2,1)}, u32[]{:S(2)}, u32[]{:S(2)}) collective-permute-start(bf16[256,512]{1,0:T(8,128)(2,1)} %convolution_convert_fusion.17), channel_id=1, source_target_pairs={{0,8},{8,24},{24,16},{16,0},{1,9},{9,25},{25,17},{17,1},{2,10},{10... | collective-permute-start | bytes 786440 | tf_op jit(solution)/shard_map/ppermute | solution.py:157
  537.7 79.2 %collective-permute-start.27 = (bf16[256,512]{1,0:T(8,128)(2,1)}, bf16[256,512]{1,0:T(8,128)(2,1)S(1)}, u32[]{:S(2)}, u32[]{:S(2)}) collective-permute-start(bf16[256,512]{1,0:T(8,128)(2,1)} %convolution_convert_fusion.18), channel_id=1, source_target_pairs={{8,0},{24,8},{16,24},{0,16},{9,1},{25,9},{17,25},{1,17},{10,2},{26... | collective-permute-start | bytes 786440 | tf_op jit(solution)/shard_map/ppermute | solution.py:160
  545.7 71.3 %collective-permute-start.26 = (bf16[256,512]{1,0:T(8,128)(2,1)}, bf16[256,512]{1,0:T(8,128)(2,1)}, u32[]{:S(2)}, u32[]{:S(2)}) collective-permute-start(bf16[256,512]{1,0:T(8,128)(2,1)} %convolution_convert_fusion.19), channel_id=1, source_target_pairs={{0,8},{8,24},{24,16},{16,0},{1,9},{9,25},{25,17},{17,1},{2,10},{10... | collective-permute-start | bytes 786440 | tf_op jit(solution)/shard_map/ppermute | solution.py:159
  546.3 70.7 %collective-permute-start.25 = (bf16[256,512]{1,0:T(8,128)(2,1)}, bf16[256,512]{1,0:T(8,128)(2,1)}, u32[]{:S(2)}, u32[]{:S(2)}) collective-permute-start(bf16[256,512]{1,0:T(8,128)(2,1)} %convolution_convert_fusion.20), channel_id=1, source_target_pairs={{8,0},{24,8},{16,24},{0,16},{9,1},{25,9},{17,25},{1,17},{10,2},{26... | collective-permute-start | bytes 786440 | tf_op jit(solution)/shard_map/ppermute | solution.py:158
  548.6 68.4 %collective-permute-start.24 = (bf16[256,512]{1,0:T(8,128)(2,1)}, bf16[256,512]{1,0:T(8,128)(2,1)}, u32[]{:S(2)}, u32[]{:S(2)}) collective-permute-start(bf16[256,512]{1,0:T(8,128)(2,1)} %convolution_convert_fusion.21), channel_id=1, source_target_pairs={{0,8},{8,24},{24,16},{16,0},{1,9},{9,25},{25,17},{17,1},{2,10},{10... | collective-permute-start | bytes 786440 | tf_op jit(solution)/shard_map/ppermute | solution.py:157
  566.2 50.8 %all-to-all-start.3 = ((bf16[8,64,1408]{2,1,0:T(8,128)(2,1)}), bf16[8,64,1408]{2,1,0:T(8,128)(2,1)}, u32[]{:S(2)}, u32[]{:S(2)}) async-start(bf16[8,64,1408]{2,1,0:T(8,128)(2,1)} %bitcast.14), calls=%async_computation.6 | async-start | bytes 2883584 | tf_op jit(solution)/shard_map/all_to_all | solution.py:194
  570.7 222.7 %reduce-scatter.11.cloned.1.call-start = ((), (), s32[]{:S(2)}) async-start(), calls=%async_computation.19 | async-start | bytes 4718592 | tf_op jit(solution)/shard_map/reduce_scatter | solution.py:897
  659.3 11.0 %collective-permute-start.42 = (f32[5120]{0:T(1024)S(1)}, f32[5120]{0:T(1024)S(1)}, u32[]{:S(2)}, u32[]{:S(2)}) collective-permute-start(f32[5120]{0:T(1024)S(1)} %pad.9), channel_id=1, source_target_pairs={{0,8},{8,0},{16,24},{24,16},{1,9},{9,1},{17,25},{25,17},{2,10},{10... | collective-permute-start | bytes 61448 | tf_op jit(solution)/shard_map/ppermute | solution.py:205
  668.8 18.6 %collective-permute-start.41 = (bf16[256,512]{1,0:T(8,128)(2,1)}, bf16[256,512]{1,0:T(8,128)(2,1)}, u32[]{:S(2)}, u32[]{:S(2)}) collective-permute-start(bf16[256,512]{1,0:T(8,128)(2,1)} %fusion.59), channel_id=1, source_target_pairs={{8,0},{24,8},{16,24},{0,16},{9,1},{25,9},{17,25},{1,17},{10,2},{26... | collective-permute-start | bytes 786440 | tf_op jit(solution)/shard_map/ppermute | solution.py:173
  670.3 7.3 collective-permute-start.43
  673.2 14.3 %collective-permute-start.40 = (bf16[256,512]{1,0:T(8,128)(2,1)}, bf16[256,512]{1,0:T(8,128)(2,1)}, u32[]{:S(2)}, u32[]{:S(2)}) collective-permute-start(bf16[256,512]{1,0:T(8,128)(2,1)} %fusion.67), channel_id=1, source_target_pairs={{0,8},{8,24},{24,16},{16,0},{1,9},{9,25},{25,17},{17,1},{2,10},{10... | collective-permute-start | bytes 786440 | tf_op jit(solution)/shard_map/ppermute | solution.py:172
  673.7 35.6 %collective-permute-start.35 = (bf16[256,1152]{1,0:T(8,128)(2,1)}, bf16[256,1152]{1,0:T(8,128)(2,1)}, u32[]{:S(2)}, u32[]{:S(2)}) collective-permute-start(bf16[256,1152]{1,0:T(8,128)(2,1)} %convolution_convert_fusion.2), channel_id=1, source_target_pairs={{8,0},{24,8},{16,24},{0,16},{9,1},{25,9},{17,25},{1,17},{10,2},{26... | collective-permute-start | bytes 1769480 | tf_op jit(solution)/shard_map/ppermute | solution.py:158
  675.2 34.2 %collective-permute-start.34 = (bf16[256,1152]{1,0:T(8,128)(2,1)}, bf16[256,1152]{1,0:T(8,128)(2,1)}, u32[]{:S(2)}, u32[]{:S(2)}) collective-permute-start(bf16[256,1152]{1,0:T(8,128)(2,1)} %convolution_convert_fusion.3), channel_id=1, source_target_pairs={{0,8},{8,24},{24,16},{16,0},{1,9},{9,25},{25,17},{17,1},{2,10},{10... | collective-permute-start | bytes 1769480 | tf_op jit(solution)/shard_map/ppermute | solution.py:157
  677.6 2.6 collective-permute-start.44
  680.3 4.5 collective-permute-start.45
  684.8 44.0 %collective-permute-start.33 = (bf16[256,1152]{1,0:T(8,128)(2,1)}, bf16[256,1152]{1,0:T(8,128)(2,1)}, u32[]{:S(2)}, u32[]{:S(2)}) collective-permute-start(bf16[256,1152]{1,0:T(8,128)(2,1)} %convolution_convert_fusion.4), channel_id=1, source_target_pairs={{8,0},{24,8},{16,24},{0,16},{9,1},{25,9},{17,25},{1,17},{10,2},{26... | collective-permute-start | bytes 1769480 | tf_op jit(solution)/shard_map/ppermute | solution.py:160
  687.4 20.9 %collective-permute-start.39 = (bf16[256,512]{1,0:T(8,128)(2,1)}, bf16[256,512]{1,0:T(8,128)(2,1)}, u32[]{:S(2)}, u32[]{:S(2)}) collective-permute-start(bf16[256,512]{1,0:T(8,128)(2,1)} %add_convert_fusion.5), channel_id=1, source_target_pairs={{8,0},{24,8},{16,24},{0,16},{9,1},{25,9},{17,25},{1,17},{10,2},{26... | collective-permute-start | bytes 786440 | tf_op jit(solution)/shard_map/ppermute | solution.py:173
  687.5 21.9 %collective-permute-start.38 = (bf16[256,512]{1,0:T(8,128)(2,1)}, bf16[256,512]{1,0:T(8,128)(2,1)}, u32[]{:S(2)}, u32[]{:S(2)}) collective-permute-start(bf16[256,512]{1,0:T(8,128)(2,1)} %add_convert_fusion.6), channel_id=1, source_target_pairs={{0,8},{8,24},{24,16},{16,0},{1,9},{9,25},{25,17},{17,1},{2,10},{10... | collective-permute-start | bytes 786440 | tf_op jit(solution)/shard_map/ppermute | solution.py:172
  692.5 28.7 %all-to-all-start.7 = ((bf16[8,64,512]{2,1,0:T(8,128)(2,1)}), bf16[8,64,512]{2,1,0:T(8,128)(2,1)S(1)}, u32[]{:S(2)}, u32[]{:S(2)}) async-start(bf16[8,64,512]{2,1,0:T(8,128)(2,1)} %bitcast.181), calls=%async_computation.11 | async-start | bytes 1048576 | tf_op jit(solution)/shard_map/all_to_all | solution.py:194
  708.3 20.6 %collective-permute-start.32 = (bf16[256,1152]{1,0:T(8,128)(2,1)}, bf16[256,1152]{1,0:T(8,128)(2,1)}, u32[]{:S(2)}, u32[]{:S(2)}) collective-permute-start(bf16[256,1152]{1,0:T(8,128)(2,1)} %convolution_convert_fusion.5), channel_id=1, source_target_pairs={{0,8},{8,24},{24,16},{16,0},{1,9},{9,25},{25,17},{17,1},{2,10},{10... | collective-permute-start | bytes 1769480 | tf_op jit(solution)/shard_map/ppermute | solution.py:159
  712.3 16.5 %collective-permute-start.37 = (bf16[256,1152]{1,0:T(8,128)(2,1)}, bf16[256,1152]{1,0:T(8,128)(2,1)}, u32[]{:S(2)}, u32[]{:S(2)}) collective-permute-start(bf16[256,1152]{1,0:T(8,128)(2,1)} %fusion.21), channel_id=1, source_target_pairs={{8,0},{24,8},{16,24},{0,16},{9,1},{25,9},{17,25},{1,17},{10,2},{26... | collective-permute-start | bytes 1769480 | tf_op jit(solution)/shard_map/ppermute | solution.py:173
  716.2 19.6 %collective-permute-start.36 = (bf16[256,1152]{1,0:T(8,128)(2,1)}, bf16[256,1152]{1,0:T(8,128)(2,1)}, u32[]{:S(2)}, u32[]{:S(2)}) collective-permute-start(bf16[256,1152]{1,0:T(8,128)(2,1)} %fusion.20), channel_id=1, source_target_pairs={{0,8},{8,24},{24,16},{16,0},{1,9},{9,25},{25,17},{17,1},{2,10},{10... | collective-permute-start | bytes 1769480 | tf_op jit(solution)/shard_map/ppermute | solution.py:172
  721.2 29.3 %all-to-all-start.6 = ((bf16[8,64,512]{2,1,0:T(8,128)(2,1)}), bf16[8,64,512]{2,1,0:T(8,128)(2,1)}, u32[]{:S(2)}, u32[]{:S(2)}) async-start(bf16[8,64,512]{2,1,0:T(8,128)(2,1)} %bitcast.182), calls=%async_computation.10 | async-start | bytes 1048576 | tf_op jit(solution)/shard_map/all_to_all | solution.py:194
  726.0 28.2 %collective-permute-start.46 = (f32[4,5120]{1,0:T(4,128)}, f32[4,5120]{1,0:T(4,128)S(1)}, u32[]{:S(2)}, u32[]{:S(2)}) collective-permute-start(f32[4,5120]{1,0:T(4,128)} %pad_maximum_fusion.2), channel_id=1, source_target_pairs={{0,4},{1,5},{2,6},{3,7},{4,0},{5,1},{6,2},{7,3},{8,12},{9,13},{10,... | collective-permute-start | bytes 245768 | tf_op jit(solution)/shard_map/ppermute | solution.py:211
  750.5 33.1 %all-to-all-start.5 = ((bf16[8,64,1152]{2,1,0:T(8,128)(2,1)}), bf16[8,64,1152]{2,1,0:T(8,128)(2,1)S(1)}, u32[]{:S(2)}, u32[]{:S(2)}) async-start(bf16[8,64,1152]{2,1,0:T(8,128)(2,1)} %bitcast.172), calls=%async_computation.9 | async-start | bytes 2359296 | tf_op jit(solution)/shard_map/all_to_all | solution.py:194
  (70 other events, 1215.2 us)
Sparse Core Ops, SparseCore 0:
  53.1 51.4 all-gather.4
  119.5 47.7 all-gather.6
  241.4 48.8 reduce-scatter.4
  303.8 45.4 all-gather.8
  377.0 48.7 reduce-scatter.6
  429.8 45.2 all-gather.10
  504.6 61.3 reduce-scatter.8
  680.3 68.6 reduce-scatter.10

commit v5 on v4

--- a/solution.py
+++ b/solution.py
@@ -185,9 +185,12 @@
         return (own + from_left + from_right).astype(BF)
 
 
+def rank_major(packed):
+    return jnp.transpose(packed, (1, 0, 2)).reshape(-1, packed.shape[2])
+
+
 def exchange(packed):
-    turned = jnp.transpose(packed, (1, 0, 2)).reshape(-1, packed.shape[2])
-    return lax.all_to_all(turned, "seq", 0, 0, tiled=True)
+    return lax.all_to_all(packed, "seq", 0, 0, tiled=True)
 
 
 def to_rows(mine, ranks):
@@ -199,13 +202,13 @@
     count = lax.axis_size("dp")
     ranks = lax.axis_size("seq")
     if count & (count - 1) or ranks & (ranks - 1):
-        return lax.all_gather(lax.psum(values, "dp"), "seq", axis=0, tiled=False)
+        return lax.all_gather(lax.psum(values, "dp"), "seq", axis=0, tiled=True)
     step = 1
     while step < count:
         values = values + lax.ppermute(values, "dp", [(i, i ^ step) for i in range(count)])
         step *= 2
     rank = lax.axis_index("seq")
-    held = values.reshape(1, -1)
+    held = values
     step = 1
     while step < ranks:
         other = lax.ppermute(held, "seq", [(i, i ^ step) for i in range(ranks)])
@@ -400,8 +403,8 @@
 
 def bwd_kernel(
     hp, dk, dv, pre_ref, small_ref, rider_ref, taps_ref, const_ref,
-    state_ref, upd_ref, inv_ref, seen_ref, dm_ref,
-    dpre_ref, dtaps_ref, sums_ref,
+    state_ref, upd_ref, inv_ref, seen_ref, dm_ref, gain_ref,
+    dpre_ref, dtaps_ref,
     qkv_ref, cols_ref, conv_ref, dcon_ref, dcols_ref, du_ref, ds_ref, cur_ref,
 ):
     n = CHUNK
@@ -412,7 +415,7 @@
     wide = 2 * hp * dk + hp * dv
     cur_ref[...] = jnp.zeros_like(cur_ref)
     dtaps_ref[...] = jnp.zeros_like(dtaps_ref)
-    sums_ref[...] = jnp.zeros_like(sums_ref)
+    dtaps_ref[6:7, : gain_ref.shape[1]] = gain_ref[0:1, :]
     dcon_ref[total:, :] = jnp.zeros((dcon_ref.shape[0] - total, wide), F32)
     cols_ref[total:, :] = jnp.zeros((cols_ref.shape[0] - total, LANES), F32)
 
@@ -532,8 +535,8 @@
         d_small = jnp.where(lane < hp, d_cols * slope, d_cols * cols * (1.0 - cols))
         d_small = jnp.where(lane < 2 * hp, d_small, 0.0)
         dpre_ref[rows, wide:] = d_small.astype(BF)
-        sums_ref[0:1, :] += jnp.sum(d_small, axis=0, keepdims=True)
-        sums_ref[1:2, :] += jnp.sum(d_cols * cols, axis=0, keepdims=True)
+        dtaps_ref[4:5, :LANES] += jnp.sum(d_small, axis=0, keepdims=True)
+        dtaps_ref[5:6, :LANES] += jnp.sum(d_cols * cols, axis=0, keepdims=True)
         return carry
 
     lax.fori_loop(0, chunks, spread, 0)
@@ -569,11 +572,53 @@
         dgate_ref[:, at] = (d_ref[:, at] * m * gain * slope).astype(BF)
 
 
+def pack_kernel(ranks, *refs):
+    *ins, out_ref = refs
+    rows = ins[0].shape[0]
+    parts = [ref[...].astype(F32) for ref in ins]
+    for r in range(ranks):
+        pieces = [p[:, r * (p.shape[1] // ranks) : (r + 1) * (p.shape[1] // ranks)] for p in parts]
+        out_ref[r * rows : (r + 1) * rows, :] = jnp.concatenate(pieces, axis=1).astype(BF)
+
+
+def unpack_kernel(ranks, in_ref, *outs):
+    rows = outs[0].shape[0]
+    for i, out_ref in enumerate(outs):
+        size = out_ref.shape[1] // ranks
+        pieces = [
+            in_ref[r * rows : (r + 1) * rows, :].astype(F32)[:, i * size : (i + 1) * size]
+            for r in range(ranks)
+        ]
+        out_ref[...] = jnp.concatenate(pieces, axis=1)
+
+
 VMEM_LIMIT = 60 * 2**20
 
 
 def shape_of(*dims, dtype=F32):
     return jax.ShapeDtypeStruct(dims, dtype)
+
+
+def pack_even(ranks, *arrays):
+    rows = arrays[0].shape[0]
+    wide = sum(a.shape[1] for a in arrays) // ranks
+    return pl.pallas_call(
+        functools.partial(pack_kernel, ranks),
+        out_shape=shape_of(ranks * rows, wide, dtype=BF),
+        compiler_params=pltpu.CompilerParams(vmem_limit_bytes=VMEM_LIMIT),
+        name="pack_even",
+    )(*arrays)
+
+
+def unpack_even(ranks, packed, count):
+    rows = packed.shape[0] // ranks
+    size = packed.shape[1] // count
+    return pl.pallas_call(
+        functools.partial(unpack_kernel, ranks),
+        out_shape=(shape_of(rows, ranks * size),) * count,
+        compiler_params=pltpu.CompilerParams(vmem_limit_bytes=VMEM_LIMIT),
+        name="unpack_even",
+    )(packed)
 
 
 def delta_forward(pre, small, rider, taps, const, hp, dk, dv):
@@ -604,7 +649,7 @@
     )(pre, small, rider, taps, const)
 
 
-def delta_backward(pre, small, rider, taps, const, saved, d_mixed, hp, dk, dv):
+def delta_backward(pre, small, rider, taps, const, saved, d_mixed, gain, hp, dk, dv):
     total, wide = pre.shape
     jobs = total // CHUNK * hp
     return pl.pallas_call(
@@ -612,7 +657,6 @@
         out_shape=(
             shape_of(total, wide + LANES, dtype=BF),
             shape_of(8, wide),
-            shape_of(8, LANES),
         ),
         scratch_shapes=[
             pltpu.VMEM((total, wide), F32),
@@ -631,7 +675,7 @@
             bytes_accessed=total * wide * 20,
         ),
         name="delta_backward",
-    )(pre, small, rider, taps, const, *saved, d_mixed)
+    )(pre, small, rider, taps, const, *saved, d_mixed, gain)
 
 
 GATE_ROWS = 256
@@ -722,7 +766,7 @@
         ],
         axis=2,
     )
-    mix_own = exchange(
+    mix_pack = rank_major(
         jnp.concatenate(
             [
                 plan.split_keys(w_query),
@@ -733,36 +777,27 @@
             axis=2,
         )
     )
-    gathered = lax.all_gather(
-        after(jnp.concatenate([own_tokens, rider], axis=1), mix_own), "seq", axis=0, tiled=True
-    )
+    side_pack = rank_major(
+        jnp.concatenate([plan.split_even(w_gate), plan.split_even(w_out)], axis=2)
+    )
+    mlp_pack = pack_even(ranks, w_hidden, w_up, w_down)
+    mix_own = exchange(mix_pack)
+    held = lax.optimization_barrier(
+        (jnp.concatenate([own_tokens, rider], axis=1), side_pack, mlp_pack, mix_own)
+    )
+    gathered = lax.all_gather(held[0], "seq", axis=0, tiled=True)
+    side_own = exchange(held[1])
+    mix_own = held[3]
     w_mix = gather_end(mix_own, gather_start(mix_own))
-    side_own = exchange(
-        after(
-            jnp.concatenate([plan.split_even(w_gate), plan.split_even(w_out)], axis=2), mix_own
-        )
-    )
+    mlp_own_cols = exchange(after(held[2], side_own, gathered))
     side_own = after(side_own, w_mix)
-    w_side = gather_end(side_own, gather_start(side_own))
-    mlp_own_cols = exchange(
-        after(
-            jnp.concatenate(
-                [plan.split_even(w_hidden), plan.split_even(w_up), plan.split_even(w_down)],
-                axis=2,
-            ),
-            side_own,
-            gathered,
-        )
-    )
-    mlp_near = gather_start(after(mlp_own_cols, w_side))
+    side_near = gather_start(side_own)
 
     at_k = hp * dk
     at_v = 2 * hp * dk
     at_s = at_v + hp * dv
     attn_gain_full = w_mix[:, at_s + 2 * hp].astype(F32)
     mlp_gain_full = w_mix[:, at_s + 2 * hp + 1].astype(F32)
-    gate_cols = w_side[:, : hp * dv]
-    out_cols = w_side[:, hp * dv :]
 
     tokens_all = gathered[:, :width].astype(F32)
     normed_all = tokens_all * rms_scale(tokens_all)
@@ -770,8 +805,6 @@
     pre = nn(attn, w_mix[:, :at_s]).astype(BF)
     pre_small = nn(attn, w_mix[:, at_s:])
     cot_all = lax.all_gather(after(own_cot, pre), "seq", axis=0, tiled=True)
-    pre_gate = nn(attn, gate_cols)
-
     group = rank // vs
     taps_query = lax.dynamic_slice_in_dim(conv_query, group * hp * dk, hp * dk, 1)
     taps_key = lax.dynamic_slice_in_dim(conv_key, group * hp * dk, hp * dk, 1)
@@ -785,6 +818,12 @@
     pre, pre_small = lax.optimization_barrier((pre, pre_small, side_own))[:2]
     rider_all = gathered[:, width:]
     mixed, *saved = delta_forward(pre, pre_small, rider_all, taps, const, hp, dk, dv)
+    mixed, *side_near = lax.optimization_barrier((mixed,) + tuple(side_near))
+    w_side = gather_end(side_own, side_near)
+    gate_cols = w_side[:, : hp * dv]
+    out_cols = w_side[:, hp * dv :]
+    mlp_near = gather_start(after(mlp_own_cols, w_side))
+    pre_gate = nn(attn, gate_cols)
 
     def by_head(array):
         return array.reshape(length, hp, -1)
@@ -863,9 +902,9 @@
         d_mixed, d_gate, gain_part = gate_backward(
             d_gated, mixed, pre_gate, own_gain[None], hp, dv
         )
-        grad_out_gain = gain_part[0]
     else:
-        d_mixed, d_gate, grad_out_gain = gate_apply_back(d_gated, mixed, pre_gate, own_gain)
+        d_mixed, d_gate, gain_part = gate_apply_back(d_gated, mixed, pre_gate, own_gain)
+        gain_part = jnp.pad(gain_part[None], ((0, 7), (0, 0)))
     gate_sum = RingGrad(attn, d_gate)
     out_sum = RingGrad(d_branch_all, gated)
     d_attn_gate = nt(d_gate, gate_cols)
@@ -879,14 +918,15 @@
         mlp_part,
         d_attn_gate,
     )
-    both_rows = to_rows(both_sum.total(d_mixed), ranks)
-    down_rows = to_rows(down_sum.total(d_mixed), ranks)
-    d_pre, d_taps, d_sums = delta_backward(
-        pre, pre_small, rider_all, taps, const, saved, d_mixed, hp, dk, dv
-    )
-    d_pre, d_taps, d_sums, mlp_out, both_rows, down_rows = lax.optimization_barrier(
-        (d_pre, d_taps, d_sums, mlp_out, both_rows, down_rows) + gate_sum.near + out_sum.near
-    )[:6]
+    mlp_rows = exchange(
+        jnp.concatenate([both_sum.total(d_mixed), down_sum.total(d_mixed)], axis=1)
+    )
+    d_pre, d_sums = delta_backward(
+        pre, pre_small, rider_all, taps, const, saved, d_mixed, gain_part, hp, dk, dv
+    )
+    d_pre, d_sums, mlp_out, mlp_rows = lax.optimization_barrier(
+        (d_pre, d_sums, mlp_out, mlp_rows) + gate_sum.near + out_sum.near
+    )[:4]
     mix_sum = RingGrad(attn, d_pre)
     gate_sum.second(d_pre)
     out_sum.second(d_pre)
@@ -905,37 +945,22 @@
         (d_middle + rms_scale(inputs) * (e - n * jnp.mean(e * n, axis=-1, keepdims=True))).astype(BF)
     )
 
-    sums = jnp.concatenate(
-        [
-            d_taps[:KERNEL, :at_k].reshape(-1),
-            d_taps[:KERNEL, at_k:at_v].reshape(-1),
-            d_taps[:KERNEL, at_v:].reshape(-1),
-            d_sums[1, :hp],
-            d_sums[0, :hp],
-            grad_out_gain,
-        ]
-    )
-    every = sum_everywhere(jnp.pad(sums, (0, -sums.shape[0] % 1024)))
+    every = sum_everywhere(d_sums).reshape(ranks, 8, -1)
 
     def per_head(part, lead):
         part = part.reshape(ranks // vs, vs, lead, -1).sum(axis=1)
         return jnp.transpose(part, (1, 0, 2)).reshape(lead, -1)
 
-    a0 = KERNEL * hp * dk
-    a1 = 2 * a0
-    a2 = a1 + KERNEL * hp * dv
-    grad_conv_value = jnp.transpose(
-        every[:, a1:a2].reshape(ranks, KERNEL, -1), (1, 0, 2)
-    ).reshape(KERNEL, -1)
-    gain_sum = every[:, a2 + 2 * hp : a2 + 2 * hp + dv].reshape(ranks // vs, vs, dv).sum(axis=0).reshape(-1)
+    every_taps = every[:, :KERNEL]
+    grad_conv_value = jnp.transpose(every_taps[:, :, at_v:], (1, 0, 2)).reshape(KERNEL, -1)
+    gain_sum = every[:, 6, :dv].reshape(ranks // vs, vs, dv).sum(axis=0).reshape(-1)
     grad_query = plan.join_keys(mix_rows[:, :, :at_k])
     grad_key = plan.join_keys(mix_rows[:, :, at_k:at_v])
     grad_value = plan.join_even(mix_rows[:, :, at_v:at_s])
     grad_decay = plan.join_keys(mix_rows[:, :, at_s : at_s + hp])
     grad_beta = plan.join_keys(mix_rows[:, :, at_s + hp : at_s + 2 * hp])
     grad_gate = plan.join_even(gate_rows)
-    grad_hidden = plan.join_even(both_rows[:, :, :ff])
-    grad_up = plan.join_even(both_rows[:, :, ff:])
+    grad_hidden, grad_up, grad_down = unpack_even(ranks, mlp_rows, 3)
 
     def gain_grad(gain, pairs):
         total = sum(jnp.sum(w.astype(F32) * g, axis=1) for w, g in pairs)
@@ -962,16 +987,16 @@
         grad_beta,
         grad_gate,
         plan.join_even(out_rows),
-        per_head(every[:, :a0], KERNEL),
-        per_head(every[:, a0:a1], KERNEL),
+        per_head(every_taps[:, :, :at_k], KERNEL),
+        per_head(every_taps[:, :, at_k:at_v], KERNEL),
         grad_conv_value,
-        per_head(every[:, a2 : a2 + hp], 1)[0],
-        per_head(every[:, a2 + hp : a2 + 2 * hp], 1)[0],
+        per_head(every[:, 5, :hp], 1)[0],
+        per_head(every[:, 4, :hp], 1)[0],
         gain_sum,
         gain_grad(mlp_gain, ((w_hidden, grad_hidden), (w_up, grad_up))),
         grad_hidden,
         grad_up,
-        plan.join_even(down_rows),
+        grad_down,
     )
 
 

time: 812 us -> 747 us (0.920)
  local copies, waits for them, and re-layouts: 125 us -> 85.9 us
  starting transfers between devices: 98.2 us -> 83.5 us
  waiting for transfers between devices: 264 us -> 253 us
  matrix products: 179 us -> 169 us
    all_to_all x5 -> x3, waiting for transfers between devices: 48.7 us -> 0.01 us  [to_rows(): turned = lax.all_to_all(mine, 'seq', 0, 0, tiled=True)]
    ppermute x3, waiting for transfers between devices: 0.01 us -> 30.6 us  [sum_everywhere(): other = lax.ppermute(held, 'seq', [(i, i ^ step) for i in range(ranks)])]
    ppermute x6, waiting for transfers between devices: 46.5 us -> 20.4 us  [gather_start(): return (lax.ppermute(own, 'dp', right), lax.ppermute(own, 'dp', left))]
    convert_element_type x9 -> x3, local copies, waits for them, and re-layouts: 17.2 us -> 2.21 us  [join_even(): jnp.transpose(array, (1, 0, 2)).reshape(array.shape[1], -1).astype(F32)]
    reshape x6 -> x0, local copies, waits for them, and re-layouts: 12.1 us -> none  [split_even(): return array.reshape(array.shape[0], self.ranks, -1)]
    ppermute x3, waiting for transfers between devices: 8.96 us -> 18.8 us  [gather_end(): far_a = lax.ppermute(from_left[:half], 'dp', right)]
    all_gather x1, starting transfers between devices: 9.74 us -> 0.04 us  [local(): mlp_all = lax.all_gather(mlp_own, 'seq', axis=0, tiled=True)]
    reduce_scatter x1, waiting for transfers between devices: 34.7 us -> 44.3 us  [local(): lax.psum_scatter(nt(gated, out_cols).astype(BF), 'seq', scatter_dimension...]
  transfers between devices with their start and end apart: 63 -> 62, of which waited for: 24 -> 22; matrix products, arithmetic and copies ran while one was open for 31% -> 32% of each run, Pallas kernels for 11% -> 12%
where the time goes in v5:
time: 747 us; the launch traced here: 736 us
  waiting for transfers between devices  253 us (34%)
  matrix products  169 us (23%)
  Pallas kernels  92.8 us (12%)
  local copies, waits for them, and re-layouts  85.9 us (11%)
  starting transfers between devices  83.5 us (11%)
  other arithmetic  36.3 us (5%)
  between operations  15.7 us (2%)
    dot_general x46, matrix products, dot_f32(): lax.dot_general(left, right, (dims, ((), ())), preferred_element_type=F32)  169 us
    all_to_all x4, waiting for transfers between devices, exchange(): return lax.all_to_all(packed, 'seq', 0, 0, tiled=True)  50.3 us
    pallas_call x1, Pallas kernels, delta_backward(): pl.pallas_call(functools.partial(bwd_kernel, hp, dk, dv), out_shape=(shap...  46 us
    reduce_scatter x1, waiting for transfers between devices, local(): lax.psum_scatter(nt(gated, out_cols).astype(BF), 'seq', scatter_dimension...  44.3 us
    unnamed x153, local copies, waits for them, and re-layouts  35.3 us
    ppermute x3, waiting for transfers between devices, sum_everywhere(): other = lax.ppermute(held, 'seq', [(i, i ^ step) for i in range(ranks)])  30.6 us
    pallas_call x1, Pallas kernels, delta_forward(): pl.pallas_call(functools.partial(fwd_kernel, hp, dk, dv), out_shape=(shap...  29.5 us
    all_gather x1, waiting for transfers between devices, local(): d_branch_all = lax.all_gather(d_branch_own, 'seq', axis=0, tiled=True)  24.1 us
  transfers between devices with their start and end apart: 62, of which 22 were waited for; matrix products, arithmetic and copies ran while one was open for 32% of the time, Pallas kernels for 12%

profile of v5, /device:TPU:0, one launch (start us, length us, event | category | flops | bytes accessed | tf_op | source)
XLA Modules:
  0.0 736.4 jit_solution(13271974632110093917)
XLA Ops:
  17.2 6.3 all-to-all-start
  25.8 3.4 pack_even.1
  30.4 22.5 %all-to-all-done = bf16[8,64,1152]{2,1,0:T(8,128)(2,1)S(1)} async-done(((bf16[8,64,1152]{2,1,0:T(8,128)(2,1)}), bf16[8,64,1152]{2,1,0:T(8,128)(2,1)S(1)}, u32[]{:S(2)}, u32[]{:S(2)}) %all-to-all-start) | async-done | bytes 1179680 | tf_op jit(solution)/shard_map/all_to_all | solution.py:193
  60.8 19.8 %collective-permute-done.1 = bf16[512,1152]{1,0:T(8,128)(2,1)S(1)} collective-permute-done((bf16[512,1152]{1,0:T(8,128)(2,1)S(1)}, bf16[512,1152]{1,0:T(8,128)(2,1)S(1)}, u32[]{:S(2)}, u32[]{:S(2)}) %collective-permute-start.1) | collective-permute-done | bytes 1179680 | tf_op jit(solution)/shard_map/ppermute | solution.py:132
  87.4 4.2 all-to-all-start.1
  105.9 3.2 fusion
  109.2 2.9 fusion.2
  114.2 5.7 fusion.22.pre_ref
  124.7 4.3 fusion.87.small_ref
  129.1 5.1 all-to-all-start.2
  136.1 29.5 %delta_forward.1 = (f32[1024,512]{1,0:T(8,128)}, f32[16,128,256]{2,1,0:T(8,128)}, f32[1024,512]{1,0:T(8,128)}, f32[16,128,128]{2,1,0:T(8,128)}, f32[1024,256]{1,0:T(8,128)}) custom-call(bf16[1024,1024]{1,0:T(8,128)(2,1)} %fusion.22.pre_ref, f32[1024,128]{1,0:T(8,128)} %fusion.87.small_ref, bf16[1024,128]{1,0:T(8,128)(2,1)} %slice.296.rider_ref, ...), custom_call_target="tpu_custom_call" | custom-call | flops 43008000000 | bytes 16777216 | tf_op jit(solution)/shard_map/delta_forward/pallas_call | solution.py:627
  172.7 8.6 %collective-permute-done.6 = bf16[256,1024]{1,0:T(8,128)(2,1)S(1)} collective-permute-done((bf16[256,1024]{1,0:T(8,128)(2,1)S(1)}, bf16[256,1024]{1,0:T(8,128)(2,1)S(1)}, u32[]{:S(2)}, u32[]{:S(2)}) %collective-permute-start.6) | collective-permute-done | bytes 524320 | tf_op jit(solution)/shard_map/ppermute | solution.py:141
  185.3 3.7 fusion.30.gate_ref
  188.9 4.3 gate_forward.1
  193.2 21.9 %all-to-all-done.2 = bf16[8,64,2112]{2,1,0:T(8,128)(2,1)S(1)} async-done(((bf16[8,64,2112]{2,1,0:T(8,128)(2,1)}), bf16[8,64,2112]{2,1,0:T(8,128)(2,1)S(1)}, u32[]{:S(2)}, u32[]{:S(2)}) %all-to-all-start.2) | async-done | bytes 2162720 | tf_op jit(solution)/shard_map/all_to_all | solution.py:193
  215.1 6.4 convolution_convert_fusion.1
  226.0 44.3 %reduce-scatter.5.cloned.1.call-done = bf16[128,2048]{1,0:T(8,128)(2,1)} async-done(((bf16[1024,2048]{1,0:T(8,128)(2,1)}), bf16[128,2048]{1,0:T(8,128)(2,1)}) %reduce-scatter.5.cloned.1.call-update) | async-done | bytes 524304 | tf_op jit(solution)/shard_map/reduce_scatter | solution.py:858
  282.7 4.0 copy.162
  286.8 2.9 copy.165
  289.7 3.2 constant_dynamic-update-slice_fusion.13
  292.9 8.6 %collective-permute-done.10 = bf16[256,2112]{0,1:T(8,128)(2,1)} collective-permute-done((bf16[256,2112]{0,1:T(8,128)(2,1)}, bf16[256,2112]{0,1:T(8,128)(2,1)}, u32[]{:S(2)}, u32[]{:S(2)}) %collective-permute-start.10) | collective-permute-done | bytes 1081376 | tf_op jit(solution)/shard_map/ppermute | solution.py:141
  312.6 7.0 all-gather.9.cloned.1.call-done
  319.6 11.5 %fusion.5 = f32[1024,1408]{0,1:T(8,128)} fusion(bf16[1024,2048]{1,0:T(8,128)(2,1)} %all-gather.9.cloned.1.call-done, bf16[2048,2112]{1,0:T(8,128)(2,1)} %constant_dynamic-update-slice_fusion.10), kind=kOutput, calls=%fused_computation.8 | convolution fusion | flops 5905580032 | bytes 15728640 | tf_op jit(solution)/shard_map/dot_general | solution.py:22
  331.1 6.2 multiply_convert_fusion.2
  338.9 8.3 %fusion.9 = bf16[1024,2048]{1,0:T(8,128)(2,1)} fusion(bf16[2048,2112]{1,0:T(8,128)(2,1)S(1)} %copy-done.20, bf16[1024,704]{0,1:T(8,128)(2,1)S(1)} %get-tuple-element.161, bf16[1024,704]{0,1:T(8,128)(2,1)S(1)} %get-tuple-element.160), kind=kOutput, calls=%fused_computation.12 | convolution fusion | flops 5913444352 | bytes 12845056 | tf_op jit(solution)/shard_map/dot_general | solution.py:22
  347.3 4.0 convolution_convert_fusion.6
  353.2 3.0 convolution_convert_fusion.7
  356.7 3.0 convolution_convert_fusion.8
  361.1 3.0 convolution_convert_fusion.9
  367.8 2.9 convolution_convert_fusion.12
  370.7 2.8 convolution_convert_fusion.13
  373.5 22.6 %reduce-scatter.7.cloned.1.call-done = bf16[128,2048]{1,0:T(8,128)(2,1)} async-done(((bf16[1024,2048]{1,0:T(8,128)(2,1)}), bf16[128,2048]{1,0:T(8,128)(2,1)}) %reduce-scatter.7.cloned.1.call-update) | async-done | bytes 524304 | tf_op jit(solution)/shard_map/reduce_scatter | solution.py:886
  404.1 8.0 %convolution_convert_fusion = bf16[1024,2048]{1,0:T(8,128)(2,1)} fusion(bf16[1024,704]{0,1:T(8,128)(2,1)} %copy-done.50, bf16[2048,2112]{1,0:T(8,128)(2,1)} %constant_dynamic-update-slice_fusion.10), kind=kOutput, calls=%fused_computation.13 | convolution fusion | flops 2954887168 | bytes 8781824 | tf_op jit(solution)/shard_map/dot_general | solution.py:22
  412.2 4.3 add_convert_fusion.2
  418.1 3.2 add_convert_fusion.3
  421.3 24.1 %all-gather.11.cloned.1.call-done = bf16[1024,2048]{1,0:T(8,128)(2,1)} async-done(((bf16[128,2048]{1,0:T(8,128)(2,1)}), bf16[1024,2048]{1,0:T(8,128)(2,1)}) %all-gather.11.cloned.1.call-update) | async-done | bytes 4194320 | tf_op jit(solution)/shard_map/all_gather | solution.py:896
  445.4 6.5 fusion.25.d_ref
  451.9 5.6 gate_backward.1
  457.5 2.7 convolution_convert_fusion.18
  460.1 2.7 convolution_convert_fusion.19
  477.2 7.2 fusion.28
  494.6 4.1 collective-permute-done.20
  502.5 2.6 add_convert_fusion.1
  505.2 4.0 fusion.14
  510.7 3.6 all-to-all-start.3
  517.0 46.0 %delta_backward.1 = (bf16[1024,1152]{1,0:T(8,128)(2,1)}, f32[8,1024]{1,0:T(8,128)}) custom-call(bf16[1024,1024]{1,0:T(8,128)(2,1)} %fusion.22.pre_ref, f32[1024,128]{1,0:T(8,128)} %fusion.87.small_ref, bf16[1024,128]{1,0:T(8,128)(2,1)} %slice.296.rider_ref, f32[4,1024]{1,0:T(4,128)} %pad_maximum_fusion.4.taps_ref, f32[2,128]{1,0:T(2,128)} %select_maximum_fusion.const_ref, ...), custom_call_target="tpu_custom_call" | custom-call | flops 69632000000 | bytes 20971520 | tf_op jit(solution)/shard_map/delta_backward/pallas_call | solution.py:655
  564.4 5.8 all-to-all-done.3
  571.6 4.0 unpack_even.1
  577.1 10.8 %add_convert_fusion = bf16[1024,2048]{1,0:T(8,128)(2,1)} fusion(f32[1024,2048]{1,0:T(8,128)} %fusion.28, bf16[1024,1152]{1,0:T(8,128)(2,1)} %get-tuple-element.132, bf16[2048,1152]{1,0:T(8,128)(2,1)} %constant_dynamic-update-slice_fusion), kind=kOutput, calls=%fused_computation.5 | convolution fusion | flops 4836032512 | bytes 19660800 | tf_op jit(solution)/shard_map/dot_general | solution.py:22
  594.1 2.7 convolution_convert_fusion.2
  609.1 6.4 collective-permute-done.43
  617.7 2.9 fusion.35
  620.6 4.2 all-to-all-start.6
  624.8 10.2 %collective-permute-done.39 = bf16[256,512]{1,0:T(8,128)(2,1)} collective-permute-done((bf16[256,512]{1,0:T(8,128)(2,1)}, bf16[256,512]{1,0:T(8,128)(2,1)}, u32[]{:S(2)}, u32[]{:S(2)}) %collective-permute-start.39) | collective-permute-done | bytes 262176 | tf_op jit(solution)/shard_map/ppermute | solution.py:173
  635.1 3.4 fusion.34
  638.4 2.9 fusion.21
  643.4 2.9 fusion.20
  646.3 4.1 all-to-all-start.5
  650.5 3.1 multiply_reduce_fusion
  657.4 4.6 collective-permute-done.36
  662.1 4.5 fusion.15
  666.6 4.0 all-to-all-start.4
  671.5 2.9 collective-permute-start.46
  675.0 30.6 %collective-permute-done.46 = f32[32,1024]{1,0:T(8,128)S(1)} collective-permute-done((f32[32,1024]{1,0:T(8,128)S(1)}, f32[32,1024]{1,0:T(8,128)S(1)}, u32[]{:S(2)}, u32[]{:S(2)}) %collective-permute-start.46) | collective-permute-done | bytes 131104 | tf_op jit(solution)/shard_map/ppermute | solution.py:214
  (368 shorter events, 196.8 us)
Async XLA Ops:
  7.2 114.9 %copy-start = (f32[4,4096]{1,0:T(4,128)S(1)}, f32[4,4096]{1,0:T(4,128)}, u32[]{:S(2)}) copy-start(f32[4,4096]{1,0:T(4,128)} %param.32) | copy-start | bytes 196612
  17.2 35.7 %all-to-all-start = ((bf16[8,64,1152]{2,1,0:T(8,128)(2,1)}), bf16[8,64,1152]{2,1,0:T(8,128)(2,1)S(1)}, u32[]{:S(2)}, u32[]{:S(2)}) async-start(bf16[8,64,1152]{2,1,0:T(8,128)(2,1)} %copy.159), calls=%async_computation | async-start | bytes 2359296 | tf_op jit(solution)/shard_map/all_to_all | solution.py:193
  23.5 82.4 %all-gather.5.cloned.1.call-start = ((), (), s32[]{:S(2)}) async-start(), calls=%async_computation.11 | async-start | bytes 5013504 | tf_op jit(solution)/shard_map/all_gather | solution.py:788
  53.0 27.6 %collective-permute-start.1 = (bf16[512,1152]{1,0:T(8,128)(2,1)S(1)}, bf16[512,1152]{1,0:T(8,128)(2,1)S(1)}, u32[]{:S(2)}, u32[]{:S(2)}) collective-permute-start(bf16[512,1152]{1,0:T(8,128)(2,1)S(1)} %bitcast.125), channel_id=1, source_target_pairs={{0,8},{8,24},{24,16},{16,0},{1,9},{9,25},{25,17},{17,1},{2,10},{10... | collective-permute-start | bytes 3538952 | tf_op jit(solution)/shard_map/ppermute | solution.py:132
  55.5 28.2 %collective-permute-start = (bf16[512,1152]{1,0:T(8,128)(2,1)S(1)}, bf16[512,1152]{1,0:T(8,128)(2,1)}, u32[]{:S(2)}, u32[]{:S(2)}) collective-permute-start(bf16[512,1152]{1,0:T(8,128)(2,1)S(1)} %bitcast.126), channel_id=1, source_target_pairs={{8,0},{24,8},{16,24},{0,16},{9,1},{25,9},{17,25},{1,17},{10,2},{26... | collective-permute-start | bytes 3538952 | tf_op jit(solution)/shard_map/ppermute | solution.py:132
  81.4 14.4 %collective-permute-start.2 = (bf16[256,1152]{1,0:T(8,128)(2,1)}, bf16[256,1152]{1,0:T(8,128)(2,1)}, u32[]{:S(2)}, u32[]{:S(2)}) collective-permute-start(bf16[256,1152]{1,0:T(8,128)(2,1)} %slice.291), channel_id=1, source_target_pairs={{0,8},{8,24},{24,16},{16,0},{1,9},{9,25},{25,17},{17,1},{2,10},{10... | collective-permute-start | bytes 1769480 | tf_op jit(solution)/shard_map/ppermute | solution.py:141
  85.7 14.1 %collective-permute-start.3 = (bf16[256,1152]{1,0:T(8,128)(2,1)}, bf16[256,1152]{1,0:T(8,128)(2,1)}, u32[]{:S(2)}, u32[]{:S(2)}) collective-permute-start(bf16[256,1152]{1,0:T(8,128)(2,1)} %slice.292), channel_id=1, source_target_pairs={{8,0},{24,8},{16,24},{0,16},{9,1},{25,9},{17,25},{1,17},{10,2},{26... | collective-permute-start | bytes 1769480 | tf_op jit(solution)/shard_map/ppermute | solution.py:142
  87.4 35.3 %all-to-all-start.1 = ((bf16[8,64,1024]{2,1,0:T(8,128)(2,1)}), bf16[8,64,1024]{2,1,0:T(8,128)(2,1)}, u32[]{:S(2)}, u32[]{:S(2)}) async-start(bf16[8,64,1024]{2,1,0:T(8,128)(2,1)} %bitcast.8), calls=%async_computation.1 | async-start | bytes 2097152 | tf_op jit(solution)/shard_map/all_to_all | solution.py:193
  91.6 123.5 %all-gather.7.cloned.1.call-start = ((), (), s32[]{:S(2)}) async-start(), calls=%async_computation.12 | async-start | bytes 4718592 | tf_op jit(solution)/shard_map/all_gather | solution.py:807
  122.7 42.9 %collective-permute-start.4 = (bf16[512,1024]{1,0:T(8,128)(2,1)}, bf16[512,1024]{1,0:T(8,128)(2,1)}, u32[]{:S(2)}, u32[]{:S(2)}) collective-permute-start(bf16[512,1024]{1,0:T(8,128)(2,1)} %bitcast.9), channel_id=1, source_target_pairs={{0,8},{8,24},{24,16},{16,0},{1,9},{9,25},{25,17},{17,1},{2,10},{10... | collective-permute-start | bytes 3145736 | tf_op jit(solution)/shard_map/ppermute | solution.py:132
  124.1 41.4 %collective-permute-start.5 = (bf16[512,1024]{1,0:T(8,128)(2,1)}, bf16[512,1024]{1,0:T(8,128)(2,1)}, u32[]{:S(2)}, u32[]{:S(2)}) collective-permute-start(bf16[512,1024]{1,0:T(8,128)(2,1)} %bitcast.9), channel_id=1, source_target_pairs={{8,0},{24,8},{16,24},{0,16},{9,1},{25,9},{17,25},{1,17},{10,2},{26... | collective-permute-start | bytes 3145736 | tf_op jit(solution)/shard_map/ppermute | solution.py:132
  129.1 86.0 %all-to-all-start.2 = ((bf16[8,64,2112]{2,1,0:T(8,128)(2,1)}), bf16[8,64,2112]{2,1,0:T(8,128)(2,1)S(1)}, u32[]{:S(2)}, u32[]{:S(2)}) async-start(bf16[8,64,2112]{2,1,0:T(8,128)(2,1)} %bitcast.122), calls=%async_computation.2 | async-start | bytes 4456448 | tf_op jit(solution)/shard_map/all_to_all | solution.py:193
  134.2 136.2 %reduce-scatter.5.cloned.1.call-start = ((), (), s32[]{:S(2)}) async-start(), calls=%async_computation.13 | async-start | bytes 4718592 | tf_op jit(solution)/shard_map/reduce_scatter | solution.py:858
  166.6 14.6 %collective-permute-start.6 = (bf16[256,1024]{1,0:T(8,128)(2,1)S(1)}, bf16[256,1024]{1,0:T(8,128)(2,1)S(1)}, u32[]{:S(2)}, u32[]{:S(2)}) collective-permute-start(bf16[256,1024]{1,0:T(8,128)(2,1)S(1)} %slice.228), channel_id=1, source_target_pairs={{0,8},{8,24},{24,16},{16,0},{1,9},{9,25},{25,17},{17,1},{2,10},{10... | collective-permute-start | bytes 1572872 | tf_op jit(solution)/shard_map/ppermute | solution.py:141
  169.8 14.1 %collective-permute-start.7 = (bf16[256,1024]{1,0:T(8,128)(2,1)S(1)}, bf16[256,1024]{1,0:T(8,128)(2,1)S(1)}, u32[]{:S(2)}, u32[]{:S(2)}) collective-permute-start(bf16[256,1024]{1,0:T(8,128)(2,1)S(1)} %slice.229), channel_id=1, source_target_pairs={{8,0},{24,8},{16,24},{0,16},{9,1},{25,9},{17,25},{1,17},{10,2},{26... | collective-permute-start | bytes 1572872 | tf_op jit(solution)/shard_map/ppermute | solution.py:142
  221.5 98.1 %all-gather.9.cloned.1.call-start = ((), (), s32[]{:S(2)}) async-start(), calls=%async_computation.14 | async-start | bytes 4718592 | tf_op jit(solution)/shard_map/all_gather | solution.py:870
  224.0 49.7 %collective-permute-start.8 = (bf16[512,2112]{0,1:T(8,128)(2,1)}, bf16[512,2112]{0,1:T(8,128)(2,1)}, u32[]{:S(2)}, u32[]{:S(2)}) collective-permute-start(bf16[512,2112]{0,1:T(8,128)(2,1)} %copy.160), channel_id=1, source_target_pairs={{0,8},{8,24},{24,16},{16,0},{1,9},{9,25},{25,17},{17,1},{2,10},{10... | collective-permute-start | bytes 6488072 | tf_op jit(solution)/shard_map/ppermute | solution.py:132
  225.4 48.9 %collective-permute-start.9 = (bf16[512,2112]{0,1:T(8,128)(2,1)}, bf16[512,2112]{0,1:T(8,128)(2,1)}, u32[]{:S(2)}, u32[]{:S(2)}) collective-permute-start(bf16[512,2112]{0,1:T(8,128)(2,1)} %copy.160), channel_id=1, source_target_pairs={{8,0},{24,8},{16,24},{0,16},{9,1},{25,9},{17,25},{1,17},{10,2},{26... | collective-permute-start | bytes 6488072 | tf_op jit(solution)/shard_map/ppermute | solution.py:132
  274.4 121.7 %reduce-scatter.7.cloned.1.call-start = ((), (), s32[]{:S(2)}) async-start(), calls=%async_computation.15 | async-start | bytes 4718592 | tf_op jit(solution)/shard_map/reduce_scatter | solution.py:886
  276.7 24.8 %collective-permute-start.10 = (bf16[256,2112]{0,1:T(8,128)(2,1)}, bf16[256,2112]{0,1:T(8,128)(2,1)}, u32[]{:S(2)}, u32[]{:S(2)}) collective-permute-start(bf16[256,2112]{0,1:T(8,128)(2,1)} %slice.236), channel_id=1, source_target_pairs={{0,8},{8,24},{24,16},{16,0},{1,9},{9,25},{25,17},{17,1},{2,10},{10... | collective-permute-start | bytes 3244040 | tf_op jit(solution)/shard_map/ppermute | solution.py:141
  280.5 24.7 %collective-permute-start.11 = (bf16[256,2112]{0,1:T(8,128)(2,1)}, bf16[256,2112]{0,1:T(8,128)(2,1)}, u32[]{:S(2)}, u32[]{:S(2)}) collective-permute-start(bf16[256,2112]{0,1:T(8,128)(2,1)} %slice.237), channel_id=1, source_target_pairs={{8,0},{24,8},{16,24},{0,16},{9,1},{25,9},{17,25},{1,17},{10,2},{26... | collective-permute-start | bytes 3244040 | tf_op jit(solution)/shard_map/ppermute | solution.py:142
  347.2 98.2 %all-gather.11.cloned.1.call-start = ((), (), s32[]{:S(2)}) async-start(), calls=%async_computation.16 | async-start | bytes 4718592 | tf_op jit(solution)/shard_map/all_gather | solution.py:896
  351.3 48.6 %collective-permute-start.15 = (bf16[256,1408]{1,0:T(8,128)(2,1)}, bf16[256,1408]{1,0:T(8,128)(2,1)S(1)}, u32[]{:S(2)}, u32[]{:S(2)}) collective-permute-start(bf16[256,1408]{1,0:T(8,128)(2,1)} %convolution_convert_fusion.6), channel_id=1, source_target_pairs={{8,0},{24,8},{16,24},{0,16},{9,1},{25,9},{17,25},{1,17},{10,2},{26... | collective-permute-start | bytes 2162696 | tf_op jit(solution)/shard_map/ppermute | solution.py:160
  356.1 43.7 %collective-permute-start.14 = (bf16[256,1408]{1,0:T(8,128)(2,1)}, bf16[256,1408]{1,0:T(8,128)(2,1)}, u32[]{:S(2)}, u32[]{:S(2)}) collective-permute-start(bf16[256,1408]{1,0:T(8,128)(2,1)} %convolution_convert_fusion.7), channel_id=1, source_target_pairs={{0,8},{8,24},{24,16},{16,0},{1,9},{9,25},{25,17},{17,1},{2,10},{10... | collective-permute-start | bytes 2162696 | tf_op jit(solution)/shard_map/ppermute | solution.py:159
  359.7 40.2 %collective-permute-start.13 = (bf16[256,1408]{1,0:T(8,128)(2,1)}, bf16[256,1408]{1,0:T(8,128)(2,1)}, u32[]{:S(2)}, u32[]{:S(2)}) collective-permute-start(bf16[256,1408]{1,0:T(8,128)(2,1)} %convolution_convert_fusion.8), channel_id=1, source_target_pairs={{8,0},{24,8},{16,24},{0,16},{9,1},{25,9},{17,25},{1,17},{10,2},{26... | collective-permute-start | bytes 2162696 | tf_op jit(solution)/shard_map/ppermute | solution.py:158
  364.1 35.8 %collective-permute-start.12 = (bf16[256,1408]{1,0:T(8,128)(2,1)}, bf16[256,1408]{1,0:T(8,128)(2,1)}, u32[]{:S(2)}, u32[]{:S(2)}) collective-permute-start(bf16[256,1408]{1,0:T(8,128)(2,1)} %convolution_convert_fusion.9), channel_id=1, source_target_pairs={{0,8},{8,24},{24,16},{16,0},{1,9},{9,25},{25,17},{17,1},{2,10},{10... | collective-permute-start | bytes 2162696 | tf_op jit(solution)/shard_map/ppermute | solution.py:157
  367.8 29.7 %copy-start.13 = (bf16[128,4096]{1,0:T(8,128)(2,1)S(1)}, bf16[128,4096]{1,0:T(8,128)(2,1)}, u32[]{:S(2)}) copy-start(bf16[128,4096]{1,0:T(8,128)(2,1)} %copy-done.12) | copy-start | bytes 3145732
  399.9 170.3 %reduce-scatter.9.cloned.1.call-start = ((), (), s32[]{:S(2)}) async-start(), calls=%async_computation.17 | async-start | bytes 4718592 | tf_op jit(solution)/shard_map/reduce_scatter | solution.py:898
  400.0 67.2 %collective-permute-start.19 = (bf16[256,704]{1,0:T(8,128)(2,1)}, bf16[256,704]{1,0:T(8,128)(2,1)S(1)}, u32[]{:S(2)}, u32[]{:S(2)}) collective-permute-start(bf16[256,704]{1,0:T(8,128)(2,1)} %convolution_convert_fusion.12), channel_id=1, source_target_pairs={{8,0},{24,8},{16,24},{0,16},{9,1},{25,9},{17,25},{1,17},{10,2},{26... | collective-permute-start | bytes 1081352 | tf_op jit(solution)/shard_map/ppermute | solution.py:158
  401.6 67.1 %collective-permute-start.18 = (bf16[256,704]{1,0:T(8,128)(2,1)}, bf16[256,704]{1,0:T(8,128)(2,1)S(1)}, u32[]{:S(2)}, u32[]{:S(2)}) collective-permute-start(bf16[256,704]{1,0:T(8,128)(2,1)} %convolution_convert_fusion.13), channel_id=1, source_target_pairs={{0,8},{8,24},{24,16},{16,0},{1,9},{9,25},{25,17},{17,1},{2,10},{10... | collective-permute-start | bytes 1081352 | tf_op jit(solution)/shard_map/ppermute | solution.py:157
  402.1 98.1 %collective-permute-start.23 = (bf16[256,704]{1,0:T(8,128)(2,1)}, bf16[256,704]{1,0:T(8,128)(2,1)}, u32[]{:S(2)}, u32[]{:S(2)}) collective-permute-start(bf16[256,704]{1,0:T(8,128)(2,1)} %convolution_convert_fusion.10), channel_id=1, source_target_pairs={{8,0},{24,8},{16,24},{0,16},{9,1},{25,9},{17,25},{1,17},{10,2},{26... | collective-permute-start | bytes 1081352 | tf_op jit(solution)/shard_map/ppermute | solution.py:160
  403.6 97.2 %collective-permute-start.22 = (bf16[256,704]{1,0:T(8,128)(2,1)}, bf16[256,704]{1,0:T(8,128)(2,1)}, u32[]{:S(2)}, u32[]{:S(2)}) collective-permute-start(bf16[256,704]{1,0:T(8,128)(2,1)} %convolution_convert_fusion.11), channel_id=1, source_target_pairs={{0,8},{8,24},{24,16},{16,0},{1,9},{9,25},{25,17},{17,1},{2,10},{10... | collective-permute-start | bytes 1081352 | tf_op jit(solution)/shard_map/ppermute | solution.py:159
  416.4 70.3 %collective-permute-start.17 = (bf16[256,1408]{1,0:T(8,128)(2,1)}, bf16[256,1408]{1,0:T(8,128)(2,1)}, u32[]{:S(2)}, u32[]{:S(2)}) collective-permute-start(bf16[256,1408]{1,0:T(8,128)(2,1)} %add_convert_fusion.2), channel_id=1, source_target_pairs={{8,0},{24,8},{16,24},{0,16},{9,1},{25,9},{17,25},{1,17},{10,2},{26... | collective-permute-start | bytes 2162696 | tf_op jit(solution)/shard_map/ppermute | solution.py:173
  467.2 25.4 %collective-permute-start.16 = (bf16[256,1408]{1,0:T(8,128)(2,1)}, bf16[256,1408]{1,0:T(8,128)(2,1)}, u32[]{:S(2)}, u32[]{:S(2)}) collective-permute-start(bf16[256,1408]{1,0:T(8,128)(2,1)} %add_convert_fusion.3), channel_id=1, source_target_pairs={{0,8},{8,24},{24,16},{16,0},{1,9},{9,25},{25,17},{17,1},{2,10},{10... | collective-permute-start | bytes 2162696 | tf_op jit(solution)/shard_map/ppermute | solution.py:172
  471.9 21.3 %collective-permute-start.21 = (bf16[256,704]{1,0:T(8,128)(2,1)}, bf16[256,704]{1,0:T(8,128)(2,1)}, u32[]{:S(2)}, u32[]{:S(2)}) collective-permute-start(bf16[256,704]{1,0:T(8,128)(2,1)} %fusion.37), channel_id=1, source_target_pairs={{8,0},{24,8},{16,24},{0,16},{9,1},{25,9},{17,25},{1,17},{10,2},{26... | collective-permute-start | bytes 1081352 | tf_op jit(solution)/shard_map/ppermute | solution.py:173
  486.7 12.0 %collective-permute-start.20 = (bf16[256,704]{1,0:T(8,128)(2,1)S(1)}, bf16[256,704]{1,0:T(8,128)(2,1)S(1)}, u32[]{:S(2)}, u32[]{:S(2)}) collective-permute-start(bf16[256,704]{1,0:T(8,128)(2,1)S(1)} %copy-done.44), channel_id=1, source_target_pairs={{0,8},{8,24},{24,16},{16,0},{1,9},{9,25},{25,17},{17,1},{2,10},{10... | collective-permute-start | bytes 1081352 | tf_op jit(solution)/shard_map/ppermute | solution.py:172
  492.6 21.7 %collective-permute-start.31 = (bf16[256,512]{1,0:T(8,128)(2,1)}, bf16[256,512]{1,0:T(8,128)(2,1)}, u32[]{:S(2)}, u32[]{:S(2)}) collective-permute-start(bf16[256,512]{1,0:T(8,128)(2,1)} %convolution_convert_fusion.14), channel_id=1, source_target_pairs={{8,0},{24,8},{16,24},{0,16},{9,1},{25,9},{17,25},{1,17},{10,2},{26... | collective-permute-start | bytes 786440 | tf_op jit(solution)/shard_map/ppermute | solution.py:160
  493.2 21.8 %collective-permute-start.30 = (bf16[256,512]{1,0:T(8,128)(2,1)}, bf16[256,512]{1,0:T(8,128)(2,1)}, u32[]{:S(2)}, u32[]{:S(2)}) collective-permute-start(bf16[256,512]{1,0:T(8,128)(2,1)} %convolution_convert_fusion.15), channel_id=1, source_target_pairs={{0,8},{8,24},{24,16},{16,0},{1,9},{9,25},{25,17},{17,1},{2,10},{10... | collective-permute-start | bytes 786440 | tf_op jit(solution)/shard_map/ppermute | solution.py:159
  498.7 17.7 %collective-permute-start.29 = (bf16[256,512]{1,0:T(8,128)(2,1)}, bf16[256,512]{1,0:T(8,128)(2,1)}, u32[]{:S(2)}, u32[]{:S(2)}) collective-permute-start(bf16[256,512]{1,0:T(8,128)(2,1)} %convolution_convert_fusion.16), channel_id=1, source_target_pairs={{8,0},{24,8},{16,24},{0,16},{9,1},{25,9},{17,25},{1,17},{10,2},{26... | collective-permute-start | bytes 786440 | tf_op jit(solution)/shard_map/ppermute | solution.py:158
  500.2 62.8 %collective-permute-start.28 = (bf16[256,512]{1,0:T(8,128)(2,1)}, bf16[256,512]{1,0:T(8,128)(2,1)}, u32[]{:S(2)}, u32[]{:S(2)}) collective-permute-start(bf16[256,512]{1,0:T(8,128)(2,1)} %convolution_convert_fusion.17), channel_id=1, source_target_pairs={{0,8},{8,24},{24,16},{16,0},{1,9},{9,25},{25,17},{17,1},{2,10},{10... | collective-permute-start | bytes 786440 | tf_op jit(solution)/shard_map/ppermute | solution.py:157
  500.8 62.2 %collective-permute-start.27 = (bf16[256,512]{1,0:T(8,128)(2,1)}, bf16[256,512]{1,0:T(8,128)(2,1)}, u32[]{:S(2)}, u32[]{:S(2)}) collective-permute-start(bf16[256,512]{1,0:T(8,128)(2,1)} %convolution_convert_fusion.18), channel_id=1, source_target_pairs={{8,0},{24,8},{16,24},{0,16},{9,1},{25,9},{17,25},{1,17},{10,2},{26... | collective-permute-start | bytes 786440 | tf_op jit(solution)/shard_map/ppermute | solution.py:160
  510.7 59.6 %all-to-all-start.3 = ((bf16[8,64,2112]{2,1,0:T(8,128)(2,1)}), bf16[8,64,2112]{2,1,0:T(8,128)(2,1)S(1)}, u32[]{:S(2)}, u32[]{:S(2)}) async-start(bf16[8,64,2112]{2,1,0:T(8,128)(2,1)} %bitcast.124), calls=%async_computation.6 | async-start | bytes 4456448 | tf_op jit(solution)/shard_map/all_to_all | solution.py:193
  514.3 208.9 %reduce-scatter.11.cloned.1.call-start = ((), (), s32[]{:S(2)}) async-start(), calls=%async_computation.18 | async-start | bytes 4718592 | tf_op jit(solution)/shard_map/reduce_scatter | solution.py:937
  514.4 48.6 %collective-permute-start.26 = (bf16[256,512]{1,0:T(8,128)(2,1)}, bf16[256,512]{1,0:T(8,128)(2,1)S(1)}, u32[]{:S(2)}, u32[]{:S(2)}) collective-permute-start(bf16[256,512]{1,0:T(8,128)(2,1)} %convolution_convert_fusion.19), channel_id=1, source_target_pairs={{0,8},{8,24},{24,16},{16,0},{1,9},{9,25},{25,17},{17,1},{2,10},{10... | collective-permute-start | bytes 786440 | tf_op jit(solution)/shard_map/ppermute | solution.py:159
  515.0 48.1 %collective-permute-start.25 = (bf16[256,512]{1,0:T(8,128)(2,1)}, bf16[256,512]{1,0:T(8,128)(2,1)S(1)}, u32[]{:S(2)}, u32[]{:S(2)}) collective-permute-start(bf16[256,512]{1,0:T(8,128)(2,1)} %convolution_convert_fusion.20), channel_id=1, source_target_pairs={{8,0},{24,8},{16,24},{0,16},{9,1},{25,9},{17,25},{1,17},{10,2},{26... | collective-permute-start | bytes 786440 | tf_op jit(solution)/shard_map/ppermute | solution.py:158
  516.4 48.0 %collective-permute-start.24 = (bf16[256,512]{1,0:T(8,128)(2,1)}, bf16[256,512]{1,0:T(8,128)(2,1)}, u32[]{:S(2)}, u32[]{:S(2)}) collective-permute-start(bf16[256,512]{1,0:T(8,128)(2,1)} %convolution_convert_fusion.21), channel_id=1, source_target_pairs={{0,8},{8,24},{24,16},{16,0},{1,9},{9,25},{25,17},{17,1},{2,10},{10... | collective-permute-start | bytes 786440 | tf_op jit(solution)/shard_map/ppermute | solution.py:157
  575.7 29.7 %collective-permute-start.42 = (f32[8,1024]{1,0:T(8,128)}, f32[8,1024]{1,0:T(8,128)S(1)}, u32[]{:S(2)}, u32[]{:S(2)}) collective-permute-start(f32[8,1024]{1,0:T(8,128)} %get-tuple-element.151), channel_id=1, source_target_pairs={{0,8},{8,0},{16,24},{24,16},{1,9},{9,1},{17,25},{25,17},{2,10},{10... | collective-permute-start | bytes 98312 | tf_op jit(solution)/shard_map/ppermute | solution.py:208
  590.0 25.6 %collective-permute-start.41 = (bf16[256,512]{1,0:T(8,128)(2,1)S(1)}, bf16[256,512]{1,0:T(8,128)(2,1)S(1)}, u32[]{:S(2)}, u32[]{:S(2)}) collective-permute-start(bf16[256,512]{1,0:T(8,128)(2,1)S(1)} %fusion.60), channel_id=1, source_target_pairs={{8,0},{24,8},{16,24},{0,16},{9,1},{25,9},{17,25},{1,17},{10,2},{26... | collective-permute-start | bytes 786440 | tf_op jit(solution)/shard_map/ppermute | solution.py:173
  593.5 23.1 %collective-permute-start.40 = (bf16[256,512]{1,0:T(8,128)(2,1)S(1)}, bf16[256,512]{1,0:T(8,128)(2,1)S(1)}, u32[]{:S(2)}, u32[]{:S(2)}) collective-permute-start(bf16[256,512]{1,0:T(8,128)(2,1)S(1)} %fusion.68), channel_id=1, source_target_pairs={{0,8},{8,24},{24,16},{16,0},{1,9},{9,25},{25,17},{17,1},{2,10},{10... | collective-permute-start | bytes 786440 | tf_op jit(solution)/shard_map/ppermute | solution.py:172
  596.8 41.6 %collective-permute-start.35 = (bf16[256,1152]{1,0:T(8,128)(2,1)}, bf16[256,1152]{1,0:T(8,128)(2,1)}, u32[]{:S(2)}, u32[]{:S(2)}) collective-permute-start(bf16[256,1152]{1,0:T(8,128)(2,1)} %convolution_convert_fusion.2), channel_id=1, source_target_pairs={{8,0},{24,8},{16,24},{0,16},{9,1},{25,9},{17,25},{1,17},{10,2},{26... | collective-permute-start | bytes 1769480 | tf_op jit(solution)/shard_map/ppermute | solution.py:158
  600.3 38.2 %collective-permute-start.34 = (bf16[256,1152]{1,0:T(8,128)(2,1)}, bf16[256,1152]{1,0:T(8,128)(2,1)}, u32[]{:S(2)}, u32[]{:S(2)}) collective-permute-start(bf16[256,1152]{1,0:T(8,128)(2,1)} %convolution_convert_fusion.3), channel_id=1, source_target_pairs={{0,8},{8,24},{24,16},{16,0},{1,9},{9,25},{25,17},{17,1},{2,10},{10... | collective-permute-start | bytes 1769480 | tf_op jit(solution)/shard_map/ppermute | solution.py:157
  605.4 10.2 %collective-permute-start.43 = (f32[8,1024]{1,0:T(8,128)S(1)}, f32[8,1024]{1,0:T(8,128)S(1)}, u32[]{:S(2)}, u32[]{:S(2)}) collective-permute-start(f32[8,1024]{1,0:T(8,128)S(1)} %add.230), channel_id=1, source_target_pairs={{0,16},{8,24},{16,0},{24,8},{1,17},{9,25},{17,1},{25,9},{2,18},{10... | collective-permute-start | bytes 98312 | tf_op jit(solution)/shard_map/ppermute | solution.py:208
  615.5 40.0 %collective-permute-start.33 = (bf16[256,1152]{1,0:T(8,128)(2,1)}, bf16[256,1152]{1,0:T(8,128)(2,1)}, u32[]{:S(2)}, u32[]{:S(2)}) collective-permute-start(bf16[256,1152]{1,0:T(8,128)(2,1)} %convolution_convert_fusion.4), channel_id=1, source_target_pairs={{8,0},{24,8},{16,24},{0,16},{9,1},{25,9},{17,25},{1,17},{10,2},{26... | collective-permute-start | bytes 1769480 | tf_op jit(solution)/shard_map/ppermute | solution.py:160
  615.6 19.5 %collective-permute-start.39 = (bf16[256,512]{1,0:T(8,128)(2,1)}, bf16[256,512]{1,0:T(8,128)(2,1)}, u32[]{:S(2)}, u32[]{:S(2)}) collective-permute-start(bf16[256,512]{1,0:T(8,128)(2,1)} %add_convert_fusion.5), channel_id=1, source_target_pairs={{8,0},{24,8},{16,24},{0,16},{9,1},{25,9},{17,25},{1,17},{10,2},{26... | collective-permute-start | bytes 786440 | tf_op jit(solution)/shard_map/ppermute | solution.py:173
  616.6 18.5 %collective-permute-start.38 = (bf16[256,512]{1,0:T(8,128)(2,1)}, bf16[256,512]{1,0:T(8,128)(2,1)}, u32[]{:S(2)}, u32[]{:S(2)}) collective-permute-start(bf16[256,512]{1,0:T(8,128)(2,1)} %add_convert_fusion.6), channel_id=1, source_target_pairs={{0,8},{8,24},{24,16},{16,0},{1,9},{9,25},{25,17},{17,1},{2,10},{10... | collective-permute-start | bytes 786440 | tf_op jit(solution)/shard_map/ppermute | solution.py:172
  620.6 25.7 %all-to-all-start.6 = ((bf16[8,64,512]{2,1,0:T(8,128)(2,1)}), bf16[8,64,512]{2,1,0:T(8,128)(2,1)}, u32[]{:S(2)}, u32[]{:S(2)}) async-start(bf16[8,64,512]{2,1,0:T(8,128)(2,1)} %bitcast.164), calls=%async_computation.10 | async-start | bytes 1048576 | tf_op jit(solution)/shard_map/all_to_all | solution.py:197
  635.0 20.5 %collective-permute-start.32 = (bf16[256,1152]{1,0:T(8,128)(2,1)}, bf16[256,1152]{1,0:T(8,128)(2,1)}, u32[]{:S(2)}, u32[]{:S(2)}) collective-permute-start(bf16[256,1152]{1,0:T(8,128)(2,1)} %convolution_convert_fusion.5), channel_id=1, source_target_pairs={{0,8},{8,24},{24,16},{16,0},{1,9},{9,25},{25,17},{17,1},{2,10},{10... | collective-permute-start | bytes 1769480 | tf_op jit(solution)/shard_map/ppermute | solution.py:159
  635.0 18.5 %collective-permute-start.44 = (f32[8,1024]{1,0:T(8,128)S(1)}, f32[8,1024]{1,0:T(8,128)S(1)}, u32[]{:S(2)}, u32[]{:S(2)}) collective-permute-start(f32[8,1024]{1,0:T(8,128)S(1)} %add.231), channel_id=1, source_target_pairs={{0,1},{1,0},{2,3},{3,2},{4,5},{5,4},{6,7},{7,6},{8,9},{9,8},{10,11... | collective-permute-start | bytes 98312 | tf_op jit(solution)/shard_map/ppermute | solution.py:214
  641.4 16.1 %collective-permute-start.37 = (bf16[256,1152]{1,0:T(8,128)(2,1)}, bf16[256,1152]{1,0:T(8,128)(2,1)}, u32[]{:S(2)}, u32[]{:S(2)}) collective-permute-start(bf16[256,1152]{1,0:T(8,128)(2,1)} %fusion.21), channel_id=1, source_target_pairs={{8,0},{24,8},{16,24},{0,16},{9,1},{25,9},{17,25},{1,17},{10,2},{26... | collective-permute-start | bytes 1769480 | tf_op jit(solution)/shard_map/ppermute | solution.py:173
  646.3 15.8 %collective-permute-start.36 = (bf16[256,1152]{1,0:T(8,128)(2,1)}, bf16[256,1152]{1,0:T(8,128)(2,1)}, u32[]{:S(2)}, u32[]{:S(2)}) collective-permute-start(bf16[256,1152]{1,0:T(8,128)(2,1)} %fusion.20), channel_id=1, source_target_pairs={{0,8},{8,24},{24,16},{16,0},{1,9},{9,25},{25,17},{17,1},{2,10},{10... | collective-permute-start | bytes 1769480 | tf_op jit(solution)/shard_map/ppermute | solution.py:172
  646.3 20.3 %all-to-all-start.5 = ((bf16[8,64,512]{2,1,0:T(8,128)(2,1)}), bf16[8,64,512]{2,1,0:T(8,128)(2,1)}, u32[]{:S(2)}, u32[]{:S(2)}) async-start(bf16[8,64,512]{2,1,0:T(8,128)(2,1)} %bitcast.163), calls=%async_computation.9 | async-start | bytes 1048576 | tf_op jit(solution)/shard_map/all_to_all | solution.py:197
  653.6 17.0 %collective-permute-start.45 = (f32[16,1024]{1,0:T(8,128)S(1)}, f32[16,1024]{1,0:T(8,128)}, u32[]{:S(2)}, u32[]{:S(2)}) collective-permute-start(f32[16,1024]{1,0:T(8,128)S(1)} %pad_maximum_fusion.3), channel_id=1, source_target_pairs={{0,2},{1,3},{2,0},{3,1},{4,6},{5,7},{6,4},{7,5},{8,10},{9,11},{10,... | collective-permute-start | bytes 196616 | tf_op jit(solution)/shard_map/ppermute | solution.py:214
  666.6 46.7 %all-to-all-start.4 = ((bf16[8,64,1152]{2,1,0:T(8,128)(2,1)}), bf16[8,64,1152]{2,1,0:T(8,128)(2,1)S(1)}, u32[]{:S(2)}, u32[]{:S(2)}) async-start(bf16[8,64,1152]{2,1,0:T(8,128)(2,1)} %bitcast.154), calls=%async_computation.8 | async-start | bytes 2359296 | tf_op jit(solution)/shard_map/all_to_all | solution.py:197
  671.5 34.0 %collective-permute-start.46 = (f32[32,1024]{1,0:T(8,128)S(1)}, f32[32,1024]{1,0:T(8,128)S(1)}, u32[]{:S(2)}, u32[]{:S(2)}) collective-permute-start(f32[32,1024]{1,0:T(8,128)S(1)} %pad_maximum_fusion.2), channel_id=1, source_target_pairs={{0,4},{1,5},{2,6},{3,7},{4,0},{5,1},{6,2},{7,3},{8,12},{9,13},{10,... | collective-permute-start | bytes 393224 | tf_op jit(solution)/shard_map/ppermute | solution.py:214
  (61 other events, 449.7 us)
Sparse Core Ops, SparseCore 0:
  53.1 52.7 all-gather.4
  120.1 87.6 all-gather.6
  221.6 48.6 reduce-scatter.4
  274.5 45.0 all-gather.8
  347.3 48.7 reduce-scatter.6
  400.1 45.2 all-gather.10
  475.1 51.9 reduce-scatter.8
  588.1 52.3 reduce-scatter.10

commit v6 on v5

--- a/solution.py
+++ b/solution.py
@@ -144,15 +144,63 @@
 
 
 class RingGrad:
-    def __init__(self, left, right):
+    def __init__(self, left, right, kernel=True):
         self.ring = lax.axis_size("dp") == 4
-        self.left, self.right = left, right
+        self.left, self.right, self.kernel = left, right, kernel
         rows = self.rows = left.shape[1] // lax.axis_size("dp")
-        self.half = rows // 2
-        self.sent, self.near, self.late = (), (), ()
+        half = self.half = rows // 2
+        self.sent, self.far, self.sums, self.near = (), (), (), ()
         if self.ring:
             to_right, to_left = ring_pairs(4)
-            self.sent = tuple(self.part(i).astype(BF) for i in (4, 5, 3, 6))
+            self.sent = self.products((2 * rows, half, ()), (2 * rows + half, half, ()))
+            self.far = (
+                lax.ppermute(self.sent[0], "dp", to_right),
+                lax.ppermute(self.sent[1], "dp", to_left),
+            )
+
+    def products(self, *spans):
+        if self.kernel:
+            return tuple(grad_rows(self.left, self.right, spans))
+        out = []
+        for at, size, arrived in spans:
+            total = tn(self.left[:, at : at + size], self.right)
+            for array, row in arrived:
+                rest = size - row - array.shape[0]
+                total = total + jnp.pad(array.astype(F32), ((row, rest), (0, 0)))
+            out.append(total.astype(BF))
+        return tuple(out)
+
+    def second(self, *earlier):
+        if self.ring:
+            to_right, to_left = ring_pairs(4)
+            far_a, far_b = lax.optimization_barrier(self.far + earlier)[:2]
+            rows, half = self.rows, self.half
+            self.sums = self.products(
+                (rows, rows, ((far_a, 0),)), (3 * rows, rows, ((far_b, half),))
+            )
+            self.near = (
+                lax.ppermute(self.sums[0], "dp", to_right),
+                lax.ppermute(self.sums[1], "dp", to_left),
+            )
+
+    def total(self, *earlier):
+        if not self.ring:
+            whole = tn(self.left, self.right).astype(BF)
+            return lax.psum_scatter(whole, "dp", scatter_dimension=0, tiled=True)
+        held = lax.optimization_barrier(self.near + earlier)
+        return self.products((0, self.rows, ((held[0], 0), (held[1], 0))))[0]
+
+
+class RingPair:
+    def __init__(self, *pairs):
+        self.ring = lax.axis_size("dp") == 4
+        self.pairs = pairs
+        rows = self.rows = pairs[0][0].shape[1] // lax.axis_size("dp")
+        self.half = rows // 2
+        self.sent, self.near, self.sums, self.late = (), (), (), ()
+        if self.ring:
+            to_right, to_left = ring_pairs(4)
+            self.sent = self.blocks((4, 5, 3, 6))
             self.near = (
                 lax.ppermute(self.sent[0], "dp", to_right),
                 lax.ppermute(self.sent[1], "dp", to_left),
@@ -160,29 +208,27 @@
                 lax.ppermute(self.sent[3], "dp", to_left),
             )
 
-    def part(self, index):
-        at = index * self.half
-        return tn(self.left[:, at : at + self.half], self.right)
+    def blocks(self, which, *extra):
+        return tuple(grad_blocks(self.half, which, self.pairs, *extra))
 
     def second(self, *earlier):
         if self.ring:
             to_right, to_left = ring_pairs(4)
-            far_a, far_b = lax.optimization_barrier(self.near[:2] + earlier)[:2]
+            held = lax.optimization_barrier(self.near + earlier)
+            far, self.near = held[:2], held[:4]
+            self.sums = self.blocks((2, 7), far)
             self.late = (
-                lax.ppermute((self.part(2) + far_a.astype(F32)).astype(BF), "dp", to_right),
-                lax.ppermute((self.part(7) + far_b.astype(F32)).astype(BF), "dp", to_left),
+                lax.ppermute(self.sums[0], "dp", to_right),
+                lax.ppermute(self.sums[1], "dp", to_left),
             )
 
     def total(self, *earlier):
         if not self.ring:
-            whole = tn(self.left, self.right).astype(BF)
+            whole = jnp.concatenate([tn(a, b).astype(BF) for a, b in self.pairs], axis=1)
             return lax.psum_scatter(whole, "dp", scatter_dimension=0, tiled=True)
         held = lax.optimization_barrier(self.near[2:] + self.late + earlier)
         right_b, left_a, right_a, left_b = held[:4]
-        own = tn(self.left[:, : self.rows], self.right)
-        from_left = jnp.concatenate([right_a, right_b]).astype(F32)
-        from_right = jnp.concatenate([left_a, left_b]).astype(F32)
-        return (own + from_left + from_right).astype(BF)
+        return jnp.concatenate(self.blocks((0, 1), (right_a, right_b), (left_a, left_b)))
 
 
 def rank_major(packed):
@@ -592,11 +638,102 @@
         out_ref[...] = jnp.concatenate(pieces, axis=1)
 
 
+def grad_kernel(spans, left_ref, right_ref, *refs):
+    adds, outs = refs[: -len(spans)], refs[-len(spans) :]
+    taken = 0
+    for (at, size, places), out_ref in zip(spans, outs):
+        for row in range(0, size, 256):
+            high = min(256, size - row)
+            piece = dot_f32(left_ref[:, at + row : at + row + high], right_ref[...], TN)
+            for k, (first, rows) in enumerate(places):
+                if first <= row < first + rows:
+                    piece = piece + adds[taken + k][row - first : row - first + high, :].astype(F32)
+            out_ref[row : row + high, :] = piece.astype(BF)
+        taken += len(places)
+
+
+def block_kernel(half, blocks, pairs, extra, *refs):
+    lefts, rights = refs[:pairs], refs[pairs : 2 * pairs]
+    adds, outs = refs[2 * pairs : -len(blocks)], refs[-len(blocks) :]
+    for i, block in enumerate(blocks):
+        lane = 0
+        for left_ref, right_ref in zip(lefts, rights):
+            wide = right_ref.shape[1]
+            at = slice(lane, lane + wide)
+            piece = dot_f32(left_ref[:, block * half : (block + 1) * half], right_ref[...], TN)
+            for k in range(extra):
+                piece = piece + adds[k * len(blocks) + i][:, at].astype(F32)
+            outs[i][:, at] = piece.astype(BF)
+            lane += wide
+
+
 VMEM_LIMIT = 60 * 2**20
 
 
 def shape_of(*dims, dtype=F32):
     return jax.ShapeDtypeStruct(dims, dtype)
+
+
+def grad_rows(left, right, spans):
+    wide = right.shape[1]
+    rows = sum(size for _, size, _ in spans)
+    fixed = tuple(
+        (at, size, tuple((row, x.shape[0]) for x, row in arrived)) for at, size, arrived in spans
+    )
+    return pl.pallas_call(
+        functools.partial(grad_kernel, fixed),
+        out_shape=tuple(shape_of(size, wide, dtype=BF) for _, size, _ in spans),
+        compiler_params=pltpu.CompilerParams(vmem_limit_bytes=VMEM_LIMIT),
+        cost_estimate=pl.CostEstimate(
+            flops=2 * rows * wide * left.shape[0],
+            transcendentals=0,
+            bytes_accessed=2 * (left.size + right.size + rows * wide),
+        ),
+        name="grad_rows",
+    )(left, right, *(x for _, _, arrived in spans for x, _ in arrived))
+
+
+def grad_blocks(half, blocks, pairs, *extra):
+    wide = sum(b.shape[1] for _, b in pairs)
+    arrays = [a for a, _ in pairs] + [b for _, b in pairs] + [x for xs in extra for x in xs]
+    return pl.pallas_call(
+        functools.partial(block_kernel, half, blocks, len(pairs), len(extra)),
+        out_shape=(shape_of(half, wide, dtype=BF),) * len(blocks),
+        compiler_params=pltpu.CompilerParams(vmem_limit_bytes=VMEM_LIMIT),
+        cost_estimate=pl.CostEstimate(
+            flops=half * len(blocks) * wide * pairs[0][0].shape[0] // 8,
+            transcendentals=0,
+            bytes_accessed=half * len(blocks) * wide,
+        ),
+        name="grad_blocks",
+    )(*arrays)
+
+
+def back_kernel(pairs, *refs):
+    total = dot_f32(refs[0][...], refs[pairs][...], NT)
+    for i in range(1, pairs):
+        total = total + dot_f32(refs[i][...], refs[pairs + i][...], NT)
+    refs[-1][...] = total.astype(BF)
+
+
+def back_product(*pairs):
+    total, wide = pairs[0][0].shape[0], pairs[0][1].shape[0]
+    rows = 256
+    lefts = [a for a, _ in pairs]
+    rights = [b for _, b in pairs]
+    return pl.pallas_call(
+        functools.partial(back_kernel, len(pairs)),
+        grid=(total // rows,),
+        in_specs=[pl.BlockSpec((rows, a.shape[1]), lambda i: (i, 0)) for a in lefts]
+        + [pl.BlockSpec(b.shape, lambda i: (0, 0)) for b in rights],
+        out_specs=pl.BlockSpec((rows, wide), lambda i: (i, 0)),
+        out_shape=shape_of(total, wide, dtype=BF),
+        compiler_params=pltpu.CompilerParams(vmem_limit_bytes=VMEM_LIMIT),
+        cost_estimate=pl.CostEstimate(
+            flops=total * wide * 256, transcendentals=0, bytes_accessed=total * wide
+        ),
+        name="back_product",
+    )(*lefts, *rights)
 
 
 def pack_even(ranks, *arrays):
@@ -670,7 +807,7 @@
         ],
         compiler_params=pltpu.CompilerParams(vmem_limit_bytes=VMEM_LIMIT),
         cost_estimate=pl.CostEstimate(
-            flops=total * hp * 34_000_000,
+            flops=total * hp * 5_000_000,
             transcendentals=total * hp * CHUNK,
             bytes_accessed=total * wide * 20,
         ),
@@ -889,13 +1026,19 @@
     d_output = own_cot.astype(F32)
     e2 = d_mlp * mlp_gain_full
     d_middle = d_output + r2 * (e2 - n2 * jnp.mean(e2 * n2, axis=-1, keepdims=True))
-    both_sum = RingGrad(mlp_all, d_both)
-    down_sum = RingGrad(cot_all, product)
-    d_branch_own = after(d_middle.astype(BF), *both_sum.near, *down_sum.sent)
-    both_sum.second(d_branch_own)
+    down_sum = RingGrad(cot_all, product, kernel=False)
+    both_sum = RingGrad(mlp_all, d_both, kernel=False)
+    mlp_part = nt(product, down_w).astype(BF)
+    down_sum.second(mlp_part)
+    both_sum.second(mlp_part)
+    d_branch_own = after(d_middle.astype(BF), *both_sum.sums, *down_sum.sums)
     d_branch_all = lax.all_gather(d_branch_own, "seq", axis=0, tiled=True)
-    mlp_part = after(nt(product, down_w).astype(BF), d_branch_all)
-    mlp_out = lax.psum_scatter(mlp_part, "seq", scatter_dimension=0, tiled=True)
+    mlp_mine = jnp.concatenate([both_sum.total(d_branch_own), down_sum.total(d_branch_own)], axis=1)
+    mlp_rows = exchange(mlp_mine)
+    d_branch_all = after(d_branch_all, mlp_mine)
+    mlp_out = lax.psum_scatter(
+        after(mlp_part, d_branch_all), "seq", scatter_dimension=0, tiled=True
+    )
 
     d_gated = nn(d_branch_all, out_cols)
     if vs == 1:
@@ -905,38 +1048,33 @@
     else:
         d_mixed, d_gate, gain_part = gate_apply_back(d_gated, mixed, pre_gate, own_gain)
         gain_part = jnp.pad(gain_part[None], ((0, 7), (0, 0)))
-    gate_sum = RingGrad(attn, d_gate)
-    out_sum = RingGrad(d_branch_all, gated)
-    d_attn_gate = nt(d_gate, gate_cols)
-    down_sum.second(d_branch_all)
-    d_mixed = after(
-        d_mixed,
-        *both_sum.late,
-        *down_sum.late,
-        *gate_sum.sent,
-        *out_sum.sent,
-        mlp_part,
-        d_attn_gate,
-    )
-    mlp_rows = exchange(
-        jnp.concatenate([both_sum.total(d_mixed), down_sum.total(d_mixed)], axis=1)
-    )
+    side_sum = RingPair((attn, d_gate), (d_branch_all, gated))
+    d_mixed = after(d_mixed, *side_sum.sent)
     d_pre, d_sums = delta_backward(
         pre, pre_small, rider_all, taps, const, saved, d_mixed, gain_part, hp, dk, dv
     )
-    d_pre, d_sums, mlp_out, mlp_rows = lax.optimization_barrier(
-        (d_pre, d_sums, mlp_out, mlp_rows) + gate_sum.near + out_sum.near
-    )[:4]
-    mix_sum = RingGrad(attn, d_pre)
-    gate_sum.second(d_pre)
-    out_sum.second(d_pre)
-    gate_rows = to_rows(gate_sum.total(), ranks)
-    out_rows = to_rows(out_sum.total(), ranks)
+    held = lax.optimization_barrier((d_pre, d_sums, mlp_rows) + side_sum.near)
+    d_pre, d_sums, mlp_rows = held[:3]
+    side_sum.near = held[3:]
+    d_attn_part = back_product((d_pre, w_mix), (d_gate, gate_cols))
+    d_attn = lax.psum_scatter(d_attn_part, "seq", scatter_dimension=0, tiled=True).astype(F32)
+    side_sum.second(d_attn_part)
+    mix_sum = RingGrad(attn, after(d_pre, d_attn_part))
+    every = sum_everywhere(after(d_sums, d_attn_part))
+    mlp_out, every, *held = lax.optimization_barrier(
+        (mlp_out, every) + side_sum.late + mix_sum.far
+    )
+    count = len(side_sum.late)
+    side_sum.late, mix_sum.far = tuple(held[:count]), tuple(held[count:])
     mix_sum.second()
+    side_mine = side_sum.total(*mix_sum.sums)
+    side_rows = to_rows(side_mine, ranks)
+    every = every.reshape(ranks, 8, -1)
+    held = lax.optimization_barrier((mlp_rows, mlp_out, side_rows) + mix_sum.near)
+    mlp_rows, mlp_out, side_rows = held[:3]
+    mix_sum.near = held[3:]
     mix_rows = to_rows(mix_sum.total(), ranks)
-    d_attn = lax.psum_scatter(
-        (d_attn_gate + nt(d_pre, w_mix)).astype(BF), "seq", scatter_dimension=0, tiled=True
-    ).astype(F32)
+    grad_hidden, grad_up, grad_down = unpack_even(ranks, mlp_rows, 3)
 
     output = from_ring((middle + mlp_out.astype(F32)).astype(BF))
     n = inputs * rms_scale(inputs)
@@ -944,8 +1082,6 @@
     grad_tokens = from_ring(
         (d_middle + rms_scale(inputs) * (e - n * jnp.mean(e * n, axis=-1, keepdims=True))).astype(BF)
     )
-
-    every = sum_everywhere(d_sums).reshape(ranks, 8, -1)
 
     def per_head(part, lead):
         part = part.reshape(ranks // vs, vs, lead, -1).sum(axis=1)
@@ -959,8 +1095,7 @@
     grad_value = plan.join_even(mix_rows[:, :, at_v:at_s])
     grad_decay = plan.join_keys(mix_rows[:, :, at_s : at_s + hp])
     grad_beta = plan.join_keys(mix_rows[:, :, at_s + hp : at_s + 2 * hp])
-    grad_gate = plan.join_even(gate_rows)
-    grad_hidden, grad_up, grad_down = unpack_even(ranks, mlp_rows, 3)
+    grad_gate = plan.join_even(side_rows[:, :, : hp * dv])
 
     def gain_grad(gain, pairs):
         total = sum(jnp.sum(w.astype(F32) * g, axis=1) for w, g in pairs)
@@ -986,7 +1121,7 @@
         grad_decay,
         grad_beta,
         grad_gate,
-        plan.join_even(out_rows),
+        plan.join_even(side_rows[:, :, hp * dv :]),
         per_head(every_taps[:, :, :at_k], KERNEL),
         per_head(every_taps[:, :, at_k:at_v], KERNEL),
         grad_conv_value,

time: 747 us -> 709 us (0.949)
  matrix products: 169 us -> 91.6 us
  Pallas kernels: 92.8 us -> 146 us
  starting transfers between devices: 83.5 us -> 64.6 us
  waiting for transfers between devices: 253 us -> 263 us
    dot_general x46 -> x19, matrix products: 169 us -> 91.6 us  [dot_f32(): lax.dot_general(left, right, (dims, ((), ())), preferred_element_type=F32)]
    pallas_call x0 -> x7, Pallas kernels: none -> 52.8 us  [the longest x3 20.4 us: grad_blocks(): pl.pallas_call(functools.partial(block_kernel, half, blocks, len(pairs),...]
    ppermute x10 -> x8, waiting for transfers between devices: 20.9 us -> 62 us  [the longest x4 60.5 us: second(): lax.ppermute(self.sums[0], 'dp', to_right)]
    all_gather x1, waiting for transfers between devices: 24.1 us -> 0.01 us  [local(): d_branch_all = lax.all_gather(d_branch_own, 'seq', axis=0, tiled=True)]
    reduce_scatter x1, waiting for transfers between devices: 22.6 us -> 0.01 us  [local(): lax.psum_scatter(nt(d_both, both_w).astype(BF), 'seq', scatter_dimension=...]
    ppermute x3, waiting for transfers between devices: 30.6 us -> 13.5 us  [sum_everywhere(): other = lax.ppermute(held, 'seq', [(i, i ^ step) for i in range(ranks)])]
    all_to_all x3 -> x2, waiting for transfers between devices: 0.01 us -> 13.2 us  [to_rows(): turned = lax.all_to_all(mine, 'seq', 0, 0, tiled=True)]
    ppermute x5 -> x4, waiting for transfers between devices: 0.01 us -> 9.74 us  [__init__(): lax.ppermute(self.sent[0], 'dp', to_right)]
  transfers between devices with their start and end apart: 62 -> 49, of which waited for: 22 -> 26; matrix products, arithmetic and copies ran while one was open for 32% -> 22% of each run, Pallas kernels for 12% -> 20%
where the time goes in v6:
time: 709 us; the launch traced here: 700 us
  waiting for transfers between devices  263 us (37%)
  Pallas kernels  146 us (21%)
  matrix products  91.6 us (13%)
  local copies, waits for them, and re-layouts  83.8 us (12%)
  starting transfers between devices  64.6 us (9%)
  other arithmetic  35.9 us (5%)
  between operations  15.7 us (2%)
    dot_general x19, matrix products, dot_f32(): lax.dot_general(left, right, (dims, ((), ())), preferred_element_type=F32)  91.6 us
    ppermute x4, waiting for transfers between devices, second(): lax.ppermute(self.sums[0], 'dp', to_right)  60.5 us
    all_to_all x4, waiting for transfers between devices, exchange(): return lax.all_to_all(packed, 'seq', 0, 0, tiled=True)  55.8 us
    pallas_call x1, Pallas kernels, delta_backward(): pl.pallas_call(functools.partial(bwd_kernel, hp, dk, dv), out_shape=(shap...  46.1 us
    reduce_scatter x1, waiting for transfers between devices, local(): lax.psum_scatter(nt(gated, out_cols).astype(BF), 'seq', scatter_dimension...  44.4 us
    unnamed x150, local copies, waits for them, and re-layouts  30.5 us
    pallas_call x1, Pallas kernels, delta_forward(): pl.pallas_call(functools.partial(fwd_kernel, hp, dk, dv), out_shape=(shap...  29.5 us
    pallas_call x3, Pallas kernels, grad_blocks(): pl.pallas_call(functools.partial(block_kernel, half, blocks, len(pairs),...  20.4 us
  transfers between devices with their start and end apart: 49, of which 26 were waited for; matrix products, arithmetic and copies ran while one was open for 22% of the time, Pallas kernels for 20%

profile of v6, /device:TPU:0, one launch (start us, length us, event | category | flops | bytes accessed | tf_op | source)
XLA Modules:
  0.0 700.1 jit_solution(5596416878004842276)
XLA Ops:
  13.6 2.6 concatenate.64
  16.2 6.3 all-to-all-start
  24.7 3.3 pack_even.1
  29.3 22.6 %all-to-all-done = bf16[8,64,1152]{2,1,0:T(8,128)(2,1)S(1)} async-done(((bf16[8,64,1152]{2,1,0:T(8,128)(2,1)}), bf16[8,64,1152]{2,1,0:T(8,128)(2,1)S(1)}, u32[]{:S(2)}, u32[]{:S(2)}) %all-to-all-start) | async-done | bytes 1179680 | tf_op jit(solution)/shard_map/all_to_all | solution.py:239
  59.7 19.8 %collective-permute-done.1 = bf16[512,1152]{1,0:T(8,128)(2,1)S(1)} collective-permute-done((bf16[512,1152]{1,0:T(8,128)(2,1)S(1)}, bf16[512,1152]{1,0:T(8,128)(2,1)S(1)}, u32[]{:S(2)}, u32[]{:S(2)}) %collective-permute-start.1) | collective-permute-done | bytes 1179680 | tf_op jit(solution)/shard_map/ppermute | solution.py:132
  86.2 4.2 all-to-all-start.1
  90.5 2.4 constant_dynamic-update-slice_fusion.3
  104.9 3.2 fusion
  108.2 2.9 fusion.2.refs_0_.left_ref
  113.1 5.8 fusion.16.pre_ref
  123.7 4.3 fusion.50.small_ref
  128.0 5.3 all-to-all-start.2
  135.2 29.5 %delta_forward.1 = (f32[1024,512]{1,0:T(8,128)}, f32[16,128,256]{2,1,0:T(8,128)}, f32[1024,512]{1,0:T(8,128)}, f32[16,128,128]{2,1,0:T(8,128)}, f32[1024,256]{1,0:T(8,128)}) custom-call(bf16[1024,1024]{1,0:T(8,128)(2,1)} %fusion.16.pre_ref, f32[1024,128]{1,0:T(8,128)} %fusion.50.small_ref, bf16[1024,128]{1,0:T(8,128)(2,1)} %slice.225.rider_ref, ...), custom_call_target="tpu_custom_call" | custom-call | flops 43008000000 | bytes 16777216 | tf_op jit(solution)/shard_map/delta_forward/pallas_call | solution.py:764
  171.8 8.6 %collective-permute-done.6 = bf16[256,1024]{1,0:T(8,128)(2,1)S(1)} collective-permute-done((bf16[256,1024]{1,0:T(8,128)(2,1)S(1)}, bf16[256,1024]{1,0:T(8,128)(2,1)S(1)}, u32[]{:S(2)}, u32[]{:S(2)}) %collective-permute-start.6) | collective-permute-done | bytes 524320 | tf_op jit(solution)/shard_map/ppermute | solution.py:141
  180.4 2.6 collective-permute-done.7
  184.4 3.7 fusion.59.gate_ref
  188.1 4.3 gate_forward.1.refs_3_
  192.3 21.9 %all-to-all-done.2 = bf16[8,64,2112]{2,1,0:T(8,128)(2,1)S(1)} async-done(((bf16[8,64,2112]{2,1,0:T(8,128)(2,1)}), bf16[8,64,2112]{2,1,0:T(8,128)(2,1)S(1)}, u32[]{:S(2)}, u32[]{:S(2)}) %all-to-all-start.2) | async-done | bytes 2162720 | tf_op jit(solution)/shard_map/all_to_all | solution.py:239
  214.2 6.3 convolution_convert_fusion.1
  220.6 2.4 copy.197
  225.0 44.4 %reduce-scatter.5.cloned.1.call-done = bf16[128,2048]{1,0:T(8,128)(2,1)} async-done(((bf16[1024,2048]{1,0:T(8,128)(2,1)}), bf16[128,2048]{1,0:T(8,128)(2,1)}) %reduce-scatter.5.cloned.1.call-update) | async-done | bytes 524304 | tf_op jit(solution)/shard_map/reduce_scatter | solution.py:995
  281.7 4.1 copy.199
  285.8 3.0 copy.202
  288.8 3.2 constant_dynamic-update-slice_fusion.13
  291.9 8.6 %collective-permute-done.10 = bf16[256,2112]{0,1:T(8,128)(2,1)} collective-permute-done((bf16[256,2112]{0,1:T(8,128)(2,1)}, bf16[256,2112]{0,1:T(8,128)(2,1)}, u32[]{:S(2)}, u32[]{:S(2)}) %collective-permute-start.10) | collective-permute-done | bytes 1081376 | tf_op jit(solution)/shard_map/ppermute | solution.py:141
  304.2 2.4 copy.201
  306.6 2.5 constant_dynamic-update-slice_fusion.12
  311.7 6.9 all-gather.9.cloned.1.call-done
  318.6 11.4 %fusion.5 = f32[1024,1408]{0,1:T(8,128)} fusion(bf16[1024,2048]{1,0:T(8,128)(2,1)} %all-gather.9.cloned.1.call-done, bf16[2048,2112]{1,0:T(8,128)(2,1)} %constant_dynamic-update-slice_fusion.10), kind=kOutput, calls=%fused_computation.7 | convolution fusion | flops 5905580032 | bytes 15728640 | tf_op jit(solution)/shard_map/dot_general | solution.py:22
  330.0 7.1 %multiply_convert_fusion.2 = (bf16[1024,704]{0,1:T(8,128)(2,1)S(1)}, bf16[1024,704]{0,1:T(8,128)(2,1)S(1)}, bf16[1024,704]{0,1:T(8,128)(2,1)}) fusion(f32[1024,1408]{0,1:T(8,128)} %fusion.5, bf16[1024,2048]{1,0:T(8,128)(2,1)S(1)} %copy-done.47, bf16[2048,2112]{1,0:T(8,128)(2,1)S(1)} %copy-done.30), kind=kOutput, calls=%fused_computation.20 | convolution fusion | flops 2963603456 | bytes 17432576 | tf_op jit(solution)/shard_map/dot_general | solution.py:22
  338.2 8.3 %fusion.9 = bf16[1024,2048]{1,0:T(8,128)(2,1)} fusion(bf16[2048,2112]{1,0:T(8,128)(2,1)S(1)} %copy-done.30, bf16[1024,704]{0,1:T(8,128)(2,1)S(1)} %get-tuple-element.199, bf16[1024,704]{0,1:T(8,128)(2,1)S(1)} %get-tuple-element.198), kind=kOutput, calls=%fused_computation.11 | convolution fusion | flops 5913444352 | bytes 12845056 | tf_op jit(solution)/shard_map/dot_general | solution.py:22
  346.6 3.5 convolution_convert_fusion.3
  352.0 3.0 convolution_convert_fusion.2
  362.3 7.1 %convolution_convert_fusion = bf16[1024,2048]{1,0:T(8,128)(2,1)} fusion(bf16[1024,704]{0,1:T(8,128)(2,1)S(1)} %copy-done.53, bf16[2048,2112]{1,0:T(8,128)(2,1)} %constant_dynamic-update-slice_fusion.10), kind=kOutput, calls=%fused_computation.12 | convolution fusion | flops 2954887168 | bytes 8781824 | tf_op jit(solution)/shard_map/dot_general | solution.py:22
  369.4 7.4 %collective-permute-done.14 = bf16[256,704]{0,1:T(8,128)(2,1)S(1)} collective-permute-done((bf16[256,704]{0,1:T(8,128)(2,1)}, bf16[256,704]{0,1:T(8,128)(2,1)S(1)}, u32[]{:S(2)}, u32[]{:S(2)}) %collective-permute-start.14) | collective-permute-done | bytes 360480 | tf_op jit(solution)/shard_map/ppermute | solution.py:157
  376.8 4.2 collective-permute-done.15
  381.7 3.7 fusion.22
  385.3 2.4 fusion.23
  388.6 3.0 add_convert_fusion.2
  391.7 4.2 add_convert_fusion.1
  404.0 5.8 fusion.32
  409.8 38.4 %collective-permute-done.18 = bf16[512,704]{0,1:T(8,128)(2,1)S(1)} collective-permute-done((bf16[512,704]{0,1:T(8,128)(2,1)}, bf16[512,704]{0,1:T(8,128)(2,1)S(1)}, u32[]{:S(2)}, u32[]{:S(2)}) %collective-permute-start.18) | collective-permute-done | bytes 720928 | tf_op jit(solution)/shard_map/ppermute | solution.py:182
  451.9 3.1 add_convert_fusion
  456.5 4.4 all-to-all-start.3
  460.9 3.3 slice.226.refs_3_
  464.2 5.2 fusion.19.d_ref
  469.4 5.6 gate_backward.1
  475.1 7.2 %grad_blocks.3 = (bf16[256,1024]{1,0:T(8,128)(2,1)}, bf16[256,1024]{1,0:T(8,128)(2,1)}, bf16[256,1024]{1,0:T(8,128)(2,1)}, bf16[256,1024]{1,0:T(8,128)(2,1)}) custom-call(bf16[1024,2048]{1,0:T(8,128)(2,1)} %copy-done.2, bf16[1024,2048]{1,0:T(8,128)(2,1)} %all-gather.11.cloned.1.call-done.refs_1_, bf16[1024,512]{1,0:T(8,128)(2,1)} %get-tuple-element.141.refs_2_.refs_1_, ...), custom_call_target="tpu_custom_call" | custom-call | flops 134217728 | bytes 1048576 | tf_op jit(solution)/shard_map/grad_blocks/pallas_call | solution.py:699
  486.5 46.1 %delta_backward.1 = (bf16[1024,1152]{1,0:T(8,128)(2,1)}, f32[8,1024]{1,0:T(8,128)}) custom-call(bf16[1024,1024]{1,0:T(8,128)(2,1)} %fusion.16.pre_ref, f32[1024,128]{1,0:T(8,128)} %fusion.50.small_ref, bf16[1024,128]{1,0:T(8,128)(2,1)} %slice.225.rider_ref, f32[4,1024]{1,0:T(4,128)} %pad_maximum_fusion.6.taps_ref, f32[2,128]{1,0:T(2,128)} %select_maximum_fusion.const_ref, ...), custom_call_target="tpu_custom_call" | custom-call | flops 10240000000 | bytes 20971520 | tf_op jit(solution)/shard_map/delta_backward/pallas_call | solution.py:792
  532.6 11.3 %all-to-all-done.3 = bf16[8,64,2112]{2,1,0:T(8,128)(2,1)} async-done(((bf16[8,64,2112]{2,1,0:T(8,128)(2,1)}), bf16[8,64,2112]{2,1,0:T(8,128)(2,1)}, u32[]{:S(2)}, u32[]{:S(2)}) %all-to-all-start.3) | async-done | bytes 2162720 | tf_op jit(solution)/shard_map/all_to_all | solution.py:239
  544.0 13.3 %back_product.1 = bf16[1024,2048]{1,0:T(8,128)(2,1)} custom-call(bf16[1024,1152]{1,0:T(8,128)(2,1)} %get-tuple-element.163.refs_0_.right_ref, bf16[1024,512]{1,0:T(8,128)(2,1)} %get-tuple-element.141.refs_2_.refs_1_, bf16[2048,1152]{1,0:T(8,128)(2,1)} %constant_dynamic-update-slice_fusion.refs_2_, bf16[2048,512]{1,0:T(8,128)(2,1)} %slice.226.refs_3_), custom_call_target="tpu_custom_call" | custom-call | flops 536870912 | bytes 2097152 | tf_op jit(solution)/shard_map/back_product/pallas_call | solution.py:724
  559.2 2.8 collective-permute-done.24
  562.9 3.0 collective-permute-done.25
  565.9 6.5 grad_blocks.4
  574.5 5.4 grad_rows.3
  583.7 13.5 %collective-permute-done.28 = f32[32,1024]{1,0:T(8,128)S(1)} collective-permute-done((f32[32,1024]{1,0:T(8,128)S(1)}, f32[32,1024]{1,0:T(8,128)S(1)}, u32[]{:S(2)}, u32[]{:S(2)}) %collective-permute-start.28) | collective-permute-done | bytes 131104 | tf_op jit(solution)/shard_map/ppermute | solution.py:260
  600.5 7.2 %grad_rows.4 = (bf16[512,1152]{1,0:T(8,128)(2,1)}, bf16[512,1152]{1,0:T(8,128)(2,1)}) custom-call(bf16[1024,2048]{1,0:T(8,128)(2,1)} %copy-done.2, bf16[1024,1152]{1,0:T(8,128)(2,1)} %get-tuple-element.163.refs_0_.right_ref, bf16[256,1152]{1,0:T(8,128)(2,1)} %collective-permute-done.31.refs_0_, bf16[256,1152]{1,0:T(8,128)(2,1)} %collective-permute-done.32.refs_1_), custom_call_target="tpu_custom_call" | custom-call | flops 2415919104 | bytes 8912896 | tf_op jit(solution)/shard_map/grad_rows/pallas_call | solution.py:683
  607.7 6.7 grad_blocks.5
  616.7 3.6 all-to-all-start.4
  626.8 22.1 %collective-permute-done.33.refs_0_ = bf16[512,1152]{1,0:T(8,128)(2,1)} collective-permute-done((bf16[512,1152]{1,0:T(8,128)(2,1)}, bf16[512,1152]{1,0:T(8,128)(2,1)}, u32[]{:S(2)}, u32[]{:S(2)}) %collective-permute-start.33) | collective-permute-done | bytes 1179680 | tf_op jit(solution)/shard_map/ppermute | solution.py:182
  649.2 6.5 grad_rows.5
  655.8 4.8 all-to-all-start.5
  666.7 4.1 unpack_even.1
  676.7 13.2 %all-to-all-done.5 = bf16[8,64,1152]{2,1,0:T(8,128)(2,1)S(1)} async-done(((bf16[8,64,1152]{2,1,0:T(8,128)(2,1)}), bf16[8,64,1152]{2,1,0:T(8,128)(2,1)S(1)}, u32[]{:S(2)}, u32[]{:S(2)}) %all-to-all-start.5) | async-done | bytes 1179680 | tf_op jit(solution)/shard_map/all_to_all | solution.py:243
  (324 shorter events, 139.5 us)
Async XLA Ops:
  7.2 113.8 %copy-start = (f32[4,4096]{1,0:T(4,128)S(1)}, f32[4,4096]{1,0:T(4,128)}, u32[]{:S(2)}) copy-start(f32[4,4096]{1,0:T(4,128)} %param.32) | copy-start | bytes 196612
  11.1 11.4 %copy-start.46 = (s32[1,128]{1,0:T(1,128)S(1)}, s32[1,128]{1,0:T(1,128)}, u32[]{:S(2)}) copy-start(s32[1,128]{1,0:T(1,128)} %param.40) | copy-start | bytes 1540
  16.2 35.7 %all-to-all-start = ((bf16[8,64,1152]{2,1,0:T(8,128)(2,1)}), bf16[8,64,1152]{2,1,0:T(8,128)(2,1)S(1)}, u32[]{:S(2)}, u32[]{:S(2)}) async-start(bf16[8,64,1152]{2,1,0:T(8,128)(2,1)} %bitcast.6), calls=%async_computation | async-start | bytes 2359296 | tf_op jit(solution)/shard_map/all_to_all | solution.py:239
  22.5 82.4 %all-gather.5.cloned.1.call-start = ((), (), s32[]{:S(2)}) async-start(), calls=%async_computation.10 | async-start | bytes 5013504 | tf_op jit(solution)/shard_map/all_gather | solution.py:925
  51.9 27.6 %collective-permute-start.1 = (bf16[512,1152]{1,0:T(8,128)(2,1)S(1)}, bf16[512,1152]{1,0:T(8,128)(2,1)S(1)}, u32[]{:S(2)}, u32[]{:S(2)}) collective-permute-start(bf16[512,1152]{1,0:T(8,128)(2,1)S(1)} %bitcast.105), channel_id=1, source_target_pairs={{0,8},{8,24},{24,16},{16,0},{1,9},{9,25},{25,17},{17,1},{2,10},{10... | collective-permute-start | bytes 3538952 | tf_op jit(solution)/shard_map/ppermute | solution.py:132
  54.4 28.2 %collective-permute-start = (bf16[512,1152]{1,0:T(8,128)(2,1)S(1)}, bf16[512,1152]{1,0:T(8,128)(2,1)}, u32[]{:S(2)}, u32[]{:S(2)}) collective-permute-start(bf16[512,1152]{1,0:T(8,128)(2,1)S(1)} %bitcast.106), channel_id=1, source_target_pairs={{8,0},{24,8},{16,24},{0,16},{9,1},{25,9},{17,25},{1,17},{10,2},{26... | collective-permute-start | bytes 3538952 | tf_op jit(solution)/shard_map/ppermute | solution.py:132
  59.7 22.1 %copy-start.12 = (bf16[128,4096]{1,0:T(8,128)(2,1)}, bf16[128,4096]{1,0:T(8,128)(2,1)S(1)}, u32[]{:S(2)}) copy-start(bf16[128,4096]{1,0:T(8,128)(2,1)S(1)} %slice_dynamic-update-slice_fusion.5) | copy-start | bytes 3145732
  80.3 14.4 %collective-permute-start.2 = (bf16[256,1152]{1,0:T(8,128)(2,1)}, bf16[256,1152]{1,0:T(8,128)(2,1)}, u32[]{:S(2)}, u32[]{:S(2)}) collective-permute-start(bf16[256,1152]{1,0:T(8,128)(2,1)} %slice.220), channel_id=1, source_target_pairs={{0,8},{8,24},{24,16},{16,0},{1,9},{9,25},{25,17},{17,1},{2,10},{10... | collective-permute-start | bytes 1769480 | tf_op jit(solution)/shard_map/ppermute | solution.py:141
  84.6 14.1 %collective-permute-start.3 = (bf16[256,1152]{1,0:T(8,128)(2,1)}, bf16[256,1152]{1,0:T(8,128)(2,1)}, u32[]{:S(2)}, u32[]{:S(2)}) collective-permute-start(bf16[256,1152]{1,0:T(8,128)(2,1)} %slice.221), channel_id=1, source_target_pairs={{8,0},{24,8},{16,24},{0,16},{9,1},{25,9},{17,25},{1,17},{10,2},{26... | collective-permute-start | bytes 1769480 | tf_op jit(solution)/shard_map/ppermute | solution.py:142
  86.2 35.4 %all-to-all-start.1 = ((bf16[8,64,1024]{2,1,0:T(8,128)(2,1)}), bf16[8,64,1024]{2,1,0:T(8,128)(2,1)}, u32[]{:S(2)}, u32[]{:S(2)}) async-start(bf16[8,64,1024]{2,1,0:T(8,128)(2,1)} %bitcast.8), calls=%async_computation.1 | async-start | bytes 2097152 | tf_op jit(solution)/shard_map/all_to_all | solution.py:239
  90.5 123.7 %all-gather.7.cloned.1.call-start = ((), (), s32[]{:S(2)}) async-start(), calls=%async_computation.11 | async-start | bytes 4718592 | tf_op jit(solution)/shard_map/all_gather | solution.py:944
  121.7 43.0 %collective-permute-start.4 = (bf16[512,1024]{1,0:T(8,128)(2,1)}, bf16[512,1024]{1,0:T(8,128)(2,1)}, u32[]{:S(2)}, u32[]{:S(2)}) collective-permute-start(bf16[512,1024]{1,0:T(8,128)(2,1)} %bitcast.9), channel_id=1, source_target_pairs={{0,8},{8,24},{24,16},{16,0},{1,9},{9,25},{25,17},{17,1},{2,10},{10... | collective-permute-start | bytes 3145736 | tf_op jit(solution)/shard_map/ppermute | solution.py:132
  123.1 41.5 %collective-permute-start.5 = (bf16[512,1024]{1,0:T(8,128)(2,1)}, bf16[512,1024]{1,0:T(8,128)(2,1)}, u32[]{:S(2)}, u32[]{:S(2)}) collective-permute-start(bf16[512,1024]{1,0:T(8,128)(2,1)} %bitcast.9), channel_id=1, source_target_pairs={{8,0},{24,8},{16,24},{0,16},{9,1},{25,9},{17,25},{1,17},{10,2},{26... | collective-permute-start | bytes 3145736 | tf_op jit(solution)/shard_map/ppermute | solution.py:132
  128.0 86.2 %all-to-all-start.2 = ((bf16[8,64,2112]{2,1,0:T(8,128)(2,1)}), bf16[8,64,2112]{2,1,0:T(8,128)(2,1)S(1)}, u32[]{:S(2)}, u32[]{:S(2)}) async-start(bf16[8,64,2112]{2,1,0:T(8,128)(2,1)} %bitcast.102), calls=%async_computation.2 | async-start | bytes 4456448 | tf_op jit(solution)/shard_map/all_to_all | solution.py:239
  133.3 136.1 %reduce-scatter.5.cloned.1.call-start = ((), (), s32[]{:S(2)}) async-start(), calls=%async_computation.12 | async-start | bytes 4718592 | tf_op jit(solution)/shard_map/reduce_scatter | solution.py:995
  165.8 14.6 %collective-permute-start.6 = (bf16[256,1024]{1,0:T(8,128)(2,1)S(1)}, bf16[256,1024]{1,0:T(8,128)(2,1)S(1)}, u32[]{:S(2)}, u32[]{:S(2)}) collective-permute-start(bf16[256,1024]{1,0:T(8,128)(2,1)S(1)} %slice.173), channel_id=1, source_target_pairs={{0,8},{8,24},{24,16},{16,0},{1,9},{9,25},{25,17},{17,1},{2,10},{10... | collective-permute-start | bytes 1572872 | tf_op jit(solution)/shard_map/ppermute | solution.py:141
  168.9 14.1 %collective-permute-start.7 = (bf16[256,1024]{1,0:T(8,128)(2,1)S(1)}, bf16[256,1024]{1,0:T(8,128)(2,1)S(1)}, u32[]{:S(2)}, u32[]{:S(2)}) collective-permute-start(bf16[256,1024]{1,0:T(8,128)(2,1)S(1)} %slice.174), channel_id=1, source_target_pairs={{8,0},{24,8},{16,24},{0,16},{9,1},{25,9},{17,25},{1,17},{10,2},{26... | collective-permute-start | bytes 1572872 | tf_op jit(solution)/shard_map/ppermute | solution.py:142
  170.3 14.0 %copy-start.3 = (bf16[1024,2048]{1,0:T(8,128)(2,1)S(1)}, bf16[1024,2048]{1,0:T(8,128)(2,1)}, u32[]{:S(2)}) copy-start(bf16[1024,2048]{1,0:T(8,128)(2,1)} %copy-done.2) | copy-start | bytes 12582916
  220.5 98.1 %all-gather.9.cloned.1.call-start = ((), (), s32[]{:S(2)}) async-start(), calls=%async_computation.13 | async-start | bytes 4718592 | tf_op jit(solution)/shard_map/all_gather | solution.py:1007
  223.0 49.8 %collective-permute-start.8 = (bf16[512,2112]{0,1:T(8,128)(2,1)}, bf16[512,2112]{0,1:T(8,128)(2,1)}, u32[]{:S(2)}, u32[]{:S(2)}) collective-permute-start(bf16[512,2112]{0,1:T(8,128)(2,1)} %copy.197), channel_id=1, source_target_pairs={{0,8},{8,24},{24,16},{16,0},{1,9},{9,25},{25,17},{17,1},{2,10},{10... | collective-permute-start | bytes 6488072 | tf_op jit(solution)/shard_map/ppermute | solution.py:132
  224.5 48.9 %collective-permute-start.9 = (bf16[512,2112]{0,1:T(8,128)(2,1)}, bf16[512,2112]{0,1:T(8,128)(2,1)}, u32[]{:S(2)}, u32[]{:S(2)}) collective-permute-start(bf16[512,2112]{0,1:T(8,128)(2,1)} %copy.197), channel_id=1, source_target_pairs={{8,0},{24,8},{16,24},{0,16},{9,1},{25,9},{17,25},{1,17},{10,2},{26... | collective-permute-start | bytes 6488072 | tf_op jit(solution)/shard_map/ppermute | solution.py:132
  273.4 122.5 %reduce-scatter.7.cloned.1.call-start = ((), (), s32[]{:S(2)}) async-start(), calls=%async_computation.14 | async-start | bytes 4718592 | tf_op jit(solution)/shard_map/reduce_scatter | solution.py:1023
  275.7 24.8 %collective-permute-start.10 = (bf16[256,2112]{0,1:T(8,128)(2,1)}, bf16[256,2112]{0,1:T(8,128)(2,1)}, u32[]{:S(2)}, u32[]{:S(2)}) collective-permute-start(bf16[256,2112]{0,1:T(8,128)(2,1)} %slice.181), channel_id=1, source_target_pairs={{0,8},{8,24},{24,16},{16,0},{1,9},{9,25},{25,17},{17,1},{2,10},{10... | collective-permute-start | bytes 3244040 | tf_op jit(solution)/shard_map/ppermute | solution.py:141
  279.5 24.7 %collective-permute-start.11 = (bf16[256,2112]{0,1:T(8,128)(2,1)}, bf16[256,2112]{0,1:T(8,128)(2,1)}, u32[]{:S(2)}, u32[]{:S(2)}) collective-permute-start(bf16[256,2112]{0,1:T(8,128)(2,1)} %slice.182), channel_id=1, source_target_pairs={{8,0},{24,8},{16,24},{0,16},{9,1},{25,9},{17,25},{1,17},{10,2},{26... | collective-permute-start | bytes 3244040 | tf_op jit(solution)/shard_map/ppermute | solution.py:142
  318.6 11.4 %copy-start.30 = (bf16[2048,2112]{1,0:T(8,128)(2,1)S(1)}, bf16[2048,2112]{1,0:T(8,128)(2,1)}, u32[]{:S(2)}) copy-start(bf16[2048,2112]{1,0:T(8,128)(2,1)} %constant_dynamic-update-slice_fusion.10) | copy-start | bytes 25952260
  318.6 11.4 %copy-start.47 = (bf16[1024,2048]{1,0:T(8,128)(2,1)S(1)}, bf16[1024,2048]{1,0:T(8,128)(2,1)}, u32[]{:S(2)}) copy-start(bf16[1024,2048]{1,0:T(8,128)(2,1)} %all-gather.7.cloned.1.call-done) | copy-start | bytes 12582916
  337.1 14.9 %copy-start.56 = (bf16[1024,704]{0,1:T(8,128)(2,1)}, bf16[1024,704]{0,1:T(8,128)(2,1)S(1)}, u32[]{:S(2)}) copy-start(bf16[1024,704]{0,1:T(8,128)(2,1)S(1)} %get-tuple-element.198) | copy-start | bytes 4325380
  346.6 109.9 %all-gather.11.cloned.1.call-start = ((), (), s32[]{:S(2)}) async-start(), calls=%async_computation.15 | async-start | bytes 4718592 | tf_op jit(solution)/shard_map/all_gather | solution.py:1035
  350.2 37.6 %collective-permute-start.12 = (bf16[256,1408]{1,0:T(8,128)(2,1)}, bf16[256,1408]{1,0:T(8,128)(2,1)S(1)}, u32[]{:S(2)}, u32[]{:S(2)}) collective-permute-start(bf16[256,1408]{1,0:T(8,128)(2,1)} %convolution_convert_fusion.3), channel_id=1, source_target_pairs={{0,8},{8,24},{24,16},{16,0},{1,9},{9,25},{25,17},{17,1},{2,10},{10... | collective-permute-start | bytes 2162696 | tf_op jit(solution)/shard_map/ppermute | solution.py:157
  355.0 32.8 %collective-permute-start.13 = (bf16[256,1408]{1,0:T(8,128)(2,1)}, bf16[256,1408]{1,0:T(8,128)(2,1)S(1)}, u32[]{:S(2)}, u32[]{:S(2)}) collective-permute-start(bf16[256,1408]{1,0:T(8,128)(2,1)} %convolution_convert_fusion.2), channel_id=1, source_target_pairs={{8,0},{24,8},{16,24},{0,16},{9,1},{25,9},{17,25},{1,17},{10,2},{26... | collective-permute-start | bytes 2162696 | tf_op jit(solution)/shard_map/ppermute | solution.py:158
  357.9 18.8 %collective-permute-start.14 = (bf16[256,704]{0,1:T(8,128)(2,1)}, bf16[256,704]{0,1:T(8,128)(2,1)S(1)}, u32[]{:S(2)}, u32[]{:S(2)}) collective-permute-start(bf16[256,704]{0,1:T(8,128)(2,1)} %convolution_convert_fusion.5), channel_id=1, source_target_pairs={{0,8},{8,24},{24,16},{16,0},{1,9},{9,25},{25,17},{17,1},{2,10},{10... | collective-permute-start | bytes 1081352 | tf_op jit(solution)/shard_map/ppermute | solution.py:157
  361.7 19.3 %collective-permute-start.15 = (bf16[256,704]{0,1:T(8,128)(2,1)}, bf16[256,704]{0,1:T(8,128)(2,1)S(1)}, u32[]{:S(2)}, u32[]{:S(2)}) collective-permute-start(bf16[256,704]{0,1:T(8,128)(2,1)} %convolution_convert_fusion.4), channel_id=1, source_target_pairs={{8,0},{24,8},{16,24},{0,16},{9,1},{25,9},{17,25},{1,17},{10,2},{26... | collective-permute-start | bytes 1081352 | tf_op jit(solution)/shard_map/ppermute | solution.py:158
  369.4 16.0 %copy-start.54 = (bf16[1024,704]{0,1:T(8,128)(2,1)S(1)}, bf16[1024,704]{0,1:T(8,128)(2,1)}, u32[]{:S(2)}) copy-start(bf16[1024,704]{0,1:T(8,128)(2,1)} %get-tuple-element.200) | copy-start | bytes 4325380
  399.7 200.8 %reduce-scatter.9.cloned.1.call-start = ((), (), s32[]{:S(2)}) async-start(), calls=%async_computation.16 | async-start | bytes 4718592 | tf_op jit(solution)/shard_map/reduce_scatter | solution.py:1039
  399.7 49.6 %copy-start.55 = (bf16[1024,704]{0,1:T(8,128)(2,1)S(1)}, bf16[1024,704]{0,1:T(8,128)(2,1)}, u32[]{:S(2)}) copy-start(bf16[1024,704]{0,1:T(8,128)(2,1)} %get-tuple-element.200) | copy-start | bytes 4325380
  399.7 52.1 %collective-permute-start.16 = (bf16[512,1408]{1,0:T(8,128)(2,1)}, bf16[512,1408]{1,0:T(8,128)(2,1)}, u32[]{:S(2)}, u32[]{:S(2)}) collective-permute-start(bf16[512,1408]{1,0:T(8,128)(2,1)} %add_convert_fusion.2), channel_id=1, source_target_pairs={{0,8},{8,24},{24,16},{16,0},{1,9},{9,25},{25,17},{17,1},{2,10},{10... | collective-permute-start | bytes 4325384 | tf_op jit(solution)/shard_map/ppermute | solution.py:182
  401.3 50.6 %collective-permute-start.17 = (bf16[512,1408]{1,0:T(8,128)(2,1)}, bf16[512,1408]{1,0:T(8,128)(2,1)}, u32[]{:S(2)}, u32[]{:S(2)}) collective-permute-start(bf16[512,1408]{1,0:T(8,128)(2,1)} %add_convert_fusion.1), channel_id=1, source_target_pairs={{8,0},{24,8},{16,24},{0,16},{9,1},{25,9},{17,25},{1,17},{10,2},{26... | collective-permute-start | bytes 4325384 | tf_op jit(solution)/shard_map/ppermute | solution.py:183
  401.8 46.4 %collective-permute-start.18 = (bf16[512,704]{0,1:T(8,128)(2,1)}, bf16[512,704]{0,1:T(8,128)(2,1)S(1)}, u32[]{:S(2)}, u32[]{:S(2)}) collective-permute-start(bf16[512,704]{0,1:T(8,128)(2,1)} %fusion.22), channel_id=1, source_target_pairs={{0,8},{8,24},{24,16},{16,0},{1,9},{9,25},{25,17},{17,1},{2,10},{10... | collective-permute-start | bytes 2162696 | tf_op jit(solution)/shard_map/ppermute | solution.py:182
  403.3 46.0 %collective-permute-start.19 = (bf16[512,704]{0,1:T(8,128)(2,1)S(1)}, bf16[512,704]{0,1:T(8,128)(2,1)S(1)}, u32[]{:S(2)}, u32[]{:S(2)}) collective-permute-start(bf16[512,704]{0,1:T(8,128)(2,1)S(1)} %fusion.23), channel_id=1, source_target_pairs={{8,0},{24,8},{16,24},{0,16},{9,1},{25,9},{17,25},{1,17},{10,2},{26... | collective-permute-start | bytes 2162696 | tf_op jit(solution)/shard_map/ppermute | solution.py:183
  456.5 87.4 %all-to-all-start.3 = ((bf16[8,64,2112]{2,1,0:T(8,128)(2,1)}), bf16[8,64,2112]{2,1,0:T(8,128)(2,1)}, u32[]{:S(2)}, u32[]{:S(2)}) async-start(bf16[8,64,2112]{2,1,0:T(8,128)(2,1)} %bitcast.103), calls=%async_computation.5 | async-start | bytes 4456448 | tf_op jit(solution)/shard_map/all_to_all | solution.py:239
  460.9 164.5 %reduce-scatter.11.cloned.1.call-start = ((), (), s32[]{:S(2)}) async-start(), calls=%async_computation.17 | async-start | bytes 4718592 | tf_op jit(solution)/shard_map/reduce_scatter | solution.py:1060
  482.3 61.7 %collective-permute-start.20 = (bf16[256,1024]{1,0:T(8,128)(2,1)}, bf16[256,1024]{1,0:T(8,128)(2,1)S(1)}, u32[]{:S(2)}, u32[]{:S(2)}) collective-permute-start(bf16[256,1024]{1,0:T(8,128)(2,1)} %get-tuple-element.142), channel_id=1, source_target_pairs={{0,8},{8,24},{24,16},{16,0},{1,9},{9,25},{25,17},{17,1},{2,10},{10... | collective-permute-start | bytes 1572872 | tf_op jit(solution)/shard_map/ppermute | solution.py:205
  483.2 60.7 %collective-permute-start.21 = (bf16[256,1024]{1,0:T(8,128)(2,1)}, bf16[256,1024]{1,0:T(8,128)(2,1)}, u32[]{:S(2)}, u32[]{:S(2)}) collective-permute-start(bf16[256,1024]{1,0:T(8,128)(2,1)} %get-tuple-element.143), channel_id=1, source_target_pairs={{8,0},{24,8},{16,24},{0,16},{9,1},{25,9},{17,25},{1,17},{10,2},{26... | collective-permute-start | bytes 1572872 | tf_op jit(solution)/shard_map/ppermute | solution.py:206
  484.3 59.7 %collective-permute-start.22 = (bf16[256,1024]{1,0:T(8,128)(2,1)}, bf16[256,1024]{1,0:T(8,128)(2,1)S(1)}, u32[]{:S(2)}, u32[]{:S(2)}) collective-permute-start(bf16[256,1024]{1,0:T(8,128)(2,1)} %get-tuple-element.144), channel_id=1, source_target_pairs={{0,8},{8,24},{24,16},{16,0},{1,9},{9,25},{25,17},{17,1},{2,10},{10... | collective-permute-start | bytes 1572872 | tf_op jit(solution)/shard_map/ppermute | solution.py:207
  485.2 58.7 %collective-permute-start.23 = (bf16[256,1024]{1,0:T(8,128)(2,1)}, bf16[256,1024]{1,0:T(8,128)(2,1)S(1)}, u32[]{:S(2)}, u32[]{:S(2)}) collective-permute-start(bf16[256,1024]{1,0:T(8,128)(2,1)} %get-tuple-element.145), channel_id=1, source_target_pairs={{8,0},{24,8},{16,24},{0,16},{9,1},{25,9},{17,25},{1,17},{10,2},{26... | collective-permute-start | bytes 1572872 | tf_op jit(solution)/shard_map/ppermute | solution.py:208
  544.0 13.3 %copy-start.35 = (bf16[256,1024]{1,0:T(8,128)(2,1)}, bf16[256,1024]{1,0:T(8,128)(2,1)S(1)}, u32[]{:S(2)}) copy-start(bf16[256,1024]{1,0:T(8,128)(2,1)S(1)} %collective-permute-done.20.refs_4_) | copy-start | bytes 1572868
  544.0 13.3 %copy-start.31 = (bf16[256,1024]{1,0:T(8,128)(2,1)}, bf16[256,1024]{1,0:T(8,128)(2,1)S(1)}, u32[]{:S(2)}) copy-start(bf16[256,1024]{1,0:T(8,128)(2,1)S(1)} %collective-permute-done.22.refs_5_) | copy-start | bytes 1572868
  544.0 13.3 %copy-start.32 = (bf16[256,1024]{1,0:T(8,128)(2,1)}, bf16[256,1024]{1,0:T(8,128)(2,1)S(1)}, u32[]{:S(2)}) copy-start(bf16[256,1024]{1,0:T(8,128)(2,1)S(1)} %collective-permute-done.23.refs_6_) | copy-start | bytes 1572868
  558.0 3.9 collective-permute-start.24
  562.0 3.9 collective-permute-start.25
  565.9 8.5 %collective-permute-start.26 = (f32[8,1024]{1,0:T(8,128)S(1)}, f32[8,1024]{1,0:T(8,128)S(1)}, u32[]{:S(2)}, u32[]{:S(2)}) collective-permute-start(f32[8,1024]{1,0:T(8,128)S(1)} %add.178), channel_id=1, source_target_pairs={{0,1},{1,0},{2,3},{3,2},{4,5},{5,4},{6,7},{7,6},{8,9},{9,8},{10,11... | collective-permute-start | bytes 98312 | tf_op jit(solution)/shard_map/ppermute | solution.py:260
  572.4 24.9 %collective-permute-start.29 = (bf16[256,1024]{1,0:T(8,128)(2,1)}, bf16[256,1024]{1,0:T(8,128)(2,1)S(1)}, u32[]{:S(2)}, u32[]{:S(2)}) collective-permute-start(bf16[256,1024]{1,0:T(8,128)(2,1)} %get-tuple-element.161), channel_id=1, source_target_pairs={{0,8},{8,24},{24,16},{16,0},{1,9},{9,25},{25,17},{17,1},{2,10},{10... | collective-permute-start | bytes 1572872 | tf_op jit(solution)/shard_map/ppermute | solution.py:221
  573.5 23.8 %collective-permute-start.30 = (bf16[256,1024]{1,0:T(8,128)(2,1)}, bf16[256,1024]{1,0:T(8,128)(2,1)S(1)}, u32[]{:S(2)}, u32[]{:S(2)}) collective-permute-start(bf16[256,1024]{1,0:T(8,128)(2,1)} %get-tuple-element.162), channel_id=1, source_target_pairs={{8,0},{24,8},{16,24},{0,16},{9,1},{25,9},{17,25},{1,17},{10,2},{26... | collective-permute-start | bytes 1572872 | tf_op jit(solution)/shard_map/ppermute | solution.py:222
  574.4 7.7 %collective-permute-start.27 = (f32[16,1024]{1,0:T(8,128)S(1)}, f32[16,1024]{1,0:T(8,128)S(1)}, u32[]{:S(2)}, u32[]{:S(2)}) collective-permute-start(f32[16,1024]{1,0:T(8,128)S(1)} %pad_maximum_fusion.5), channel_id=1, source_target_pairs={{0,2},{1,3},{2,0},{3,1},{4,6},{5,7},{6,4},{7,5},{8,10},{9,11},{10,... | collective-permute-start | bytes 196616 | tf_op jit(solution)/shard_map/ppermute | solution.py:260
  579.9 19.7 %collective-permute-start.31 = (bf16[256,1152]{1,0:T(8,128)(2,1)}, bf16[256,1152]{1,0:T(8,128)(2,1)}, u32[]{:S(2)}, u32[]{:S(2)}) collective-permute-start(bf16[256,1152]{1,0:T(8,128)(2,1)} %get-tuple-element.164), channel_id=1, source_target_pairs={{0,8},{8,24},{24,16},{16,0},{1,9},{9,25},{25,17},{17,1},{2,10},{10... | collective-permute-start | bytes 1769480 | tf_op jit(solution)/shard_map/ppermute | solution.py:157
  581.0 19.5 %collective-permute-start.32 = (bf16[256,1152]{1,0:T(8,128)(2,1)}, bf16[256,1152]{1,0:T(8,128)(2,1)}, u32[]{:S(2)}, u32[]{:S(2)}) collective-permute-start(bf16[256,1152]{1,0:T(8,128)(2,1)} %get-tuple-element.165), channel_id=1, source_target_pairs={{8,0},{24,8},{16,24},{0,16},{9,1},{25,9},{17,25},{1,17},{10,2},{26... | collective-permute-start | bytes 1769480 | tf_op jit(solution)/shard_map/ppermute | solution.py:158
  582.2 15.0 %collective-permute-start.28 = (f32[32,1024]{1,0:T(8,128)S(1)}, f32[32,1024]{1,0:T(8,128)S(1)}, u32[]{:S(2)}, u32[]{:S(2)}) collective-permute-start(f32[32,1024]{1,0:T(8,128)S(1)} %pad_maximum_fusion.4), channel_id=1, source_target_pairs={{0,4},{1,5},{2,6},{3,7},{4,0},{5,1},{6,2},{7,3},{8,12},{9,13},{10,... | collective-permute-start | bytes 393224 | tf_op jit(solution)/shard_map/ppermute | solution.py:260
  614.4 11.0 %copy-start.38 = (f32[2048]{0:T(1024)S(1)}, f32[2048]{0:T(1024)}, u32[]{:S(2)}) copy-start(f32[2048]{0:T(1024)} %copy-done.37) | copy-start | bytes 24580
  616.7 32.5 %all-to-all-start.4 = ((bf16[8,64,1024]{2,1,0:T(8,128)(2,1)}), bf16[8,64,1024]{2,1,0:T(8,128)(2,1)S(1)}, u32[]{:S(2)}, u32[]{:S(2)}) async-start(bf16[8,64,1024]{2,1,0:T(8,128)(2,1)} %bitcast.112), calls=%async_computation.7 | async-start | bytes 2097152 | tf_op jit(solution)/shard_map/all_to_all | solution.py:243
  620.3 28.6 %collective-permute-start.33 = (bf16[512,1152]{1,0:T(8,128)(2,1)}, bf16[512,1152]{1,0:T(8,128)(2,1)}, u32[]{:S(2)}, u32[]{:S(2)}) collective-permute-start(bf16[512,1152]{1,0:T(8,128)(2,1)} %get-tuple-element.175), channel_id=1, source_target_pairs={{0,8},{8,24},{24,16},{16,0},{1,9},{9,25},{25,17},{17,1},{2,10},{10... | collective-permute-start | bytes 3538952 | tf_op jit(solution)/shard_map/ppermute | solution.py:182
  621.0 28.3 %collective-permute-start.34 = (bf16[512,1152]{1,0:T(8,128)(2,1)}, bf16[512,1152]{1,0:T(8,128)(2,1)}, u32[]{:S(2)}, u32[]{:S(2)}) collective-permute-start(bf16[512,1152]{1,0:T(8,128)(2,1)} %get-tuple-element.176), channel_id=1, source_target_pairs={{8,0},{24,8},{16,24},{0,16},{9,1},{25,9},{17,25},{1,17},{10,2},{26... | collective-permute-start | bytes 3538952 | tf_op jit(solution)/shard_map/ppermute | solution.py:183
  626.8 33.8 %copy-start.6 = (bf16[128,2048]{1,0:T(8,128)(2,1)S(1)}, bf16[128,2048]{1,0:T(8,128)(2,1)}, u32[]{:S(2)}) copy-start(bf16[128,2048]{1,0:T(8,128)(2,1)} %reduce-scatter.7.cloned.1.call-done) | copy-start | bytes 1572868
  655.8 34.2 %all-to-all-start.5 = ((bf16[8,64,1152]{2,1,0:T(8,128)(2,1)}), bf16[8,64,1152]{2,1,0:T(8,128)(2,1)S(1)}, u32[]{:S(2)}, u32[]{:S(2)}) async-start(bf16[8,64,1152]{2,1,0:T(8,128)(2,1)} %bitcast.104), calls=%async_computation.9 | async-start | bytes 2359296 | tf_op jit(solution)/shard_map/all_to_all | solution.py:243
  675.9 14.8 %copy-start.23 = (bf16[64,4096]{1,0:T(8,128)(2,1)S(1)}, bf16[64,4096]{1,0:T(8,128)(2,1)}, u32[]{:S(2)}) copy-start(bf16[64,4096]{1,0:T(8,128)(2,1)} %param.25) | copy-start | bytes 1572868
  (48 other events, 195.9 us)
Sparse Core Ops, SparseCore 0:
  52.0 52.8 all-gather.4
  119.0 87.7 all-gather.6
  220.7 48.6 reduce-scatter.4
  273.5 45.0 all-gather.8
  346.7 48.7 reduce-scatter.6
  399.8 44.9 all-gather.10
  456.6 89.3 reduce-scatter.8
  557.4 51.8 reduce-scatter.10

commit v7 on v6

--- a/solution.py
+++ b/solution.py
@@ -244,24 +244,31 @@
     return turned.reshape(ranks, -1, mine.shape[1])
 
 
-def sum_everywhere(values):
+def sum_dp(values):
     count = lax.axis_size("dp")
-    ranks = lax.axis_size("seq")
-    if count & (count - 1) or ranks & (ranks - 1):
-        return lax.all_gather(lax.psum(values, "dp"), "seq", axis=0, tiled=True)
+    if count & (count - 1):
+        return lax.psum(values, "dp")
     step = 1
     while step < count:
         values = values + lax.ppermute(values, "dp", [(i, i ^ step) for i in range(count)])
         step *= 2
+    return values
+
+
+def gather_small(values):
+    ranks = lax.axis_size("seq")
+    if ranks & (ranks - 1):
+        return lax.all_gather(values, "seq", axis=0, tiled=True)
     rank = lax.axis_index("seq")
-    held = values
     step = 1
     while step < ranks:
-        other = lax.ppermute(held, "seq", [(i, i ^ step) for i in range(ranks)])
+        other = lax.ppermute(values, "seq", [(i, i ^ step) for i in range(ranks)])
         upper = (rank & step) != 0
-        held = jnp.concatenate([jnp.where(upper, other, held), jnp.where(upper, held, other)])
+        values = jnp.concatenate(
+            [jnp.where(upper, other, values), jnp.where(upper, values, other)]
+        )
         step *= 2
-    return held
+    return values
 
 
 class Pair:
@@ -355,8 +362,7 @@
     y = x + const_ref[1:2, :]
     logs = const_ref[0:1, :] * (jnp.maximum(y, 0.0) + jnp.log1p(jnp.exp(-jnp.abs(y))))
     beta = jax.nn.sigmoid(x)
-    rider = rider_ref[rows, :].astype(F32)
-    offs = rider[:, 0:1] * 64.0 + rider[:, 1:2]
+    offs = rider_ref[rows, 0:1]
     cols = jnp.where(lane < hp, logs, jnp.where(lane < 2 * hp, beta, 0.0))
     return jnp.where(lane == 2 * hp, offs, cols), offs
 
@@ -885,14 +891,6 @@
 
     own_tokens = to_ring(tokens[0])
     own_cot = to_ring(cotangent[0])
-    rider = jnp.concatenate(
-        [
-            (offsets[0] // 64).astype(BF)[:, None],
-            (offsets[0] % 64).astype(BF)[:, None],
-            jnp.zeros((tok, LANES - 2), BF),
-        ],
-        axis=1,
-    )
     small = jnp.concatenate(
         [
             plan.split_keys(w_decay),
@@ -919,12 +917,13 @@
     )
     mlp_pack = pack_even(ranks, w_hidden, w_up, w_down)
     mix_own = exchange(mix_pack)
+    row_offsets = gather_small(offsets.astype(F32))
     held = lax.optimization_barrier(
-        (jnp.concatenate([own_tokens, rider], axis=1), side_pack, mlp_pack, mix_own)
+        (own_tokens, side_pack, mlp_pack, mix_own, row_offsets)
     )
     gathered = lax.all_gather(held[0], "seq", axis=0, tiled=True)
     side_own = exchange(held[1])
-    mix_own = held[3]
+    mix_own, row_offsets = held[3], held[4]
     w_mix = gather_end(mix_own, gather_start(mix_own))
     mlp_own_cols = exchange(after(held[2], side_own, gathered))
     side_own = after(side_own, w_mix)
@@ -936,7 +935,7 @@
     attn_gain_full = w_mix[:, at_s + 2 * hp].astype(F32)
     mlp_gain_full = w_mix[:, at_s + 2 * hp + 1].astype(F32)
 
-    tokens_all = gathered[:, :width].astype(F32)
+    tokens_all = gathered.astype(F32)
     normed_all = tokens_all * rms_scale(tokens_all)
     attn = (normed_all * attn_gain_full).astype(BF)
     pre = nn(attn, w_mix[:, :at_s]).astype(BF)
@@ -953,7 +952,7 @@
     taps = jnp.concatenate([taps_query, taps_key, taps_value], axis=1)
     const = jnp.pad(jnp.stack([-jnp.exp(own_log), own_bias]), ((0, 0), (0, LANES - hp)))
     pre, pre_small = lax.optimization_barrier((pre, pre_small, side_own))[:2]
-    rider_all = gathered[:, width:]
+    rider_all = jnp.pad(row_offsets.reshape(length, 1), ((0, 0), (0, LANES - 1)))
     mixed, *saved = delta_forward(pre, pre_small, rider_all, taps, const, hp, dk, dv)
     mixed, *side_near = lax.optimization_barrier((mixed,) + tuple(side_near))
     w_side = gather_end(side_own, side_near)
@@ -1053,14 +1052,17 @@
     d_pre, d_sums = delta_backward(
         pre, pre_small, rider_all, taps, const, saved, d_mixed, gain_part, hp, dk, dv
     )
-    held = lax.optimization_barrier((d_pre, d_sums, mlp_rows) + side_sum.near)
+    held = lax.optimization_barrier((d_pre, d_sums) + side_sum.near)
+    d_pre, d_sums = held[:2]
+    side_sum.near = held[2:]
+    side_sum.second()
+    d_sums = sum_dp(d_sums)
+    held = lax.optimization_barrier((d_pre, d_sums, mlp_rows) + side_sum.sums)
     d_pre, d_sums, mlp_rows = held[:3]
-    side_sum.near = held[3:]
     d_attn_part = back_product((d_pre, w_mix), (d_gate, gate_cols))
     d_attn = lax.psum_scatter(d_attn_part, "seq", scatter_dimension=0, tiled=True).astype(F32)
-    side_sum.second(d_attn_part)
     mix_sum = RingGrad(attn, after(d_pre, d_attn_part))
-    every = sum_everywhere(after(d_sums, d_attn_part))
+    every = gather_small(after(d_sums, d_attn_part))
     mlp_out, every, *held = lax.optimization_barrier(
         (mlp_out, every) + side_sum.late + mix_sum.far
     )

time: 709 us -> 692 us (0.976)
  waiting for transfers between devices: 263 us -> 235 us
  starting transfers between devices: 64.6 us -> 73.2 us
    all_to_all x4, waiting for transfers between devices: 55.8 us -> 20.4 us  [exchange(): return lax.all_to_all(packed, 'seq', 0, 0, tiled=True)]
    ppermute x5 -> x8, waiting for transfers between devices: 19.2 us -> 29.9 us  [the longest x6 26.3 us: gather_small(): other = lax.ppermute(values, 'seq', [(i, i ^ step) for i in range(ranks)])]
    ppermute x5 -> x8, starting transfers between devices: 3.7 us -> 12.3 us  [the longest x6 11.2 us: gather_small(): other = lax.ppermute(values, 'seq', [(i, i ^ step) for i in range(ranks)])]
    unnamed x150 -> x146, local copies, waits for them, and re-layouts: 30.5 us -> 31.1 us
  transfers between devices with their start and end apart: 49 -> 52, of which waited for: 26 -> 24; matrix products, arithmetic and copies ran while one was open for 22% -> 23% of each run, Pallas kernels for 20% -> 20%
where the time goes in v7:
time: 692 us; the launch traced here: 682 us
  waiting for transfers between devices  235 us (34%)
  Pallas kernels  145 us (21%)
  matrix products  93.7 us (14%)
  local copies, waits for them, and re-layouts  83.5 us (12%)
  starting transfers between devices  73.2 us (11%)
  other arithmetic  35.9 us (5%)
  between operations  15.6 us (2%)
    dot_general x19, matrix products, dot_f32(): lax.dot_general(left, right, (dims, ((), ())), preferred_element_type=F32)  93.7 us
    ppermute x4, waiting for transfers between devices, second(): lax.ppermute(self.sums[0], 'dp', to_right)  60.6 us
    pallas_call x1, Pallas kernels, delta_backward(): pl.pallas_call(functools.partial(bwd_kernel, hp, dk, dv), out_shape=(shap...  45.3 us
    reduce_scatter x1, waiting for transfers between devices, local(): lax.psum_scatter(nt(gated, out_cols).astype(BF), 'seq', scatter_dimension...  44.3 us
    unnamed x146, local copies, waits for them, and re-layouts  31.1 us
    pallas_call x1, Pallas kernels, delta_forward(): pl.pallas_call(functools.partial(fwd_kernel, hp, dk, dv), out_shape=(shap...  29.6 us
    ppermute x6, waiting for transfers between devices, gather_small(): other = lax.ppermute(values, 'seq', [(i, i ^ step) for i in range(ranks)])  26.3 us
    pallas_call x3, Pallas kernels, grad_blocks(): pl.pallas_call(functools.partial(block_kernel, half, blocks, len(pairs),...  20.4 us
  transfers between devices with their start and end apart: 52, of which 24 were waited for; matrix products, arithmetic and copies ran while one was open for 23% of the time, Pallas kernels for 20%

profile of v7, /device:TPU:0, one launch (start us, length us, event | category | flops | bytes accessed | tf_op | source)
XLA Modules:
  0.0 682.4 jit_solution(11988814623018331016)
XLA Ops:
  13.6 2.6 concatenate.69
  16.2 6.5 all-to-all-start
  29.0 13.9 %collective-permute-done.1 = f32[2,128]{1,0:T(2,128)S(1)} collective-permute-done((f32[2,128]{1,0:T(2,128)S(1)}, f32[2,128]{1,0:T(2,128)S(1)}, u32[]{:S(2)}, u32[]{:S(2)}) %collective-permute-start.1) | collective-permute-done | bytes 1056 | tf_op jit(solution)/shard_map/ppermute | solution.py:265
  42.9 4.5 collective-permute-start.2
  50.1 3.3 pack_even.1
  61.2 19.5 %collective-permute-done.4 = bf16[512,1152]{1,0:T(8,128)(2,1)S(1)} collective-permute-done((bf16[512,1152]{1,0:T(8,128)(2,1)S(1)}, bf16[512,1152]{1,0:T(8,128)(2,1)S(1)}, u32[]{:S(2)}, u32[]{:S(2)}) %collective-permute-start.4) | collective-permute-done | bytes 1179680 | tf_op jit(solution)/shard_map/ppermute | solution.py:132
  87.5 4.2 all-to-all-start.1
  91.8 2.5 constant_dynamic-update-slice_fusion.3
  104.9 3.2 fusion
  111.4 5.7 fusion.16.pre_ref
  123.0 4.7 fusion.50.small_ref
  127.7 3.6 all-to-all-start.2
  131.6 29.6 %delta_forward.1 = (f32[1024,512]{1,0:T(8,128)}, f32[16,128,256]{2,1,0:T(8,128)}, f32[1024,512]{1,0:T(8,128)}, f32[16,128,128]{2,1,0:T(8,128)}, f32[1024,256]{1,0:T(8,128)}) custom-call(bf16[1024,1024]{1,0:T(8,128)(2,1)} %fusion.16.pre_ref, f32[1024,128]{1,0:T(8,128)} %fusion.50.small_ref, f32[1024,128]{1,0:T(8,128)} %pad.36.rider_ref, ...), custom_call_target="tpu_custom_call" | custom-call | flops 43008000000 | bytes 16777216 | tf_op jit(solution)/shard_map/delta_forward/pallas_call | solution.py:770
  168.2 8.2 %collective-permute-done.9 = bf16[256,1024]{1,0:T(8,128)(2,1)S(1)} collective-permute-done((bf16[256,1024]{1,0:T(8,128)(2,1)S(1)}, bf16[256,1024]{1,0:T(8,128)(2,1)S(1)}, u32[]{:S(2)}, u32[]{:S(2)}) %collective-permute-start.9) | collective-permute-done | bytes 524320 | tf_op jit(solution)/shard_map/ppermute | solution.py:141
  176.5 2.4 collective-permute-done.10
  180.3 3.7 fusion.55.gate_ref
  184.0 4.3 gate_forward.1.refs_3_
  188.2 20.4 %all-to-all-done.2 = bf16[8,64,2112]{2,1,0:T(8,128)(2,1)S(1)} async-done(((bf16[8,64,2112]{2,1,0:T(8,128)(2,1)}), bf16[8,64,2112]{2,1,0:T(8,128)(2,1)S(1)}, u32[]{:S(2)}, u32[]{:S(2)}) %all-to-all-start.2) | async-done | bytes 2162720 | tf_op jit(solution)/shard_map/all_to_all | solution.py:239
  208.7 6.2 convolution_convert_fusion.1
  215.0 2.5 copy.178
  219.5 44.3 %reduce-scatter.5.cloned.1.call-done = bf16[128,2048]{1,0:T(8,128)(2,1)} async-done(((bf16[1024,2048]{1,0:T(8,128)(2,1)}), bf16[128,2048]{1,0:T(8,128)(2,1)}) %reduce-scatter.5.cloned.1.call-update) | async-done | bytes 524304 | tf_op jit(solution)/shard_map/reduce_scatter | solution.py:994
  271.9 2.3 slice.174
  276.3 4.1 copy.180
  280.4 3.0 copy.183
  283.4 3.2 constant_dynamic-update-slice_fusion.13
  286.5 8.6 %collective-permute-done.13 = bf16[256,2112]{0,1:T(8,128)(2,1)} collective-permute-done((bf16[256,2112]{0,1:T(8,128)(2,1)}, bf16[256,2112]{0,1:T(8,128)(2,1)}, u32[]{:S(2)}, u32[]{:S(2)}) %collective-permute-start.13) | collective-permute-done | bytes 1081376 | tf_op jit(solution)/shard_map/ppermute | solution.py:141
  299.0 2.3 copy.182
  301.4 2.4 constant_dynamic-update-slice_fusion.12
  306.4 6.7 all-gather.9.cloned.1.call-done
  313.1 11.5 %fusion.5 = f32[1024,1408]{0,1:T(8,128)} fusion(bf16[1024,2048]{1,0:T(8,128)(2,1)} %all-gather.9.cloned.1.call-done, bf16[2048,2112]{1,0:T(8,128)(2,1)} %constant_dynamic-update-slice_fusion.10), kind=kOutput, calls=%fused_computation.7 | convolution fusion | flops 5905580032 | bytes 15728640 | tf_op jit(solution)/shard_map/dot_general | solution.py:22
  324.6 7.1 %multiply_convert_fusion.2 = (bf16[1024,704]{0,1:T(8,128)(2,1)S(1)}, bf16[1024,704]{0,1:T(8,128)(2,1)S(1)}, bf16[1024,704]{0,1:T(8,128)(2,1)}) fusion(f32[1024,1408]{0,1:T(8,128)} %fusion.5, bf16[1024,2048]{1,0:T(8,128)(2,1)S(1)} %copy-done.46, bf16[2048,2112]{1,0:T(8,128)(2,1)S(1)} %copy-done.30), kind=kOutput, calls=%fused_computation.20 | convolution fusion | flops 2963603456 | bytes 17432576 | tf_op jit(solution)/shard_map/dot_general | solution.py:22
  332.8 8.3 %fusion.9 = bf16[1024,2048]{1,0:T(8,128)(2,1)} fusion(bf16[2048,2112]{1,0:T(8,128)(2,1)S(1)} %copy-done.30, bf16[1024,704]{0,1:T(8,128)(2,1)S(1)} %get-tuple-element.205, bf16[1024,704]{0,1:T(8,128)(2,1)S(1)} %get-tuple-element.204), kind=kOutput, calls=%fused_computation.11 | convolution fusion | flops 5913444352 | bytes 12845056 | tf_op jit(solution)/shard_map/dot_general | solution.py:22
  341.2 2.7 convolution_convert_fusion.3
  345.8 3.5 convolution_convert_fusion.2
  356.6 7.0 %convolution_convert_fusion = bf16[1024,2048]{1,0:T(8,128)(2,1)} fusion(bf16[1024,704]{0,1:T(8,128)(2,1)S(1)} %copy-done.51, bf16[2048,2112]{1,0:T(8,128)(2,1)} %constant_dynamic-update-slice_fusion.10), kind=kOutput, calls=%fused_computation.12 | convolution fusion | flops 2954887168 | bytes 8781824 | tf_op jit(solution)/shard_map/dot_general | solution.py:22
  363.6 6.8 collective-permute-done.17
  370.4 5.0 collective-permute-done.18
  375.4 3.7 fusion.22
  379.1 3.2 fusion.23
  383.3 3.0 add_convert_fusion.2
  386.3 4.2 add_convert_fusion.1
  398.6 5.8 fusion.32
  404.4 38.4 %collective-permute-done.21 = bf16[512,704]{0,1:T(8,128)(2,1)S(1)} collective-permute-done((bf16[512,704]{0,1:T(8,128)(2,1)}, bf16[512,704]{0,1:T(8,128)(2,1)S(1)}, u32[]{:S(2)}, u32[]{:S(2)}) %collective-permute-start.21) | collective-permute-done | bytes 720928 | tf_op jit(solution)/shard_map/ppermute | solution.py:182
  446.6 3.1 add_convert_fusion
  451.2 4.4 all-to-all-start.3
  455.6 6.5 fusion.19.d_ref
  462.2 5.7 gate_backward.1
  467.9 7.2 %grad_blocks.3 = (bf16[256,1024]{1,0:T(8,128)(2,1)}, bf16[256,1024]{1,0:T(8,128)(2,1)}, bf16[256,1024]{1,0:T(8,128)(2,1)}, bf16[256,1024]{1,0:T(8,128)(2,1)}) custom-call(bf16[1024,2048]{1,0:T(8,128)(2,1)} %copy-done.2, bf16[1024,2048]{1,0:T(8,128)(2,1)} %all-gather.11.cloned.1.call-done.refs_1_, bf16[1024,512]{1,0:T(8,128)(2,1)} %get-tuple-element.145.refs_2_.refs_1_, ...), custom_call_target="tpu_custom_call" | custom-call | flops 134217728 | bytes 1048576 | tf_op jit(solution)/shard_map/grad_blocks/pallas_call | solution.py:705
  479.4 45.3 %delta_backward.1 = (bf16[1024,1152]{1,0:T(8,128)(2,1)}, f32[8,1024]{1,0:T(8,128)}) custom-call(bf16[1024,1024]{1,0:T(8,128)(2,1)} %fusion.16.pre_ref, f32[1024,128]{1,0:T(8,128)} %fusion.50.small_ref, f32[1024,128]{1,0:T(8,128)} %pad.36.rider_ref, f32[4,1024]{1,0:T(4,128)} %pad_maximum_fusion.6.taps_ref, f32[2,128]{1,0:T(2,128)} %select_maximum_fusion.const_ref, ...), custom_call_target="tpu_custom_call" | custom-call | flops 10240000000 | bytes 20971520 | tf_op jit(solution)/shard_map/delta_backward/pallas_call | solution.py:798
  525.3 3.6 collective-permute-done.27
  530.3 3.1 slice.216.refs_3_
  533.4 6.4 grad_blocks.4
  539.8 12.8 %back_product.1 = bf16[1024,2048]{1,0:T(8,128)(2,1)} custom-call(bf16[1024,1152]{1,0:T(8,128)(2,1)} %get-tuple-element.169.refs_0_.right_ref, bf16[1024,512]{1,0:T(8,128)(2,1)} %get-tuple-element.145.refs_2_.refs_1_, bf16[2048,1152]{1,0:T(8,128)(2,1)} %constant_dynamic-update-slice_fusion.refs_2_, bf16[2048,512]{1,0:T(8,128)(2,1)} %slice.216.refs_3_), custom_call_target="tpu_custom_call" | custom-call | flops 536870912 | bytes 2097152 | tf_op jit(solution)/shard_map/back_product/pallas_call | solution.py:730
  556.6 5.7 grad_rows.3
  564.6 2.4 collective-permute-start.31
  566.9 11.7 %collective-permute-done.31 = f32[32,1024]{1,0:T(8,128)S(1)} collective-permute-done((f32[32,1024]{1,0:T(8,128)S(1)}, f32[32,1024]{1,0:T(8,128)S(1)}, u32[]{:S(2)}, u32[]{:S(2)}) %collective-permute-start.31) | collective-permute-done | bytes 131104 | tf_op jit(solution)/shard_map/ppermute | solution.py:265
  580.2 7.2 %grad_rows.4 = (bf16[512,1152]{1,0:T(8,128)(2,1)}, bf16[512,1152]{1,0:T(8,128)(2,1)}) custom-call(bf16[1024,2048]{1,0:T(8,128)(2,1)} %copy-done.2, bf16[1024,1152]{1,0:T(8,128)(2,1)} %get-tuple-element.169.refs_0_.right_ref, bf16[256,1152]{1,0:T(8,128)(2,1)} %collective-permute-done.34.refs_0_, bf16[256,1152]{1,0:T(8,128)(2,1)} %collective-permute-done.35.refs_1_), custom_call_target="tpu_custom_call" | custom-call | flops 2415919104 | bytes 8912896 | tf_op jit(solution)/shard_map/grad_rows/pallas_call | solution.py:689
  587.5 6.8 %grad_blocks.5 = (bf16[256,1024]{1,0:T(8,128)(2,1)}, bf16[256,1024]{1,0:T(8,128)(2,1)}) custom-call(bf16[1024,2048]{1,0:T(8,128)(2,1)} %copy-done.2, bf16[1024,2048]{1,0:T(8,128)(2,1)} %all-gather.11.cloned.1.call-done.refs_1_, bf16[1024,512]{1,0:T(8,128)(2,1)} %get-tuple-element.145.refs_2_.refs_1_, bf16[1024,512]{1,0:T(8,128)(2,1)} %gate_forward.1.refs_3_, ...), custom_call_target="tpu_custom_call" | custom-call | flops 67108864 | bytes 524288 | tf_op jit(solution)/shard_map/grad_blocks/pallas_call | solution.py:705
  596.6 5.0 all-to-all-start.4
  608.1 22.2 %collective-permute-done.36.refs_0_ = bf16[512,1152]{1,0:T(8,128)(2,1)} collective-permute-done((bf16[512,1152]{1,0:T(8,128)(2,1)}, bf16[512,1152]{1,0:T(8,128)(2,1)}, u32[]{:S(2)}, u32[]{:S(2)}) %collective-permute-start.36) | collective-permute-done | bytes 1179680 | tf_op jit(solution)/shard_map/ppermute | solution.py:182
  631.4 6.6 grad_rows.5
  638.0 4.7 all-to-all-start.5
  648.9 4.1 unpack_even.1
  659.0 13.2 %all-to-all-done.5 = bf16[8,64,1152]{2,1,0:T(8,128)(2,1)S(1)} async-done(((bf16[8,64,1152]{2,1,0:T(8,128)(2,1)}), bf16[8,64,1152]{2,1,0:T(8,128)(2,1)S(1)}, u32[]{:S(2)}, u32[]{:S(2)}) %all-to-all-start.5) | async-done | bytes 1179680 | tf_op jit(solution)/shard_map/all_to_all | solution.py:243
  (330 shorter events, 140.4 us)
Async XLA Ops:
  7.2 112.1 %copy-start = (f32[4,4096]{1,0:T(4,128)S(1)}, f32[4,4096]{1,0:T(4,128)}, u32[]{:S(2)}) copy-start(f32[4,4096]{1,0:T(4,128)} %param.32) | copy-start | bytes 196612
  11.1 12.1 %copy-start.21 = (bf16[1,128,2048]{2,1,0:T(8,128)(2,1)S(1)}, bf16[1,128,2048]{2,1,0:T(8,128)(2,1)}, u32[]{:S(2)}) copy-start(bf16[1,128,2048]{2,1,0:T(8,128)(2,1)} %param.21) | copy-start | bytes 1572868
  16.2 11.8 %copy-start.22 = (bf16[64,4096]{1,0:T(8,128)(2,1)S(1)}, bf16[64,4096]{1,0:T(8,128)(2,1)}, u32[]{:S(2)}) copy-start(bf16[64,4096]{1,0:T(8,128)(2,1)} %param.28) | copy-start | bytes 1572868
  16.2 37.2 %all-to-all-start = ((bf16[8,64,1152]{2,1,0:T(8,128)(2,1)}), bf16[8,64,1152]{2,1,0:T(8,128)(2,1)S(1)}, u32[]{:S(2)}, u32[]{:S(2)}) async-start(bf16[8,64,1152]{2,1,0:T(8,128)(2,1)} %bitcast.5), calls=%async_computation | async-start | bytes 2359296 | tf_op jit(solution)/shard_map/all_to_all | solution.py:239
  22.6 82.2 %all-gather.5.cloned.1.call-start = ((), (), s32[]{:S(2)}) async-start(), calls=%async_computation.10 | async-start | bytes 4718592 | tf_op jit(solution)/shard_map/all_gather | solution.py:924
  22.7 1.3 collective-permute-start
  24.0 18.8 %collective-permute-start.1 = (f32[2,128]{1,0:T(2,128)S(1)}, f32[2,128]{1,0:T(2,128)S(1)}, u32[]{:S(2)}, u32[]{:S(2)}) collective-permute-start(f32[2,128]{1,0:T(2,128)S(1)} %pad_maximum_fusion.9), channel_id=1, source_target_pairs={{0,2},{1,3},{2,0},{3,1},{4,6},{5,7},{6,4},{7,5},{8,10},{9,11},{10,... | collective-permute-start | bytes 3080 | tf_op jit(solution)/shard_map/ppermute | solution.py:265
  42.9 10.5 %collective-permute-start.2 = (f32[4,128]{1,0:T(4,128)S(1)}, f32[4,128]{1,0:T(4,128)S(1)}, u32[]{:S(2)}, u32[]{:S(2)}) collective-permute-start(f32[4,128]{1,0:T(4,128)S(1)} %pad_maximum_fusion.8), channel_id=1, source_target_pairs={{0,4},{1,5},{2,6},{3,7},{4,0},{5,1},{6,2},{7,3},{8,12},{9,13},{10,... | collective-permute-start | bytes 6152 | tf_op jit(solution)/shard_map/ppermute | solution.py:265
  53.4 27.3 %collective-permute-start.4 = (bf16[512,1152]{1,0:T(8,128)(2,1)S(1)}, bf16[512,1152]{1,0:T(8,128)(2,1)S(1)}, u32[]{:S(2)}, u32[]{:S(2)}) collective-permute-start(bf16[512,1152]{1,0:T(8,128)(2,1)S(1)} %bitcast.105), channel_id=1, source_target_pairs={{0,8},{8,24},{24,16},{16,0},{1,9},{9,25},{25,17},{17,1},{2,10},{10... | collective-permute-start | bytes 3538952 | tf_op jit(solution)/shard_map/ppermute | solution.py:132
  55.9 28.0 %collective-permute-start.3 = (bf16[512,1152]{1,0:T(8,128)(2,1)S(1)}, bf16[512,1152]{1,0:T(8,128)(2,1)}, u32[]{:S(2)}, u32[]{:S(2)}) collective-permute-start(bf16[512,1152]{1,0:T(8,128)(2,1)S(1)} %bitcast.106), channel_id=1, source_target_pairs={{8,0},{24,8},{16,24},{0,16},{9,1},{25,9},{17,25},{1,17},{10,2},{26... | collective-permute-start | bytes 3538952 | tf_op jit(solution)/shard_map/ppermute | solution.py:132
  61.2 21.8 %copy-start.12 = (bf16[128,4096]{1,0:T(8,128)(2,1)}, bf16[128,4096]{1,0:T(8,128)(2,1)S(1)}, u32[]{:S(2)}) copy-start(bf16[128,4096]{1,0:T(8,128)(2,1)S(1)} %slice_dynamic-update-slice_fusion.5) | copy-start | bytes 3145732
  81.6 14.1 %collective-permute-start.5 = (bf16[256,1152]{1,0:T(8,128)(2,1)}, bf16[256,1152]{1,0:T(8,128)(2,1)}, u32[]{:S(2)}, u32[]{:S(2)}) collective-permute-start(bf16[256,1152]{1,0:T(8,128)(2,1)} %slice.211), channel_id=1, source_target_pairs={{0,8},{8,24},{24,16},{16,0},{1,9},{9,25},{25,17},{17,1},{2,10},{10... | collective-permute-start | bytes 1769480 | tf_op jit(solution)/shard_map/ppermute | solution.py:141
  85.8 13.8 %collective-permute-start.6 = (bf16[256,1152]{1,0:T(8,128)(2,1)}, bf16[256,1152]{1,0:T(8,128)(2,1)}, u32[]{:S(2)}, u32[]{:S(2)}) collective-permute-start(bf16[256,1152]{1,0:T(8,128)(2,1)} %slice.212), channel_id=1, source_target_pairs={{8,0},{24,8},{16,24},{0,16},{9,1},{25,9},{17,25},{1,17},{10,2},{26... | collective-permute-start | bytes 1769480 | tf_op jit(solution)/shard_map/ppermute | solution.py:142
  87.5 33.5 %all-to-all-start.1 = ((bf16[8,64,1024]{2,1,0:T(8,128)(2,1)}), bf16[8,64,1024]{2,1,0:T(8,128)(2,1)}, u32[]{:S(2)}, u32[]{:S(2)}) async-start(bf16[8,64,1024]{2,1,0:T(8,128)(2,1)} %bitcast.7), calls=%async_computation.1 | async-start | bytes 2097152 | tf_op jit(solution)/shard_map/all_to_all | solution.py:239
  91.7 117.0 %all-gather.7.cloned.1.call-start = ((), (), s32[]{:S(2)}) async-start(), calls=%async_computation.11 | async-start | bytes 4718592 | tf_op jit(solution)/shard_map/all_gather | solution.py:943
  121.0 40.2 %collective-permute-start.7 = (bf16[512,1024]{1,0:T(8,128)(2,1)}, bf16[512,1024]{1,0:T(8,128)(2,1)}, u32[]{:S(2)}, u32[]{:S(2)}) collective-permute-start(bf16[512,1024]{1,0:T(8,128)(2,1)} %bitcast.8), channel_id=1, source_target_pairs={{0,8},{8,24},{24,16},{16,0},{1,9},{9,25},{25,17},{17,1},{2,10},{10... | collective-permute-start | bytes 3145736 | tf_op jit(solution)/shard_map/ppermute | solution.py:132
  122.5 38.7 %collective-permute-start.8 = (bf16[512,1024]{1,0:T(8,128)(2,1)}, bf16[512,1024]{1,0:T(8,128)(2,1)}, u32[]{:S(2)}, u32[]{:S(2)}) collective-permute-start(bf16[512,1024]{1,0:T(8,128)(2,1)} %bitcast.8), channel_id=1, source_target_pairs={{8,0},{24,8},{16,24},{0,16},{9,1},{25,9},{17,25},{1,17},{10,2},{26... | collective-permute-start | bytes 3145736 | tf_op jit(solution)/shard_map/ppermute | solution.py:132
  127.7 81.0 %all-to-all-start.2 = ((bf16[8,64,2112]{2,1,0:T(8,128)(2,1)}), bf16[8,64,2112]{2,1,0:T(8,128)(2,1)S(1)}, u32[]{:S(2)}, u32[]{:S(2)}) async-start(bf16[8,64,2112]{2,1,0:T(8,128)(2,1)} %bitcast.102), calls=%async_computation.2 | async-start | bytes 4456448 | tf_op jit(solution)/shard_map/all_to_all | solution.py:239
  131.3 132.5 %reduce-scatter.5.cloned.1.call-start = ((), (), s32[]{:S(2)}) async-start(), calls=%async_computation.12 | async-start | bytes 4718592 | tf_op jit(solution)/shard_map/reduce_scatter | solution.py:994
  162.3 14.2 %collective-permute-start.9 = (bf16[256,1024]{1,0:T(8,128)(2,1)S(1)}, bf16[256,1024]{1,0:T(8,128)(2,1)S(1)}, u32[]{:S(2)}, u32[]{:S(2)}) collective-permute-start(bf16[256,1024]{1,0:T(8,128)(2,1)S(1)} %slice.165), channel_id=1, source_target_pairs={{0,8},{8,24},{24,16},{16,0},{1,9},{9,25},{25,17},{17,1},{2,10},{10... | collective-permute-start | bytes 1572872 | tf_op jit(solution)/shard_map/ppermute | solution.py:141
  165.0 13.9 %collective-permute-start.10 = (bf16[256,1024]{1,0:T(8,128)(2,1)S(1)}, bf16[256,1024]{1,0:T(8,128)(2,1)S(1)}, u32[]{:S(2)}, u32[]{:S(2)}) collective-permute-start(bf16[256,1024]{1,0:T(8,128)(2,1)S(1)} %slice.166), channel_id=1, source_target_pairs={{8,0},{24,8},{16,24},{0,16},{9,1},{25,9},{17,25},{1,17},{10,2},{26... | collective-permute-start | bytes 1572872 | tf_op jit(solution)/shard_map/ppermute | solution.py:142
  166.8 13.5 %copy-start.3 = (bf16[1024,2048]{1,0:T(8,128)(2,1)S(1)}, bf16[1024,2048]{1,0:T(8,128)(2,1)}, u32[]{:S(2)}) copy-start(bf16[1024,2048]{1,0:T(8,128)(2,1)} %copy-done.2) | copy-start | bytes 12582916
  214.9 98.2 %all-gather.9.cloned.1.call-start = ((), (), s32[]{:S(2)}) async-start(), calls=%async_computation.13 | async-start | bytes 4718592 | tf_op jit(solution)/shard_map/all_gather | solution.py:1006
  217.5 49.7 %collective-permute-start.11 = (bf16[512,2112]{0,1:T(8,128)(2,1)}, bf16[512,2112]{0,1:T(8,128)(2,1)}, u32[]{:S(2)}, u32[]{:S(2)}) collective-permute-start(bf16[512,2112]{0,1:T(8,128)(2,1)} %copy.178), channel_id=1, source_target_pairs={{0,8},{8,24},{24,16},{16,0},{1,9},{9,25},{25,17},{17,1},{2,10},{10... | collective-permute-start | bytes 6488072 | tf_op jit(solution)/shard_map/ppermute | solution.py:132
  219.0 48.9 %collective-permute-start.12 = (bf16[512,2112]{0,1:T(8,128)(2,1)}, bf16[512,2112]{0,1:T(8,128)(2,1)}, u32[]{:S(2)}, u32[]{:S(2)}) collective-permute-start(bf16[512,2112]{0,1:T(8,128)(2,1)} %copy.178), channel_id=1, source_target_pairs={{8,0},{24,8},{16,24},{0,16},{9,1},{25,9},{17,25},{1,17},{10,2},{26... | collective-permute-start | bytes 6488072 | tf_op jit(solution)/shard_map/ppermute | solution.py:132
  267.9 122.6 %reduce-scatter.7.cloned.1.call-start = ((), (), s32[]{:S(2)}) async-start(), calls=%async_computation.14 | async-start | bytes 4718592 | tf_op jit(solution)/shard_map/reduce_scatter | solution.py:1022
  270.3 24.8 %collective-permute-start.13 = (bf16[256,2112]{0,1:T(8,128)(2,1)}, bf16[256,2112]{0,1:T(8,128)(2,1)}, u32[]{:S(2)}, u32[]{:S(2)}) collective-permute-start(bf16[256,2112]{0,1:T(8,128)(2,1)} %slice.173), channel_id=1, source_target_pairs={{0,8},{8,24},{24,16},{16,0},{1,9},{9,25},{25,17},{17,1},{2,10},{10... | collective-permute-start | bytes 3244040 | tf_op jit(solution)/shard_map/ppermute | solution.py:141
  274.2 24.8 %collective-permute-start.14 = (bf16[256,2112]{0,1:T(8,128)(2,1)}, bf16[256,2112]{0,1:T(8,128)(2,1)}, u32[]{:S(2)}, u32[]{:S(2)}) collective-permute-start(bf16[256,2112]{0,1:T(8,128)(2,1)} %slice.174), channel_id=1, source_target_pairs={{8,0},{24,8},{16,24},{0,16},{9,1},{25,9},{17,25},{1,17},{10,2},{26... | collective-permute-start | bytes 3244040 | tf_op jit(solution)/shard_map/ppermute | solution.py:142
  341.1 110.1 %all-gather.11.cloned.1.call-start = ((), (), s32[]{:S(2)}) async-start(), calls=%async_computation.15 | async-start | bytes 4718592 | tf_op jit(solution)/shard_map/all_gather | solution.py:1034
  343.9 38.5 %collective-permute-start.15 = (bf16[256,1408]{1,0:T(8,128)(2,1)S(1)}, bf16[256,1408]{1,0:T(8,128)(2,1)S(1)}, u32[]{:S(2)}, u32[]{:S(2)}) collective-permute-start(bf16[256,1408]{1,0:T(8,128)(2,1)S(1)} %convolution_convert_fusion.3), channel_id=1, source_target_pairs={{0,8},{8,24},{24,16},{16,0},{1,9},{9,25},{25,17},{17,1},{2,10},{10... | collective-permute-start | bytes 2162696 | tf_op jit(solution)/shard_map/ppermute | solution.py:157
  349.3 33.1 %collective-permute-start.16 = (bf16[256,1408]{1,0:T(8,128)(2,1)}, bf16[256,1408]{1,0:T(8,128)(2,1)S(1)}, u32[]{:S(2)}, u32[]{:S(2)}) collective-permute-start(bf16[256,1408]{1,0:T(8,128)(2,1)} %convolution_convert_fusion.2), channel_id=1, source_target_pairs={{8,0},{24,8},{16,24},{0,16},{9,1},{25,9},{17,25},{1,17},{10,2},{26... | collective-permute-start | bytes 2162696 | tf_op jit(solution)/shard_map/ppermute | solution.py:158
  352.2 18.2 %collective-permute-start.17 = (bf16[256,704]{0,1:T(8,128)(2,1)}, bf16[256,704]{0,1:T(8,128)(2,1)}, u32[]{:S(2)}, u32[]{:S(2)}) collective-permute-start(bf16[256,704]{0,1:T(8,128)(2,1)} %convolution_convert_fusion.5), channel_id=1, source_target_pairs={{0,8},{8,24},{24,16},{16,0},{1,9},{9,25},{25,17},{17,1},{2,10},{10... | collective-permute-start | bytes 1081352 | tf_op jit(solution)/shard_map/ppermute | solution.py:157
  356.0 19.4 %collective-permute-start.18 = (bf16[256,704]{0,1:T(8,128)(2,1)}, bf16[256,704]{0,1:T(8,128)(2,1)}, u32[]{:S(2)}, u32[]{:S(2)}) collective-permute-start(bf16[256,704]{0,1:T(8,128)(2,1)} %convolution_convert_fusion.4), channel_id=1, source_target_pairs={{8,0},{24,8},{16,24},{0,16},{9,1},{25,9},{17,25},{1,17},{10,2},{26... | collective-permute-start | bytes 1081352 | tf_op jit(solution)/shard_map/ppermute | solution.py:158
  363.6 15.5 %copy-start.52 = (bf16[1024,704]{0,1:T(8,128)(2,1)S(1)}, bf16[1024,704]{0,1:T(8,128)(2,1)}, u32[]{:S(2)}) copy-start(bf16[1024,704]{0,1:T(8,128)(2,1)} %get-tuple-element.206) | copy-start | bytes 4325380
  394.3 185.9 %reduce-scatter.9.cloned.1.call-start = ((), (), s32[]{:S(2)}) async-start(), calls=%async_computation.16 | async-start | bytes 4718592 | tf_op jit(solution)/shard_map/reduce_scatter | solution.py:1038
  394.4 49.7 %copy-start.53 = (bf16[1024,704]{0,1:T(8,128)(2,1)S(1)}, bf16[1024,704]{0,1:T(8,128)(2,1)}, u32[]{:S(2)}) copy-start(bf16[1024,704]{0,1:T(8,128)(2,1)} %get-tuple-element.206) | copy-start | bytes 4325380
  394.4 52.2 %collective-permute-start.19 = (bf16[512,1408]{1,0:T(8,128)(2,1)}, bf16[512,1408]{1,0:T(8,128)(2,1)}, u32[]{:S(2)}, u32[]{:S(2)}) collective-permute-start(bf16[512,1408]{1,0:T(8,128)(2,1)} %add_convert_fusion.2), channel_id=1, source_target_pairs={{0,8},{8,24},{24,16},{16,0},{1,9},{9,25},{25,17},{17,1},{2,10},{10... | collective-permute-start | bytes 4325384 | tf_op jit(solution)/shard_map/ppermute | solution.py:182
  396.0 50.5 %collective-permute-start.20 = (bf16[512,1408]{1,0:T(8,128)(2,1)}, bf16[512,1408]{1,0:T(8,128)(2,1)}, u32[]{:S(2)}, u32[]{:S(2)}) collective-permute-start(bf16[512,1408]{1,0:T(8,128)(2,1)} %add_convert_fusion.1), channel_id=1, source_target_pairs={{8,0},{24,8},{16,24},{0,16},{9,1},{25,9},{17,25},{1,17},{10,2},{26... | collective-permute-start | bytes 4325384 | tf_op jit(solution)/shard_map/ppermute | solution.py:183
  396.4 46.3 %collective-permute-start.21 = (bf16[512,704]{0,1:T(8,128)(2,1)}, bf16[512,704]{0,1:T(8,128)(2,1)S(1)}, u32[]{:S(2)}, u32[]{:S(2)}) collective-permute-start(bf16[512,704]{0,1:T(8,128)(2,1)} %fusion.22), channel_id=1, source_target_pairs={{0,8},{8,24},{24,16},{16,0},{1,9},{9,25},{25,17},{17,1},{2,10},{10... | collective-permute-start | bytes 2162696 | tf_op jit(solution)/shard_map/ppermute | solution.py:182
  398.0 46.0 %collective-permute-start.22 = (bf16[512,704]{0,1:T(8,128)(2,1)}, bf16[512,704]{0,1:T(8,128)(2,1)S(1)}, u32[]{:S(2)}, u32[]{:S(2)}) collective-permute-start(bf16[512,704]{0,1:T(8,128)(2,1)} %fusion.23), channel_id=1, source_target_pairs={{8,0},{24,8},{16,24},{0,16},{9,1},{25,9},{17,25},{1,17},{10,2},{26... | collective-permute-start | bytes 2162696 | tf_op jit(solution)/shard_map/ppermute | solution.py:183
  451.2 88.6 %all-to-all-start.3 = ((bf16[8,64,2112]{2,1,0:T(8,128)(2,1)}), bf16[8,64,2112]{2,1,0:T(8,128)(2,1)}, u32[]{:S(2)}, u32[]{:S(2)}) async-start(bf16[8,64,2112]{2,1,0:T(8,128)(2,1)} %bitcast.103), calls=%async_computation.5 | async-start | bytes 4456448 | tf_op jit(solution)/shard_map/all_to_all | solution.py:239
  455.6 151.1 %reduce-scatter.11.cloned.1.call-start = ((), (), s32[]{:S(2)}) async-start(), calls=%async_computation.17 | async-start | bytes 4718592 | tf_op jit(solution)/shard_map/reduce_scatter | solution.py:1063
  475.1 49.5 %collective-permute-start.23 = (bf16[256,1024]{1,0:T(8,128)(2,1)}, bf16[256,1024]{1,0:T(8,128)(2,1)S(1)}, u32[]{:S(2)}, u32[]{:S(2)}) collective-permute-start(bf16[256,1024]{1,0:T(8,128)(2,1)} %get-tuple-element.146), channel_id=1, source_target_pairs={{0,8},{8,24},{24,16},{16,0},{1,9},{9,25},{25,17},{17,1},{2,10},{10... | collective-permute-start | bytes 1572872 | tf_op jit(solution)/shard_map/ppermute | solution.py:205
  475.7 49.0 %collective-permute-start.24 = (bf16[256,1024]{1,0:T(8,128)(2,1)}, bf16[256,1024]{1,0:T(8,128)(2,1)S(1)}, u32[]{:S(2)}, u32[]{:S(2)}) collective-permute-start(bf16[256,1024]{1,0:T(8,128)(2,1)} %get-tuple-element.147), channel_id=1, source_target_pairs={{8,0},{24,8},{16,24},{0,16},{9,1},{25,9},{17,25},{1,17},{10,2},{26... | collective-permute-start | bytes 1572872 | tf_op jit(solution)/shard_map/ppermute | solution.py:206
  477.2 47.5 %collective-permute-start.25 = (bf16[256,1024]{1,0:T(8,128)(2,1)}, bf16[256,1024]{1,0:T(8,128)(2,1)S(1)}, u32[]{:S(2)}, u32[]{:S(2)}) collective-permute-start(bf16[256,1024]{1,0:T(8,128)(2,1)} %get-tuple-element.148), channel_id=1, source_target_pairs={{0,8},{8,24},{24,16},{16,0},{1,9},{9,25},{25,17},{17,1},{2,10},{10... | collective-permute-start | bytes 1572872 | tf_op jit(solution)/shard_map/ppermute | solution.py:207
  477.7 47.0 %collective-permute-start.26 = (bf16[256,1024]{1,0:T(8,128)(2,1)}, bf16[256,1024]{1,0:T(8,128)(2,1)S(1)}, u32[]{:S(2)}, u32[]{:S(2)}) collective-permute-start(bf16[256,1024]{1,0:T(8,128)(2,1)} %get-tuple-element.149), channel_id=1, source_target_pairs={{8,0},{24,8},{16,24},{0,16},{9,1},{25,9},{17,25},{1,17},{10,2},{26... | collective-permute-start | bytes 1572872 | tf_op jit(solution)/shard_map/ppermute | solution.py:208
  524.7 15.1 %copy-start.31 = (bf16[256,1024]{1,0:T(8,128)(2,1)}, bf16[256,1024]{1,0:T(8,128)(2,1)S(1)}, u32[]{:S(2)}) copy-start(bf16[256,1024]{1,0:T(8,128)(2,1)S(1)} %collective-permute-done.25.refs_5_) | copy-start | bytes 1572868
  524.7 15.0 %copy-start.32 = (bf16[256,1024]{1,0:T(8,128)(2,1)}, bf16[256,1024]{1,0:T(8,128)(2,1)S(1)}, u32[]{:S(2)}) copy-start(bf16[256,1024]{1,0:T(8,128)(2,1)S(1)} %collective-permute-done.26.refs_6_) | copy-start | bytes 1572868
  524.7 4.2 collective-permute-start.27
  529.7 10.1 %collective-permute-start.28 = (f32[8,1024]{1,0:T(8,128)S(1)}, f32[8,1024]{1,0:T(8,128)S(1)}, u32[]{:S(2)}, u32[]{:S(2)}) collective-permute-start(f32[8,1024]{1,0:T(8,128)S(1)} %add.157), channel_id=1, source_target_pairs={{0,16},{8,24},{16,0},{24,8},{1,17},{9,25},{17,1},{25,9},{2,18},{10... | collective-permute-start | bytes 98312 | tf_op jit(solution)/shard_map/ppermute | solution.py:253
  552.6 2.2 collective-permute-start.29
  552.7 26.0 %collective-permute-start.32 = (bf16[256,1024]{1,0:T(8,128)(2,1)}, bf16[256,1024]{1,0:T(8,128)(2,1)S(1)}, u32[]{:S(2)}, u32[]{:S(2)}) collective-permute-start(bf16[256,1024]{1,0:T(8,128)(2,1)} %get-tuple-element.162), channel_id=1, source_target_pairs={{0,8},{8,24},{24,16},{16,0},{1,9},{9,25},{25,17},{17,1},{2,10},{10... | collective-permute-start | bytes 1572872 | tf_op jit(solution)/shard_map/ppermute | solution.py:221
  553.3 25.4 %collective-permute-start.33 = (bf16[256,1024]{1,0:T(8,128)(2,1)}, bf16[256,1024]{1,0:T(8,128)(2,1)S(1)}, u32[]{:S(2)}, u32[]{:S(2)}) collective-permute-start(bf16[256,1024]{1,0:T(8,128)(2,1)} %get-tuple-element.163), channel_id=1, source_target_pairs={{8,0},{24,8},{16,24},{0,16},{9,1},{25,9},{17,25},{1,17},{10,2},{26... | collective-permute-start | bytes 1572872 | tf_op jit(solution)/shard_map/ppermute | solution.py:222
  554.8 9.7 %collective-permute-start.30 = (f32[16,1024]{1,0:T(8,128)S(1)}, f32[16,1024]{1,0:T(8,128)S(1)}, u32[]{:S(2)}, u32[]{:S(2)}) collective-permute-start(f32[16,1024]{1,0:T(8,128)S(1)} %pad_maximum_fusion.5), channel_id=1, source_target_pairs={{0,2},{1,3},{2,0},{3,1},{4,6},{5,7},{6,4},{7,5},{8,10},{9,11},{10,... | collective-permute-start | bytes 196616 | tf_op jit(solution)/shard_map/ppermute | solution.py:265
  562.3 17.7 %collective-permute-start.34 = (bf16[256,1152]{1,0:T(8,128)(2,1)}, bf16[256,1152]{1,0:T(8,128)(2,1)}, u32[]{:S(2)}, u32[]{:S(2)}) collective-permute-start(bf16[256,1152]{1,0:T(8,128)(2,1)} %get-tuple-element.170), channel_id=1, source_target_pairs={{0,8},{8,24},{24,16},{16,0},{1,9},{9,25},{25,17},{17,1},{2,10},{10... | collective-permute-start | bytes 1769480 | tf_op jit(solution)/shard_map/ppermute | solution.py:157
  562.6 17.6 %collective-permute-start.35 = (bf16[256,1152]{1,0:T(8,128)(2,1)}, bf16[256,1152]{1,0:T(8,128)(2,1)}, u32[]{:S(2)}, u32[]{:S(2)}) collective-permute-start(bf16[256,1152]{1,0:T(8,128)(2,1)} %get-tuple-element.171), channel_id=1, source_target_pairs={{8,0},{24,8},{16,24},{0,16},{9,1},{25,9},{17,25},{1,17},{10,2},{26... | collective-permute-start | bytes 1769480 | tf_op jit(solution)/shard_map/ppermute | solution.py:158
  564.6 14.1 %collective-permute-start.31 = (f32[32,1024]{1,0:T(8,128)S(1)}, f32[32,1024]{1,0:T(8,128)S(1)}, u32[]{:S(2)}, u32[]{:S(2)}) collective-permute-start(f32[32,1024]{1,0:T(8,128)S(1)} %pad_maximum_fusion.4), channel_id=1, source_target_pairs={{0,4},{1,5},{2,6},{3,7},{4,0},{5,1},{6,2},{7,3},{8,12},{9,13},{10,... | collective-permute-start | bytes 393224 | tf_op jit(solution)/shard_map/ppermute | solution.py:265
  594.3 12.4 %copy-start.38 = (f32[2048]{0:T(1024)S(1)}, f32[2048]{0:T(1024)}, u32[]{:S(2)}) copy-start(f32[2048]{0:T(1024)} %copy-done.37) | copy-start | bytes 24580
  596.6 34.8 %all-to-all-start.4 = ((bf16[8,64,1024]{2,1,0:T(8,128)(2,1)}), bf16[8,64,1024]{2,1,0:T(8,128)(2,1)S(1)}, u32[]{:S(2)}, u32[]{:S(2)}) async-start(bf16[8,64,1024]{2,1,0:T(8,128)(2,1)} %bitcast.112), calls=%async_computation.7 | async-start | bytes 2097152 | tf_op jit(solution)/shard_map/all_to_all | solution.py:243
  601.6 28.7 %collective-permute-start.36 = (bf16[512,1152]{1,0:T(8,128)(2,1)}, bf16[512,1152]{1,0:T(8,128)(2,1)}, u32[]{:S(2)}, u32[]{:S(2)}) collective-permute-start(bf16[512,1152]{1,0:T(8,128)(2,1)} %get-tuple-element.181), channel_id=1, source_target_pairs={{0,8},{8,24},{24,16},{16,0},{1,9},{9,25},{25,17},{17,1},{2,10},{10... | collective-permute-start | bytes 3538952 | tf_op jit(solution)/shard_map/ppermute | solution.py:182
  603.0 28.4 %collective-permute-start.37 = (bf16[512,1152]{1,0:T(8,128)(2,1)}, bf16[512,1152]{1,0:T(8,128)(2,1)}, u32[]{:S(2)}, u32[]{:S(2)}) collective-permute-start(bf16[512,1152]{1,0:T(8,128)(2,1)} %get-tuple-element.182), channel_id=1, source_target_pairs={{8,0},{24,8},{16,24},{0,16},{9,1},{25,9},{17,25},{1,17},{10,2},{26... | collective-permute-start | bytes 3538952 | tf_op jit(solution)/shard_map/ppermute | solution.py:183
  608.1 34.7 %copy-start.6 = (bf16[128,2048]{1,0:T(8,128)(2,1)S(1)}, bf16[128,2048]{1,0:T(8,128)(2,1)}, u32[]{:S(2)}) copy-start(bf16[128,2048]{1,0:T(8,128)(2,1)} %reduce-scatter.7.cloned.1.call-done) | copy-start | bytes 1572868
  638.0 34.2 %all-to-all-start.5 = ((bf16[8,64,1152]{2,1,0:T(8,128)(2,1)}), bf16[8,64,1152]{2,1,0:T(8,128)(2,1)S(1)}, u32[]{:S(2)}, u32[]{:S(2)}) async-start(bf16[8,64,1152]{2,1,0:T(8,128)(2,1)} %bitcast.104), calls=%async_computation.9 | async-start | bytes 2359296 | tf_op jit(solution)/shard_map/all_to_all | solution.py:243
  658.1 14.8 %copy-start.23 = (bf16[64,4096]{1,0:T(8,128)(2,1)S(1)}, bf16[64,4096]{1,0:T(8,128)(2,1)}, u32[]{:S(2)}) copy-start(bf16[64,4096]{1,0:T(8,128)(2,1)} %param.25) | copy-start | bytes 1572868
  (49 other events, 226.2 us)
Sparse Core Ops, SparseCore 0:
  53.5 47.2 all-gather.4
  117.3 81.9 all-gather.6
  215.1 48.7 reduce-scatter.4
  268.0 45.0 all-gather.8
  341.2 48.7 reduce-scatter.6
  394.4 45.0 all-gather.10
  451.3 89.2 reduce-scatter.8
  552.7 53.1 reduce-scatter.10

commit v8 on v7

--- a/solution.py
+++ b/solution.py
@@ -633,6 +633,27 @@
         out_ref[r * rows : (r + 1) * rows, :] = jnp.concatenate(pieces, axis=1).astype(BF)
 
 
+def mix_pack_kernel(ranks, hp, vs, q_ref, k_ref, v_ref, decay_ref, beta_ref, gain_ref, out_ref):
+    rows = q_ref.shape[0]
+    groups = ranks // vs
+    k_wide, v_wide = q_ref.shape[1] // groups, v_ref.shape[1] // ranks
+    lane = lax.broadcasted_iota(jnp.int32, (rows, LANES), 1)
+    decay, beta = decay_ref[...].astype(F32), beta_ref[...].astype(F32)
+    gain = gain_ref[...].astype(F32)
+    for r in range(ranks):
+        at, g = slice(r * rows, (r + 1) * rows), r // vs
+        out_ref[at, :k_wide] = q_ref[:, g * k_wide : (g + 1) * k_wide]
+        out_ref[at, k_wide : 2 * k_wide] = k_ref[:, g * k_wide : (g + 1) * k_wide]
+        out_ref[at, 2 * k_wide : 2 * k_wide + v_wide] = v_ref[:, r * v_wide : (r + 1) * v_wide]
+        small = jnp.zeros((rows, LANES), F32)
+        for j in range(hp):
+            small = jnp.where(lane == j, decay[:, g * hp + j : g * hp + j + 1], small)
+            small = jnp.where(lane == hp + j, beta[:, g * hp + j : g * hp + j + 1], small)
+        small = jnp.where(lane == 2 * hp, gain[:, 0:1], small)
+        small = jnp.where(lane == 2 * hp + 1, gain[:, 1:2], small)
+        out_ref[at, 2 * k_wide + v_wide :] = small.astype(BF)
+
+
 def unpack_kernel(ranks, in_ref, *outs):
     rows = outs[0].shape[0]
     for i, out_ref in enumerate(outs):
@@ -722,16 +743,18 @@
     refs[-1][...] = total.astype(BF)
 
 
-def back_product(*pairs):
-    total, wide = pairs[0][0].shape[0], pairs[0][1].shape[0]
+def column_block(at):
+    return lambda i: (0, at)
+
+
+def back_product(*terms):
+    total, wide = terms[0][0].shape[0], terms[0][1].shape[0]
     rows = 256
-    lefts = [a for a, _ in pairs]
-    rights = [b for _, b in pairs]
     return pl.pallas_call(
-        functools.partial(back_kernel, len(pairs)),
+        functools.partial(back_kernel, len(terms)),
         grid=(total // rows,),
-        in_specs=[pl.BlockSpec((rows, a.shape[1]), lambda i: (i, 0)) for a in lefts]
-        + [pl.BlockSpec(b.shape, lambda i: (0, 0)) for b in rights],
+        in_specs=[pl.BlockSpec((rows, a.shape[1]), lambda i: (i, 0)) for a, _, _ in terms]
+        + [pl.BlockSpec((wide, a.shape[1]), column_block(at)) for a, _, at in terms],
         out_specs=pl.BlockSpec((rows, wide), lambda i: (i, 0)),
         out_shape=shape_of(total, wide, dtype=BF),
         compiler_params=pltpu.CompilerParams(vmem_limit_bytes=VMEM_LIMIT),
@@ -739,7 +762,7 @@
             flops=total * wide * 256, transcendentals=0, bytes_accessed=total * wide
         ),
         name="back_product",
-    )(*lefts, *rights)
+    )(*(a for a, _, _ in terms), *(b for _, b, _ in terms))
 
 
 def pack_even(ranks, *arrays):
@@ -751,6 +774,17 @@
         compiler_params=pltpu.CompilerParams(vmem_limit_bytes=VMEM_LIMIT),
         name="pack_even",
     )(*arrays)
+
+
+def pack_mix(ranks, hp, vs, w_query, w_key, w_value, *smalls):
+    rows = w_query.shape[0]
+    wide = 2 * w_query.shape[1] * vs // ranks + w_value.shape[1] // ranks + LANES
+    return pl.pallas_call(
+        functools.partial(mix_pack_kernel, ranks, hp, vs),
+        out_shape=shape_of(ranks * rows, wide, dtype=BF),
+        compiler_params=pltpu.CompilerParams(vmem_limit_bytes=VMEM_LIMIT),
+        name="pack_mix",
+    )(w_query, w_key, w_value, *smalls)
 
 
 def unpack_even(ranks, packed, count):
@@ -891,27 +925,8 @@
 
     own_tokens = to_ring(tokens[0])
     own_cot = to_ring(cotangent[0])
-    small = jnp.concatenate(
-        [
-            plan.split_keys(w_decay),
-            plan.split_keys(w_beta),
-            jnp.broadcast_to(attn_gain[:, None, None], (rows, ranks, 1)),
-            jnp.broadcast_to(mlp_gain[:, None, None], (rows, ranks, 1)),
-            jnp.zeros((rows, ranks, LANES - 2 - 2 * hp), BF),
-        ],
-        axis=2,
-    )
-    mix_pack = rank_major(
-        jnp.concatenate(
-            [
-                plan.split_keys(w_query),
-                plan.split_keys(w_key),
-                plan.split_even(w_value),
-                small,
-            ],
-            axis=2,
-        )
-    )
+    gains = jnp.stack([attn_gain, mlp_gain], axis=1)
+    mix_pack = pack_mix(ranks, hp, vs, w_query, w_key, w_value, w_decay, w_beta, gains)
     side_pack = rank_major(
         jnp.concatenate([plan.split_even(w_gate), plan.split_even(w_out)], axis=2)
     )
@@ -990,9 +1005,8 @@
         gated = gate_forward(mixed, pre_gate, own_gain[None], hp, dv)
     else:
         gated = gate_apply(mixed, pre_gate, own_gain).astype(BF)
-    gated = after(gated, mlp_own_cols, cot_all)
     branch = lax.psum_scatter(
-        nt(gated, out_cols).astype(BF), "seq", scatter_dimension=0, tiled=True
+        after(nt(gated, out_cols).astype(BF), mlp_own_cols, cot_all), "seq", scatter_dimension=0, tiled=True
     )
     inputs = own_tokens.astype(F32)
     middle = inputs + branch.astype(F32)
@@ -1059,7 +1073,7 @@
     d_sums = sum_dp(d_sums)
     held = lax.optimization_barrier((d_pre, d_sums, mlp_rows) + side_sum.sums)
     d_pre, d_sums, mlp_rows = held[:3]
-    d_attn_part = back_product((d_pre, w_mix), (d_gate, gate_cols))
+    d_attn_part = back_product((d_pre, w_mix, 0), (d_gate, w_side, 0))
     d_attn = lax.psum_scatter(d_attn_part, "seq", scatter_dimension=0, tiled=True).astype(F32)
     mix_sum = RingGrad(attn, after(d_pre, d_attn_part))
     every = gather_small(after(d_sums, d_attn_part))

time: 692 us -> 685 us (0.990)
    unnamed x146 -> x152, local copies, waits for them, and re-layouts: 31.1 us -> 37.5 us
    pallas_call x1 -> x2, Pallas kernels: 12.8 us -> 15.2 us  [the longest x1 12.7 us: back_product(): pl.pallas_call(functools.partial(back_kernel, len(terms)), grid=(total //...]
  transfers between devices with their start and end apart: 52 -> 52, of which waited for: 24 -> 25; matrix products, arithmetic and copies ran while one was open for 23% -> 25% of each run, Pallas kernels for 20% -> 21%
where the time goes in v8:
time: 685 us; the launch traced here: 675 us
  waiting for transfers between devices  231 us (34%)
  Pallas kernels  148 us (22%)
  matrix products  94.6 us (14%)
  local copies, waits for them, and re-layouts  79.7 us (12%)
  starting transfers between devices  69.9 us (10%)
  other arithmetic  36.6 us (5%)
  between operations  15.6 us (2%)
    dot_general x19, matrix products, dot_f32(): lax.dot_general(left, right, (dims, ((), ())), preferred_element_type=F32)  94.6 us
    ppermute x4, waiting for transfers between devices, second(): lax.ppermute(self.sums[0], 'dp', to_right)  60.4 us
    pallas_call x1, Pallas kernels, delta_backward(): pl.pallas_call(functools.partial(bwd_kernel, hp, dk, dv), out_shape=(shap...  45.3 us
    reduce_scatter x1, waiting for transfers between devices, local(): lax.psum_scatter(after(nt(gated, out_cols).astype(BF), mlp_own_cols, cot_...  44.2 us
    unnamed x152, local copies, waits for them, and re-layouts  37.5 us
    pallas_call x1, Pallas kernels, delta_forward(): pl.pallas_call(functools.partial(fwd_kernel, hp, dk, dv), out_shape=(shap...  29.6 us
    ppermute x6, waiting for transfers between devices, gather_small(): other = lax.ppermute(values, 'seq', [(i, i ^ step) for i in range(ranks)])  26.6 us
    pallas_call x3, Pallas kernels, grad_blocks(): pl.pallas_call(functools.partial(block_kernel, half, blocks, len(pairs),...  20.5 us
  transfers between devices with their start and end apart: 52, of which 25 were waited for; matrix products, arithmetic and copies ran while one was open for 25% of the time, Pallas kernels for 21%

profile of v8, /device:TPU:0, one launch (start us, length us, event | category | flops | bytes accessed | tf_op | source)
XLA Modules:
  0.0 675.1 jit_solution(3807326412331034357)
XLA Ops:
  11.4 2.5 pack_mix.1
  13.9 6.5 all-to-all-start
  27.5 13.1 %collective-permute-done.1 = f32[2,128]{1,0:T(2,128)S(1)} collective-permute-done((f32[2,128]{1,0:T(2,128)S(1)}, f32[2,128]{1,0:T(2,128)S(1)}, u32[]{:S(2)}, u32[]{:S(2)}) %collective-permute-start.1) | collective-permute-done | bytes 1056 | tf_op jit(solution)/shard_map/ppermute | solution.py:265
  40.6 4.5 collective-permute-start.2
  48.0 3.3 pack_even.1
  59.1 19.5 %collective-permute-done.4 = bf16[512,1152]{1,0:T(8,128)(2,1)S(1)} collective-permute-done((bf16[512,1152]{1,0:T(8,128)(2,1)S(1)}, bf16[512,1152]{1,0:T(8,128)(2,1)S(1)}, u32[]{:S(2)}, u32[]{:S(2)}) %collective-permute-start.4) | collective-permute-done | bytes 1179680 | tf_op jit(solution)/shard_map/ppermute | solution.py:132
  86.4 4.3 all-to-all-start.1
  90.7 2.6 constant_dynamic-update-slice_fusion.3
  103.6 3.2 fusion
  110.2 5.7 fusion.18.pre_ref
  121.8 4.7 fusion.52.small_ref
  126.5 3.6 all-to-all-start.2
  130.3 29.6 %delta_forward.1 = (f32[1024,512]{1,0:T(8,128)}, f32[16,128,256]{2,1,0:T(8,128)}, f32[1024,512]{1,0:T(8,128)}, f32[16,128,128]{2,1,0:T(8,128)}, f32[1024,256]{1,0:T(8,128)}) custom-call(bf16[1024,1024]{1,0:T(8,128)(2,1)} %fusion.18.pre_ref, f32[1024,128]{1,0:T(8,128)} %fusion.52.small_ref, f32[1024,128]{1,0:T(8,128)} %pad.36.rider_ref, ...), custom_call_target="tpu_custom_call" | custom-call | flops 43008000000 | bytes 16777216 | tf_op jit(solution)/shard_map/delta_forward/pallas_call | solution.py:804
  167.0 8.3 %collective-permute-done.9 = bf16[256,1024]{1,0:T(8,128)(2,1)S(1)} collective-permute-done((bf16[256,1024]{1,0:T(8,128)(2,1)S(1)}, bf16[256,1024]{1,0:T(8,128)(2,1)S(1)}, u32[]{:S(2)}, u32[]{:S(2)}) %collective-permute-start.9) | collective-permute-done | bytes 524320 | tf_op jit(solution)/shard_map/ppermute | solution.py:141
  175.3 2.4 collective-permute-done.10
  179.1 3.7 fusion.16.gate_ref
  182.8 4.3 gate_forward.1.refs_3_
  187.1 6.3 convolution_convert_fusion.1
  193.3 13.9 %all-to-all-done.2 = bf16[8,64,2112]{2,1,0:T(8,128)(2,1)S(1)} async-done(((bf16[8,64,2112]{2,1,0:T(8,128)(2,1)}), bf16[8,64,2112]{2,1,0:T(8,128)(2,1)S(1)}, u32[]{:S(2)}, u32[]{:S(2)}) %all-to-all-start.2) | async-done | bytes 2162720 | tf_op jit(solution)/shard_map/all_to_all | solution.py:239
  207.3 2.5 copy.169
  211.9 44.2 %reduce-scatter.5.cloned.1.call-done = bf16[128,2048]{1,0:T(8,128)(2,1)} async-done(((bf16[1024,2048]{1,0:T(8,128)(2,1)}), bf16[128,2048]{1,0:T(8,128)(2,1)}) %reduce-scatter.5.cloned.1.call-update) | async-done | bytes 524304 | tf_op jit(solution)/shard_map/reduce_scatter | solution.py:1008
  264.1 2.3 slice.174
  268.7 4.1 copy.171
  272.7 2.9 copy.174
  275.7 3.2 constant_dynamic-update-slice_fusion.13
  278.9 8.6 %collective-permute-done.13 = bf16[256,2112]{0,1:T(8,128)(2,1)} collective-permute-done((bf16[256,2112]{0,1:T(8,128)(2,1)}, bf16[256,2112]{0,1:T(8,128)(2,1)}, u32[]{:S(2)}, u32[]{:S(2)}) %collective-permute-start.13) | collective-permute-done | bytes 1081376 | tf_op jit(solution)/shard_map/ppermute | solution.py:141
  287.5 2.3 copy.172
  291.1 2.3 copy.173
  293.5 2.4 constant_dynamic-update-slice_fusion.12
  298.6 6.8 %all-gather.9.cloned.1.call-done = bf16[1024,2048]{1,0:T(8,128)(2,1)} async-done(((bf16[128,2048]{1,0:T(8,128)(2,1)}), bf16[1024,2048]{1,0:T(8,128)(2,1)}) %all-gather.9.cloned.1.call-update) | async-done | bytes 4194320 | tf_op jit(solution)/shard_map/all_gather | solution.py:1020
  305.4 11.5 %fusion.5 = f32[1024,1408]{0,1:T(8,128)} fusion(bf16[1024,2048]{1,0:T(8,128)(2,1)} %all-gather.9.cloned.1.call-done, bf16[2048,2112]{1,0:T(8,128)(2,1)} %constant_dynamic-update-slice_fusion.10), kind=kOutput, calls=%fused_computation.7 | convolution fusion | flops 5905580032 | bytes 15728640 | tf_op jit(solution)/shard_map/dot_general | solution.py:22
  316.9 7.1 %multiply_convert_fusion.2 = (bf16[1024,704]{0,1:T(8,128)(2,1)S(1)}, bf16[1024,704]{0,1:T(8,128)(2,1)S(1)}, bf16[1024,704]{0,1:T(8,128)(2,1)}) fusion(f32[1024,1408]{0,1:T(8,128)} %fusion.5, bf16[1024,2048]{1,0:T(8,128)(2,1)S(1)} %copy-done.48, bf16[2048,2112]{1,0:T(8,128)(2,1)S(1)} %copy-done.33), kind=kOutput, calls=%fused_computation.20 | convolution fusion | flops 2963603456 | bytes 17432576 | tf_op jit(solution)/shard_map/dot_general | solution.py:22
  325.1 8.3 %fusion.9 = bf16[1024,2048]{1,0:T(8,128)(2,1)} fusion(bf16[2048,2112]{1,0:T(8,128)(2,1)S(1)} %copy-done.33, bf16[1024,704]{0,1:T(8,128)(2,1)S(1)} %get-tuple-element.205, bf16[1024,704]{0,1:T(8,128)(2,1)S(1)} %get-tuple-element.204), kind=kOutput, calls=%fused_computation.11 | convolution fusion | flops 5913444352 | bytes 12845056 | tf_op jit(solution)/shard_map/dot_general | solution.py:22
  333.5 2.7 convolution_convert_fusion.3
  338.1 3.5 convolution_convert_fusion.2
  348.9 7.0 %convolution_convert_fusion = bf16[1024,2048]{1,0:T(8,128)(2,1)} fusion(bf16[1024,704]{0,1:T(8,128)(2,1)S(1)} %copy-done.53, bf16[2048,2112]{1,0:T(8,128)(2,1)} %constant_dynamic-update-slice_fusion.10), kind=kOutput, calls=%fused_computation.12 | convolution fusion | flops 2954887168 | bytes 8781824 | tf_op jit(solution)/shard_map/dot_general | solution.py:22
  355.9 6.8 %collective-permute-done.17 = bf16[256,704]{0,1:T(8,128)(2,1)} collective-permute-done((bf16[256,704]{0,1:T(8,128)(2,1)}, bf16[256,704]{0,1:T(8,128)(2,1)}, u32[]{:S(2)}, u32[]{:S(2)}) %collective-permute-start.17) | collective-permute-done | bytes 360480 | tf_op jit(solution)/shard_map/ppermute | solution.py:157
  362.7 5.0 collective-permute-done.18
  367.7 3.7 fusion.24
  371.4 3.3 fusion.25
  375.6 3.0 add_convert_fusion.2
  378.5 4.2 add_convert_fusion.1
  390.9 5.8 fusion.34
  396.7 38.4 %collective-permute-done.21 = bf16[512,704]{0,1:T(8,128)(2,1)S(1)} collective-permute-done((bf16[512,704]{0,1:T(8,128)(2,1)}, bf16[512,704]{0,1:T(8,128)(2,1)S(1)}, u32[]{:S(2)}, u32[]{:S(2)}) %collective-permute-start.21) | collective-permute-done | bytes 720928 | tf_op jit(solution)/shard_map/ppermute | solution.py:182
  436.3 3.1 add_convert_fusion.3
  442.7 3.1 add_convert_fusion
  447.4 4.4 all-to-all-start.3
  451.8 6.5 fusion.21.d_ref
  458.4 5.7 gate_backward.1
  464.1 7.2 %grad_blocks.3 = (bf16[256,1024]{1,0:T(8,128)(2,1)}, bf16[256,1024]{1,0:T(8,128)(2,1)}, bf16[256,1024]{1,0:T(8,128)(2,1)}, bf16[256,1024]{1,0:T(8,128)(2,1)}) custom-call(bf16[1024,2048]{1,0:T(8,128)(2,1)} %copy-done.2, bf16[1024,2048]{1,0:T(8,128)(2,1)} %all-gather.11.cloned.1.call-done.refs_1_, bf16[1024,512]{1,0:T(8,128)(2,1)} %get-tuple-element.145.refs_2_.refs_1_, ...), custom_call_target="tpu_custom_call" | custom-call | flops 134217728 | bytes 1048576 | tf_op jit(solution)/shard_map/grad_blocks/pallas_call | solution.py:726
  475.6 45.3 %delta_backward.1 = (bf16[1024,1152]{1,0:T(8,128)(2,1)}, f32[8,1024]{1,0:T(8,128)}) custom-call(bf16[1024,1024]{1,0:T(8,128)(2,1)} %fusion.18.pre_ref, f32[1024,128]{1,0:T(8,128)} %fusion.52.small_ref, f32[1024,128]{1,0:T(8,128)} %pad.36.rider_ref, f32[4,1024]{1,0:T(4,128)} %pad_maximum_fusion.6.taps_ref, f32[2,128]{1,0:T(2,128)} %select_maximum_fusion.const_ref, ...), custom_call_target="tpu_custom_call" | custom-call | flops 10240000000 | bytes 20971520 | tf_op jit(solution)/shard_map/delta_backward/pallas_call | solution.py:832
  521.5 3.6 collective-permute-done.27
  526.5 6.4 grad_blocks.4
  534.8 12.7 %back_product.1 = bf16[1024,2048]{1,0:T(8,128)(2,1)} custom-call(bf16[1024,1152]{1,0:T(8,128)(2,1)} %get-tuple-element.169.refs_0_.right_ref, bf16[1024,512]{1,0:T(8,128)(2,1)} %get-tuple-element.145.refs_2_.refs_1_, bf16[2048,1152]{1,0:T(8,128)(2,1)} %constant_dynamic-update-slice_fusion.refs_2_, bf16[2048,1024]{1,0:T(8,128)(2,1)} %copy-done.6), custom_call_target="tpu_custom_call" | custom-call | flops 536870912 | bytes 2097152 | tf_op jit(solution)/shard_map/back_product/pallas_call | solution.py:753
  549.8 5.7 grad_rows.3
  560.0 12.8 %collective-permute-done.31 = f32[32,1024]{1,0:T(8,128)S(1)} collective-permute-done((f32[32,1024]{1,0:T(8,128)S(1)}, f32[32,1024]{1,0:T(8,128)S(1)}, u32[]{:S(2)}, u32[]{:S(2)}) %collective-permute-start.31) | collective-permute-done | bytes 131104 | tf_op jit(solution)/shard_map/ppermute | solution.py:265
  575.4 7.2 %grad_rows.4 = (bf16[512,1152]{1,0:T(8,128)(2,1)}, bf16[512,1152]{1,0:T(8,128)(2,1)}) custom-call(bf16[1024,2048]{1,0:T(8,128)(2,1)} %copy-done.2, bf16[1024,1152]{1,0:T(8,128)(2,1)} %get-tuple-element.169.refs_0_.right_ref, bf16[256,1152]{1,0:T(8,128)(2,1)} %collective-permute-done.34.refs_0_, bf16[256,1152]{1,0:T(8,128)(2,1)} %collective-permute-done.35.refs_1_), custom_call_target="tpu_custom_call" | custom-call | flops 2415919104 | bytes 8912896 | tf_op jit(solution)/shard_map/grad_rows/pallas_call | solution.py:710
  582.6 6.9 %grad_blocks.5 = (bf16[256,1024]{1,0:T(8,128)(2,1)}, bf16[256,1024]{1,0:T(8,128)(2,1)}) custom-call(bf16[1024,2048]{1,0:T(8,128)(2,1)} %copy-done.2, bf16[1024,2048]{1,0:T(8,128)(2,1)} %all-gather.11.cloned.1.call-done.refs_1_, bf16[1024,512]{1,0:T(8,128)(2,1)} %get-tuple-element.145.refs_2_.refs_1_, bf16[1024,512]{1,0:T(8,128)(2,1)} %gate_forward.1.refs_3_, ...), custom_call_target="tpu_custom_call" | custom-call | flops 67108864 | bytes 524288 | tf_op jit(solution)/shard_map/grad_blocks/pallas_call | solution.py:726
  591.7 3.6 all-to-all-start.4
  601.8 22.1 %collective-permute-done.36.refs_0_ = bf16[512,1152]{1,0:T(8,128)(2,1)} collective-permute-done((bf16[512,1152]{1,0:T(8,128)(2,1)}, bf16[512,1152]{1,0:T(8,128)(2,1)}, u32[]{:S(2)}, u32[]{:S(2)}) %collective-permute-start.36) | collective-permute-done | bytes 1179680 | tf_op jit(solution)/shard_map/ppermute | solution.py:182
  624.2 6.6 grad_rows.5
  630.8 4.7 all-to-all-start.5
  641.5 4.1 unpack_even.1
  651.5 13.4 %all-to-all-done.5 = bf16[8,64,1152]{2,1,0:T(8,128)(2,1)S(1)} async-done(((bf16[8,64,1152]{2,1,0:T(8,128)(2,1)}), bf16[8,64,1152]{2,1,0:T(8,128)(2,1)S(1)}, u32[]{:S(2)}, u32[]{:S(2)}) %all-to-all-start.5) | async-done | bytes 1179680 | tf_op jit(solution)/shard_map/all_to_all | solution.py:243
  (329 shorter events, 140.7 us)
Async XLA Ops:
  7.2 110.9 %copy-start = (f32[4,4096]{1,0:T(4,128)S(1)}, f32[4,4096]{1,0:T(4,128)}, u32[]{:S(2)}) copy-start(f32[4,4096]{1,0:T(4,128)} %param.32) | copy-start | bytes 196612
  7.2 13.2 %copy-start.45 = (s32[1,128]{1,0:T(1,128)S(1)}, s32[1,128]{1,0:T(1,128)}, u32[]{:S(2)}) copy-start(s32[1,128]{1,0:T(1,128)} %param.40) | copy-start | bytes 1540
  7.2 13.8 %copy-start.25 = (bf16[1,128,2048]{2,1,0:T(8,128)(2,1)S(1)}, bf16[1,128,2048]{2,1,0:T(8,128)(2,1)}, u32[]{:S(2)}) copy-start(bf16[1,128,2048]{2,1,0:T(8,128)(2,1)} %param.21) | copy-start | bytes 1572868
  13.9 12.6 %copy-start.26 = (bf16[64,4096]{1,0:T(8,128)(2,1)S(1)}, bf16[64,4096]{1,0:T(8,128)(2,1)}, u32[]{:S(2)}) copy-start(bf16[64,4096]{1,0:T(8,128)(2,1)} %param.28) | copy-start | bytes 1572868
  13.9 37.4 %all-to-all-start = ((bf16[8,64,1152]{2,1,0:T(8,128)(2,1)}), bf16[8,64,1152]{2,1,0:T(8,128)(2,1)S(1)}, u32[]{:S(2)}, u32[]{:S(2)}) async-start(bf16[8,64,1152]{2,1,0:T(8,128)(2,1)} %bitcast.96), calls=%async_computation | async-start | bytes 2359296 | tf_op jit(solution)/shard_map/all_to_all | solution.py:239
  20.4 83.2 %all-gather.5.cloned.1.call-start = ((), (), s32[]{:S(2)}) async-start(), calls=%async_computation.10 | async-start | bytes 4718592 | tf_op jit(solution)/shard_map/all_gather | solution.py:939
  20.5 1.3 collective-permute-start
  21.8 18.8 %collective-permute-start.1 = (f32[2,128]{1,0:T(2,128)S(1)}, f32[2,128]{1,0:T(2,128)S(1)}, u32[]{:S(2)}, u32[]{:S(2)}) collective-permute-start(f32[2,128]{1,0:T(2,128)S(1)} %pad_maximum_fusion.9), channel_id=1, source_target_pairs={{0,2},{1,3},{2,0},{3,1},{4,6},{5,7},{6,4},{7,5},{8,10},{9,11},{10,... | collective-permute-start | bytes 3080 | tf_op jit(solution)/shard_map/ppermute | solution.py:265
  40.6 10.6 %collective-permute-start.2 = (f32[4,128]{1,0:T(4,128)S(1)}, f32[4,128]{1,0:T(4,128)S(1)}, u32[]{:S(2)}, u32[]{:S(2)}) collective-permute-start(f32[4,128]{1,0:T(4,128)S(1)} %pad_maximum_fusion.8), channel_id=1, source_target_pairs={{0,4},{1,5},{2,6},{3,7},{4,0},{5,1},{6,2},{7,3},{8,12},{9,13},{10,... | collective-permute-start | bytes 6152 | tf_op jit(solution)/shard_map/ppermute | solution.py:265
  51.3 27.3 %collective-permute-start.4 = (bf16[512,1152]{1,0:T(8,128)(2,1)S(1)}, bf16[512,1152]{1,0:T(8,128)(2,1)S(1)}, u32[]{:S(2)}, u32[]{:S(2)}) collective-permute-start(bf16[512,1152]{1,0:T(8,128)(2,1)S(1)} %bitcast.93), channel_id=1, source_target_pairs={{0,8},{8,24},{24,16},{16,0},{1,9},{9,25},{25,17},{17,1},{2,10},{10... | collective-permute-start | bytes 3538952 | tf_op jit(solution)/shard_map/ppermute | solution.py:132
  53.9 29.0 %collective-permute-start.3 = (bf16[512,1152]{1,0:T(8,128)(2,1)S(1)}, bf16[512,1152]{1,0:T(8,128)(2,1)}, u32[]{:S(2)}, u32[]{:S(2)}) collective-permute-start(bf16[512,1152]{1,0:T(8,128)(2,1)S(1)} %bitcast.94), channel_id=1, source_target_pairs={{8,0},{24,8},{16,24},{0,16},{9,1},{25,9},{17,25},{1,17},{10,2},{26... | collective-permute-start | bytes 3538952 | tf_op jit(solution)/shard_map/ppermute | solution.py:132
  59.1 27.3 %copy-start.13 = (bf16[128,4096]{1,0:T(8,128)(2,1)}, bf16[128,4096]{1,0:T(8,128)(2,1)S(1)}, u32[]{:S(2)}) copy-start(bf16[128,4096]{1,0:T(8,128)(2,1)S(1)} %slice_dynamic-update-slice_fusion.5) | copy-start | bytes 3145732
  80.5 14.1 %collective-permute-start.5 = (bf16[256,1152]{1,0:T(8,128)(2,1)}, bf16[256,1152]{1,0:T(8,128)(2,1)}, u32[]{:S(2)}, u32[]{:S(2)}) collective-permute-start(bf16[256,1152]{1,0:T(8,128)(2,1)} %slice.211), channel_id=1, source_target_pairs={{0,8},{8,24},{24,16},{16,0},{1,9},{9,25},{25,17},{17,1},{2,10},{10... | collective-permute-start | bytes 1769480 | tf_op jit(solution)/shard_map/ppermute | solution.py:141
  84.8 13.8 %collective-permute-start.6 = (bf16[256,1152]{1,0:T(8,128)(2,1)}, bf16[256,1152]{1,0:T(8,128)(2,1)}, u32[]{:S(2)}, u32[]{:S(2)}) collective-permute-start(bf16[256,1152]{1,0:T(8,128)(2,1)} %slice.212), channel_id=1, source_target_pairs={{8,0},{24,8},{16,24},{0,16},{9,1},{25,9},{17,25},{1,17},{10,2},{26... | collective-permute-start | bytes 1769480 | tf_op jit(solution)/shard_map/ppermute | solution.py:142
  86.4 33.4 %all-to-all-start.1 = ((bf16[8,64,1024]{2,1,0:T(8,128)(2,1)}), bf16[8,64,1024]{2,1,0:T(8,128)(2,1)}, u32[]{:S(2)}, u32[]{:S(2)}) async-start(bf16[8,64,1024]{2,1,0:T(8,128)(2,1)} %bitcast.7), calls=%async_computation.1 | async-start | bytes 2097152 | tf_op jit(solution)/shard_map/all_to_all | solution.py:239
  90.7 116.6 %all-gather.7.cloned.1.call-start = ((), (), s32[]{:S(2)}) async-start(), calls=%async_computation.11 | async-start | bytes 4718592 | tf_op jit(solution)/shard_map/all_gather | solution.py:958
  119.8 40.2 %collective-permute-start.7 = (bf16[512,1024]{1,0:T(8,128)(2,1)}, bf16[512,1024]{1,0:T(8,128)(2,1)}, u32[]{:S(2)}, u32[]{:S(2)}) collective-permute-start(bf16[512,1024]{1,0:T(8,128)(2,1)} %bitcast.8), channel_id=1, source_target_pairs={{0,8},{8,24},{24,16},{16,0},{1,9},{9,25},{25,17},{17,1},{2,10},{10... | collective-permute-start | bytes 3145736 | tf_op jit(solution)/shard_map/ppermute | solution.py:132
  121.3 38.7 %collective-permute-start.8 = (bf16[512,1024]{1,0:T(8,128)(2,1)}, bf16[512,1024]{1,0:T(8,128)(2,1)}, u32[]{:S(2)}, u32[]{:S(2)}) collective-permute-start(bf16[512,1024]{1,0:T(8,128)(2,1)} %bitcast.8), channel_id=1, source_target_pairs={{8,0},{24,8},{16,24},{0,16},{9,1},{25,9},{17,25},{1,17},{10,2},{26... | collective-permute-start | bytes 3145736 | tf_op jit(solution)/shard_map/ppermute | solution.py:132
  126.5 80.8 %all-to-all-start.2 = ((bf16[8,64,2112]{2,1,0:T(8,128)(2,1)}), bf16[8,64,2112]{2,1,0:T(8,128)(2,1)S(1)}, u32[]{:S(2)}, u32[]{:S(2)}) async-start(bf16[8,64,2112]{2,1,0:T(8,128)(2,1)} %bitcast.90), calls=%async_computation.2 | async-start | bytes 4456448 | tf_op jit(solution)/shard_map/all_to_all | solution.py:239
  130.1 126.0 %reduce-scatter.5.cloned.1.call-start = ((), (), s32[]{:S(2)}) async-start(), calls=%async_computation.12 | async-start | bytes 4718592 | tf_op jit(solution)/shard_map/reduce_scatter | solution.py:1008
  161.0 14.2 %collective-permute-start.9 = (bf16[256,1024]{1,0:T(8,128)(2,1)S(1)}, bf16[256,1024]{1,0:T(8,128)(2,1)S(1)}, u32[]{:S(2)}, u32[]{:S(2)}) collective-permute-start(bf16[256,1024]{1,0:T(8,128)(2,1)S(1)} %slice.165), channel_id=1, source_target_pairs={{0,8},{8,24},{24,16},{16,0},{1,9},{9,25},{25,17},{17,1},{2,10},{10... | collective-permute-start | bytes 1572872 | tf_op jit(solution)/shard_map/ppermute | solution.py:141
  163.7 14.0 %collective-permute-start.10 = (bf16[256,1024]{1,0:T(8,128)(2,1)S(1)}, bf16[256,1024]{1,0:T(8,128)(2,1)S(1)}, u32[]{:S(2)}, u32[]{:S(2)}) collective-permute-start(bf16[256,1024]{1,0:T(8,128)(2,1)S(1)} %slice.166), channel_id=1, source_target_pairs={{8,0},{24,8},{16,24},{0,16},{9,1},{25,9},{17,25},{1,17},{10,2},{26... | collective-permute-start | bytes 1572872 | tf_op jit(solution)/shard_map/ppermute | solution.py:142
  165.5 13.5 %copy-start.3 = (bf16[1024,2048]{1,0:T(8,128)(2,1)S(1)}, bf16[1024,2048]{1,0:T(8,128)(2,1)}, u32[]{:S(2)}) copy-start(bf16[1024,2048]{1,0:T(8,128)(2,1)} %copy-done.2) | copy-start | bytes 12582916
  207.3 98.1 %all-gather.9.cloned.1.call-start = ((), (), s32[]{:S(2)}) async-start(), calls=%async_computation.13 | async-start | bytes 4718592 | tf_op jit(solution)/shard_map/all_gather | solution.py:1020
  209.8 49.6 %collective-permute-start.11 = (bf16[512,2112]{0,1:T(8,128)(2,1)}, bf16[512,2112]{0,1:T(8,128)(2,1)}, u32[]{:S(2)}, u32[]{:S(2)}) collective-permute-start(bf16[512,2112]{0,1:T(8,128)(2,1)} %copy.169), channel_id=1, source_target_pairs={{0,8},{8,24},{24,16},{16,0},{1,9},{9,25},{25,17},{17,1},{2,10},{10... | collective-permute-start | bytes 6488072 | tf_op jit(solution)/shard_map/ppermute | solution.py:132
  211.3 48.9 %collective-permute-start.12 = (bf16[512,2112]{0,1:T(8,128)(2,1)}, bf16[512,2112]{0,1:T(8,128)(2,1)}, u32[]{:S(2)}, u32[]{:S(2)}) collective-permute-start(bf16[512,2112]{0,1:T(8,128)(2,1)} %copy.169), channel_id=1, source_target_pairs={{8,0},{24,8},{16,24},{0,16},{9,1},{25,9},{17,25},{1,17},{10,2},{26... | collective-permute-start | bytes 6488072 | tf_op jit(solution)/shard_map/ppermute | solution.py:132
  260.3 122.5 %reduce-scatter.7.cloned.1.call-start = ((), (), s32[]{:S(2)}) async-start(), calls=%async_computation.14 | async-start | bytes 4718592 | tf_op jit(solution)/shard_map/reduce_scatter | solution.py:1036
  262.6 24.9 %collective-permute-start.13 = (bf16[256,2112]{0,1:T(8,128)(2,1)}, bf16[256,2112]{0,1:T(8,128)(2,1)}, u32[]{:S(2)}, u32[]{:S(2)}) collective-permute-start(bf16[256,2112]{0,1:T(8,128)(2,1)} %slice.173), channel_id=1, source_target_pairs={{0,8},{8,24},{24,16},{16,0},{1,9},{9,25},{25,17},{17,1},{2,10},{10... | collective-permute-start | bytes 3244040 | tf_op jit(solution)/shard_map/ppermute | solution.py:141
  266.4 24.7 %collective-permute-start.14 = (bf16[256,2112]{0,1:T(8,128)(2,1)}, bf16[256,2112]{0,1:T(8,128)(2,1)}, u32[]{:S(2)}, u32[]{:S(2)}) collective-permute-start(bf16[256,2112]{0,1:T(8,128)(2,1)} %slice.174), channel_id=1, source_target_pairs={{8,0},{24,8},{16,24},{0,16},{9,1},{25,9},{17,25},{1,17},{10,2},{26... | collective-permute-start | bytes 3244040 | tf_op jit(solution)/shard_map/ppermute | solution.py:142
  333.4 114.0 %all-gather.11.cloned.1.call-start = ((), (), s32[]{:S(2)}) async-start(), calls=%async_computation.15 | async-start | bytes 4718592 | tf_op jit(solution)/shard_map/all_gather | solution.py:1048
  336.1 38.5 %collective-permute-start.15 = (bf16[256,1408]{1,0:T(8,128)(2,1)S(1)}, bf16[256,1408]{1,0:T(8,128)(2,1)S(1)}, u32[]{:S(2)}, u32[]{:S(2)}) collective-permute-start(bf16[256,1408]{1,0:T(8,128)(2,1)S(1)} %convolution_convert_fusion.3), channel_id=1, source_target_pairs={{0,8},{8,24},{24,16},{16,0},{1,9},{9,25},{25,17},{17,1},{2,10},{10... | collective-permute-start | bytes 2162696 | tf_op jit(solution)/shard_map/ppermute | solution.py:157
  341.6 33.1 %collective-permute-start.16 = (bf16[256,1408]{1,0:T(8,128)(2,1)}, bf16[256,1408]{1,0:T(8,128)(2,1)S(1)}, u32[]{:S(2)}, u32[]{:S(2)}) collective-permute-start(bf16[256,1408]{1,0:T(8,128)(2,1)} %convolution_convert_fusion.2), channel_id=1, source_target_pairs={{8,0},{24,8},{16,24},{0,16},{9,1},{25,9},{17,25},{1,17},{10,2},{26... | collective-permute-start | bytes 2162696 | tf_op jit(solution)/shard_map/ppermute | solution.py:158
  344.5 18.2 %collective-permute-start.17 = (bf16[256,704]{0,1:T(8,128)(2,1)}, bf16[256,704]{0,1:T(8,128)(2,1)}, u32[]{:S(2)}, u32[]{:S(2)}) collective-permute-start(bf16[256,704]{0,1:T(8,128)(2,1)} %convolution_convert_fusion.5), channel_id=1, source_target_pairs={{0,8},{8,24},{24,16},{16,0},{1,9},{9,25},{25,17},{17,1},{2,10},{10... | collective-permute-start | bytes 1081352 | tf_op jit(solution)/shard_map/ppermute | solution.py:157
  348.2 19.5 %collective-permute-start.18 = (bf16[256,704]{0,1:T(8,128)(2,1)}, bf16[256,704]{0,1:T(8,128)(2,1)}, u32[]{:S(2)}, u32[]{:S(2)}) collective-permute-start(bf16[256,704]{0,1:T(8,128)(2,1)} %convolution_convert_fusion.4), channel_id=1, source_target_pairs={{8,0},{24,8},{16,24},{0,16},{9,1},{25,9},{17,25},{1,17},{10,2},{26... | collective-permute-start | bytes 1081352 | tf_op jit(solution)/shard_map/ppermute | solution.py:158
  355.9 15.5 %copy-start.54 = (bf16[1024,704]{0,1:T(8,128)(2,1)S(1)}, bf16[1024,704]{0,1:T(8,128)(2,1)}, u32[]{:S(2)}) copy-start(bf16[1024,704]{0,1:T(8,128)(2,1)} %get-tuple-element.206) | copy-start | bytes 4325380
  386.6 188.8 %reduce-scatter.9.cloned.1.call-start = ((), (), s32[]{:S(2)}) async-start(), calls=%async_computation.16 | async-start | bytes 4718592 | tf_op jit(solution)/shard_map/reduce_scatter | solution.py:1052
  386.6 49.7 %copy-start.55 = (bf16[1024,704]{0,1:T(8,128)(2,1)S(1)}, bf16[1024,704]{0,1:T(8,128)(2,1)}, u32[]{:S(2)}) copy-start(bf16[1024,704]{0,1:T(8,128)(2,1)} %get-tuple-element.206) | copy-start | bytes 4325380
  386.6 55.0 %collective-permute-start.19 = (bf16[512,1408]{1,0:T(8,128)(2,1)}, bf16[512,1408]{1,0:T(8,128)(2,1)S(1)}, u32[]{:S(2)}, u32[]{:S(2)}) collective-permute-start(bf16[512,1408]{1,0:T(8,128)(2,1)} %add_convert_fusion.2), channel_id=1, source_target_pairs={{0,8},{8,24},{24,16},{16,0},{1,9},{9,25},{25,17},{17,1},{2,10},{10... | collective-permute-start | bytes 4325384 | tf_op jit(solution)/shard_map/ppermute | solution.py:182
  388.3 54.5 %collective-permute-start.20 = (bf16[512,1408]{1,0:T(8,128)(2,1)}, bf16[512,1408]{1,0:T(8,128)(2,1)}, u32[]{:S(2)}, u32[]{:S(2)}) collective-permute-start(bf16[512,1408]{1,0:T(8,128)(2,1)} %add_convert_fusion.1), channel_id=1, source_target_pairs={{8,0},{24,8},{16,24},{0,16},{9,1},{25,9},{17,25},{1,17},{10,2},{26... | collective-permute-start | bytes 4325384 | tf_op jit(solution)/shard_map/ppermute | solution.py:183
  388.7 46.3 %collective-permute-start.21 = (bf16[512,704]{0,1:T(8,128)(2,1)}, bf16[512,704]{0,1:T(8,128)(2,1)S(1)}, u32[]{:S(2)}, u32[]{:S(2)}) collective-permute-start(bf16[512,704]{0,1:T(8,128)(2,1)} %fusion.24), channel_id=1, source_target_pairs={{0,8},{8,24},{24,16},{16,0},{1,9},{9,25},{25,17},{17,1},{2,10},{10... | collective-permute-start | bytes 2162696 | tf_op jit(solution)/shard_map/ppermute | solution.py:182
  390.3 46.0 %collective-permute-start.22 = (bf16[512,704]{0,1:T(8,128)(2,1)}, bf16[512,704]{0,1:T(8,128)(2,1)S(1)}, u32[]{:S(2)}, u32[]{:S(2)}) collective-permute-start(bf16[512,704]{0,1:T(8,128)(2,1)} %fusion.25), channel_id=1, source_target_pairs={{8,0},{24,8},{16,24},{0,16},{9,1},{25,9},{17,25},{1,17},{10,2},{26... | collective-permute-start | bytes 2162696 | tf_op jit(solution)/shard_map/ppermute | solution.py:183
  447.4 87.4 %all-to-all-start.3 = ((bf16[8,64,2112]{2,1,0:T(8,128)(2,1)}), bf16[8,64,2112]{2,1,0:T(8,128)(2,1)}, u32[]{:S(2)}, u32[]{:S(2)}) async-start(bf16[8,64,2112]{2,1,0:T(8,128)(2,1)} %bitcast.91), calls=%async_computation.5 | async-start | bytes 4456448 | tf_op jit(solution)/shard_map/all_to_all | solution.py:239
  451.8 148.6 %reduce-scatter.11.cloned.1.call-start = ((), (), s32[]{:S(2)}) async-start(), calls=%async_computation.17 | async-start | bytes 4718592 | tf_op jit(solution)/shard_map/reduce_scatter | solution.py:1077
  471.3 49.5 %collective-permute-start.23 = (bf16[256,1024]{1,0:T(8,128)(2,1)}, bf16[256,1024]{1,0:T(8,128)(2,1)S(1)}, u32[]{:S(2)}, u32[]{:S(2)}) collective-permute-start(bf16[256,1024]{1,0:T(8,128)(2,1)} %get-tuple-element.146), channel_id=1, source_target_pairs={{0,8},{8,24},{24,16},{16,0},{1,9},{9,25},{25,17},{17,1},{2,10},{10... | collective-permute-start | bytes 1572872 | tf_op jit(solution)/shard_map/ppermute | solution.py:205
  471.9 49.0 %collective-permute-start.24 = (bf16[256,1024]{1,0:T(8,128)(2,1)}, bf16[256,1024]{1,0:T(8,128)(2,1)S(1)}, u32[]{:S(2)}, u32[]{:S(2)}) collective-permute-start(bf16[256,1024]{1,0:T(8,128)(2,1)} %get-tuple-element.147), channel_id=1, source_target_pairs={{8,0},{24,8},{16,24},{0,16},{9,1},{25,9},{17,25},{1,17},{10,2},{26... | collective-permute-start | bytes 1572872 | tf_op jit(solution)/shard_map/ppermute | solution.py:206
  473.3 47.5 %collective-permute-start.25 = (bf16[256,1024]{1,0:T(8,128)(2,1)}, bf16[256,1024]{1,0:T(8,128)(2,1)S(1)}, u32[]{:S(2)}, u32[]{:S(2)}) collective-permute-start(bf16[256,1024]{1,0:T(8,128)(2,1)} %get-tuple-element.148), channel_id=1, source_target_pairs={{0,8},{8,24},{24,16},{16,0},{1,9},{9,25},{25,17},{17,1},{2,10},{10... | collective-permute-start | bytes 1572872 | tf_op jit(solution)/shard_map/ppermute | solution.py:207
  473.9 47.0 %collective-permute-start.26 = (bf16[256,1024]{1,0:T(8,128)(2,1)}, bf16[256,1024]{1,0:T(8,128)(2,1)S(1)}, u32[]{:S(2)}, u32[]{:S(2)}) collective-permute-start(bf16[256,1024]{1,0:T(8,128)(2,1)} %get-tuple-element.149), channel_id=1, source_target_pairs={{8,0},{24,8},{16,24},{0,16},{9,1},{25,9},{17,25},{1,17},{10,2},{26... | collective-permute-start | bytes 1572872 | tf_op jit(solution)/shard_map/ppermute | solution.py:208
  520.9 12.0 %copy-start.34 = (bf16[256,1024]{1,0:T(8,128)(2,1)}, bf16[256,1024]{1,0:T(8,128)(2,1)S(1)}, u32[]{:S(2)}) copy-start(bf16[256,1024]{1,0:T(8,128)(2,1)S(1)} %collective-permute-done.25.refs_5_) | copy-start | bytes 1572868
  520.9 12.0 %copy-start.35 = (bf16[256,1024]{1,0:T(8,128)(2,1)}, bf16[256,1024]{1,0:T(8,128)(2,1)S(1)}, u32[]{:S(2)}) copy-start(bf16[256,1024]{1,0:T(8,128)(2,1)S(1)} %collective-permute-done.26.refs_6_) | copy-start | bytes 1572868
  520.9 4.2 collective-permute-start.27
  525.8 7.0 %collective-permute-start.28 = (f32[8,1024]{1,0:T(8,128)S(1)}, f32[8,1024]{1,0:T(8,128)S(1)}, u32[]{:S(2)}, u32[]{:S(2)}) collective-permute-start(f32[8,1024]{1,0:T(8,128)S(1)} %add.157), channel_id=1, source_target_pairs={{0,16},{8,24},{16,0},{24,8},{1,17},{9,25},{17,1},{25,9},{2,18},{10... | collective-permute-start | bytes 98312 | tf_op jit(solution)/shard_map/ppermute | solution.py:253
  547.5 2.2 collective-permute-start.29
  547.6 25.3 %collective-permute-start.32 = (bf16[256,1024]{1,0:T(8,128)(2,1)}, bf16[256,1024]{1,0:T(8,128)(2,1)S(1)}, u32[]{:S(2)}, u32[]{:S(2)}) collective-permute-start(bf16[256,1024]{1,0:T(8,128)(2,1)} %get-tuple-element.162), channel_id=1, source_target_pairs={{0,8},{8,24},{24,16},{16,0},{1,9},{9,25},{25,17},{17,1},{2,10},{10... | collective-permute-start | bytes 1572872 | tf_op jit(solution)/shard_map/ppermute | solution.py:221
  548.4 24.5 %collective-permute-start.33 = (bf16[256,1024]{1,0:T(8,128)(2,1)}, bf16[256,1024]{1,0:T(8,128)(2,1)}, u32[]{:S(2)}, u32[]{:S(2)}) collective-permute-start(bf16[256,1024]{1,0:T(8,128)(2,1)} %get-tuple-element.163), channel_id=1, source_target_pairs={{8,0},{24,8},{16,24},{0,16},{9,1},{25,9},{17,25},{1,17},{10,2},{26... | collective-permute-start | bytes 1572872 | tf_op jit(solution)/shard_map/ppermute | solution.py:222
  549.7 8.0 %collective-permute-start.30 = (f32[16,1024]{1,0:T(8,128)S(1)}, f32[16,1024]{1,0:T(8,128)S(1)}, u32[]{:S(2)}, u32[]{:S(2)}) collective-permute-start(f32[16,1024]{1,0:T(8,128)S(1)} %pad_maximum_fusion.5), channel_id=1, source_target_pairs={{0,2},{1,3},{2,0},{3,1},{4,6},{5,7},{6,4},{7,5},{8,10},{9,11},{10,... | collective-permute-start | bytes 196616 | tf_op jit(solution)/shard_map/ppermute | solution.py:265
  555.5 19.4 %collective-permute-start.34 = (bf16[256,1152]{1,0:T(8,128)(2,1)}, bf16[256,1152]{1,0:T(8,128)(2,1)}, u32[]{:S(2)}, u32[]{:S(2)}) collective-permute-start(bf16[256,1152]{1,0:T(8,128)(2,1)} %get-tuple-element.170), channel_id=1, source_target_pairs={{0,8},{8,24},{24,16},{16,0},{1,9},{9,25},{25,17},{17,1},{2,10},{10... | collective-permute-start | bytes 1769480 | tf_op jit(solution)/shard_map/ppermute | solution.py:157
  555.9 19.5 %collective-permute-start.35 = (bf16[256,1152]{1,0:T(8,128)(2,1)}, bf16[256,1152]{1,0:T(8,128)(2,1)}, u32[]{:S(2)}, u32[]{:S(2)}) collective-permute-start(bf16[256,1152]{1,0:T(8,128)(2,1)} %get-tuple-element.171), channel_id=1, source_target_pairs={{8,0},{24,8},{16,24},{0,16},{9,1},{25,9},{17,25},{1,17},{10,2},{26... | collective-permute-start | bytes 1769480 | tf_op jit(solution)/shard_map/ppermute | solution.py:158
  557.8 15.0 %collective-permute-start.31 = (f32[32,1024]{1,0:T(8,128)S(1)}, f32[32,1024]{1,0:T(8,128)S(1)}, u32[]{:S(2)}, u32[]{:S(2)}) collective-permute-start(f32[32,1024]{1,0:T(8,128)S(1)} %pad_maximum_fusion.4), channel_id=1, source_target_pairs={{0,4},{1,5},{2,6},{3,7},{4,0},{5,1},{6,2},{7,3},{8,12},{9,13},{10,... | collective-permute-start | bytes 393224 | tf_op jit(solution)/shard_map/ppermute | solution.py:265
  591.7 32.5 %all-to-all-start.4 = ((bf16[8,64,1024]{2,1,0:T(8,128)(2,1)}), bf16[8,64,1024]{2,1,0:T(8,128)(2,1)S(1)}, u32[]{:S(2)}, u32[]{:S(2)}) async-start(bf16[8,64,1024]{2,1,0:T(8,128)(2,1)} %bitcast.101), calls=%async_computation.7 | async-start | bytes 2097152 | tf_op jit(solution)/shard_map/all_to_all | solution.py:243
  595.3 28.6 %collective-permute-start.36 = (bf16[512,1152]{1,0:T(8,128)(2,1)}, bf16[512,1152]{1,0:T(8,128)(2,1)}, u32[]{:S(2)}, u32[]{:S(2)}) collective-permute-start(bf16[512,1152]{1,0:T(8,128)(2,1)} %get-tuple-element.181), channel_id=1, source_target_pairs={{0,8},{8,24},{24,16},{16,0},{1,9},{9,25},{25,17},{17,1},{2,10},{10... | collective-permute-start | bytes 3538952 | tf_op jit(solution)/shard_map/ppermute | solution.py:182
  595.8 28.4 %collective-permute-start.37 = (bf16[512,1152]{1,0:T(8,128)(2,1)}, bf16[512,1152]{1,0:T(8,128)(2,1)}, u32[]{:S(2)}, u32[]{:S(2)}) collective-permute-start(bf16[512,1152]{1,0:T(8,128)(2,1)} %get-tuple-element.182), channel_id=1, source_target_pairs={{8,0},{24,8},{16,24},{0,16},{9,1},{25,9},{17,25},{1,17},{10,2},{26... | collective-permute-start | bytes 3538952 | tf_op jit(solution)/shard_map/ppermute | solution.py:183
  601.8 33.7 %copy-start.7 = (bf16[128,2048]{1,0:T(8,128)(2,1)S(1)}, bf16[128,2048]{1,0:T(8,128)(2,1)}, u32[]{:S(2)}) copy-start(bf16[128,2048]{1,0:T(8,128)(2,1)} %reduce-scatter.7.cloned.1.call-done) | copy-start | bytes 1572868
  630.8 34.1 %all-to-all-start.5 = ((bf16[8,64,1152]{2,1,0:T(8,128)(2,1)}), bf16[8,64,1152]{2,1,0:T(8,128)(2,1)S(1)}, u32[]{:S(2)}, u32[]{:S(2)}) async-start(bf16[8,64,1152]{2,1,0:T(8,128)(2,1)} %bitcast.92), calls=%async_computation.9 | async-start | bytes 2359296 | tf_op jit(solution)/shard_map/all_to_all | solution.py:243
  650.7 15.0 %copy-start.20 = (bf16[64,4096]{1,0:T(8,128)(2,1)S(1)}, bf16[64,4096]{1,0:T(8,128)(2,1)}, u32[]{:S(2)}) copy-start(bf16[64,4096]{1,0:T(8,128)(2,1)} %v_ref.1) | copy-start | bytes 1572868
  (51 other events, 226.5 us)
Sparse Core Ops, SparseCore 0:
  51.5 46.4 all-gather.4
  116.1 81.5 all-gather.6
  207.4 48.6 reduce-scatter.4
  260.4 44.9 all-gather.8
  333.5 48.7 reduce-scatter.6
  386.7 44.8 all-gather.10
  447.5 89.2 reduce-scatter.8
  547.7 51.0 reduce-scatter.10

commit v9 on v8

--- a/solution.py
+++ b/solution.py
@@ -1021,6 +1021,7 @@
     both_w = mlp_cols[:, : 2 * ff]
     down_w = mlp_cols[:, 2 * ff :]
     d_product = nn(cot_all, down_w)
+    mlp_all, d_product = lax.optimization_barrier((mlp_all, d_product))
     both_pre = nn(mlp_all, both_w)
     hidden_pre = both_pre[:, :ff]
     up_pre = both_pre[:, ff:]

time: 685 us -> 683 us (level)
  starting transfers between devices: 69.9 us -> 80.7 us
  waiting for transfers between devices: 231 us -> 223 us
    ppermute x3, starting transfers between devices: 1.79 us -> 12.7 us  [gather_end(): far_b = lax.ppermute(from_right[half:], 'dp', left)]
    ppermute x3, waiting for transfers between devices: 5.79 us -> 14.3 us  [gather_end(): far_b = lax.ppermute(from_right[half:], 'dp', left)]
    ppermute x3, waiting for transfers between devices: 18.1 us -> 9.65 us  [gather_end(): far_a = lax.ppermute(from_left[:half], 'dp', right)]
    unnamed x152 -> x150, local copies, waits for them, and re-layouts: 37.5 us -> 37.3 us
  transfers between devices with their start and end apart: 52 -> 52, of which waited for: 25 -> 24; matrix products, arithmetic and copies ran while one was open for 25% -> 26% of each run, Pallas kernels for 21% -> 20%
where the time goes in v9:
time: 683 us; the launch traced here: 679 us
  waiting for transfers between devices  223 us (33%)
  Pallas kernels  147 us (22%)
  matrix products  94.2 us (14%)
  starting transfers between devices  80.7 us (12%)
  local copies, waits for them, and re-layouts  79.5 us (12%)
  other arithmetic  38.8 us (6%)
  between operations  15.4 us (2%)
    dot_general x19, matrix products, dot_f32(): lax.dot_general(left, right, (dims, ((), ())), preferred_element_type=F32)  94.2 us
    ppermute x4, waiting for transfers between devices, second(): lax.ppermute(self.sums[0], 'dp', to_right)  59.1 us
    pallas_call x1, Pallas kernels, delta_backward(): pl.pallas_call(functools.partial(bwd_kernel, hp, dk, dv), out_shape=(shap...  45.3 us
    reduce_scatter x1, waiting for transfers between devices, local(): lax.psum_scatter(after(nt(gated, out_cols).astype(BF), mlp_own_cols, cot_...  44.2 us
    unnamed x150, local copies, waits for them, and re-layouts  37.3 us
    pallas_call x1, Pallas kernels, delta_forward(): pl.pallas_call(functools.partial(fwd_kernel, hp, dk, dv), out_shape=(shap...  29.6 us
    ppermute x6, waiting for transfers between devices, gather_small(): other = lax.ppermute(values, 'seq', [(i, i ^ step) for i in range(ranks)])  26.6 us
    pallas_call x3, Pallas kernels, grad_blocks(): pl.pallas_call(functools.partial(block_kernel, half, blocks, len(pairs),...  20.4 us
  transfers between devices with their start and end apart: 52, of which 24 were waited for; matrix products, arithmetic and copies ran while one was open for 26% of the time, Pallas kernels for 20%

profile of v9, /device:TPU:0, one launch (start us, length us, event | category | flops | bytes accessed | tf_op | source)
XLA Modules:
  0.0 678.9 jit_solution(1144540391100922475)
XLA Ops:
  11.4 2.5 pack_mix.1
  13.9 6.5 all-to-all-start
  27.5 13.1 %collective-permute-done.1 = f32[2,128]{1,0:T(2,128)S(1)} collective-permute-done((f32[2,128]{1,0:T(2,128)S(1)}, f32[2,128]{1,0:T(2,128)S(1)}, u32[]{:S(2)}, u32[]{:S(2)}) %collective-permute-start.1) | collective-permute-done | bytes 1056 | tf_op jit(solution)/shard_map/ppermute | solution.py:265
  40.6 4.5 collective-permute-start.2
  48.0 3.3 pack_even.1
  59.1 19.5 %collective-permute-done.4 = bf16[512,1152]{1,0:T(8,128)(2,1)S(1)} collective-permute-done((bf16[512,1152]{1,0:T(8,128)(2,1)S(1)}, bf16[512,1152]{1,0:T(8,128)(2,1)S(1)}, u32[]{:S(2)}, u32[]{:S(2)}) %collective-permute-start.4) | collective-permute-done | bytes 1179680 | tf_op jit(solution)/shard_map/ppermute | solution.py:132
  86.4 4.3 all-to-all-start.1
  90.8 2.5 constant_dynamic-update-slice_fusion.3
  103.7 3.2 fusion
  110.2 5.7 fusion.18.pre_ref
  121.8 4.7 fusion.50.small_ref
  126.5 3.6 all-to-all-start.2
  130.4 29.6 %delta_forward.1 = (f32[1024,512]{1,0:T(8,128)}, f32[16,128,256]{2,1,0:T(8,128)}, f32[1024,512]{1,0:T(8,128)}, f32[16,128,128]{2,1,0:T(8,128)}, f32[1024,256]{1,0:T(8,128)}) custom-call(bf16[1024,1024]{1,0:T(8,128)(2,1)} %fusion.18.pre_ref, f32[1024,128]{1,0:T(8,128)} %fusion.50.small_ref, f32[1024,128]{1,0:T(8,128)} %pad.36.rider_ref, ...), custom_call_target="tpu_custom_call" | custom-call | flops 43008000000 | bytes 16777216 | tf_op jit(solution)/shard_map/delta_forward/pallas_call | solution.py:804
  167.1 8.3 %collective-permute-done.9 = bf16[256,1024]{1,0:T(8,128)(2,1)S(1)} collective-permute-done((bf16[256,1024]{1,0:T(8,128)(2,1)S(1)}, bf16[256,1024]{1,0:T(8,128)(2,1)S(1)}, u32[]{:S(2)}, u32[]{:S(2)}) %collective-permute-start.9) | collective-permute-done | bytes 524320 | tf_op jit(solution)/shard_map/ppermute | solution.py:141
  175.5 2.4 collective-permute-done.10
  179.2 3.7 fusion.16.gate_ref
  182.9 4.3 gate_forward.1.refs_3_
  187.2 6.2 convolution_convert_fusion.1
  193.4 13.8 %all-to-all-done.2 = bf16[8,64,2112]{2,1,0:T(8,128)(2,1)S(1)} async-done(((bf16[8,64,2112]{2,1,0:T(8,128)(2,1)}), bf16[8,64,2112]{2,1,0:T(8,128)(2,1)S(1)}, u32[]{:S(2)}, u32[]{:S(2)}) %all-to-all-start.2) | async-done | bytes 2162720 | tf_op jit(solution)/shard_map/all_to_all | solution.py:239
  207.3 2.5 copy.169
  211.9 44.2 %reduce-scatter.5.cloned.1.call-done = bf16[128,2048]{1,0:T(8,128)(2,1)} async-done(((bf16[1024,2048]{1,0:T(8,128)(2,1)}), bf16[128,2048]{1,0:T(8,128)(2,1)}) %reduce-scatter.5.cloned.1.call-update) | async-done | bytes 524304 | tf_op jit(solution)/shard_map/reduce_scatter | solution.py:1008
  264.1 2.3 slice.174
  266.4 11.6 %collective-permute-start.14 = (bf16[256,2112]{0,1:T(8,128)(2,1)}, bf16[256,2112]{0,1:T(8,128)(2,1)}, u32[]{:S(2)}, u32[]{:S(2)}) collective-permute-start(bf16[256,2112]{0,1:T(8,128)(2,1)} %slice.174), channel_id=1, source_target_pairs={{8,0},{24,8},{16,24},{0,16},{9,1},{25,9},{17,25},{1,17},{10,2},{26... | collective-permute-start | bytes 3244040 | tf_op jit(solution)/shard_map/ppermute | solution.py:142
  279.5 4.1 copy.171
  283.6 2.9 copy.174
  286.6 3.2 constant_dynamic-update-slice_fusion.13
  292.1 9.9 %collective-permute-done.14 = bf16[256,2112]{0,1:T(8,128)(2,1)} collective-permute-done((bf16[256,2112]{0,1:T(8,128)(2,1)}, bf16[256,2112]{0,1:T(8,128)(2,1)}, u32[]{:S(2)}, u32[]{:S(2)}) %collective-permute-start.14) | collective-permute-done | bytes 1081376 | tf_op jit(solution)/shard_map/ppermute | solution.py:142
  304.4 2.4 constant_dynamic-update-slice_fusion.12
  310.2 6.7 fusion.14
  316.9 10.3 %fusion.5 = f32[1024,1408]{0,1:T(8,128)S(1)} fusion(bf16[1024,2048]{1,0:T(8,128)(2,1)} %all-gather.9.cloned.1.call-done, bf16[2048,2112]{1,0:T(8,128)(2,1)} %constant_dynamic-update-slice_fusion.10), kind=kOutput, calls=%fused_computation.7 | convolution fusion | flops 5905580032 | bytes 15728640 | tf_op jit(solution)/shard_map/dot_general | solution.py:22
  331.7 8.3 %fusion.9 = bf16[1024,2048]{1,0:T(8,128)(2,1)} fusion(bf16[2048,2112]{1,0:T(8,128)(2,1)S(1)} %copy-done.41, bf16[1024,704]{0,1:T(8,128)(2,1)S(1)} %get-tuple-element.209, bf16[1024,704]{0,1:T(8,128)(2,1)S(1)} %get-tuple-element.208), kind=kOutput, calls=%fused_computation.11 | convolution fusion | flops 5913444352 | bytes 12845056 | tf_op jit(solution)/shard_map/dot_general | solution.py:22
  340.0 4.0 convolution_convert_fusion.3
  344.7 3.0 convolution_convert_fusion.2
  355.8 7.4 %convolution_convert_fusion = bf16[1024,2048]{1,0:T(8,128)(2,1)} fusion(bf16[1024,704]{0,1:T(8,128)(2,1)S(1)} %get-tuple-element.210, bf16[2048,2112]{1,0:T(8,128)(2,1)} %constant_dynamic-update-slice_fusion.10), kind=kOutput, calls=%fused_computation.12 | convolution fusion | flops 2954887168 | bytes 8781824 | tf_op jit(solution)/shard_map/dot_general | solution.py:22
  363.2 4.5 collective-permute-done.17
  367.7 3.3 collective-permute-done.18
  371.0 3.2 fusion.24
  374.2 3.2 fusion.25
  377.5 3.0 add_convert_fusion.2
  380.5 4.2 add_convert_fusion.1
  384.7 3.1 reduce-scatter.7.cloned.1.call-done
  395.8 5.8 fusion.35
  401.6 37.0 %collective-permute-done.21 = bf16[512,704]{0,1:T(8,128)(2,1)S(1)} collective-permute-done((bf16[512,704]{0,1:T(8,128)(2,1)}, bf16[512,704]{0,1:T(8,128)(2,1)S(1)}, u32[]{:S(2)}, u32[]{:S(2)}) %collective-permute-start.21) | collective-permute-done | bytes 720928 | tf_op jit(solution)/shard_map/ppermute | solution.py:182
  439.8 3.1 add_convert_fusion.3
  445.2 3.2 add_convert_fusion
  449.9 4.4 all-to-all-start.3
  454.5 6.9 %fusion.21.d_ref = f32[1024,512]{1,0:T(8,128)} fusion(bf16[1024,2048]{1,0:T(8,128)(2,1)} %all-gather.11.cloned.1.call-done.refs_1_, bf16[2048,1024]{1,0:T(8,128)(2,1)} %copy-done.6), kind=kOutput, calls=%fused_computation.32 | convolution fusion | flops 2147483648 | bytes 8388608 | tf_op jit(solution)/shard_map/dot_general | solution.py:22
  461.4 5.6 gate_backward.1
  467.0 7.2 %grad_blocks.3 = (bf16[256,1024]{1,0:T(8,128)(2,1)}, bf16[256,1024]{1,0:T(8,128)(2,1)}, bf16[256,1024]{1,0:T(8,128)(2,1)}, bf16[256,1024]{1,0:T(8,128)(2,1)}) custom-call(bf16[1024,2048]{1,0:T(8,128)(2,1)} %copy-done.2, bf16[1024,2048]{1,0:T(8,128)(2,1)} %all-gather.11.cloned.1.call-done.refs_1_, bf16[1024,512]{1,0:T(8,128)(2,1)} %get-tuple-element.149.refs_2_.refs_1_, ...), custom_call_target="tpu_custom_call" | custom-call | flops 134217728 | bytes 1048576 | tf_op jit(solution)/shard_map/grad_blocks/pallas_call | solution.py:726
  478.2 45.3 %delta_backward.1 = (bf16[1024,1152]{1,0:T(8,128)(2,1)}, f32[8,1024]{1,0:T(8,128)}) custom-call(bf16[1024,1024]{1,0:T(8,128)(2,1)} %fusion.18.pre_ref, f32[1024,128]{1,0:T(8,128)} %fusion.50.small_ref, f32[1024,128]{1,0:T(8,128)} %pad.36.rider_ref, f32[4,1024]{1,0:T(4,128)} %pad_maximum_fusion.6.taps_ref, f32[2,128]{1,0:T(2,128)} %select_maximum_fusion.const_ref, ...), custom_call_target="tpu_custom_call" | custom-call | flops 10240000000 | bytes 20971520 | tf_op jit(solution)/shard_map/delta_backward/pallas_call | solution.py:832
  525.1 2.7 collective-permute-done.27
  529.0 6.3 grad_blocks.4
  537.7 12.8 %back_product.1 = bf16[1024,2048]{1,0:T(8,128)(2,1)} custom-call(bf16[1024,1152]{1,0:T(8,128)(2,1)} %get-tuple-element.173.refs_0_.right_ref, bf16[1024,512]{1,0:T(8,128)(2,1)} %get-tuple-element.149.refs_2_.refs_1_, bf16[2048,1152]{1,0:T(8,128)(2,1)} %constant_dynamic-update-slice_fusion.refs_2_, bf16[2048,1024]{1,0:T(8,128)(2,1)} %copy-done.6), custom_call_target="tpu_custom_call" | custom-call | flops 536870912 | bytes 2097152 | tf_op jit(solution)/shard_map/back_product/pallas_call | solution.py:753
  552.9 5.5 grad_rows.3
  562.4 12.8 %collective-permute-done.31 = f32[32,1024]{1,0:T(8,128)S(1)} collective-permute-done((f32[32,1024]{1,0:T(8,128)S(1)}, f32[32,1024]{1,0:T(8,128)S(1)}, u32[]{:S(2)}, u32[]{:S(2)}) %collective-permute-start.31) | collective-permute-done | bytes 131104 | tf_op jit(solution)/shard_map/ppermute | solution.py:265
  575.3 2.6 collective-permute-done.34.refs_0_
  579.2 7.2 %grad_rows.4 = (bf16[512,1152]{1,0:T(8,128)(2,1)}, bf16[512,1152]{1,0:T(8,128)(2,1)}) custom-call(bf16[1024,2048]{1,0:T(8,128)(2,1)} %copy-done.2, bf16[1024,1152]{1,0:T(8,128)(2,1)} %get-tuple-element.173.refs_0_.right_ref, bf16[256,1152]{1,0:T(8,128)(2,1)} %collective-permute-done.34.refs_0_, bf16[256,1152]{1,0:T(8,128)(2,1)} %collective-permute-done.35.refs_1_), custom_call_target="tpu_custom_call" | custom-call | flops 2415919104 | bytes 8912896 | tf_op jit(solution)/shard_map/grad_rows/pallas_call | solution.py:710
  586.4 6.9 %grad_blocks.5 = (bf16[256,1024]{1,0:T(8,128)(2,1)}, bf16[256,1024]{1,0:T(8,128)(2,1)}) custom-call(bf16[1024,2048]{1,0:T(8,128)(2,1)} %copy-done.2, bf16[1024,2048]{1,0:T(8,128)(2,1)} %all-gather.11.cloned.1.call-done.refs_1_, bf16[1024,512]{1,0:T(8,128)(2,1)} %get-tuple-element.149.refs_2_.refs_1_, bf16[1024,512]{1,0:T(8,128)(2,1)} %gate_forward.1.refs_3_, ...), custom_call_target="tpu_custom_call" | custom-call | flops 67108864 | bytes 524288 | tf_op jit(solution)/shard_map/grad_blocks/pallas_call | solution.py:726
  595.5 3.6 all-to-all-start.4
  605.6 22.1 %collective-permute-done.36.refs_0_ = bf16[512,1152]{1,0:T(8,128)(2,1)} collective-permute-done((bf16[512,1152]{1,0:T(8,128)(2,1)}, bf16[512,1152]{1,0:T(8,128)(2,1)}, u32[]{:S(2)}, u32[]{:S(2)}) %collective-permute-start.36) | collective-permute-done | bytes 1179680 | tf_op jit(solution)/shard_map/ppermute | solution.py:182
  628.1 6.6 grad_rows.5
  634.7 4.7 all-to-all-start.5
  645.4 4.1 unpack_even.1
  655.5 13.4 %all-to-all-done.5 = bf16[8,64,1152]{2,1,0:T(8,128)(2,1)S(1)} async-done(((bf16[8,64,1152]{2,1,0:T(8,128)(2,1)}), bf16[8,64,1152]{2,1,0:T(8,128)(2,1)S(1)}, u32[]{:S(2)}, u32[]{:S(2)}) %all-to-all-start.5) | async-done | bytes 1179680 | tf_op jit(solution)/shard_map/all_to_all | solution.py:243
  (328 shorter events, 144.5 us)
Async XLA Ops:
  7.2 110.9 %copy-start = (f32[4,4096]{1,0:T(4,128)S(1)}, f32[4,4096]{1,0:T(4,128)}, u32[]{:S(2)}) copy-start(f32[4,4096]{1,0:T(4,128)} %param.32) | copy-start | bytes 196612
  7.2 13.2 %copy-start.53 = (s32[1,128]{1,0:T(1,128)S(1)}, s32[1,128]{1,0:T(1,128)}, u32[]{:S(2)}) copy-start(s32[1,128]{1,0:T(1,128)} %param.40) | copy-start | bytes 1540
  7.2 13.8 %copy-start.26 = (bf16[1,128,2048]{2,1,0:T(8,128)(2,1)S(1)}, bf16[1,128,2048]{2,1,0:T(8,128)(2,1)}, u32[]{:S(2)}) copy-start(bf16[1,128,2048]{2,1,0:T(8,128)(2,1)} %param.21) | copy-start | bytes 1572868
  13.9 12.6 %copy-start.27 = (bf16[64,4096]{1,0:T(8,128)(2,1)S(1)}, bf16[64,4096]{1,0:T(8,128)(2,1)}, u32[]{:S(2)}) copy-start(bf16[64,4096]{1,0:T(8,128)(2,1)} %param.28) | copy-start | bytes 1572868
  13.9 37.4 %all-to-all-start = ((bf16[8,64,1152]{2,1,0:T(8,128)(2,1)}), bf16[8,64,1152]{2,1,0:T(8,128)(2,1)S(1)}, u32[]{:S(2)}, u32[]{:S(2)}) async-start(bf16[8,64,1152]{2,1,0:T(8,128)(2,1)} %bitcast.96), calls=%async_computation | async-start | bytes 2359296 | tf_op jit(solution)/shard_map/all_to_all | solution.py:239
  20.4 83.2 %all-gather.5.cloned.1.call-start = ((), (), s32[]{:S(2)}) async-start(), calls=%async_computation.10 | async-start | bytes 4718592 | tf_op jit(solution)/shard_map/all_gather | solution.py:939
  20.5 1.3 collective-permute-start
  21.8 18.8 %collective-permute-start.1 = (f32[2,128]{1,0:T(2,128)S(1)}, f32[2,128]{1,0:T(2,128)S(1)}, u32[]{:S(2)}, u32[]{:S(2)}) collective-permute-start(f32[2,128]{1,0:T(2,128)S(1)} %pad_maximum_fusion.9), channel_id=1, source_target_pairs={{0,2},{1,3},{2,0},{3,1},{4,6},{5,7},{6,4},{7,5},{8,10},{9,11},{10,... | collective-permute-start | bytes 3080 | tf_op jit(solution)/shard_map/ppermute | solution.py:265
  40.6 10.6 %collective-permute-start.2 = (f32[4,128]{1,0:T(4,128)S(1)}, f32[4,128]{1,0:T(4,128)S(1)}, u32[]{:S(2)}, u32[]{:S(2)}) collective-permute-start(f32[4,128]{1,0:T(4,128)S(1)} %pad_maximum_fusion.8), channel_id=1, source_target_pairs={{0,4},{1,5},{2,6},{3,7},{4,0},{5,1},{6,2},{7,3},{8,12},{9,13},{10,... | collective-permute-start | bytes 6152 | tf_op jit(solution)/shard_map/ppermute | solution.py:265
  51.3 27.3 %collective-permute-start.4 = (bf16[512,1152]{1,0:T(8,128)(2,1)S(1)}, bf16[512,1152]{1,0:T(8,128)(2,1)S(1)}, u32[]{:S(2)}, u32[]{:S(2)}) collective-permute-start(bf16[512,1152]{1,0:T(8,128)(2,1)S(1)} %bitcast.93), channel_id=1, source_target_pairs={{0,8},{8,24},{24,16},{16,0},{1,9},{9,25},{25,17},{17,1},{2,10},{10... | collective-permute-start | bytes 3538952 | tf_op jit(solution)/shard_map/ppermute | solution.py:132
  53.9 29.0 %collective-permute-start.3 = (bf16[512,1152]{1,0:T(8,128)(2,1)S(1)}, bf16[512,1152]{1,0:T(8,128)(2,1)}, u32[]{:S(2)}, u32[]{:S(2)}) collective-permute-start(bf16[512,1152]{1,0:T(8,128)(2,1)S(1)} %bitcast.94), channel_id=1, source_target_pairs={{8,0},{24,8},{16,24},{0,16},{9,1},{25,9},{17,25},{1,17},{10,2},{26... | collective-permute-start | bytes 3538952 | tf_op jit(solution)/shard_map/ppermute | solution.py:132
  59.1 27.3 %copy-start.13 = (bf16[128,4096]{1,0:T(8,128)(2,1)}, bf16[128,4096]{1,0:T(8,128)(2,1)S(1)}, u32[]{:S(2)}) copy-start(bf16[128,4096]{1,0:T(8,128)(2,1)S(1)} %slice_dynamic-update-slice_fusion.5) | copy-start | bytes 3145732
  80.5 14.1 %collective-permute-start.5 = (bf16[256,1152]{1,0:T(8,128)(2,1)}, bf16[256,1152]{1,0:T(8,128)(2,1)}, u32[]{:S(2)}, u32[]{:S(2)}) collective-permute-start(bf16[256,1152]{1,0:T(8,128)(2,1)} %slice.211), channel_id=1, source_target_pairs={{0,8},{8,24},{24,16},{16,0},{1,9},{9,25},{25,17},{17,1},{2,10},{10... | collective-permute-start | bytes 1769480 | tf_op jit(solution)/shard_map/ppermute | solution.py:141
  84.8 13.8 %collective-permute-start.6 = (bf16[256,1152]{1,0:T(8,128)(2,1)}, bf16[256,1152]{1,0:T(8,128)(2,1)}, u32[]{:S(2)}, u32[]{:S(2)}) collective-permute-start(bf16[256,1152]{1,0:T(8,128)(2,1)} %slice.212), channel_id=1, source_target_pairs={{8,0},{24,8},{16,24},{0,16},{9,1},{25,9},{17,25},{1,17},{10,2},{26... | collective-permute-start | bytes 1769480 | tf_op jit(solution)/shard_map/ppermute | solution.py:142
  86.4 33.4 %all-to-all-start.1 = ((bf16[8,64,1024]{2,1,0:T(8,128)(2,1)}), bf16[8,64,1024]{2,1,0:T(8,128)(2,1)}, u32[]{:S(2)}, u32[]{:S(2)}) async-start(bf16[8,64,1024]{2,1,0:T(8,128)(2,1)} %bitcast.7), calls=%async_computation.1 | async-start | bytes 2097152 | tf_op jit(solution)/shard_map/all_to_all | solution.py:239
  90.7 116.6 %all-gather.7.cloned.1.call-start = ((), (), s32[]{:S(2)}) async-start(), calls=%async_computation.11 | async-start | bytes 4718592 | tf_op jit(solution)/shard_map/all_gather | solution.py:958
  119.8 40.3 %collective-permute-start.7 = (bf16[512,1024]{1,0:T(8,128)(2,1)}, bf16[512,1024]{1,0:T(8,128)(2,1)}, u32[]{:S(2)}, u32[]{:S(2)}) collective-permute-start(bf16[512,1024]{1,0:T(8,128)(2,1)} %bitcast.8), channel_id=1, source_target_pairs={{0,8},{8,24},{24,16},{16,0},{1,9},{9,25},{25,17},{17,1},{2,10},{10... | collective-permute-start | bytes 3145736 | tf_op jit(solution)/shard_map/ppermute | solution.py:132
  121.3 38.7 %collective-permute-start.8 = (bf16[512,1024]{1,0:T(8,128)(2,1)}, bf16[512,1024]{1,0:T(8,128)(2,1)}, u32[]{:S(2)}, u32[]{:S(2)}) collective-permute-start(bf16[512,1024]{1,0:T(8,128)(2,1)} %bitcast.8), channel_id=1, source_target_pairs={{8,0},{24,8},{16,24},{0,16},{9,1},{25,9},{17,25},{1,17},{10,2},{26... | collective-permute-start | bytes 3145736 | tf_op jit(solution)/shard_map/ppermute | solution.py:132
  126.5 80.8 %all-to-all-start.2 = ((bf16[8,64,2112]{2,1,0:T(8,128)(2,1)}), bf16[8,64,2112]{2,1,0:T(8,128)(2,1)S(1)}, u32[]{:S(2)}, u32[]{:S(2)}) async-start(bf16[8,64,2112]{2,1,0:T(8,128)(2,1)} %bitcast.90), calls=%async_computation.2 | async-start | bytes 4456448 | tf_op jit(solution)/shard_map/all_to_all | solution.py:239
  130.1 126.0 %reduce-scatter.5.cloned.1.call-start = ((), (), s32[]{:S(2)}) async-start(), calls=%async_computation.12 | async-start | bytes 4718592 | tf_op jit(solution)/shard_map/reduce_scatter | solution.py:1008
  161.2 14.3 %collective-permute-start.9 = (bf16[256,1024]{1,0:T(8,128)(2,1)S(1)}, bf16[256,1024]{1,0:T(8,128)(2,1)S(1)}, u32[]{:S(2)}, u32[]{:S(2)}) collective-permute-start(bf16[256,1024]{1,0:T(8,128)(2,1)S(1)} %slice.165), channel_id=1, source_target_pairs={{0,8},{8,24},{24,16},{16,0},{1,9},{9,25},{25,17},{17,1},{2,10},{10... | collective-permute-start | bytes 1572872 | tf_op jit(solution)/shard_map/ppermute | solution.py:141
  163.8 14.0 %collective-permute-start.10 = (bf16[256,1024]{1,0:T(8,128)(2,1)S(1)}, bf16[256,1024]{1,0:T(8,128)(2,1)S(1)}, u32[]{:S(2)}, u32[]{:S(2)}) collective-permute-start(bf16[256,1024]{1,0:T(8,128)(2,1)S(1)} %slice.166), channel_id=1, source_target_pairs={{8,0},{24,8},{16,24},{0,16},{9,1},{25,9},{17,25},{1,17},{10,2},{26... | collective-permute-start | bytes 1572872 | tf_op jit(solution)/shard_map/ppermute | solution.py:142
  165.7 13.5 %copy-start.3 = (bf16[1024,2048]{1,0:T(8,128)(2,1)S(1)}, bf16[1024,2048]{1,0:T(8,128)(2,1)}, u32[]{:S(2)}) copy-start(bf16[1024,2048]{1,0:T(8,128)(2,1)} %copy-done.2) | copy-start | bytes 12582916
  207.3 109.6 %all-gather.9.cloned.1.call-start = ((), (), s32[]{:S(2)}) async-start(), calls=%async_computation.13 | async-start | bytes 4718592 | tf_op jit(solution)/shard_map/all_gather | solution.py:1020
  209.9 49.6 %collective-permute-start.11 = (bf16[512,2112]{0,1:T(8,128)(2,1)}, bf16[512,2112]{0,1:T(8,128)(2,1)}, u32[]{:S(2)}, u32[]{:S(2)}) collective-permute-start(bf16[512,2112]{0,1:T(8,128)(2,1)} %copy.169), channel_id=1, source_target_pairs={{0,8},{8,24},{24,16},{16,0},{1,9},{9,25},{25,17},{17,1},{2,10},{10... | collective-permute-start | bytes 6488072 | tf_op jit(solution)/shard_map/ppermute | solution.py:132
  211.3 48.9 %collective-permute-start.12 = (bf16[512,2112]{0,1:T(8,128)(2,1)}, bf16[512,2112]{0,1:T(8,128)(2,1)}, u32[]{:S(2)}, u32[]{:S(2)}) collective-permute-start(bf16[512,2112]{0,1:T(8,128)(2,1)} %copy.169), channel_id=1, source_target_pairs={{8,0},{24,8},{16,24},{0,16},{9,1},{25,9},{17,25},{1,17},{10,2},{26... | collective-permute-start | bytes 6488072 | tf_op jit(solution)/shard_map/ppermute | solution.py:132
  260.3 127.6 %reduce-scatter.7.cloned.1.call-start = ((), (), s32[]{:S(2)}) async-start(), calls=%async_computation.14 | async-start | bytes 4718592 | tf_op jit(solution)/shard_map/reduce_scatter | solution.py:1037
  262.6 27.1 %collective-permute-start.13 = (bf16[256,2112]{0,1:T(8,128)(2,1)}, bf16[256,2112]{0,1:T(8,128)(2,1)}, u32[]{:S(2)}, u32[]{:S(2)}) collective-permute-start(bf16[256,2112]{0,1:T(8,128)(2,1)} %slice.173), channel_id=1, source_target_pairs={{0,8},{8,24},{24,16},{16,0},{1,9},{9,25},{25,17},{17,1},{2,10},{10... | collective-permute-start | bytes 3244040 | tf_op jit(solution)/shard_map/ppermute | solution.py:141
  266.4 35.6 %collective-permute-start.14 = (bf16[256,2112]{0,1:T(8,128)(2,1)}, bf16[256,2112]{0,1:T(8,128)(2,1)}, u32[]{:S(2)}, u32[]{:S(2)}) collective-permute-start(bf16[256,2112]{0,1:T(8,128)(2,1)} %slice.174), channel_id=1, source_target_pairs={{8,0},{24,8},{16,24},{0,16},{9,1},{25,9},{17,25},{1,17},{10,2},{26... | collective-permute-start | bytes 3244040 | tf_op jit(solution)/shard_map/ppermute | solution.py:142
  329.4 44.8 %copy-start.30 = (bf16[1024,704]{0,1:T(8,128)(2,1)}, bf16[1024,704]{0,1:T(8,128)(2,1)S(1)}, u32[]{:S(2)}) copy-start(bf16[1024,704]{0,1:T(8,128)(2,1)S(1)} %get-tuple-element.210) | copy-start | bytes 4325380
  340.0 109.9 %all-gather.11.cloned.1.call-start = ((), (), s32[]{:S(2)}) async-start(), calls=%async_computation.15 | async-start | bytes 4718592 | tf_op jit(solution)/shard_map/all_gather | solution.py:1049
  344.0 33.4 %collective-permute-start.15 = (bf16[256,1408]{1,0:T(8,128)(2,1)}, bf16[256,1408]{1,0:T(8,128)(2,1)S(1)}, u32[]{:S(2)}, u32[]{:S(2)}) collective-permute-start(bf16[256,1408]{1,0:T(8,128)(2,1)} %convolution_convert_fusion.3), channel_id=1, source_target_pairs={{0,8},{8,24},{24,16},{16,0},{1,9},{9,25},{25,17},{17,1},{2,10},{10... | collective-permute-start | bytes 2162696 | tf_op jit(solution)/shard_map/ppermute | solution.py:157
  347.6 29.8 %collective-permute-start.16 = (bf16[256,1408]{1,0:T(8,128)(2,1)}, bf16[256,1408]{1,0:T(8,128)(2,1)}, u32[]{:S(2)}, u32[]{:S(2)}) collective-permute-start(bf16[256,1408]{1,0:T(8,128)(2,1)} %convolution_convert_fusion.2), channel_id=1, source_target_pairs={{8,0},{24,8},{16,24},{0,16},{9,1},{25,9},{17,25},{1,17},{10,2},{26... | collective-permute-start | bytes 2162696 | tf_op jit(solution)/shard_map/ppermute | solution.py:158
  351.4 16.2 %collective-permute-start.17 = (bf16[256,704]{0,1:T(8,128)(2,1)}, bf16[256,704]{0,1:T(8,128)(2,1)}, u32[]{:S(2)}, u32[]{:S(2)}) collective-permute-start(bf16[256,704]{0,1:T(8,128)(2,1)} %convolution_convert_fusion.5), channel_id=1, source_target_pairs={{0,8},{8,24},{24,16},{16,0},{1,9},{9,25},{25,17},{17,1},{2,10},{10... | collective-permute-start | bytes 1081352 | tf_op jit(solution)/shard_map/ppermute | solution.py:157
  354.3 16.7 %collective-permute-start.18 = (bf16[256,704]{0,1:T(8,128)(2,1)}, bf16[256,704]{0,1:T(8,128)(2,1)}, u32[]{:S(2)}, u32[]{:S(2)}) collective-permute-start(bf16[256,704]{0,1:T(8,128)(2,1)} %convolution_convert_fusion.4), channel_id=1, source_target_pairs={{8,0},{24,8},{16,24},{0,16},{9,1},{25,9},{17,25},{1,17},{10,2},{26... | collective-permute-start | bytes 1081352 | tf_op jit(solution)/shard_map/ppermute | solution.py:158
  391.7 48.2 %copy-start.31 = (bf16[1024,704]{0,1:T(8,128)(2,1)S(1)}, bf16[1024,704]{0,1:T(8,128)(2,1)}, u32[]{:S(2)}) copy-start(bf16[1024,704]{0,1:T(8,128)(2,1)} %copy-done.30) | copy-start | bytes 4325380
  391.7 187.5 %reduce-scatter.9.cloned.1.call-start = ((), (), s32[]{:S(2)}) async-start(), calls=%async_computation.16 | async-start | bytes 4718592 | tf_op jit(solution)/shard_map/reduce_scatter | solution.py:1053
  391.7 53.4 %collective-permute-start.19 = (bf16[512,1408]{1,0:T(8,128)(2,1)}, bf16[512,1408]{1,0:T(8,128)(2,1)}, u32[]{:S(2)}, u32[]{:S(2)}) collective-permute-start(bf16[512,1408]{1,0:T(8,128)(2,1)} %add_convert_fusion.2), channel_id=1, source_target_pairs={{0,8},{8,24},{24,16},{16,0},{1,9},{9,25},{25,17},{17,1},{2,10},{10... | collective-permute-start | bytes 4325384 | tf_op jit(solution)/shard_map/ppermute | solution.py:182
  393.3 51.9 %collective-permute-start.20 = (bf16[512,1408]{1,0:T(8,128)(2,1)}, bf16[512,1408]{1,0:T(8,128)(2,1)}, u32[]{:S(2)}, u32[]{:S(2)}) collective-permute-start(bf16[512,1408]{1,0:T(8,128)(2,1)} %add_convert_fusion.1), channel_id=1, source_target_pairs={{8,0},{24,8},{16,24},{0,16},{9,1},{25,9},{17,25},{1,17},{10,2},{26... | collective-permute-start | bytes 4325384 | tf_op jit(solution)/shard_map/ppermute | solution.py:183
  393.8 44.8 %collective-permute-start.21 = (bf16[512,704]{0,1:T(8,128)(2,1)}, bf16[512,704]{0,1:T(8,128)(2,1)S(1)}, u32[]{:S(2)}, u32[]{:S(2)}) collective-permute-start(bf16[512,704]{0,1:T(8,128)(2,1)} %fusion.24), channel_id=1, source_target_pairs={{0,8},{8,24},{24,16},{16,0},{1,9},{9,25},{25,17},{17,1},{2,10},{10... | collective-permute-start | bytes 2162696 | tf_op jit(solution)/shard_map/ppermute | solution.py:182
  395.3 44.5 %collective-permute-start.22 = (bf16[512,704]{0,1:T(8,128)(2,1)}, bf16[512,704]{0,1:T(8,128)(2,1)S(1)}, u32[]{:S(2)}, u32[]{:S(2)}) collective-permute-start(bf16[512,704]{0,1:T(8,128)(2,1)} %fusion.25), channel_id=1, source_target_pairs={{8,0},{24,8},{16,24},{0,16},{9,1},{25,9},{17,25},{1,17},{10,2},{26... | collective-permute-start | bytes 2162696 | tf_op jit(solution)/shard_map/ppermute | solution.py:183
  449.9 87.8 %all-to-all-start.3 = ((bf16[8,64,2112]{2,1,0:T(8,128)(2,1)}), bf16[8,64,2112]{2,1,0:T(8,128)(2,1)}, u32[]{:S(2)}, u32[]{:S(2)}) async-start(bf16[8,64,2112]{2,1,0:T(8,128)(2,1)} %bitcast.91), calls=%async_computation.5 | async-start | bytes 4456448 | tf_op jit(solution)/shard_map/all_to_all | solution.py:239
  454.3 150.0 %reduce-scatter.11.cloned.1.call-start = ((), (), s32[]{:S(2)}) async-start(), calls=%async_computation.17 | async-start | bytes 4718592 | tf_op jit(solution)/shard_map/reduce_scatter | solution.py:1078
  474.2 49.3 %collective-permute-start.23 = (bf16[256,1024]{1,0:T(8,128)(2,1)}, bf16[256,1024]{1,0:T(8,128)(2,1)S(1)}, u32[]{:S(2)}, u32[]{:S(2)}) collective-permute-start(bf16[256,1024]{1,0:T(8,128)(2,1)} %get-tuple-element.150), channel_id=1, source_target_pairs={{0,8},{8,24},{24,16},{16,0},{1,9},{9,25},{25,17},{17,1},{2,10},{10... | collective-permute-start | bytes 1572872 | tf_op jit(solution)/shard_map/ppermute | solution.py:205
  475.6 47.9 %collective-permute-start.24 = (bf16[256,1024]{1,0:T(8,128)(2,1)}, bf16[256,1024]{1,0:T(8,128)(2,1)S(1)}, u32[]{:S(2)}, u32[]{:S(2)}) collective-permute-start(bf16[256,1024]{1,0:T(8,128)(2,1)} %get-tuple-element.151), channel_id=1, source_target_pairs={{8,0},{24,8},{16,24},{0,16},{9,1},{25,9},{17,25},{1,17},{10,2},{26... | collective-permute-start | bytes 1572872 | tf_op jit(solution)/shard_map/ppermute | solution.py:206
  476.2 47.3 %collective-permute-start.25 = (bf16[256,1024]{1,0:T(8,128)(2,1)}, bf16[256,1024]{1,0:T(8,128)(2,1)S(1)}, u32[]{:S(2)}, u32[]{:S(2)}) collective-permute-start(bf16[256,1024]{1,0:T(8,128)(2,1)} %get-tuple-element.152), channel_id=1, source_target_pairs={{0,8},{8,24},{24,16},{16,0},{1,9},{9,25},{25,17},{17,1},{2,10},{10... | collective-permute-start | bytes 1572872 | tf_op jit(solution)/shard_map/ppermute | solution.py:207
  477.7 45.9 %collective-permute-start.26 = (bf16[256,1024]{1,0:T(8,128)(2,1)}, bf16[256,1024]{1,0:T(8,128)(2,1)S(1)}, u32[]{:S(2)}, u32[]{:S(2)}) collective-permute-start(bf16[256,1024]{1,0:T(8,128)(2,1)} %get-tuple-element.153), channel_id=1, source_target_pairs={{8,0},{24,8},{16,24},{0,16},{9,1},{25,9},{17,25},{1,17},{10,2},{26... | collective-permute-start | bytes 1572872 | tf_op jit(solution)/shard_map/ppermute | solution.py:208
  523.5 11.8 %copy-start.42 = (bf16[256,1024]{1,0:T(8,128)(2,1)}, bf16[256,1024]{1,0:T(8,128)(2,1)S(1)}, u32[]{:S(2)}) copy-start(bf16[256,1024]{1,0:T(8,128)(2,1)S(1)} %collective-permute-done.25.refs_5_) | copy-start | bytes 1572868
  523.6 11.8 %copy-start.43 = (bf16[256,1024]{1,0:T(8,128)(2,1)}, bf16[256,1024]{1,0:T(8,128)(2,1)S(1)}, u32[]{:S(2)}) copy-start(bf16[256,1024]{1,0:T(8,128)(2,1)S(1)} %collective-permute-done.26.refs_6_) | copy-start | bytes 1572868
  523.6 4.2 collective-permute-start.27
  528.5 6.8 %collective-permute-start.28 = (f32[8,1024]{1,0:T(8,128)S(1)}, f32[8,1024]{1,0:T(8,128)S(1)}, u32[]{:S(2)}, u32[]{:S(2)}) collective-permute-start(f32[8,1024]{1,0:T(8,128)S(1)} %add.157), channel_id=1, source_target_pairs={{0,16},{8,24},{16,0},{24,8},{1,17},{9,25},{17,1},{25,9},{2,18},{10... | collective-permute-start | bytes 98312 | tf_op jit(solution)/shard_map/ppermute | solution.py:253
  550.5 2.4 collective-permute-start.29
  550.6 24.7 %collective-permute-start.32 = (bf16[256,1024]{1,0:T(8,128)(2,1)}, bf16[256,1024]{1,0:T(8,128)(2,1)S(1)}, u32[]{:S(2)}, u32[]{:S(2)}) collective-permute-start(bf16[256,1024]{1,0:T(8,128)(2,1)} %get-tuple-element.166), channel_id=1, source_target_pairs={{0,8},{8,24},{24,16},{16,0},{1,9},{9,25},{25,17},{17,1},{2,10},{10... | collective-permute-start | bytes 1572872 | tf_op jit(solution)/shard_map/ppermute | solution.py:221
  552.1 23.2 %collective-permute-start.33 = (bf16[256,1024]{1,0:T(8,128)(2,1)}, bf16[256,1024]{1,0:T(8,128)(2,1)}, u32[]{:S(2)}, u32[]{:S(2)}) collective-permute-start(bf16[256,1024]{1,0:T(8,128)(2,1)} %get-tuple-element.167), channel_id=1, source_target_pairs={{8,0},{24,8},{16,24},{0,16},{9,1},{25,9},{17,25},{1,17},{10,2},{26... | collective-permute-start | bytes 1572872 | tf_op jit(solution)/shard_map/ppermute | solution.py:222
  552.9 7.6 %collective-permute-start.30 = (f32[16,1024]{1,0:T(8,128)S(1)}, f32[16,1024]{1,0:T(8,128)S(1)}, u32[]{:S(2)}, u32[]{:S(2)}) collective-permute-start(f32[16,1024]{1,0:T(8,128)S(1)} %pad_maximum_fusion.5), channel_id=1, source_target_pairs={{0,2},{1,3},{2,0},{3,1},{4,6},{5,7},{6,4},{7,5},{8,10},{9,11},{10,... | collective-permute-start | bytes 196616 | tf_op jit(solution)/shard_map/ppermute | solution.py:265
  558.5 19.4 %collective-permute-start.34 = (bf16[256,1152]{1,0:T(8,128)(2,1)}, bf16[256,1152]{1,0:T(8,128)(2,1)}, u32[]{:S(2)}, u32[]{:S(2)}) collective-permute-start(bf16[256,1152]{1,0:T(8,128)(2,1)} %get-tuple-element.174), channel_id=1, source_target_pairs={{0,8},{8,24},{24,16},{16,0},{1,9},{9,25},{25,17},{17,1},{2,10},{10... | collective-permute-start | bytes 1769480 | tf_op jit(solution)/shard_map/ppermute | solution.py:157
  559.7 19.5 %collective-permute-start.35 = (bf16[256,1152]{1,0:T(8,128)(2,1)}, bf16[256,1152]{1,0:T(8,128)(2,1)}, u32[]{:S(2)}, u32[]{:S(2)}) collective-permute-start(bf16[256,1152]{1,0:T(8,128)(2,1)} %get-tuple-element.175), channel_id=1, source_target_pairs={{8,0},{24,8},{16,24},{0,16},{9,1},{25,9},{17,25},{1,17},{10,2},{26... | collective-permute-start | bytes 1769480 | tf_op jit(solution)/shard_map/ppermute | solution.py:158
  560.5 14.7 %collective-permute-start.31 = (f32[32,1024]{1,0:T(8,128)S(1)}, f32[32,1024]{1,0:T(8,128)S(1)}, u32[]{:S(2)}, u32[]{:S(2)}) collective-permute-start(f32[32,1024]{1,0:T(8,128)S(1)} %pad_maximum_fusion.4), channel_id=1, source_target_pairs={{0,4},{1,5},{2,6},{3,7},{4,0},{5,1},{6,2},{7,3},{8,12},{9,13},{10,... | collective-permute-start | bytes 393224 | tf_op jit(solution)/shard_map/ppermute | solution.py:265
  595.5 32.6 %all-to-all-start.4 = ((bf16[8,64,1024]{2,1,0:T(8,128)(2,1)}), bf16[8,64,1024]{2,1,0:T(8,128)(2,1)S(1)}, u32[]{:S(2)}, u32[]{:S(2)}) async-start(bf16[8,64,1024]{2,1,0:T(8,128)(2,1)} %bitcast.101), calls=%async_computation.7 | async-start | bytes 2097152 | tf_op jit(solution)/shard_map/all_to_all | solution.py:243
  599.1 28.6 %collective-permute-start.36 = (bf16[512,1152]{1,0:T(8,128)(2,1)}, bf16[512,1152]{1,0:T(8,128)(2,1)}, u32[]{:S(2)}, u32[]{:S(2)}) collective-permute-start(bf16[512,1152]{1,0:T(8,128)(2,1)} %get-tuple-element.185), channel_id=1, source_target_pairs={{0,8},{8,24},{24,16},{16,0},{1,9},{9,25},{25,17},{17,1},{2,10},{10... | collective-permute-start | bytes 3538952 | tf_op jit(solution)/shard_map/ppermute | solution.py:182
  599.7 28.4 %collective-permute-start.37 = (bf16[512,1152]{1,0:T(8,128)(2,1)}, bf16[512,1152]{1,0:T(8,128)(2,1)}, u32[]{:S(2)}, u32[]{:S(2)}) collective-permute-start(bf16[512,1152]{1,0:T(8,128)(2,1)} %get-tuple-element.186), channel_id=1, source_target_pairs={{8,0},{24,8},{16,24},{0,16},{9,1},{25,9},{17,25},{1,17},{10,2},{26... | collective-permute-start | bytes 3538952 | tf_op jit(solution)/shard_map/ppermute | solution.py:183
  605.6 33.8 %copy-start.7 = (bf16[128,2048]{1,0:T(8,128)(2,1)S(1)}, bf16[128,2048]{1,0:T(8,128)(2,1)}, u32[]{:S(2)}) copy-start(bf16[128,2048]{1,0:T(8,128)(2,1)} %reduce-scatter.7.cloned.1.call-done) | copy-start | bytes 1572868
  634.7 34.1 %all-to-all-start.5 = ((bf16[8,64,1152]{2,1,0:T(8,128)(2,1)}), bf16[8,64,1152]{2,1,0:T(8,128)(2,1)S(1)}, u32[]{:S(2)}, u32[]{:S(2)}) async-start(bf16[8,64,1152]{2,1,0:T(8,128)(2,1)} %bitcast.92), calls=%async_computation.9 | async-start | bytes 2359296 | tf_op jit(solution)/shard_map/all_to_all | solution.py:243
  654.6 15.0 %copy-start.21 = (bf16[64,4096]{1,0:T(8,128)(2,1)S(1)}, bf16[64,4096]{1,0:T(8,128)(2,1)}, u32[]{:S(2)}) copy-start(bf16[64,4096]{1,0:T(8,128)(2,1)} %v_ref.1) | copy-start | bytes 1572868
  (50 other events, 209.9 us)
Sparse Core Ops, SparseCore 0:
  51.5 46.4 all-gather.4
  116.1 81.5 all-gather.6
  207.4 48.6 reduce-scatter.4
  260.4 44.9 all-gather.8
  340.1 47.7 reduce-scatter.6
  391.8 45.2 all-gather.10
  450.0 91.6 reduce-scatter.8
  550.6 51.8 reduce-scatter.10
